TPU v7x, 256 devices: a whole 4x4x8 slice. The times are simulated.
256 devices in a mesh: req: 8 (over z_lo, core), tile: 16 (over x, y), blk: 2 (over z_hi).
Axes of the slice: x: 4, y: 4, z: 8 (z_hi: 2, z_lo: 4; z = z_hi * 4 + z_lo), core: 2. Of those that a mesh axis runs over, the one named last changes fastest.
Arguments:
- image_tokens: bfloat16 [16, 1024, 1536], P(('req', 'blk'), 'tile'), may hold values from -6 to 6
- latent: float32 [16, 512, 128], P(('req', 'blk'), 'tile'), may hold values from -6 to 6
- modulation: float32 [16, 8, 1536], P(('req', 'blk')), may hold values from -3 to 3
- text_kv: bfloat16 [16, 154, 2, 1536], P(('req', 'blk')), as said below
- text_len: int32 [16], P(('req', 'blk')), may hold values from 38 to 154, as said below
- timestep: int32 [16], P(('req', 'blk')), may hold values from 0 to 7
- w_qkv: bfloat16 [1536, 3, 1536], P(None, None, 'tile'), may hold values from -0.15625 to 0.15625
- w_out: bfloat16 [1536, 1536], P('tile'), may hold values from -0.15625 to 0.15625
- w_up: bfloat16 [1536, 6144], P(None, 'tile'), may hold values from -0.15625 to 0.15625
- w_down: bfloat16 [6144, 1536], P('tile'), may hold values from -0.078125 to 0.078125
- w_final: bfloat16 [1536, 64], replicated, may hold values from -0.15625 to 0.15625
Outputs:
- image_state: bfloat16 [16, 1024, 1536], P(('req', 'blk'), 'tile')
- latent_next: float32 [16, 512, 128], P(('req', 'blk'), 'tile')
Inputs may be any that keep to these rules, and one draw needn't show every extreme that they name: `text_len`: each request has 38 to 154 live text tokens; some request has 154 and some 154 // 4. `text_kv`: keys and values of text tokens, finite.
All inputs are finite; a program needn't handle non-finite values.
Results may differ from a plain program's by a relative error of at most 0.014.
Values may be sent and summed in bfloat16 or wider, within the bound.
No kernel may reach another device: no remote copies, remote signals or barrier semaphores. Data moves between devices by JAX's collectives and lax.ppermute only.
A program may use at most 64 MiB of HBM per device.

v0:
```python
import jax
import jax.numpy as jnp
from jax import lax
from jax.sharding import PartitionSpec as P

HEAD_DIM = 64
TXT = 154
STEPS = 8


def normed(value, shift, scale):
    full = value.astype(jnp.float32)
    mean = jnp.mean(full, axis=-1, keepdims=True)
    spread = jnp.mean(jnp.square(full - mean), axis=-1, keepdims=True)
    return (full - mean) * lax.rsqrt(spread + 1e-06) * (1.0 + scale) + shift


def sigma_at(index):
    frac = 1.0 - index.astype(jnp.float32) / STEPS
    return 3.0 * frac / (1.0 + 2.0 * frac)


def on_device(
    image_tokens,
    latent,
    modulation,
    text_kv,
    text_len,
    timestep,
    w_qkv,
    w_out,
    w_up,
    w_down,
    w_final,
):
    tokens = image_tokens[0]
    mods = modulation[0]
    rows_here = tokens.shape[0]
    width = tokens.shape[1]
    heads = width // HEAD_DIM
    scale_factor = HEAD_DIM ** (-0.5)
    h1 = normed(tokens, mods[0], mods[1]).astype(jnp.bfloat16)
    qkv_all = jnp.einsum(
        "nd,dkc->nkc",
        lax.all_gather(h1, "tile", axis=0, tiled=True),
        w_qkv,
        preferred_element_type=jnp.float32,
    ).astype(jnp.bfloat16)
    qkv = lax.all_to_all(qkv_all, "tile", split_axis=0, concat_axis=2, tiled=True)
    query = qkv[:, 0].reshape(rows_here, heads, HEAD_DIM)
    keyval = qkv[:, 1:]
    text_pair = text_kv[0]
    text_keys = text_pair[:, 0].reshape(TXT, heads, HEAD_DIM)
    text_values = text_pair[:, 1].reshape(TXT, heads, HEAD_DIM)
    live = jnp.arange(TXT, dtype=jnp.int32) < text_len[0]
    text_scores = (
        jnp.einsum("qhe,khe->hqk", query, text_keys, preferred_element_type=jnp.float32)
        * scale_factor
    )
    text_scores = jnp.where(live[None, None, :], text_scores, -jnp.inf)
    top_start = jnp.max(text_scores, axis=-1)
    text_weights = jnp.exp(text_scores - top_start[:, :, None])
    total_start = jnp.sum(text_weights, axis=-1)
    acc_start = jnp.einsum(
        "hqk,khe->hqe",
        text_weights.astype(jnp.bfloat16),
        text_values,
        preferred_element_type=jnp.float32,
    )
    piece = lax.all_gather(keyval, "tile", axis=0, tiled=True)
    total = total_start
    acc = acc_start
    count = piece.shape[0]
    piece_keys = piece[:, 0].reshape(count, heads, HEAD_DIM)
    piece_values = piece[:, 1].reshape(count, heads, HEAD_DIM)
    scores = (
        jnp.einsum("qhe,khe->hqk", query, piece_keys, preferred_element_type=jnp.float32)
        * scale_factor
    )
    new_top = jnp.maximum(top_start, jnp.max(scores, axis=-1))
    factor = jnp.exp(top_start - new_top)
    weights = jnp.exp(scores - new_top[:, :, None])
    total = total * factor + jnp.sum(weights, axis=-1)
    acc = acc * factor[:, :, None] + jnp.einsum(
        "hqk,khe->hqe",
        weights.astype(jnp.bfloat16),
        piece_values,
        preferred_element_type=jnp.float32,
    )
    summed = acc / total[:, :, None]
    attended = jnp.transpose(summed, (1, 0, 2)).reshape(rows_here, width).astype(jnp.bfloat16)
    columns = lax.all_to_all(attended, "tile", split_axis=1, concat_axis=0, tiled=True)
    block_rows = columns
    proj = lax.psum_scatter(
        jnp.dot(block_rows, w_out, preferred_element_type=jnp.float32).astype(jnp.bfloat16),
        "tile",
        scatter_dimension=0,
        tiled=True,
    ).astype(jnp.float32)
    second = (tokens.astype(jnp.float32) + mods[2] * proj).astype(jnp.bfloat16)
    h2 = normed(second, mods[3], mods[4]).astype(jnp.bfloat16)
    hidden = jax.nn.gelu(
        jnp.dot(
            lax.all_gather(h2, "tile", axis=0, tiled=True), w_up, preferred_element_type=jnp.float32
        ),
        approximate=True,
    ).astype(jnp.bfloat16)
    block_rows = hidden
    ffn = lax.psum_scatter(
        jnp.dot(block_rows, w_down, preferred_element_type=jnp.float32).astype(jnp.bfloat16),
        "tile",
        scatter_dimension=0,
        tiled=True,
    ).astype(jnp.float32)
    state = (second.astype(jnp.float32) + mods[5] * ffn).astype(jnp.bfloat16)
    final_in = normed(state, mods[6], mods[7]).astype(jnp.bfloat16)
    velocity = jnp.dot(final_in, w_final, preferred_element_type=jnp.float32)
    step_index = timestep[0]
    delta = sigma_at(step_index + 1) - sigma_at(step_index)
    moved = latent[0] + delta * velocity.reshape(rows_here // 2, 2 * velocity.shape[1])
    return (state[None], moved[None])


def solution(mesh):
    in_specs = (
        P(("req", "blk"), "tile", None),
        P(("req", "blk"), "tile", None),
        P(("req", "blk"), None, None),
        P(("req", "blk"), None, None, None),
        P(("req", "blk")),
        P(("req", "blk")),
        P(None, None, "tile"),
        P("tile", None),
        P(None, "tile"),
        P("tile", None),
        P(),
    )
    out_specs = (P(("req", "blk"), "tile", None), P(("req", "blk"), "tile", None))
    return jax.shard_map(
        on_device, mesh=mesh, in_specs=in_specs, out_specs=out_specs, check_vma=False
    )
```

profile of v0, /device:TPU:128, one launch (start us, length us, event | category | flops | bytes accessed | tf_op | source)
XLA Modules:
  0.0 428.8 jit_solution(14177773688961563732)
XLA Ops:
  7.2 1.4 add_reduce_fusion
  8.6 1.1 convert_reduce_fusion.2
  9.7 1.2 fusion.46
  10.8 1.8 fusion.49
  12.7 54.6 %all-gather.4.cloned.1.call-done = bf16[1024,1536]{1,0:T(8,128)(2,1)} async-done(((bf16[64,1536]{1,0:T(8,128)(2,1)}), bf16[1024,1536]{1,0:T(8,128)(2,1)}) %all-gather.4.cloned.1.call-update) | async-done | bytes 3145744 | tf_op jit(solution)/shard_map/all_gather | solution.py:45
  67.3 3.2 fusion.74
  70.6 0.7 copy.25
  71.3 20.9 %all_to_all.34 = bf16[1024,3,96]{2,1,0:T(4,128)(2,1)S(1)} all-to-all(bf16[1024,3,96]{2,1,0:T(4,128)(2,1)S(1)} %copy.25), channel_id=1, replica_groups=mesh['req'=8,'tile'=16,'blk'=2] {'tile'}, dimensions={0} | all-to-all | bytes 1179648 | tf_op jit(solution)/shard_map/all_to_all | solution.py:49
  92.9 0.9 all_to_all.28
  93.8 0.9 slice.67
  94.8 2.1 fusion.70
  96.9 3.1 copy.28
  100.7 1.9 copy.30
  102.8 1.6 fusion.71
  105.0 54.2 %all-gather.6.cloned.1.call-done = bf16[1024,2,1536]{2,0,1:T(8,128)(2,1)} async-done(((bf16[64,2,1536]{2,0,1:T(8,128)(2,1)}), bf16[1024,2,1536]{2,0,1:T(8,128)(2,1)}) %all-gather.6.cloned.1.call-update) | async-done | bytes 6291472 | tf_op jit(solution)/shard_map/all_gather | solution.py:70
  159.1 5.9 %fusion.69 = (bf16[1024,1,1536]{2,0,1:T(8,128)(2,1)}, bf16[1024,1,1536]{2,0,1:T(8,128)(2,1)}) fusion(bf16[1024,2,1536]{2,0,1:T(8,128)(2,1)} %all-gather.6.cloned.1.call-done), kind=kLoop, calls=%fused_computation.94 | loop fusion | bytes 12582912 | tf_op jit(solution)/shard_map/slice | solution.py:74
  165.0 4.6 %copy.33 = bf16[1024,1,1536]{0,2,1:T(8,128)(2,1)} copy(bf16[1024,1,1536]{2,0,1:T(8,128)(2,1)} %get-tuple-element.17) | data formatting | bytes 6291456 | tf_op jit(solution)/shard_map/slice | solution.py:75
  169.7 4.7 %copy.31 = bf16[1024,1,1536]{0,2,1:T(8,128)(2,1)} copy(bf16[1024,1,1536]{2,0,1:T(8,128)(2,1)} %get-tuple-element.16) | data formatting | bytes 6291456 | tf_op jit(solution)/shard_map/slice | solution.py:74
  174.4 2.9 multiply_reduce_fusion
  177.3 1.3 fusion
  179.2 1.6 fusion.16
  180.8 0.8 fusion.22
  182.3 13.6 %all_to_all.35 = bf16[64,16,96]{2,0,1:T(8,128)(2,1)S(1)} all-to-all(bf16[64,16,96]{2,0,1:T(8,128)(2,1)S(1)} %copy.35), channel_id=1, replica_groups=mesh['req'=8,'tile'=16,'blk'=2] {'tile'}, dimensions={1} | all-to-all | bytes 393216 | tf_op jit(solution)/shard_map/all_to_all | solution.py:92
  195.8 2.6 convolution_convert_fusion.1
  198.5 79.0 %reduce-scatter.3.cloned.1.call-done = bf16[64,1536]{1,0:T(8,128)(2,1)} async-done(((bf16[1024,1536]{1,0:T(8,128)(2,1)}), bf16[64,1536]{1,0:T(8,128)(2,1)}) %reduce-scatter.3.cloned.1.call-update) | async-done | bytes 196624 | tf_op jit(solution)/shard_map/reduce_scatter | solution.py:94
  277.6 1.1 convert_reduce_fusion
  278.9 0.8 fusion.41
  279.9 53.0 %all-gather.8.cloned.1.call-done = bf16[1024,1536]{1,0:T(8,128)(2,1)} async-done(((bf16[64,1536]{1,0:T(8,128)(2,1)}), bf16[1024,1536]{1,0:T(8,128)(2,1)}) %all-gather.8.cloned.1.call-update) | async-done | bytes 3145744 | tf_op jit(solution)/shard_map/all_gather | solution.py:104
  332.8 7.2 %convolution_convert_fusion = bf16[1024,1536]{1,0:T(8,128)(2,1)} fusion(bf16[384,1536]{1,0:T(8,128)(2,1)S(1)} %copy-done, bf16[1024,1536]{1,0:T(8,128)(2,1)} %all-gather.8.cloned.1.call-done, bf16[1536,384]{1,0:T(8,128)(2,1)S(1)} %copy-done.9), kind=kOutput, calls=%fused_computation.4 | convolution fusion | flops 2421030912 | bytes 8650752 | tf_op jit(solution)/shard_map/dot_general | solution.py:110
  340.8 79.1 %reduce-scatter.5.cloned.1.call-done = bf16[64,1536]{1,0:T(8,128)(2,1)} async-done(((bf16[1024,1536]{1,0:T(8,128)(2,1)}), bf16[64,1536]{1,0:T(8,128)(2,1)}) %reduce-scatter.5.cloned.1.call-update) | async-done | bytes 196624 | tf_op jit(solution)/shard_map/reduce_scatter | solution.py:109
  420.0 1.1 convert_reduce_fusion.1
  421.7 0.6 add.157
  (55 shorter events, 3.9 us)
Async XLA Ops:
  7.2 325.7 %copy-start = (bf16[384,1536]{1,0:T(8,128)(2,1)S(1)}, bf16[384,1536]{1,0:T(8,128)(2,1)}, u32[]{:S(2)}) copy-start(bf16[384,1536]{1,0:T(8,128)(2,1)} %param.20) | copy-start | bytes 3538948
  7.2 60.1 %all-gather.4.cloned.1.call-start = ((), (), s32[]{:S(2)}) async-start(), calls=%async_computation.4 | async-start | bytes 3342336 | tf_op jit(solution)/shard_map/all_gather | solution.py:45
  12.6 146.5 %all-gather.6.cloned.1.call-start = ((), (), s32[]{:S(2)}) async-start(), calls=%async_computation.5 | async-start | bytes 6684672 | tf_op jit(solution)/shard_map/all_gather | solution.py:70
  92.2 2.6 copy-start.2
  93.8 1.1 copy-start.4
  94.7 182.9 %reduce-scatter.3.cloned.1.call-start = ((), (), s32[]{:S(2)}) async-start(), calls=%async_computation.6 | async-start | bytes 3342336 | tf_op jit(solution)/shard_map/reduce_scatter | solution.py:94
  94.8 7.8 %slice-start = ((bf16[64,3,1536]{2,0,1:T(8,128)(2,1)}), bf16[64,1,1536]{2,0,1:T(8,128)(2,1)S(1)}, s32[]{:S(2)}) async-start(bf16[64,3,1536]{2,0,1:T(8,128)(2,1)} %copy-done.4), calls=%async_computation.9 | async-start | bytes 393216 | tf_op jit(solution)/shard_map/slice | solution.py:50
  177.3 1.9 copy-start.1
  179.2 1.6 copy-start.5
  180.8 15.0 %copy-start.7 = (bf16[96,1536]{1,0:T(8,128)(2,1)S(1)}, bf16[96,1536]{1,0:T(8,128)(2,1)}, u32[]{:S(2)}) copy-start(bf16[96,1536]{1,0:T(8,128)(2,1)} %param.18) | copy-start | bytes 884740
  195.8 81.8 %copy-start.3 = (bf16[1,64,1536]{2,1,0:T(8,128)(2,1)S(1)}, bf16[1,64,1536]{2,1,0:T(8,128)(2,1)}, u32[]{:S(2)}) copy-start(bf16[1,64,1536]{2,1,0:T(8,128)(2,1)} %param.11) | copy-start | bytes 589828
  198.5 134.4 %copy-start.9 = (bf16[1536,384]{1,0:T(8,128)(2,1)S(1)}, bf16[1536,384]{1,0:T(8,128)(2,1)}, u32[]{:S(2)}) copy-start(bf16[1536,384]{1,0:T(8,128)(2,1)} %param.19) | copy-start | bytes 3538948
  198.5 134.3 %all-gather.8.cloned.1.call-start = ((), (), s32[]{:S(2)}) async-start(), calls=%async_computation.7 | async-start | bytes 3342336 | tf_op jit(solution)/shard_map/all_gather | solution.py:104
  279.8 140.2 %reduce-scatter.5.cloned.1.call-start = ((), (), s32[]{:S(2)}) async-start(), calls=%async_computation.8 | async-start | bytes 3342336 | tf_op jit(solution)/shard_map/reduce_scatter | solution.py:109
  340.0 81.3 %copy-start.10 = (bf16[1536,64]{0,1:T(8,128)(2,1)S(1)}, bf16[1536,64]{0,1:T(8,128)(2,1)}, u32[]{:S(2)}) copy-start(bf16[1536,64]{0,1:T(8,128)(2,1)} %param.21) | copy-start | bytes 589828
  340.0 81.7 %copy-start.8 = (f32[1,32,128]{2,1,0:T(8,128)S(1)}, f32[1,32,128]{2,1,0:T(8,128)}, u32[]{:S(2)}) copy-start(f32[1,32,128]{2,1,0:T(8,128)} %param.12) | copy-start | bytes 49156
  421.1 1.2 copy-start.6
Sparse Core Ops, SparseCore 0:
  12.7 54.4 all-gather.3
  94.8 64.2 all-gather.5
  198.6 78.9 reduce-scatter.2
  280.5 52.2 all-gather.7
  340.2 79.7 reduce-scatter.4
where the time goes:
time: 431 us; the launch traced here: 429 us
  waiting for transfers between devices  320 us (74%)
  blocking collectives  34.5 us (8%)
  local copies, waits for them, and re-layouts  27 us (6%)
  matrix products  20.2 us (5%)
  between operations  15.4 us (4%)
  other arithmetic  11.4 us (3%)
    reduce_scatter x1, waiting for transfers between devices, on_device(): lax.psum_scatter(jnp.dot(block_rows, w_down, preferred_element_type=jnp.f...  79.1 us
    reduce_scatter x1, waiting for transfers between devices, on_device(): lax.psum_scatter(jnp.dot(block_rows, w_out, preferred_element_type=jnp.fl...  79 us
    all_gather x1, waiting for transfers between devices, on_device(): lax.all_gather(h1, 'tile', axis=0, tiled=True)  54.6 us
    all_gather x1, waiting for transfers between devices, on_device(): piece = lax.all_gather(keyval, 'tile', axis=0, tiled=True)  54.2 us
    all_gather x1, waiting for transfers between devices, on_device(): lax.all_gather(h2, 'tile', axis=0, tiled=True)  53 us
    all_to_all x1, blocking collectives, on_device(): lax.all_to_all(qkv_all, 'tile', split_axis=0, concat_axis=2, tiled=True)  20.9 us
    all_to_all x1, blocking collectives, on_device(): lax.all_to_all(attended, 'tile', split_axis=1, concat_axis=0, tiled=True)  13.6 us
    slice x2, local copies, waits for them, and re-layouts, on_device(): piece_keys = piece[:, 0].reshape(count, heads, HEAD_DIM)  10.6 us
  transfers between devices with their start and end apart: 5, of which 5 were waited for; matrix products, arithmetic and copies ran while one was open for 2% of the time, Pallas kernels for 0%

commit v1 on v0

v1 whole, which is shorter than its diff:
```python
import functools

import jax
import jax.numpy as jnp
from jax import lax
from jax.experimental import pallas as pl
from jax.experimental.pallas import tpu as pltpu
from jax.sharding import Mesh, PartitionSpec as P

HEAD_DIM = 64
TXT = 154
STEPS = 8
BF = jnp.bfloat16
F32 = jnp.float32
NT = (((1,), (1,)), ((), ()))
NN = (((1,), (0,)), ((), ()))


def params():
    return pltpu.CompilerParams(vmem_limit_bytes=50 * 1024 * 1024)


def layer_norm(full, shift, scale):
    mean = jnp.mean(full, axis=-1, keepdims=True)
    cent = full - mean
    spread = jnp.mean(jnp.square(cent), axis=-1, keepdims=True)
    return cent * lax.rsqrt(spread + 1e-06) * (1.0 + scale) + shift


def sigma_at(index):
    frac = 1.0 - index.astype(F32) / STEPS
    return 3.0 * frac / (1.0 + 2.0 * frac)


def norm_kernel(copies, x_ref, mod_ref, out_ref):
    h = layer_norm(x_ref[...].astype(F32), mod_ref[0:1, :], mod_ref[1:2, :]).astype(BF)
    for i in range(copies):
        out_ref[i] = h


def first_norm(tokens, mods, copies):
    rows, width = tokens.shape
    return pl.pallas_call(
        functools.partial(norm_kernel, copies),
        out_shape=jax.ShapeDtypeStruct((copies, rows, width), BF),
        compiler_params=params(),
        name="first_norm",
    )(tokens, mods)


def qkv_kernel(pos_ref, h_ref, own_ref, near_ref, far_ref, out_ref, w_ref):
    side = pos_ref[0]
    core = pos_ref[1]
    for k in range(3):
        w_ref[k, side, 0] = own_ref[k, 0:48, :]
        w_ref[k, side, 1] = own_ref[k, 48:96, :]
        w_ref[k, 1 - side, core] = near_ref[k]
        w_ref[k, 1 - side, 1 - core] = far_ref[k]
    h = h_ref[...]
    for k in range(3):
        w = w_ref[k].reshape(192, h.shape[1])
        out_ref[k] = lax.dot_general(h, w, NT, preferred_element_type=F32).astype(BF)


def project_qkv(pos, h, own, near, far):
    rows, width = h.shape
    return pl.pallas_call(
        qkv_kernel,
        out_shape=jax.ShapeDtypeStruct((3, rows, 192), BF),
        in_specs=[pl.BlockSpec(memory_space=pltpu.SMEM)]
        + [pl.BlockSpec(memory_space=pltpu.VMEM)] * 4,
        scratch_shapes=[pltpu.VMEM((3, 2, 2, 48, width), BF)],
        compiler_params=params(),
        name="project_qkv",
    )(pos, h, own, near, far)


QB = 256


def own_attention_kernel(len_ref, q_ref, kv_ref, text_ref, acc_ref, top_ref, tot_ref):
    lane = lax.broadcasted_iota(jnp.int32, (QB, 192), 1) // HEAD_DIM
    live = lax.broadcasted_iota(jnp.int32, (QB, TXT), 1) < len_ref[0]
    keys = kv_ref[0]
    values = kv_ref[1]
    tkeys = text_ref[0]
    tvalues = text_ref[1]
    for b in range(q_ref.shape[0] // QB):
        rows = pl.ds(b * QB, QB)
        q = q_ref[rows, :]
        acc = jnp.zeros((QB, 192), F32)
        tops = jnp.zeros((QB, 192), F32)
        tots = jnp.zeros((QB, 192), F32)
        for h in range(3):
            here = lane == h
            qh = jnp.where(here, q, jnp.zeros_like(q))
            s = lax.dot_general(qh, keys, NT, preferred_element_type=F32) * 0.125
            st = lax.dot_general(qh, tkeys, NT, preferred_element_type=F32) * 0.125
            st = jnp.where(live, st, -jnp.inf)
            top = jnp.maximum(
                jnp.max(s, axis=1, keepdims=True), jnp.max(st, axis=1, keepdims=True)
            )
            p = jnp.exp(s - top)
            pt = jnp.exp(st - top)
            tot = jnp.sum(p, axis=1, keepdims=True) + jnp.sum(pt, axis=1, keepdims=True)
            part = lax.dot_general(p.astype(BF), values, NN, preferred_element_type=F32)
            part += lax.dot_general(pt.astype(BF), tvalues, NN, preferred_element_type=F32)
            acc = jnp.where(here, part, acc)
            tops = jnp.where(here, top, tops)
            tots = jnp.where(here, tot, tots)
        acc_ref[rows, :] = acc
        top_ref[rows, :] = tops
        tot_ref[rows, :] = tots


def own_attention(length, q, kv, text):
    rows = q.shape[0]
    return pl.pallas_call(
        own_attention_kernel,
        out_shape=[jax.ShapeDtypeStruct((rows, 192), F32)] * 3,
        in_specs=[pl.BlockSpec(memory_space=pltpu.SMEM)]
        + [pl.BlockSpec(memory_space=pltpu.VMEM)] * 3,
        compiler_params=params(),
        name="own_attention",
    )(length, q, kv, text)


def far_attention_kernel(q_ref, kv_ref, acc_ref, top_ref, tot_ref, out_ref):
    lane = lax.broadcasted_iota(jnp.int32, (QB, 192), 1) // HEAD_DIM
    keys = kv_ref[0]
    values = kv_ref[1]
    for b in range(q_ref.shape[0] // QB):
        rows = pl.ds(b * QB, QB)
        q = q_ref[rows, :]
        tops = top_ref[rows, :]
        acc = jnp.zeros((QB, 192), F32)
        new_tops = tops
        tots = jnp.zeros((QB, 192), F32)
        for h in range(3):
            here = lane == h
            qh = jnp.where(here, q, jnp.zeros_like(q))
            s = lax.dot_general(qh, keys, NT, preferred_element_type=F32) * 0.125
            old = tops[:, h * HEAD_DIM : h * HEAD_DIM + 1]
            top = jnp.maximum(jnp.max(s, axis=1, keepdims=True), old)
            p = jnp.exp(s - top)
            tot = jnp.sum(p, axis=1, keepdims=True)
            part = lax.dot_general(p.astype(BF), values, NN, preferred_element_type=F32)
            acc = jnp.where(here, part, acc)
            new_tops = jnp.where(here, top, new_tops)
            tots = jnp.where(here, tot, tots)
        factor = jnp.exp(tops - new_tops)
        total = tot_ref[rows, :] * factor + tots
        out_ref[rows, :] = ((acc_ref[rows, :] * factor + acc) / total).astype(BF)


def far_attention(q, kv, acc, top, tot):
    return pl.pallas_call(
        far_attention_kernel,
        out_shape=jax.ShapeDtypeStruct(q.shape, BF),
        compiler_params=params(),
        name="far_attention",
    )(q, kv, acc, top, tot)


def out_kernel(a_ref, w_ref, out_ref):
    out_ref[...] = lax.dot_general(
        a_ref[...], w_ref[...], NN, preferred_element_type=F32
    ).astype(BF)


def out_projection(a, w):
    return pl.pallas_call(
        out_kernel,
        out_shape=jax.ShapeDtypeStruct((a.shape[0], w.shape[1]), BF),
        compiler_params=params(),
        name="out_projection",
    )(a, w)


def second_norm_kernel(x_ref, part_ref, mod_ref, second_ref, out_ref):
    proj = part_ref[0].astype(F32)
    for i in range(1, part_ref.shape[0]):
        proj += part_ref[i].astype(F32)
    second = (x_ref[...].astype(F32) + mod_ref[2:3, :] * proj).astype(BF)
    second_ref[...] = second
    h = layer_norm(second.astype(F32), mod_ref[3:4, :], mod_ref[4:5, :]).astype(BF)
    for i in range(out_ref.shape[0]):
        out_ref[i] = h


def second_norm(tokens, parts, mods):
    return pl.pallas_call(
        second_norm_kernel,
        out_shape=[
            jax.ShapeDtypeStruct(tokens.shape, BF),
            jax.ShapeDtypeStruct(parts.shape, BF),
        ],
        compiler_params=params(),
        name="second_norm",
    )(tokens, parts, mods)


def ffn_kernel(h_ref, up_ref, down_ref, out_ref, acc_ref):
    step = pl.program_id(0)
    part = up_ref.shape[-1]
    hidden = jax.nn.gelu(
        lax.dot_general(h_ref[...], up_ref[0, 0], NN, preferred_element_type=F32),
        approximate=True,
    ).astype(BF)
    for s in range(4):
        value = lax.dot_general(
            hidden,
            down_ref[0, 0, s * part : (s + 1) * part, :],
            NN,
            preferred_element_type=F32,
        )
        cols = slice(s * part, (s + 1) * part)

        @pl.when(step == 0)
        def _():
            acc_ref[:, cols] = value

        @pl.when(step > 0)
        def _():
            acc_ref[:, cols] += value

    @pl.when(step == pl.num_programs(0) - 1)
    def _():
        out_ref[...] = acc_ref[...].astype(BF)


def feed_forward(h, weights):
    rows, width = h.shape
    part = weights.shape[3]
    return pl.pallas_call(
        ffn_kernel,
        grid=(4,),
        out_shape=jax.ShapeDtypeStruct((rows, width), BF),
        in_specs=[
            pl.BlockSpec((rows, width), lambda i: (0, 0)),
            pl.BlockSpec((1, 1, width, part), lambda i: (0, i, 0, 0)),
            pl.BlockSpec((1, 1, width, part), lambda i: (1, i, 0, 0)),
        ],
        out_specs=pl.BlockSpec((rows, width), lambda i: (0, 0)),
        scratch_shapes=[pltpu.VMEM((rows, width), F32)],
        compiler_params=params(),
        name="feed_forward",
    )(h, weights, weights)


def last_kernel(second_ref, part_ref, mod_ref, w_ref, state_ref, vel_ref):
    ffn = part_ref[0].astype(F32)
    for i in range(1, part_ref.shape[0]):
        ffn += part_ref[i].astype(F32)
    state = (second_ref[...].astype(F32) + mod_ref[5:6, :] * ffn).astype(BF)
    state_ref[...] = state
    h = layer_norm(state.astype(F32), mod_ref[6:7, :], mod_ref[7:8, :]).astype(BF)
    vel_ref[...] = lax.dot_general(h, w_ref[...], NN, preferred_element_type=F32)


def last_stage(second, parts, mods, w_final):
    return pl.pallas_call(
        last_kernel,
        out_shape=[
            jax.ShapeDtypeStruct(second.shape, BF),
            jax.ShapeDtypeStruct((second.shape[0], w_final.shape[1]), F32),
        ],
        compiler_params=params(),
        name="last_stage",
    )(second, parts, mods, w_final)


def on_device(
    image_tokens,
    latent,
    modulation,
    text_kv,
    text_len,
    timestep,
    w_qkv,
    w_out,
    w_up,
    w_down,
    w_final,
):
    tokens = image_tokens[0]
    mods = modulation[0]
    rows, width = tokens.shape
    core = lax.axis_index("core")
    side = lax.axis_index("yl")
    high = lax.axis_index("yh")
    swap2 = [(0, 1), (1, 0)]

    own_qkv = jnp.transpose(w_qkv, (1, 2, 0))
    half_qkv = lax.dynamic_slice_in_dim(own_qkv, core * 48, 48, 1)
    near_qkv = lax.ppermute(half_qkv, "yl", swap2)
    far_qkv = lax.ppermute(near_qkv, "core", swap2)

    half_out = lax.dynamic_slice_in_dim(w_out, core * 48, 48, 0)
    out_full = lax.all_gather(half_out, ("yh", "yl", "core"), axis=0, tiled=True)

    part = w_up.shape[1]
    slabs = jnp.transpose(w_down.reshape(part, 4, part), (1, 0, 2)).reshape(width, part)
    half_ffn = jnp.where(core == 0, w_up, slabs)
    ffn_full = lax.all_gather(half_ffn, ("core", "yh", "yl"), axis=0, tiled=False)
    ffn_full = ffn_full.reshape(2, 4, width, part)

    h1 = first_norm(tokens, mods, 8)
    h1 = lax.all_to_all(h1, ("tx", "yh"), split_axis=0, concat_axis=0, tiled=True)
    h1 = h1.reshape(8 * rows, width)
    pos = jnp.stack([side, core]).astype(jnp.int32)
    qkv = project_qkv(pos, h1, own_qkv, near_qkv, far_qkv)
    kv_far = lax.ppermute(qkv[1:], "yl", swap2)

    head_cols = (lax.axis_index("tx") * 2 + high) * 192
    text = lax.dynamic_slice_in_dim(text_kv[0], head_cols, 192, 2)
    text = jnp.transpose(text, (1, 0, 2))
    acc, top, tot = own_attention(text_len, qkv[0], qkv[1:], text)
    attended = far_attention(qkv[0], kv_far, acc, top, tot)

    lines = attended.reshape(4, 2, rows, 192)
    mine = lax.dynamic_index_in_dim(lines, high, 1, False)
    other = lax.dynamic_index_in_dim(lines, 1 - high, 1, False)
    got = lax.ppermute(other, "yh", swap2)
    low = jnp.where(high == 0, mine, got)
    upper = jnp.where(high == 0, got, mine)
    joined = jnp.concatenate([low, upper], axis=2).reshape(4 * rows, 384)

    partial = out_projection(joined, out_full).reshape(4, rows, width)
    partial = lax.all_to_all(partial, "tx", split_axis=0, concat_axis=0, tiled=True)
    second, h2 = second_norm(tokens, partial, mods)
    h2 = lax.all_to_all(h2, "tx", split_axis=0, concat_axis=0, tiled=True)
    partial = feed_forward(h2.reshape(4 * rows, width), ffn_full).reshape(4, rows, width)
    partial = lax.all_to_all(partial, "tx", split_axis=0, concat_axis=0, tiled=True)
    state, velocity = last_stage(second, partial, mods, w_final)

    step_index = timestep[0]
    delta = sigma_at(step_index + 1) - sigma_at(step_index)
    moved = latent[0] + delta * velocity.reshape(rows // 2, 2 * velocity.shape[1])
    return (state[None], moved[None])


def solution(mesh):
    fine = Mesh(
        mesh.devices.reshape(mesh.shape["req"] // 2, 2, 4, 2, 2, mesh.shape["blk"]),
        ("zl", "core", "tx", "yh", "yl", "blk"),
    )
    group = ("zl", "core", "blk")
    tile = ("tx", "yh", "yl")
    in_specs = (
        P(group, tile, None),
        P(group, tile, None),
        P(group, None, None),
        P(group, None, None, None),
        P(group),
        P(group),
        P(None, None, tile),
        P(tile, None),
        P(None, tile),
        P(tile, None),
        P(),
    )
    out_specs = (P(group, tile, None), P(group, tile, None))
    return jax.shard_map(
        on_device, mesh=fine, in_specs=in_specs, out_specs=out_specs, check_vma=False
    )
```

time: 431 us -> 157 us (0.36)
  waiting for transfers between devices: 320 us -> 63.8 us
  Pallas kernels: 0 us -> 20.9 us
  matrix products: 20.2 us -> 0 us
  starting transfers between devices: 0.21 us -> 17.6 us
  local copies, waits for them, and re-layouts: 27 us -> 10.1 us
  other arithmetic: 11.4 us -> 2.1 us
  blocking collectives: 34.5 us -> 25.6 us
    all_gather x3 -> x2, waiting for transfers between devices: 162 us -> 0.02 us  [the longest x1 0.02 us: on_device(): lax.all_gather(half_out, ('yh', 'yl', 'core'), axis=0, tiled=True)]
    reduce_scatter x2 -> x0, waiting for transfers between devices: 158 us -> none  [the longest x1 79.1 us: on_device(): lax.psum_scatter(jnp.dot(block_rows, w_down, preferred_element_type=jnp.f...]
    ppermute x0 -> x4, waiting for transfers between devices: none -> 55.3 us  [the longest x1 31.6 us: on_device(): near_qkv = lax.ppermute(half_qkv, 'yl', swap2)]
    slice x9 -> x1, local copies, waits for them, and re-layouts: 23.2 us -> 0.04 us  [on_device(): kv_far = lax.ppermute(qkv[1:], 'yl', swap2)]
    pallas_call x0 -> x8, Pallas kernels: none -> 20.9 us  [the longest x1 9.88 us: feed_forward(): pl.pallas_call(ffn_kernel, grid=(4,), out_shape=jax.ShapeDtypeStruct((row...]
    dot_general x7 -> x0, matrix products: 17 us -> none  [the longest x1 7.19 us: on_device(): jnp.dot(block_rows, w_down, preferred_element_type=jnp.float32)]
    all_to_all x0 -> x2, starting transfers between devices: none -> 10.7 us  [the longest x1 7.06 us: on_device(): lax.all_to_all(h1, ('tx', 'yh'), split_axis=0, concat_axis=0, tiled=True)]
    all_to_all x2, blocking collectives: 34.5 us -> 25.6 us  [the longest x1 13.8 us: on_device(): lax.all_to_all(partial, 'tx', split_axis=0, concat_axis=0, tiled=True)]
  transfers between devices with their start and end apart: 5 -> 8, of which waited for: 5 -> 5; matrix products, arithmetic and copies ran while one was open for 2% -> 3% of each run, Pallas kernels for 0% -> 6%
where the time goes in v1:
time: 157 us; the launch traced here: 156 us
  waiting for transfers between devices  63.8 us (41%)
  blocking collectives  25.6 us (16%)
  Pallas kernels  20.9 us (13%)
  starting transfers between devices  17.6 us (11%)
  between operations  15.7 us (10%)
  local copies, waits for them, and re-layouts  10.1 us (6%)
  other arithmetic  2.1 us (1%)
    ppermute x1, waiting for transfers between devices, on_device(): near_qkv = lax.ppermute(half_qkv, 'yl', swap2)  31.6 us
    ppermute x1, waiting for transfers between devices, on_device(): kv_far = lax.ppermute(qkv[1:], 'yl', swap2)  15.8 us
    all_to_all x1, blocking collectives, on_device(): lax.all_to_all(partial, 'tx', split_axis=0, concat_axis=0, tiled=True)  13.8 us
    all_to_all x1, blocking collectives, on_device(): h2 = lax.all_to_all(h2, 'tx', split_axis=0, concat_axis=0, tiled=True)  11.9 us
    pallas_call x1, Pallas kernels, feed_forward(): pl.pallas_call(ffn_kernel, grid=(4,), out_shape=jax.ShapeDtypeStruct((row...  9.88 us
    all_to_all x1, waiting for transfers between devices, on_device(): lax.all_to_all(partial, 'tx', split_axis=0, concat_axis=0, tiled=True)  8.44 us
    all_to_all x1, starting transfers between devices, on_device(): lax.all_to_all(h1, ('tx', 'yh'), split_axis=0, concat_axis=0, tiled=True)  7.06 us
    ppermute x1, waiting for transfers between devices, on_device(): got = lax.ppermute(other, 'yh', swap2)  6.16 us
  transfers between devices with their start and end apart: 8, of which 5 were waited for; matrix products, arithmetic and copies ran while one was open for 3% of the time, Pallas kernels for 6%

profile of v1, /device:TPU:128, one launch (start us, length us, event | category | flops | bytes accessed | tf_op | source)
XLA Modules:
  0.0 155.8 jit_solution(15820189123289699079)
XLA Ops:
  7.2 1.7 %constant_dynamic-slice_fusion = bf16[48,1536]{1,0:T(8,128)(2,1)} fusion(bf16[96,1536]{1,0:T(8,128)(2,1)} %param.18, s32[]{:T(128)S(6)} %select_n.35), kind=kLoop, calls=%fused_computation.9 | loop fusion | bytes 294916 | tf_op jit(solution)/shard_map/dynamic_slice | solution.py:299
  9.0 2.5 %reshape.66 = bf16[384,4,384]{2,1,0:T(4,128)(2,1)S(1)} reshape(bf16[384,1536]{1,0:T(8,128)(2,1)} %param.20) | data formatting | bytes 2359296 | tf_op jit(solution)/shard_map/reshape | solution.py:303
  11.5 0.2 copy.14
  11.7 1.1 copy-done.7
  12.8 1.3 bitcast_select_fusion
  14.1 0.9 copy-done.3
  15.0 1.5 first_norm.1
  16.4 7.1 %all-to-all-start = ((bf16[8,64,1536]{2,1,0:T(8,128)(2,1)}), bf16[8,64,1536]{2,1,0:T(8,128)(2,1)}, u32[]{:S(2)}, u32[]{:S(2)}) async-start(bf16[8,64,1536]{2,1,0:T(8,128)(2,1)} %first_norm.1), calls=%async_computation | async-start | bytes 3145728 | tf_op jit(solution)/shard_map/all_to_all | solution.py:309
  23.6 0.8 collective-permute-start
  24.3 31.6 %collective-permute-done.near_ref = bf16[3,48,1536]{2,1,0:T(8,128)(2,1)S(1)} collective-permute-done((bf16[3,48,1536]{2,1,0:T(8,128)(2,1)S(1)}, bf16[3,48,1536]{2,1,0:T(8,128)(2,1)S(1)}, u32[]{:S(2)}, u32[]{:S(2)}) %collective-permute-start) | collective-permute-done | bytes 442400 | tf_op jit(solution)/shard_map/ppermute | solution.py:296
  56.0 1.7 %collective-permute-done.1.far_ref = bf16[3,48,1536]{2,1,0:T(8,128)(2,1)S(1)} collective-permute-done((bf16[3,48,1536]{2,1,0:T(8,128)(2,1)S(1)}, bf16[3,48,1536]{2,1,0:T(8,128)(2,1)S(1)}, u32[]{:S(2)}, u32[]{:S(2)}) %collective-permute-start.1) | collective-permute-done | bytes 442400 | tf_op jit(solution)/shard_map/ppermute | solution.py:297
  57.7 0.8 copy-done.4
  58.5 1.0 copy-done.5
  59.5 2.9 %project_qkv.1 = bf16[3,512,192]{2,1,0:T(8,128)(2,1)S(1)} custom-call(s32[2]{0:T(128)S(1)} %pad_add_fusion.pos_ref, bf16[512,1536]{1,0:T(8,128)(2,1)} %bitcast.4.h_ref, bf16[3,96,1536]{2,1,0:T(8,128)(2,1)S(1)} %bitcast.33, bf16[3,48,1536]{2,1,0:T(8,128)(2,1)S(1)} %collective-permute-done.near_ref, bf16[3,48,1536]{2,1,0:T(8,128)(2,1)S(1)} %copy-done.5), custom_call_target="tpu_custom_call" | custom-call | tf_op jit(solution)/shard_map/project_qkv/pallas_call | solution.py:67
  62.5 1.4 collective-permute-start.2
  64.5 0.3 constant_dynamic-slice_fusion.1
  64.9 2.4 %own_attention.1 = (f32[512,192]{1,0:T(8,128)S(1)}, f32[512,192]{1,0:T(8,128)S(1)}, f32[512,192]{1,0:T(8,128)S(1)}) custom-call(s32[1]{0:T(128)S(6)} %copy.18.len_ref, bf16[512,192]{1,0:T(8,128)(2,1)S(1)} %slice_bitcast_fusion.q_ref, bf16[2,512,192]{2,1,0:T(8,128)(2,1)S(1)} %slice.11.kv_ref, bf16[2,154,192]{2,1,0:T(8,128)(2,1)S(1)} %bitcast.39), custom_call_target="tpu_custom_call" | custom-call | tf_op jit(solution)/shard_map/own_attention/pallas_call | solution.py:118
  67.2 15.8 %collective-permute-done.2.kv_ref = bf16[2,512,192]{2,1,0:T(8,128)(2,1)S(1)} collective-permute-done((bf16[2,512,192]{2,1,0:T(8,128)(2,1)S(1)}, bf16[2,512,192]{2,1,0:T(8,128)(2,1)S(1)}, u32[]{:S(2)}, u32[]{:S(2)}) %collective-permute-start.2) | collective-permute-done | bytes 393248 | tf_op jit(solution)/shard_map/ppermute | solution.py:313
  83.1 2.2 %far_attention.1 = bf16[512,192]{1,0:T(8,128)(2,1)S(1)} custom-call(bf16[512,192]{1,0:T(8,128)(2,1)S(1)} %slice_bitcast_fusion.q_ref, bf16[2,512,192]{2,1,0:T(8,128)(2,1)S(1)} %collective-permute-done.2.kv_ref, f32[512,192]{1,0:T(8,128)S(1)} %get-tuple-element.9.acc_ref, f32[512,192]{1,0:T(8,128)S(1)} %get-tuple-element.10.top_ref, ...), custom_call_target="tpu_custom_call" | custom-call | tf_op jit(solution)/shard_map/far_attention/pallas_call | solution.py:157
  85.3 4.7 %collective-permute-start.3 = (bf16[4,64,192]{2,1,0:T(8,128)(2,1)S(1)}, bf16[4,64,192]{2,1,0:T(8,128)(2,1)S(1)}, u32[]{:S(2)}, u32[]{:S(2)}) collective-permute-start(bf16[4,64,192]{2,1,0:T(8,128)(2,1)S(1)} %dynamic-slice_bitcast_fusion.1), channel_id=1, source_target_pairs={{0,4},{4,0},{1,5},{5,1},{2,6},{6,2},{3,7},{7,3},{8,12},{12,8},{9,1... | collective-permute-start | bytes 294920 | tf_op jit(solution)/shard_map/ppermute | solution.py:324
  90.0 6.2 %collective-permute-done.3 = bf16[4,64,192]{2,1,0:T(8,128)(2,1)S(1)} collective-permute-done((bf16[4,64,192]{2,1,0:T(8,128)(2,1)S(1)}, bf16[4,64,192]{2,1,0:T(8,128)(2,1)S(1)}, u32[]{:S(2)}, u32[]{:S(2)}) %collective-permute-start.3) | collective-permute-done | bytes 98336 | tf_op jit(solution)/shard_map/ppermute | solution.py:324
  96.3 1.3 copy-done.2
  97.6 0.6 out_projection.1
  98.2 13.8 %all_to_all.20.part_ref = bf16[4,64,1536]{2,1,0:T(8,128)(2,1)S(1)} all-to-all(bf16[4,64,1536]{2,1,0:T(8,128)(2,1)S(1)} %bitcast.32), channel_id=1, replica_groups=mesh['zl'=4,'core'=2,'tx'=4,'yh'=2,'yl'=2,'blk'=2] {'tx'}, dimensions={0} | all-to-all | bytes 1572864 | tf_op jit(solution)/shard_map/all_to_all | solution.py:330
  111.9 0.4 second_norm.1
  112.3 11.9 %all_to_all.21 = bf16[4,64,1536]{2,1,0:T(8,128)(2,1)S(1)} all-to-all(bf16[4,64,1536]{2,1,0:T(8,128)(2,1)S(1)} %get-tuple-element.13), channel_id=1, replica_groups=mesh['zl'=4,'core'=2,'tx'=4,'yh'=2,'yl'=2,'blk'=2] {'tx'}, dimensions={0} | all-to-all | bytes 1572864 | tf_op jit(solution)/shard_map/all_to_all | solution.py:332
  124.2 9.9 %feed_forward.1 = bf16[256,1536]{1,0:T(8,128)(2,1)} custom-call(bf16[256,1536]{1,0:T(8,128)(2,1)S(1)} %bitcast.31, bf16[2,4,1536,384]{3,2,1,0:T(8,128)(2,1)} %bitcast.43, bf16[2,4,1536,384]{3,2,1,0:T(8,128)(2,1)} %bitcast.44), custom_call_target="tpu_custom_call" | custom-call | tf_op jit(solution)/shard_map/feed_forward/pallas_call | solution.py:235
  134.1 3.6 %all-to-all-start.3 = ((bf16[4,64,1536]{2,1,0:T(8,128)(2,1)}), bf16[4,64,1536]{2,1,0:T(8,128)(2,1)S(1)}, u32[]{:S(2)}, u32[]{:S(2)}) async-start(bf16[4,64,1536]{2,1,0:T(8,128)(2,1)} %bitcast.19), calls=%async_computation.3 | async-start | bytes 1572864 | tf_op jit(solution)/shard_map/all_to_all | solution.py:334
  138.4 0.2 copy.15.w_ref
  138.7 8.4 %all-to-all-done.3.part_ref = bf16[4,64,1536]{2,1,0:T(8,128)(2,1)S(1)} async-done(((bf16[4,64,1536]{2,1,0:T(8,128)(2,1)}), bf16[4,64,1536]{2,1,0:T(8,128)(2,1)S(1)}, u32[]{:S(2)}, u32[]{:S(2)}) %all-to-all-start.3) | async-done | bytes 786464 | tf_op jit(solution)/shard_map/all_to_all | solution.py:334
  147.2 1.1 last_stage.1
  148.3 0.6 add.40
  (33 shorter events, 0.6 us)
Async XLA Ops:
  7.2 57.4 %copy-start = (bf16[1,154,2,1536]{3,2,1,0:T(2,128)(2,1)S(1)}, bf16[1,154,2,1536]{3,2,1,0:T(2,128)(2,1)}, u32[]{:S(2)}) copy-start(bf16[1,154,2,1536]{3,2,1,0:T(2,128)(2,1)} %param.14) | copy-start | bytes 2838532
  7.2 89.1 %all-gather.4.cloned.1.call-start = ((), (), s32[]{:S(2)}) async-start(), calls=%async_computation.4 | async-start | bytes 1327104 | tf_op jit(solution)/shard_map/all_gather | solution.py:300
  8.9 115.3 %all-gather.6.cloned.1.call-start = ((), (), s32[]{:S(2)}) async-start(), calls=%async_computation.5 | async-start | bytes 10616832 | tf_op jit(solution)/shard_map/all_gather | solution.py:305
  11.5 1.3 copy-start.7
  14.0 0.9 copy-start.3
  14.0 0.9 copy-start.6
  16.4 7.1 %copy-start.1 = (bf16[1536,3,96]{0,2,1:T(8,128)(2,1)S(1)}, bf16[1536,3,96]{0,2,1:T(8,128)(2,1)}, u32[]{:S(2)}) copy-start(bf16[1536,3,96]{0,2,1:T(8,128)(2,1)} %param.17) | copy-start | bytes 2654212
  16.4 42.0 %all-to-all-start = ((bf16[8,64,1536]{2,1,0:T(8,128)(2,1)}), bf16[8,64,1536]{2,1,0:T(8,128)(2,1)}, u32[]{:S(2)}, u32[]{:S(2)}) async-start(bf16[8,64,1536]{2,1,0:T(8,128)(2,1)} %first_norm.1), calls=%async_computation | async-start | bytes 3145728 | tf_op jit(solution)/shard_map/all_to_all | solution.py:309
  23.6 32.4 %collective-permute-start = (bf16[3,48,1536]{2,1,0:T(8,128)(2,1)S(1)}, bf16[3,48,1536]{2,1,0:T(8,128)(2,1)S(1)}, u32[]{:S(2)}, u32[]{:S(2)}) collective-permute-start(bf16[3,48,1536]{2,1,0:T(8,128)(2,1)S(1)} %dynamic-slice_bitcast_fusion), channel_id=1, source_target_pairs={{0,2},{2,0},{1,3},{3,1},{4,6},{6,4},{5,7},{7,5},{8,10},{10,8},{9,1... | collective-permute-start | bytes 1327112 | tf_op jit(solution)/shard_map/ppermute | solution.py:296
  55.9 1.8 %collective-permute-start.1 = (bf16[3,48,1536]{2,1,0:T(8,128)(2,1)S(1)}, bf16[3,48,1536]{2,1,0:T(8,128)(2,1)S(1)}, u32[]{:S(2)}, u32[]{:S(2)}) collective-permute-start(bf16[3,48,1536]{2,1,0:T(8,128)(2,1)S(1)} %collective-permute-done.near_ref), channel_id=1, source_target_pairs={{0,32},{32,0},{1,33},{33,1},{2,34},{34,2},{3,35},{35,3},{4,36},{36... | collective-permute-start | bytes 1327112 | tf_op jit(solution)/shard_map/ppermute | solution.py:297
  57.7 0.8 copy-start.4
  58.5 1.0 copy-start.5
  62.5 20.6 %collective-permute-start.2 = (bf16[2,512,192]{2,1,0:T(8,128)(2,1)S(1)}, bf16[2,512,192]{2,1,0:T(8,128)(2,1)S(1)}, u32[]{:S(2)}, u32[]{:S(2)}) collective-permute-start(bf16[2,512,192]{2,1,0:T(8,128)(2,1)S(1)} %slice.11.kv_ref), channel_id=1, source_target_pairs={{0,2},{2,0},{1,3},{3,1},{4,6},{6,4},{5,7},{7,5},{8,10},{10,8},{9,1... | collective-permute-start | bytes 1179656 | tf_op jit(solution)/shard_map/ppermute | solution.py:313
  85.3 10.9 %collective-permute-start.3 = (bf16[4,64,192]{2,1,0:T(8,128)(2,1)S(1)}, bf16[4,64,192]{2,1,0:T(8,128)(2,1)S(1)}, u32[]{:S(2)}, u32[]{:S(2)}) collective-permute-start(bf16[4,64,192]{2,1,0:T(8,128)(2,1)S(1)} %dynamic-slice_bitcast_fusion.1), channel_id=1, source_target_pairs={{0,4},{4,0},{1,5},{5,1},{2,6},{6,2},{3,7},{7,3},{8,12},{12,8},{9,1... | collective-permute-start | bytes 294920 | tf_op jit(solution)/shard_map/ppermute | solution.py:324
  96.3 1.3 copy-start.2
  134.1 4.3 %copy-start.8 = (bf16[1536,64]{0,1:T(8,128)(2,1)S(1)}, bf16[1536,64]{0,1:T(8,128)(2,1)}, u32[]{:S(2)}) copy-start(bf16[1536,64]{0,1:T(8,128)(2,1)} %param.21) | copy-start | bytes 589828
  134.1 13.1 %all-to-all-start.3 = ((bf16[4,64,1536]{2,1,0:T(8,128)(2,1)}), bf16[4,64,1536]{2,1,0:T(8,128)(2,1)S(1)}, u32[]{:S(2)}, u32[]{:S(2)}) async-start(bf16[4,64,1536]{2,1,0:T(8,128)(2,1)} %bitcast.19), calls=%async_computation.3 | async-start | bytes 1572864 | tf_op jit(solution)/shard_map/all_to_all | solution.py:334
  137.7 10.6 %copy-start.9 = (f32[1,32,128]{2,1,0:T(8,128)S(1)}, f32[1,32,128]{2,1,0:T(8,128)}, u32[]{:S(2)}) copy-start(f32[1,32,128]{2,1,0:T(8,128)} %param.12) | copy-start | bytes 49156
Sparse Core Ops, SparseCore 0:
  10.4 41.8 all-gather.3
  54.1 64.7 all-gather.5

commit v2 on v1

v2 whole, which is shorter than its diff:
```python
import functools

import jax
import jax.numpy as jnp
from jax import lax
from jax.experimental import pallas as pl
from jax.experimental.pallas import tpu as pltpu
from jax.sharding import Mesh, PartitionSpec as P

HEAD_DIM = 64
TXT = 154
STEPS = 8
BF = jnp.bfloat16
F32 = jnp.float32
NT = (((1,), (1,)), ((), ()))
NN = (((1,), (0,)), ((), ()))
STRIDES = (1, 3, 2)


def params():
    return pltpu.CompilerParams(vmem_limit_bytes=50 * 1024 * 1024)


def layer_norm(full, shift, scale):
    mean = jnp.mean(full, axis=-1, keepdims=True)
    cent = full - mean
    spread = jnp.mean(jnp.square(cent), axis=-1, keepdims=True)
    return cent * lax.rsqrt(spread + 1e-06) * (1.0 + scale) + shift


def sigma_at(index):
    frac = 1.0 - index.astype(F32) / STEPS
    return 3.0 * frac / (1.0 + 2.0 * frac)


def norm_kernel(copies, x_ref, mod_ref, out_ref):
    h = layer_norm(x_ref[...].astype(F32), mod_ref[0:1, :], mod_ref[1:2, :]).astype(BF)
    for i in range(copies):
        out_ref[i] = h


def first_norm(tokens, mods, copies):
    rows, width = tokens.shape
    return pl.pallas_call(
        functools.partial(norm_kernel, copies),
        out_shape=jax.ShapeDtypeStruct((copies, rows, width), BF),
        compiler_params=params(),
        name="first_norm",
    )(tokens, mods)


def assemble(pos_ref, own_ref, near_refs, far_ref, store):
    core = pos_ref[0]
    row = pos_ref[1]
    store(row, 0, own_ref, 0)
    store(row, 1, own_ref, 1)
    for i, (near_ref, step) in enumerate(zip(near_refs, STRIDES)):
        source = lax.rem(row + 4 - step, 4)
        store(source, core, near_ref, None)
        store(source, 1 - core, far_ref, i)


def qkv_kernel(pos_ref, h_ref, own_ref, n0_ref, n1_ref, n2_ref, far_ref, q_ref, kv_ref, w_ref):
    def store(source, half, ref, index):
        for k in range(3):
            if ref is own_ref:
                value = ref[k, index * 48 : index * 48 + 48, :]
            elif index is None:
                value = ref[k]
            else:
                value = ref[index, k]
            w_ref[k, source, half] = value

    assemble(pos_ref, own_ref, (n0_ref, n1_ref, n2_ref), far_ref, store)
    h = h_ref[...]
    for k in range(3):
        w = w_ref[k].reshape(384, h.shape[1])
        value = lax.dot_general(h, w, NT, preferred_element_type=F32).astype(BF)
        if k == 0:
            q_ref[...] = value
        else:
            kv_ref[k - 1] = value


def project_qkv(pos, h, own, near, far):
    rows, width = h.shape
    return pl.pallas_call(
        qkv_kernel,
        out_shape=[
            jax.ShapeDtypeStruct((rows, 384), BF),
            jax.ShapeDtypeStruct((2, rows, 384), BF),
        ],
        in_specs=[pl.BlockSpec(memory_space=pltpu.SMEM)]
        + [pl.BlockSpec(memory_space=pltpu.VMEM)] * 6,
        scratch_shapes=[pltpu.VMEM((3, 4, 2, 48, width), BF)],
        compiler_params=params(),
        name="project_qkv",
    )(pos, h, own, *near, far)


def attention_kernel(chunks, has_text, has_state, last, *refs):
    refs = list(refs)
    len_ref = refs.pop(0) if has_text else None
    q_ref = refs.pop(0)
    kv_refs = [refs.pop(0) for _ in range(chunks)]
    text_ref = refs.pop(0) if has_text else None
    state_refs = [refs.pop(0) for _ in range(3)] if has_state else None
    rows = q_ref.shape[0]
    if has_text:
        live = lax.broadcasted_iota(jnp.int32, (rows, TXT), 1) < len_ref[0]
    first = lax.broadcasted_iota(jnp.int32, (rows, 128), 1) < HEAD_DIM
    for g in range(q_ref.shape[1] // 128):
        cols = slice(g * 128, g * 128 + 128)
        q = q_ref[:, cols]
        sides = []
        for side in range(2):
            here = first if side == 0 else jnp.logical_not(first)
            qh = jnp.where(here, q, jnp.zeros_like(q))
            parts = []
            for ref in kv_refs:
                s = lax.dot_general(qh, ref[0, :, cols], NT, preferred_element_type=F32) * 0.125
                parts.append((s, ref[1, :, cols]))
            if has_text:
                s = (
                    lax.dot_general(qh, text_ref[0, :, cols], NT, preferred_element_type=F32)
                    * 0.125
                )
                parts.append((jnp.where(live, s, -jnp.inf), text_ref[1, :, cols]))
            top = None
            for s, _ in parts:
                peak = jnp.max(s, axis=1, keepdims=True)
                top = peak if top is None else jnp.maximum(top, peak)
            if has_state:
                lane = g * 128 + side * HEAD_DIM
                top = jnp.maximum(top, state_refs[1][:, lane : lane + 1])
            total = None
            acc = None
            for s, values in parts:
                p = jnp.exp(s - top)
                amount = jnp.sum(p, axis=1, keepdims=True)
                part = lax.dot_general(p.astype(BF), values, NN, preferred_element_type=F32)
                total = amount if total is None else total + amount
                acc = part if acc is None else acc + part
            sides.append((acc, top, total))
        acc = jnp.where(first, sides[0][0], sides[1][0])
        top = jnp.where(first, sides[0][1], sides[1][1])
        total = jnp.where(first, sides[0][2], sides[1][2])
        if has_state:
            factor = jnp.exp(state_refs[1][:, cols] - top)
            acc = acc + state_refs[0][:, cols] * factor
            total = total + state_refs[2][:, cols] * factor
        if last:
            refs[0][:, cols] = (acc / total).astype(BF)
        else:
            refs[0][:, cols] = acc
            refs[1][:, cols] = top
            refs[2][:, cols] = total


def attention(q, kvs, text=None, length=None, state=None, last=False):
    args = []
    specs = []
    if text is not None:
        args.append(length)
        specs.append(pl.BlockSpec(memory_space=pltpu.SMEM))
    rest = [q, *kvs] + ([text] if text is not None else []) + list(state or [])
    args += rest
    specs += [pl.BlockSpec(memory_space=pltpu.VMEM)] * len(rest)
    if last:
        out = jax.ShapeDtypeStruct(q.shape, BF)
    else:
        out = [jax.ShapeDtypeStruct(q.shape, F32)] * 3
    return pl.pallas_call(
        functools.partial(
            attention_kernel, len(kvs), text is not None, state is not None, last
        ),
        out_shape=out,
        in_specs=specs,
        compiler_params=params(),
        name="attention",
    )(*args)


def out_kernel(pos_ref, a_ref, own_ref, n0_ref, n1_ref, n2_ref, far_ref, out_ref, w_ref):
    def store(source, half, ref, index):
        if ref is own_ref:
            value = ref[index * 48 : index * 48 + 48, :]
        elif index is None:
            value = ref[...]
        else:
            value = ref[index]
        w_ref[source, half] = value

    assemble(pos_ref, own_ref, (n0_ref, n1_ref, n2_ref), far_ref, store)
    w = w_ref[...].reshape(384, out_ref.shape[1])
    out_ref[...] = lax.dot_general(
        a_ref[...], w, NN, preferred_element_type=F32
    ).astype(BF)


def out_projection(pos, a, own, near, far):
    width = own.shape[1]
    return pl.pallas_call(
        out_kernel,
        out_shape=jax.ShapeDtypeStruct((a.shape[0], width), BF),
        in_specs=[pl.BlockSpec(memory_space=pltpu.SMEM)]
        + [pl.BlockSpec(memory_space=pltpu.VMEM)] * 6,
        scratch_shapes=[pltpu.VMEM((4, 2, 48, width), BF)],
        compiler_params=params(),
        name="out_projection",
    )(pos, a, own, *near, far)


def pack_kernel(pos_ref, up_ref, down_ref, out_ref, sem):
    @pl.when(pos_ref[0] == 0)
    def _():
        copy = pltpu.make_async_copy(up_ref, out_ref, sem.at[0])
        copy.start()
        copy.wait()

    @pl.when(pos_ref[0] == 1)
    def _():
        part = down_ref.shape[0]
        copies = []
        for s in range(4):
            copies.append(
                pltpu.make_async_copy(
                    down_ref.at[:, pl.ds(s * part, part)],
                    out_ref.at[pl.ds(s * part, part), :],
                    sem.at[s],
                )
            )
        for copy in copies:
            copy.start()
        for copy in copies:
            copy.wait()


def pack_ffn(pos, w_up, w_down):
    return pl.pallas_call(
        pack_kernel,
        out_shape=jax.ShapeDtypeStruct(w_up.shape, BF),
        in_specs=[
            pl.BlockSpec(memory_space=pltpu.SMEM),
            pl.BlockSpec(memory_space=pl.ANY),
            pl.BlockSpec(memory_space=pl.ANY),
        ],
        out_specs=pl.BlockSpec(memory_space=pl.ANY),
        scratch_shapes=[pltpu.SemaphoreType.DMA((4,))],
        compiler_params=params(),
        name="pack_ffn",
    )(pos, w_up, w_down)


def second_norm_kernel(x_ref, part_ref, mod_ref, second_ref, out_ref):
    proj = part_ref[0].astype(F32)
    for i in range(1, part_ref.shape[0]):
        proj += part_ref[i].astype(F32)
    second = (x_ref[...].astype(F32) + mod_ref[2:3, :] * proj).astype(BF)
    second_ref[...] = second
    h = layer_norm(second.astype(F32), mod_ref[3:4, :], mod_ref[4:5, :]).astype(BF)
    for i in range(out_ref.shape[0]):
        out_ref[i] = h


def second_norm(tokens, parts, mods):
    return pl.pallas_call(
        second_norm_kernel,
        out_shape=[
            jax.ShapeDtypeStruct(tokens.shape, BF),
            jax.ShapeDtypeStruct(parts.shape, BF),
        ],
        compiler_params=params(),
        name="second_norm",
    )(tokens, parts, mods)


def ffn_kernel(h_ref, up_ref, down_ref, out_ref, acc_ref):
    step = pl.program_id(0)
    part = up_ref.shape[-1]
    hidden = jax.nn.gelu(
        lax.dot_general(h_ref[...], up_ref[0, 0], NN, preferred_element_type=F32),
        approximate=True,
    ).astype(BF)
    for s in range(4):
        value = lax.dot_general(
            hidden,
            down_ref[0, 0, s * part : (s + 1) * part, :],
            NN,
            preferred_element_type=F32,
        )
        cols = slice(s * part, (s + 1) * part)

        @pl.when(step == 0)
        def _():
            acc_ref[:, cols] = value

        @pl.when(step > 0)
        def _():
            acc_ref[:, cols] += value

    @pl.when(step == pl.num_programs(0) - 1)
    def _():
        out_ref[...] = acc_ref[...].astype(BF)


def feed_forward(h, weights):
    rows, width = h.shape
    part = weights.shape[3]
    return pl.pallas_call(
        ffn_kernel,
        grid=(4,),
        out_shape=jax.ShapeDtypeStruct((rows, width), BF),
        in_specs=[
            pl.BlockSpec((rows, width), lambda i: (0, 0)),
            pl.BlockSpec((1, 1, width, part), lambda i: (0, i, 0, 0)),
            pl.BlockSpec((1, 1, width, part), lambda i: (1, i, 0, 0)),
        ],
        out_specs=pl.BlockSpec((rows, width), lambda i: (0, 0)),
        scratch_shapes=[pltpu.VMEM((rows, width), F32)],
        compiler_params=params(),
        name="feed_forward",
    )(h, weights, weights)


def last_kernel(second_ref, part_ref, mod_ref, w_ref, state_ref, vel_ref):
    ffn = part_ref[0].astype(F32)
    for i in range(1, part_ref.shape[0]):
        ffn += part_ref[i].astype(F32)
    state = (second_ref[...].astype(F32) + mod_ref[5:6, :] * ffn).astype(BF)
    state_ref[...] = state
    h = layer_norm(state.astype(F32), mod_ref[6:7, :], mod_ref[7:8, :]).astype(BF)
    vel_ref[...] = lax.dot_general(h, w_ref[...], NN, preferred_element_type=F32)


def last_stage(second, parts, mods, w_final):
    return pl.pallas_call(
        last_kernel,
        out_shape=[
            jax.ShapeDtypeStruct(second.shape, BF),
            jax.ShapeDtypeStruct((second.shape[0], w_final.shape[1]), F32),
        ],
        compiler_params=params(),
        name="last_stage",
    )(second, parts, mods, w_final)


def on_device(
    image_tokens,
    latent,
    modulation,
    text_kv,
    text_len,
    timestep,
    w_qkv,
    w_out,
    w_up,
    w_down,
    w_final,
):
    tokens = image_tokens[0]
    mods = modulation[0]
    rows, width = tokens.shape
    core = lax.axis_index("core")
    pos = jnp.stack([core, lax.axis_index("ty")]).astype(jnp.int32)
    swap2 = [(0, 1), (1, 0)]

    def to_lines(value, step):
        return lax.ppermute(value, "ty", [(i, (i + step) % 4) for i in range(4)])

    half_ffn = pack_ffn(pos, w_up, w_down)
    ffn_full = lax.all_gather(half_ffn, ("core", "tx"), axis=0, tiled=False)
    ffn_full = ffn_full.reshape(2, 4, width, w_up.shape[1])

    own_qkv = jnp.transpose(w_qkv, (1, 2, 0))
    half_qkv = lax.dynamic_slice_in_dim(own_qkv, core * 48, 48, 1)
    h1 = first_norm(tokens, mods, 4)
    h1, half_qkv = lax.optimization_barrier((h1, half_qkv))
    near_qkv = [to_lines(half_qkv, step) for step in STRIDES]
    h1 = lax.all_to_all(h1, "tx", split_axis=0, concat_axis=0, tiled=True)
    *near_qkv, h1 = lax.optimization_barrier((*near_qkv, h1))
    far_qkv = lax.ppermute(jnp.stack(near_qkv), "core", swap2)
    h1 = h1.reshape(4 * rows, width)
    query, keyval = project_qkv(pos, h1, own_qkv, near_qkv, far_qkv)

    half_out = lax.dynamic_slice_in_dim(w_out, core * 48, 48, 0)
    half_out, keyval = lax.optimization_barrier((half_out, keyval))
    chunks = [to_lines(keyval, step) for step in STRIDES]
    near_out = [to_lines(half_out, step) for step in STRIDES]
    text = lax.dynamic_slice_in_dim(text_kv[0], lax.axis_index("tx") * 384, 384, 2)
    text = jnp.transpose(text, (1, 0, 2))
    state = attention(query, [keyval], text=text, length=text_len)
    state = attention(query, chunks[:2], state=state)
    *near_out, across, totals = lax.optimization_barrier((*near_out, chunks[2], state[2]))
    state = (state[0], state[1], totals)
    far_out = lax.ppermute(jnp.stack(near_out), "core", swap2)
    attended = attention(query, [across], state=state, last=True)

    partial = out_projection(pos, attended, w_out, near_out, far_out)
    partial = partial.reshape(4, rows, width)
    partial = lax.all_to_all(partial, "tx", split_axis=0, concat_axis=0, tiled=True)
    second, h2 = second_norm(tokens, partial, mods)
    h2 = lax.all_to_all(h2, "ty", split_axis=0, concat_axis=0, tiled=True)
    partial = feed_forward(h2.reshape(4 * rows, width), ffn_full).reshape(4, rows, width)
    partial = lax.all_to_all(partial, "ty", split_axis=0, concat_axis=0, tiled=True)
    state, velocity = last_stage(second, partial, mods, w_final)

    step_index = timestep[0]
    delta = sigma_at(step_index + 1) - sigma_at(step_index)
    moved = latent[0] + delta * velocity.reshape(rows // 2, 2 * velocity.shape[1])
    return (state[None], moved[None])


def solution(mesh):
    fine = Mesh(
        mesh.devices.reshape(mesh.shape["req"] // 2, 2, 4, 4, mesh.shape["blk"]),
        ("zl", "core", "tx", "ty", "blk"),
    )
    group = ("zl", "core", "blk")
    tile = ("tx", "ty")
    in_specs = (
        P(group, tile, None),
        P(group, tile, None),
        P(group, None, None),
        P(group, None, None, None),
        P(group),
        P(group),
        P(None, None, tile),
        P(tile, None),
        P(None, tile),
        P(tile, None),
        P(),
    )
    out_specs = (P(group, tile, None), P(group, tile, None))
    return jax.shard_map(
        on_device, mesh=fine, in_specs=in_specs, out_specs=out_specs, check_vma=False
    )
```

time: 157 us -> 154 us (0.981)
  waiting for transfers between devices: 63.8 us -> 45.8 us
  blocking collectives: 25.6 us -> 34.2 us
  Pallas kernels: 20.9 us -> 27.9 us
  starting transfers between devices: 17.6 us -> 20.1 us
  local copies, waits for them, and re-layouts: 10.1 us -> 8.18 us
    ppermute x4 -> x11, waiting for transfers between devices: 55.3 us -> 36.2 us  [the longest x9 33.7 us: to_lines(): return lax.ppermute(value, 'ty', [(i, (i + step) % 4) for i in range(4)])]
    pallas_call x4 -> x6, Pallas kernels: 8.1 us -> 15.3 us  [the longest x3 8.62 us: attention(): pl.pallas_call(functools.partial(attention_kernel, len(kvs), text is not...]
    ppermute x4 -> x11, starting transfers between devices: 6.85 us -> 12.1 us  [the longest x9 12 us: to_lines(): return lax.ppermute(value, 'ty', [(i, (i + step) % 4) for i in range(4)])]
    all_to_all x1, blocking collectives: 11.9 us -> 16.4 us  [on_device(): h2 = lax.all_to_all(h2, 'ty', split_axis=0, concat_axis=0, tiled=True)]
    all_to_all x1, blocking collectives: 13.8 us -> 17.8 us  [on_device(): lax.all_to_all(partial, 'tx', split_axis=0, concat_axis=0, tiled=True)]
    all_to_all x2, starting transfers between devices: 10.7 us -> 7.92 us  [the longest x1 4.29 us: on_device(): h1 = lax.all_to_all(h1, 'tx', split_axis=0, concat_axis=0, tiled=True)]
    reshape x1 -> x0, local copies, waits for them, and re-layouts: 2.52 us -> none  [on_device(): w_down.reshape(part, 4, part)]
    unnamed x21 -> x29, local copies, waits for them, and re-layouts: 5.31 us -> 6.42 us
  transfers between devices with their start and end apart: 8 -> 14, of which waited for: 5 -> 6; matrix products, arithmetic and copies ran while one was open for 3% -> 2% of each run, Pallas kernels for 6% -> 10%
where the time goes in v2:
time: 154 us
  waiting for transfers between devices  45.8 us (30%)
  blocking collectives  34.2 us (22%)
  Pallas kernels  27.9 us (18%)
  starting transfers between devices  20.1 us (13%)
  between operations  15.7 us (10%)
  local copies, waits for them, and re-layouts  8.18 us (5%)
  other arithmetic  1.94 us (1%)
    ppermute x9, waiting for transfers between devices, to_lines(): return lax.ppermute(value, 'ty', [(i, (i + step) % 4) for i in range(4)])  33.7 us
    all_to_all x1, blocking collectives, on_device(): lax.all_to_all(partial, 'tx', split_axis=0, concat_axis=0, tiled=True)  17.8 us
    all_to_all x1, blocking collectives, on_device(): h2 = lax.all_to_all(h2, 'ty', split_axis=0, concat_axis=0, tiled=True)  16.4 us
    ppermute x9, starting transfers between devices, to_lines(): return lax.ppermute(value, 'ty', [(i, (i + step) % 4) for i in range(4)])  12 us
    pallas_call x1, Pallas kernels, feed_forward(): pl.pallas_call(ffn_kernel, grid=(4,), out_shape=jax.ShapeDtypeStruct((row...  9.92 us
    all_to_all x1, waiting for transfers between devices, on_device(): lax.all_to_all(partial, 'ty', split_axis=0, concat_axis=0, tiled=True)  9.56 us
    pallas_call x3, Pallas kernels, attention(): pl.pallas_call(functools.partial(attention_kernel, len(kvs), text is not...  8.62 us
    unnamed x29, local copies, waits for them, and re-layouts  6.42 us
  transfers between devices with their start and end apart: 14, of which 6 were waited for; matrix products, arithmetic and copies ran while one was open for 2% of the time, Pallas kernels for 10%

profile of v2, /device:TPU:128, one launch (start us, length us, event | category | flops | bytes accessed | tf_op | source)
XLA Modules:
  0.0 153.8 jit_solution(14127613710297962808)
XLA Ops:
  7.3 1.3 copy-done.4
  8.7 1.3 copy-done.5
  9.9 1.6 %pack_ffn.1 = bf16[1536,384]{1,0:T(8,128)(2,1)} custom-call(s32[2]{0:T(128)S(1)} %pad_add_fusion.pos_ref, bf16[1536,384]{1,0:T(8,128)(2,1)S(1)} %copy-done.4, bf16[384,1536]{1,0:T(8,128)(2,1)S(1)} %copy-done.5), custom_call_target="tpu_custom_call" | custom-call | tf_op jit(solution)/shard_map/pack_ffn/pallas_call | solution.py:240
  11.6 0.9 copy-done.6
  12.5 1.2 first_norm.1
  14.4 4.3 %all-to-all-start = ((bf16[4,64,1536]{2,1,0:T(8,128)(2,1)}), bf16[4,64,1536]{2,1,0:T(8,128)(2,1)S(1)}, u32[]{:S(2)}, u32[]{:S(2)}) async-start(bf16[4,64,1536]{2,1,0:T(8,128)(2,1)} %first_norm.1), calls=%async_computation | async-start | bytes 1572864 | tf_op jit(solution)/shard_map/all_to_all | solution.py:380
  18.7 1.6 %collective-permute-start = (bf16[3,48,1536]{2,1,0:T(8,128)(2,1)}, bf16[3,48,1536]{2,1,0:T(8,128)(2,1)S(1)}, u32[]{:S(2)}, u32[]{:S(2)}) collective-permute-start(bf16[3,48,1536]{2,1,0:T(8,128)(2,1)} %dynamic-slice_bitcast_fusion), channel_id=1, source_target_pairs={{0,2},{2,4},{4,6},{6,0},{1,3},{3,5},{5,7},{7,1},{8,10},{10,12},{12... | collective-permute-start | bytes 1327112 | tf_op jit(solution)/shard_map/ppermute | solution.py:369
  20.3 1.7 %collective-permute-start.1 = (bf16[3,48,1536]{2,1,0:T(8,128)(2,1)}, bf16[3,48,1536]{2,1,0:T(8,128)(2,1)S(1)}, u32[]{:S(2)}, u32[]{:S(2)}) collective-permute-start(bf16[3,48,1536]{2,1,0:T(8,128)(2,1)} %dynamic-slice_bitcast_fusion), channel_id=1, source_target_pairs={{0,6},{2,0},{4,2},{6,4},{1,7},{3,1},{5,3},{7,5},{8,14},{10,8},{12,... | collective-permute-start | bytes 1327112 | tf_op jit(solution)/shard_map/ppermute | solution.py:369
  22.0 2.0 %collective-permute-start.2 = (bf16[3,48,1536]{2,1,0:T(8,128)(2,1)}, bf16[3,48,1536]{2,1,0:T(8,128)(2,1)}, u32[]{:S(2)}, u32[]{:S(2)}) collective-permute-start(bf16[3,48,1536]{2,1,0:T(8,128)(2,1)} %dynamic-slice_bitcast_fusion), channel_id=1, source_target_pairs={{0,4},{2,6},{4,0},{6,2},{1,5},{3,7},{5,1},{7,3},{8,12},{10,14},{12... | collective-permute-start | bytes 1327112 | tf_op jit(solution)/shard_map/ppermute | solution.py:369
  23.9 8.2 %collective-permute-done.n0_ref = bf16[3,48,1536]{2,1,0:T(8,128)(2,1)S(1)} collective-permute-done((bf16[3,48,1536]{2,1,0:T(8,128)(2,1)}, bf16[3,48,1536]{2,1,0:T(8,128)(2,1)S(1)}, u32[]{:S(2)}, u32[]{:S(2)}) %collective-permute-start) | collective-permute-done | bytes 442400 | tf_op jit(solution)/shard_map/ppermute | solution.py:369
  32.1 1.5 collective-permute-done.1.n1_ref
  33.6 9.0 %collective-permute-done.2.n2_ref = bf16[3,48,1536]{2,1,0:T(8,128)(2,1)} collective-permute-done((bf16[3,48,1536]{2,1,0:T(8,128)(2,1)}, bf16[3,48,1536]{2,1,0:T(8,128)(2,1)}, u32[]{:S(2)}, u32[]{:S(2)}) %collective-permute-start.2) | collective-permute-done | bytes 442400 | tf_op jit(solution)/shard_map/ppermute | solution.py:369
  42.6 1.2 pad_maximum_fusion
  44.6 2.5 %collective-permute-done.3.far_ref = bf16[3,3,48,1536]{3,2,1,0:T(8,128)(2,1)S(1)} collective-permute-done((bf16[3,3,48,1536]{3,2,1,0:T(8,128)(2,1)S(1)}, bf16[3,3,48,1536]{3,2,1,0:T(8,128)(2,1)S(1)}, u32[]{:S(2)}, u32[]{:S(2)}) %collective-permute-start.3) | collective-permute-done | bytes 1327136 | tf_op jit(solution)/shard_map/ppermute | solution.py:382
  47.1 1.1 copy-done.11
  48.2 3.9 %project_qkv.1 = (bf16[256,384]{1,0:T(8,128)(2,1)S(1)}, bf16[2,256,384]{2,1,0:T(8,128)(2,1)}) custom-call(s32[2]{0:T(128)S(1)} %pad_add_fusion.pos_ref, bf16[256,1536]{1,0:T(8,128)(2,1)S(1)} %bitcast.26, bf16[3,96,1536]{2,1,0:T(8,128)(2,1)S(1)} %bitcast.28, bf16[3,48,1536]{2,1,0:T(8,128)(2,1)S(1)} %collective-permute-done.n0_ref, ...), custom_call_target="tpu_custom_call" | custom-call | tf_op jit(solution)/shard_map/project_qkv/pallas_call | solution.py:87
  52.8 1.4 collective-permute-start.8
  54.2 1.8 %collective-permute-start.9 = (bf16[2,256,384]{2,1,0:T(8,128)(2,1)}, bf16[2,256,384]{2,1,0:T(8,128)(2,1)S(1)}, u32[]{:S(2)}, u32[]{:S(2)}) collective-permute-start(bf16[2,256,384]{2,1,0:T(8,128)(2,1)} %get-tuple-element.36.refs_2_), channel_id=1, source_target_pairs={{0,6},{2,0},{4,2},{6,4},{1,7},{3,1},{5,3},{7,5},{8,14},{10,8},{12,... | collective-permute-start | bytes 1179656 | tf_op jit(solution)/shard_map/ppermute | solution.py:369
  56.3 0.9 collective-permute-start.4
  57.2 2.3 %collective-permute-start.5 = (bf16[48,1536]{1,0:T(8,128)(2,1)}, bf16[48,1536]{1,0:T(8,128)(2,1)S(1)}, u32[]{:S(2)}, u32[]{:S(2)}) collective-permute-start(bf16[48,1536]{1,0:T(8,128)(2,1)} %constant_dynamic-slice_fusion.1), channel_id=1, source_target_pairs={{0,6},{2,0},{4,2},{6,4},{1,7},{3,1},{5,3},{7,5},{8,14},{10,8},{12,... | collective-permute-start | bytes 442376 | tf_op jit(solution)/shard_map/ppermute | solution.py:369
  59.5 15.1 %collective-permute-done.8.refs_1_ = bf16[2,256,384]{2,1,0:T(8,128)(2,1)S(1)} collective-permute-done((bf16[2,256,384]{2,1,0:T(8,128)(2,1)}, bf16[2,256,384]{2,1,0:T(8,128)(2,1)S(1)}, u32[]{:S(2)}, u32[]{:S(2)}) %collective-permute-start.8) | collective-permute-done | bytes 393248 | tf_op jit(solution)/shard_map/ppermute | solution.py:369
  75.5 0.9 copy-done.3
  76.4 3.0 %attention.3 = (f32[256,384]{1,0:T(8,128)S(1)}, f32[256,384]{1,0:T(8,128)S(1)}, f32[256,384]{1,0:T(8,128)S(1)}) custom-call(s32[1]{0:T(128)S(6)} %copy.17.refs_0_, bf16[256,384]{1,0:T(8,128)(2,1)S(1)} %copy-done.3, bf16[2,256,384]{2,1,0:T(8,128)(2,1)} %get-tuple-element.36.refs_2_, bf16[2,154,384]{2,1,0:T(8,128)(2,1)S(1)} %bitcast.31), custom_call_target="tpu_custom_call" | custom-call | tf_op jit(solution)/shard_map/attention/pallas_call | solution.py:173
  79.4 2.8 %attention.4 = (f32[256,384]{1,0:T(8,128)S(1)}, f32[256,384]{1,0:T(8,128)S(1)}, f32[256,384]{1,0:T(8,128)S(1)}) custom-call(bf16[256,384]{1,0:T(8,128)(2,1)S(1)} %copy-done.3, bf16[2,256,384]{2,1,0:T(8,128)(2,1)S(1)} %collective-permute-done.8.refs_1_, bf16[2,256,384]{2,1,0:T(8,128)(2,1)S(1)} %collective-permute-done.9.refs_2_, ...), custom_call_target="tpu_custom_call" | custom-call | tf_op jit(solution)/shard_map/attention/pallas_call | solution.py:173
  82.4 2.8 %attention.5.a_ref = bf16[256,384]{1,0:T(8,128)(2,1)S(1)} custom-call(bf16[256,384]{1,0:T(8,128)(2,1)S(1)} %copy-done.3, bf16[2,256,384]{2,1,0:T(8,128)(2,1)S(1)} %collective-permute-done.7.refs_1_, f32[256,384]{1,0:T(8,128)S(1)} %get-tuple-element.42.refs_2_, f32[256,384]{1,0:T(8,128)S(1)} %get-tuple-element.43.refs_3_, ...), custom_call_target="tpu_custom_call" | custom-call | tf_op jit(solution)/shard_map/attention/pallas_call | solution.py:173
  85.3 1.2 out_projection.1
  86.5 17.8 %all_to_all.20.part_ref = bf16[4,64,1536]{2,1,0:T(8,128)(2,1)S(1)} all-to-all(bf16[4,64,1536]{2,1,0:T(8,128)(2,1)S(1)} %bitcast.27), channel_id=1, replica_groups=mesh['zl'=4,'core'=2,'tx'=4,'ty'=4,'blk'=2] {'tx'}, dimensions={0} | all-to-all | bytes 1572864 | tf_op jit(solution)/shard_map/all_to_all | solution.py:401
  104.6 16.4 %all_to_all.21 = bf16[4,64,1536]{2,1,0:T(8,128)(2,1)S(1)} all-to-all(bf16[4,64,1536]{2,1,0:T(8,128)(2,1)S(1)} %get-tuple-element.49), channel_id=1, replica_groups=mesh['zl'=4,'core'=2,'tx'=4,'ty'=4,'blk'=2] {'ty'}, dimensions={0} | all-to-all | bytes 1572864 | tf_op jit(solution)/shard_map/all_to_all | solution.py:403
  121.1 9.9 %feed_forward.1 = bf16[256,1536]{1,0:T(8,128)(2,1)} custom-call(bf16[256,1536]{1,0:T(8,128)(2,1)S(1)} %bitcast.25, bf16[2,4,1536,384]{3,2,1,0:T(8,128)(2,1)} %bitcast.40, bf16[2,4,1536,384]{3,2,1,0:T(8,128)(2,1)} %bitcast.41), custom_call_target="tpu_custom_call" | custom-call | tf_op jit(solution)/shard_map/feed_forward/pallas_call | solution.py:310
  131.0 3.6 %all-to-all-start.3 = ((bf16[4,64,1536]{2,1,0:T(8,128)(2,1)}), bf16[4,64,1536]{2,1,0:T(8,128)(2,1)S(1)}, u32[]{:S(2)}, u32[]{:S(2)}) async-start(bf16[4,64,1536]{2,1,0:T(8,128)(2,1)} %bitcast.18), calls=%async_computation.3 | async-start | bytes 1572864 | tf_op jit(solution)/shard_map/all_to_all | solution.py:405
  135.6 9.6 %all-to-all-done.3.part_ref = bf16[4,64,1536]{2,1,0:T(8,128)(2,1)S(1)} async-done(((bf16[4,64,1536]{2,1,0:T(8,128)(2,1)}), bf16[4,64,1536]{2,1,0:T(8,128)(2,1)S(1)}, u32[]{:S(2)}, u32[]{:S(2)}) %all-to-all-start.3) | async-done | bytes 786464 | tf_op jit(solution)/shard_map/all_to_all | solution.py:405
  145.2 1.1 last_stage.1
  (48 shorter events, 4.4 us)
Async XLA Ops:
  7.2 68.1 %copy-start = (bf16[1,154,2,1536]{3,2,1,0:T(2,128)(2,1)S(1)}, bf16[1,154,2,1536]{3,2,1,0:T(2,128)(2,1)}, u32[]{:S(2)}) copy-start(bf16[1,154,2,1536]{3,2,1,0:T(2,128)(2,1)} %param.14) | copy-start | bytes 2838532
  7.2 113.9 %all-gather.3.cloned.1.call-start = ((), (), s32[]{:S(2)}) async-start(), calls=%async_computation.4 | async-start | bytes 10616832 | tf_op jit(solution)/shard_map/all_gather | solution.py:372
  7.3 1.3 copy-start.4
  8.6 1.3 copy-start.5
  9.9 1.7 %copy-start.10 = (f32[1,8,1536]{2,1,0:T(8,128)S(1)}, f32[1,8,1536]{2,1,0:T(8,128)}, u32[]{:S(2)}) copy-start(f32[1,8,1536]{2,1,0:T(8,128)} %param.13) | copy-start | bytes 147460
  11.5 0.9 copy-start.6
  11.5 2.1 %copy-start.1 = (bf16[1536,3,96]{0,2,1:T(8,128)(2,1)S(1)}, bf16[1536,3,96]{0,2,1:T(8,128)(2,1)}, u32[]{:S(2)}) copy-start(bf16[1536,3,96]{0,2,1:T(8,128)(2,1)} %param.17) | copy-start | bytes 2654212
  14.4 28.2 %all-to-all-start = ((bf16[4,64,1536]{2,1,0:T(8,128)(2,1)}), bf16[4,64,1536]{2,1,0:T(8,128)(2,1)S(1)}, u32[]{:S(2)}, u32[]{:S(2)}) async-start(bf16[4,64,1536]{2,1,0:T(8,128)(2,1)} %first_norm.1), calls=%async_computation | async-start | bytes 1572864 | tf_op jit(solution)/shard_map/all_to_all | solution.py:380
  18.7 13.4 %collective-permute-start = (bf16[3,48,1536]{2,1,0:T(8,128)(2,1)}, bf16[3,48,1536]{2,1,0:T(8,128)(2,1)S(1)}, u32[]{:S(2)}, u32[]{:S(2)}) collective-permute-start(bf16[3,48,1536]{2,1,0:T(8,128)(2,1)} %dynamic-slice_bitcast_fusion), channel_id=1, source_target_pairs={{0,2},{2,4},{4,6},{6,0},{1,3},{3,5},{5,7},{7,1},{8,10},{10,12},{12... | collective-permute-start | bytes 1327112 | tf_op jit(solution)/shard_map/ppermute | solution.py:369
  20.3 13.3 %collective-permute-start.1 = (bf16[3,48,1536]{2,1,0:T(8,128)(2,1)}, bf16[3,48,1536]{2,1,0:T(8,128)(2,1)S(1)}, u32[]{:S(2)}, u32[]{:S(2)}) collective-permute-start(bf16[3,48,1536]{2,1,0:T(8,128)(2,1)} %dynamic-slice_bitcast_fusion), channel_id=1, source_target_pairs={{0,6},{2,0},{4,2},{6,4},{1,7},{3,1},{5,3},{7,5},{8,14},{10,8},{12,... | collective-permute-start | bytes 1327112 | tf_op jit(solution)/shard_map/ppermute | solution.py:369
  22.0 20.6 %collective-permute-start.2 = (bf16[3,48,1536]{2,1,0:T(8,128)(2,1)}, bf16[3,48,1536]{2,1,0:T(8,128)(2,1)}, u32[]{:S(2)}, u32[]{:S(2)}) collective-permute-start(bf16[3,48,1536]{2,1,0:T(8,128)(2,1)} %dynamic-slice_bitcast_fusion), channel_id=1, source_target_pairs={{0,4},{2,6},{4,0},{6,2},{1,5},{3,7},{5,1},{7,3},{8,12},{10,14},{12... | collective-permute-start | bytes 1327112 | tf_op jit(solution)/shard_map/ppermute | solution.py:369
  42.6 1.3 copy-start.8
  43.8 3.3 %collective-permute-start.3 = (bf16[3,3,48,1536]{3,2,1,0:T(8,128)(2,1)S(1)}, bf16[3,3,48,1536]{3,2,1,0:T(8,128)(2,1)S(1)}, u32[]{:S(2)}, u32[]{:S(2)}) collective-permute-start(bf16[3,3,48,1536]{3,2,1,0:T(8,128)(2,1)S(1)} %pad_maximum_fusion), channel_id=1, source_target_pairs={{0,32},{32,0},{1,33},{33,1},{2,34},{34,2},{3,35},{35,3},{4,36},{36... | collective-permute-start | bytes 3981320 | tf_op jit(solution)/shard_map/ppermute | solution.py:382
  47.1 1.1 copy-start.11
  52.1 0.7 copy-start.2
  52.8 21.8 %collective-permute-start.8 = (bf16[2,256,384]{2,1,0:T(8,128)(2,1)}, bf16[2,256,384]{2,1,0:T(8,128)(2,1)S(1)}, u32[]{:S(2)}, u32[]{:S(2)}) collective-permute-start(bf16[2,256,384]{2,1,0:T(8,128)(2,1)} %get-tuple-element.36.refs_2_), channel_id=1, source_target_pairs={{0,2},{2,4},{4,6},{6,0},{1,3},{3,5},{5,7},{7,1},{8,10},{10,12},{12... | collective-permute-start | bytes 1179656 | tf_op jit(solution)/shard_map/ppermute | solution.py:369
  54.2 25.2 %collective-permute-start.9 = (bf16[2,256,384]{2,1,0:T(8,128)(2,1)}, bf16[2,256,384]{2,1,0:T(8,128)(2,1)S(1)}, u32[]{:S(2)}, u32[]{:S(2)}) collective-permute-start(bf16[2,256,384]{2,1,0:T(8,128)(2,1)} %get-tuple-element.36.refs_2_), channel_id=1, source_target_pairs={{0,6},{2,0},{4,2},{6,4},{1,7},{3,1},{5,3},{7,5},{8,14},{10,8},{12,... | collective-permute-start | bytes 1179656 | tf_op jit(solution)/shard_map/ppermute | solution.py:369
  56.0 26.2 %collective-permute-start.7 = (bf16[2,256,384]{2,1,0:T(8,128)(2,1)}, bf16[2,256,384]{2,1,0:T(8,128)(2,1)S(1)}, u32[]{:S(2)}, u32[]{:S(2)}) collective-permute-start(bf16[2,256,384]{2,1,0:T(8,128)(2,1)} %get-tuple-element.36.refs_2_), channel_id=1, source_target_pairs={{0,4},{2,6},{4,0},{6,2},{1,5},{3,7},{5,1},{7,3},{8,12},{10,14},{12... | collective-permute-start | bytes 1179656 | tf_op jit(solution)/shard_map/ppermute | solution.py:369
  56.3 25.9 %collective-permute-start.4 = (bf16[48,1536]{1,0:T(8,128)(2,1)}, bf16[48,1536]{1,0:T(8,128)(2,1)S(1)}, u32[]{:S(2)}, u32[]{:S(2)}) collective-permute-start(bf16[48,1536]{1,0:T(8,128)(2,1)} %constant_dynamic-slice_fusion.1), channel_id=1, source_target_pairs={{0,2},{2,4},{4,6},{6,0},{1,3},{3,5},{5,7},{7,1},{8,10},{10,12},{12... | collective-permute-start | bytes 442376 | tf_op jit(solution)/shard_map/ppermute | solution.py:369
  57.2 25.0 %collective-permute-start.5 = (bf16[48,1536]{1,0:T(8,128)(2,1)}, bf16[48,1536]{1,0:T(8,128)(2,1)S(1)}, u32[]{:S(2)}, u32[]{:S(2)}) collective-permute-start(bf16[48,1536]{1,0:T(8,128)(2,1)} %constant_dynamic-slice_fusion.1), channel_id=1, source_target_pairs={{0,6},{2,0},{4,2},{6,4},{1,7},{3,1},{5,3},{7,5},{8,14},{10,8},{12,... | collective-permute-start | bytes 442376 | tf_op jit(solution)/shard_map/ppermute | solution.py:369
  74.6 7.7 %collective-permute-start.6 = (bf16[48,1536]{1,0:T(8,128)(2,1)}, bf16[48,1536]{1,0:T(8,128)(2,1)S(1)}, u32[]{:S(2)}, u32[]{:S(2)}) collective-permute-start(bf16[48,1536]{1,0:T(8,128)(2,1)} %constant_dynamic-slice_fusion.1), channel_id=1, source_target_pairs={{0,4},{2,6},{4,0},{6,2},{1,5},{3,7},{5,1},{7,3},{8,12},{10,14},{12... | collective-permute-start | bytes 442376 | tf_op jit(solution)/shard_map/ppermute | solution.py:369
  75.5 0.9 copy-start.3
  82.2 3.0 %copy-start.9 = (bf16[96,1536]{1,0:T(8,128)(2,1)S(1)}, bf16[96,1536]{1,0:T(8,128)(2,1)}, u32[]{:S(2)}) copy-start(bf16[96,1536]{1,0:T(8,128)(2,1)} %own_ref.1) | copy-start | bytes 884740
  82.3 2.9 %collective-permute-start.10 = (bf16[3,48,1536]{2,1,0:T(8,128)(2,1)S(1)}, bf16[3,48,1536]{2,1,0:T(8,128)(2,1)S(1)}, u32[]{:S(2)}, u32[]{:S(2)}) collective-permute-start(bf16[3,48,1536]{2,1,0:T(8,128)(2,1)S(1)} %pad_maximum_fusion.1), channel_id=1, source_target_pairs={{0,32},{32,0},{1,33},{33,1},{2,34},{34,2},{3,35},{35,3},{4,36},{36... | collective-permute-start | bytes 1327112 | tf_op jit(solution)/shard_map/ppermute | solution.py:396
  86.5 17.8 %copy-start.7 = (bf16[1,64,1536]{2,1,0:T(8,128)(2,1)S(1)}, bf16[1,64,1536]{2,1,0:T(8,128)(2,1)}, u32[]{:S(2)}) copy-start(bf16[1,64,1536]{2,1,0:T(8,128)(2,1)} %param.11) | copy-start | bytes 589828
  131.0 4.3 %copy-start.12 = (bf16[1536,64]{0,1:T(8,128)(2,1)S(1)}, bf16[1536,64]{0,1:T(8,128)(2,1)}, u32[]{:S(2)}) copy-start(bf16[1536,64]{0,1:T(8,128)(2,1)} %param.21) | copy-start | bytes 589828
  131.0 14.2 %all-to-all-start.3 = ((bf16[4,64,1536]{2,1,0:T(8,128)(2,1)}), bf16[4,64,1536]{2,1,0:T(8,128)(2,1)S(1)}, u32[]{:S(2)}, u32[]{:S(2)}) async-start(bf16[4,64,1536]{2,1,0:T(8,128)(2,1)} %bitcast.18), calls=%async_computation.3 | async-start | bytes 1572864 | tf_op jit(solution)/shard_map/all_to_all | solution.py:405
  134.6 11.7 %copy-start.13 = (f32[1,32,128]{2,1,0:T(8,128)S(1)}, f32[1,32,128]{2,1,0:T(8,128)}, u32[]{:S(2)}) copy-start(f32[1,32,128]{2,1,0:T(8,128)} %param.12) | copy-start | bytes 49156
Sparse Core Ops, SparseCore 0:
  11.7 59.0 all-gather.2

commit v3 on v2

--- a/solution.py
+++ b/solution.py
@@ -60,11 +60,13 @@
         store(source, 1 - core, far_ref, i)
 
 
-def qkv_kernel(pos_ref, h_ref, own_ref, n0_ref, n1_ref, n2_ref, far_ref, q_ref, kv_ref, w_ref):
+def project_kernel(first, pos_ref, h_ref, own_ref, n0_ref, n1_ref, n2_ref, far_ref, out_ref, w_ref):
+    count = out_ref.shape[0]
+
     def store(source, half, ref, index):
-        for k in range(3):
+        for k in range(count):
             if ref is own_ref:
-                value = ref[k, index * 48 : index * 48 + 48, :]
+                value = ref[first + k, index * 48 : index * 48 + 48, :]
             elif index is None:
                 value = ref[k]
             else:
@@ -73,28 +75,22 @@
 
     assemble(pos_ref, own_ref, (n0_ref, n1_ref, n2_ref), far_ref, store)
     h = h_ref[...]
-    for k in range(3):
+    for k in range(count):
         w = w_ref[k].reshape(384, h.shape[1])
-        value = lax.dot_general(h, w, NT, preferred_element_type=F32).astype(BF)
-        if k == 0:
-            q_ref[...] = value
-        else:
-            kv_ref[k - 1] = value
-
-
-def project_qkv(pos, h, own, near, far):
+        out_ref[k] = lax.dot_general(h, w, NT, preferred_element_type=F32).astype(BF)
+
+
+def project(pos, h, own, first, near, far):
     rows, width = h.shape
-    return pl.pallas_call(
-        qkv_kernel,
-        out_shape=[
-            jax.ShapeDtypeStruct((rows, 384), BF),
-            jax.ShapeDtypeStruct((2, rows, 384), BF),
-        ],
+    count = near[0].shape[0]
+    return pl.pallas_call(
+        functools.partial(project_kernel, first),
+        out_shape=jax.ShapeDtypeStruct((count, rows, 384), BF),
         in_specs=[pl.BlockSpec(memory_space=pltpu.SMEM)]
         + [pl.BlockSpec(memory_space=pltpu.VMEM)] * 6,
-        scratch_shapes=[pltpu.VMEM((3, 4, 2, 48, width), BF)],
-        compiler_params=params(),
-        name="project_qkv",
+        scratch_shapes=[pltpu.VMEM((count, 4, 2, 48, width), BF)],
+        compiler_params=params(),
+        name="project",
     )(pos, h, own, *near, far)
 
 
@@ -181,34 +177,19 @@
     )(*args)
 
 
-def out_kernel(pos_ref, a_ref, own_ref, n0_ref, n1_ref, n2_ref, far_ref, out_ref, w_ref):
-    def store(source, half, ref, index):
-        if ref is own_ref:
-            value = ref[index * 48 : index * 48 + 48, :]
-        elif index is None:
-            value = ref[...]
-        else:
-            value = ref[index]
-        w_ref[source, half] = value
-
-    assemble(pos_ref, own_ref, (n0_ref, n1_ref, n2_ref), far_ref, store)
-    w = w_ref[...].reshape(384, out_ref.shape[1])
+def out_kernel(a_ref, w_ref, out_ref):
     out_ref[...] = lax.dot_general(
-        a_ref[...], w, NN, preferred_element_type=F32
+        a_ref[...], w_ref[...], NN, preferred_element_type=F32
     ).astype(BF)
 
 
-def out_projection(pos, a, own, near, far):
-    width = own.shape[1]
+def out_projection(a, w):
     return pl.pallas_call(
         out_kernel,
-        out_shape=jax.ShapeDtypeStruct((a.shape[0], width), BF),
-        in_specs=[pl.BlockSpec(memory_space=pltpu.SMEM)]
-        + [pl.BlockSpec(memory_space=pltpu.VMEM)] * 6,
-        scratch_shapes=[pltpu.VMEM((4, 2, 48, width), BF)],
+        out_shape=jax.ShapeDtypeStruct((a.shape[0], w.shape[1]), BF),
         compiler_params=params(),
         name="out_projection",
-    )(pos, a, own, *near, far)
+    )(a, w)
 
 
 def pack_kernel(pos_ref, up_ref, down_ref, out_ref, sem):
@@ -242,10 +223,10 @@
         out_shape=jax.ShapeDtypeStruct(w_up.shape, BF),
         in_specs=[
             pl.BlockSpec(memory_space=pltpu.SMEM),
-            pl.BlockSpec(memory_space=pl.ANY),
-            pl.BlockSpec(memory_space=pl.ANY),
+            pl.BlockSpec(memory_space=pltpu.HBM),
+            pl.BlockSpec(memory_space=pltpu.HBM),
         ],
-        out_specs=pl.BlockSpec(memory_space=pl.ANY),
+        out_specs=pl.BlockSpec(memory_space=pltpu.HBM),
         scratch_shapes=[pltpu.SemaphoreType.DMA((4,))],
         compiler_params=params(),
         name="pack_ffn",
@@ -275,33 +256,31 @@
     )(tokens, parts, mods)
 
 
-def ffn_kernel(h_ref, up_ref, down_ref, out_ref, acc_ref):
+def ffn_kernel(h_ref, up_ref, down_ref, out_ref, hidden_ref):
     step = pl.program_id(0)
     part = up_ref.shape[-1]
-    hidden = jax.nn.gelu(
-        lax.dot_general(h_ref[...], up_ref[0, 0], NN, preferred_element_type=F32),
-        approximate=True,
-    ).astype(BF)
-    for s in range(4):
-        value = lax.dot_general(
-            hidden,
-            down_ref[0, 0, s * part : (s + 1) * part, :],
-            NN,
-            preferred_element_type=F32,
+
+    @pl.when(step < 2)
+    def _():
+        up = jnp.concatenate([up_ref[0, 0], up_ref[0, 1]], axis=1)
+        hidden_ref[lax.rem(step, 2)] = jax.nn.gelu(
+            lax.dot_general(h_ref[...], up, NN, preferred_element_type=F32),
+            approximate=True,
+        ).astype(BF)
+
+    @pl.when(step >= 2)
+    def _():
+        hidden = jnp.concatenate([hidden_ref[0], hidden_ref[1]], axis=1)
+        down = jnp.concatenate(
+            [
+                jnp.concatenate([down_ref[0, y, :part], down_ref[0, y, part:]], axis=1)
+                for y in range(4)
+            ],
+            axis=0,
         )
-        cols = slice(s * part, (s + 1) * part)
-
-        @pl.when(step == 0)
-        def _():
-            acc_ref[:, cols] = value
-
-        @pl.when(step > 0)
-        def _():
-            acc_ref[:, cols] += value
-
-    @pl.when(step == pl.num_programs(0) - 1)
-    def _():
-        out_ref[...] = acc_ref[...].astype(BF)
+        out_ref[...] = lax.dot_general(
+            hidden, down, NN, preferred_element_type=F32
+        ).astype(BF)
 
 
 def feed_forward(h, weights):
@@ -313,11 +292,11 @@
         out_shape=jax.ShapeDtypeStruct((rows, width), BF),
         in_specs=[
             pl.BlockSpec((rows, width), lambda i: (0, 0)),
-            pl.BlockSpec((1, 1, width, part), lambda i: (0, i, 0, 0)),
-            pl.BlockSpec((1, 1, width, part), lambda i: (1, i, 0, 0)),
+            pl.BlockSpec((1, 2, width, part), lambda i: (0, jnp.minimum(i, 1), 0, 0)),
+            pl.BlockSpec((1, 4, 2 * part, part), lambda i: (1, 0, jnp.maximum(i - 2, 0), 0)),
         ],
-        out_specs=pl.BlockSpec((rows, width), lambda i: (0, 0)),
-        scratch_shapes=[pltpu.VMEM((rows, width), F32)],
+        out_specs=pl.BlockSpec((rows, 2 * part), lambda i: (0, jnp.maximum(i - 2, 0))),
+        scratch_shapes=[pltpu.VMEM((2, rows, 2 * part), BF)],
         compiler_params=params(),
         name="feed_forward",
     )(h, weights, weights)
@@ -368,35 +347,36 @@
     def to_lines(value, step):
         return lax.ppermute(value, "ty", [(i, (i + step) % 4) for i in range(4)])
 
+    half_out = lax.dynamic_slice_in_dim(w_out, core * 48, 48, 0)
+    out_full = lax.all_gather(half_out, ("ty", "core"), axis=0, tiled=True)
+
+    own_qkv = jnp.transpose(w_qkv, (1, 2, 0))
+    half_qkv = lax.dynamic_slice_in_dim(own_qkv, core * 48, 48, 1)
+    h1 = first_norm(tokens, mods, 4)
+    h1, half_qkv, pos = lax.optimization_barrier((h1, half_qkv, pos))
+    near_kv = [to_lines(half_qkv[1:], step) for step in STRIDES]
     half_ffn = pack_ffn(pos, w_up, w_down)
     ffn_full = lax.all_gather(half_ffn, ("core", "tx"), axis=0, tiled=False)
     ffn_full = ffn_full.reshape(2, 4, width, w_up.shape[1])
-
-    own_qkv = jnp.transpose(w_qkv, (1, 2, 0))
-    half_qkv = lax.dynamic_slice_in_dim(own_qkv, core * 48, 48, 1)
-    h1 = first_norm(tokens, mods, 4)
-    h1, half_qkv = lax.optimization_barrier((h1, half_qkv))
-    near_qkv = [to_lines(half_qkv, step) for step in STRIDES]
     h1 = lax.all_to_all(h1, "tx", split_axis=0, concat_axis=0, tiled=True)
-    *near_qkv, h1 = lax.optimization_barrier((*near_qkv, h1))
-    far_qkv = lax.ppermute(jnp.stack(near_qkv), "core", swap2)
+
+    *near_kv, h1, half_q = lax.optimization_barrier((*near_kv, h1, half_qkv[:1]))
+    far_kv = lax.ppermute(jnp.stack(near_kv), "core", swap2)
+    near_q = [to_lines(half_q, step) for step in STRIDES]
     h1 = h1.reshape(4 * rows, width)
-    query, keyval = project_qkv(pos, h1, own_qkv, near_qkv, far_qkv)
-
-    half_out = lax.dynamic_slice_in_dim(w_out, core * 48, 48, 0)
-    half_out, keyval = lax.optimization_barrier((half_out, keyval))
+    keyval = project(pos, h1, own_qkv, 1, near_kv, far_kv)
     chunks = [to_lines(keyval, step) for step in STRIDES]
-    near_out = [to_lines(half_out, step) for step in STRIDES]
+    *near_q, keyval = lax.optimization_barrier((*near_q, keyval))
+    far_q = lax.ppermute(jnp.stack(near_q), "core", swap2)
+    query = project(pos, h1, own_qkv, 0, near_q, far_q)[0]
+
     text = lax.dynamic_slice_in_dim(text_kv[0], lax.axis_index("tx") * 384, 384, 2)
     text = jnp.transpose(text, (1, 0, 2))
     state = attention(query, [keyval], text=text, length=text_len)
     state = attention(query, chunks[:2], state=state)
-    *near_out, across, totals = lax.optimization_barrier((*near_out, chunks[2], state[2]))
-    state = (state[0], state[1], totals)
-    far_out = lax.ppermute(jnp.stack(near_out), "core", swap2)
-    attended = attention(query, [across], state=state, last=True)
-
-    partial = out_projection(pos, attended, w_out, near_out, far_out)
+    attended = attention(query, chunks[2:], state=state, last=True)
+
+    partial = out_projection(attended, out_full)
     partial = partial.reshape(4, rows, width)
     partial = lax.all_to_all(partial, "tx", split_axis=0, concat_axis=0, tiled=True)
     second, h2 = second_norm(tokens, partial, mods)

time: 154 us -> 157 us (1.019)
  the two profiles are of different devices: /device:TPU:128 before, /device:TPU:32 now
where the time goes in v3:
time: 157 us; the launch traced here: 156 us
  blocking collectives  40.9 us (26%)
  waiting for transfers between devices  38.4 us (24%)
  Pallas kernels  25.9 us (16%)
  starting transfers between devices  21.5 us (14%)
  between operations  15.7 us (10%)
  local copies, waits for them, and re-layouts  11 us (7%)
  other arithmetic  2.66 us (2%)
    ppermute x9, waiting for transfers between devices, to_lines(): return lax.ppermute(value, 'ty', [(i, (i + step) % 4) for i in range(4)])  28.7 us
    all_to_all x1, blocking collectives, on_device(): lax.all_to_all(partial, 'tx', split_axis=0, concat_axis=0, tiled=True)  25.3 us
    all_to_all x1, blocking collectives, on_device(): h2 = lax.all_to_all(h2, 'ty', split_axis=0, concat_axis=0, tiled=True)  15.7 us
    ppermute x9, starting transfers between devices, to_lines(): return lax.ppermute(value, 'ty', [(i, (i + step) % 4) for i in range(4)])  13.4 us
    pallas_call x3, Pallas kernels, attention(): pl.pallas_call(functools.partial(attention_kernel, len(kvs), text is not...  9.78 us
    all_to_all x1, waiting for transfers between devices, on_device(): lax.all_to_all(partial, 'ty', split_axis=0, concat_axis=0, tiled=True)  9.6 us
    pallas_call x1, Pallas kernels, feed_forward(): pl.pallas_call(ffn_kernel, grid=(4,), out_shape=jax.ShapeDtypeStruct((row...  7.5 us
    unnamed x39, local copies, waits for them, and re-layouts  7.39 us
  transfers between devices with their start and end apart: 15, of which 7 were waited for; matrix products, arithmetic and copies ran while one was open for 3% of the time, Pallas kernels for 11%

profile of v3, /device:TPU:32, one launch (start us, length us, event | category | flops | bytes accessed | tf_op | source)
XLA Modules:
  0.0 156.1 jit_solution(5105104233555679355)
XLA Ops:
  7.3 1.7 %constant_dynamic-slice_fusion = bf16[48,1536]{1,0:T(8,128)(2,1)} fusion(bf16[96,1536]{1,0:T(8,128)(2,1)} %param.18, s32[]{:T(128)S(6)} %select_n.7), kind=kLoop, calls=%fused_computation.5 | loop fusion | bytes 294916 | tf_op jit(solution)/shard_map/dynamic_slice | solution.py:350
  10.8 1.2 first_norm.1
  12.1 1.3 copy-done.6
  13.4 1.6 %pack_ffn.1 = bf16[1536,384]{1,0:T(8,128)(2,1)} custom-call(s32[2]{0:T(128)S(1)} %pad_add_fusion.pos_ref, bf16[1536,384]{1,0:T(8,128)(2,1)S(1)} %copy-done.5, bf16[384,1536]{1,0:T(8,128)(2,1)S(1)} %copy-done.6), custom_call_target="tpu_custom_call" | custom-call | tf_op jit(solution)/shard_map/pack_ffn/pallas_call | solution.py:221
  15.0 4.3 %all-to-all-start = ((bf16[4,64,1536]{2,1,0:T(8,128)(2,1)}), bf16[4,64,1536]{2,1,0:T(8,128)(2,1)S(1)}, u32[]{:S(2)}, u32[]{:S(2)}) async-start(bf16[4,64,1536]{2,1,0:T(8,128)(2,1)} %first_norm.1), calls=%async_computation | async-start | bytes 1572864 | tf_op jit(solution)/shard_map/all_to_all | solution.py:361
  19.3 1.7 %collective-permute-start = (bf16[2,48,1536]{2,1,0:T(8,128)(2,1)S(1)}, bf16[2,48,1536]{2,1,0:T(8,128)(2,1)S(1)}, u32[]{:S(2)}, u32[]{:S(2)}) collective-permute-start(bf16[2,48,1536]{2,1,0:T(8,128)(2,1)S(1)} %slice.8), channel_id=1, source_target_pairs={{0,2},{2,4},{4,6},{6,0},{1,3},{3,5},{5,7},{7,1},{8,10},{10,12},{12... | collective-permute-start | bytes 884744 | tf_op jit(solution)/shard_map/ppermute | solution.py:348
  21.0 1.7 %collective-permute-start.1 = (bf16[2,48,1536]{2,1,0:T(8,128)(2,1)S(1)}, bf16[2,48,1536]{2,1,0:T(8,128)(2,1)S(1)}, u32[]{:S(2)}, u32[]{:S(2)}) collective-permute-start(bf16[2,48,1536]{2,1,0:T(8,128)(2,1)S(1)} %slice.8), channel_id=1, source_target_pairs={{0,6},{2,0},{4,2},{6,4},{1,7},{3,1},{5,3},{7,5},{8,14},{10,8},{12,... | collective-permute-start | bytes 884744 | tf_op jit(solution)/shard_map/ppermute | solution.py:348
  22.6 2.0 %collective-permute-start.2 = (bf16[2,48,1536]{2,1,0:T(8,128)(2,1)S(1)}, bf16[2,48,1536]{2,1,0:T(8,128)(2,1)}, u32[]{:S(2)}, u32[]{:S(2)}) collective-permute-start(bf16[2,48,1536]{2,1,0:T(8,128)(2,1)S(1)} %slice.8), channel_id=1, source_target_pairs={{0,4},{2,6},{4,0},{6,2},{1,5},{3,7},{5,1},{7,3},{8,12},{10,14},{12... | collective-permute-start | bytes 884744 | tf_op jit(solution)/shard_map/ppermute | solution.py:348
  24.6 1.6 %slice.9 = bf16[1,48,1536]{2,1,0:T(8,128)(2,1)} slice(bf16[3,48,1536]{2,1,0:T(8,128)(2,1)} %copy-done.15), slice={[0:1], [0:48], [0:1536]} | slice | bytes 294912 | tf_op jit(solution)/shard_map/slice | solution.py:363
  26.2 4.9 %collective-permute-done.n0_ref = bf16[2,48,1536]{2,1,0:T(8,128)(2,1)S(1)} collective-permute-done((bf16[2,48,1536]{2,1,0:T(8,128)(2,1)S(1)}, bf16[2,48,1536]{2,1,0:T(8,128)(2,1)S(1)}, u32[]{:S(2)}, u32[]{:S(2)}) %collective-permute-start) | collective-permute-done | bytes 294944 | tf_op jit(solution)/shard_map/ppermute | solution.py:348
  31.1 3.2 %collective-permute-done.1.n1_ref = bf16[2,48,1536]{2,1,0:T(8,128)(2,1)S(1)} collective-permute-done((bf16[2,48,1536]{2,1,0:T(8,128)(2,1)S(1)}, bf16[2,48,1536]{2,1,0:T(8,128)(2,1)S(1)}, u32[]{:S(2)}, u32[]{:S(2)}) %collective-permute-start.1) | collective-permute-done | bytes 294944 | tf_op jit(solution)/shard_map/ppermute | solution.py:348
  34.3 7.2 %collective-permute-done.2.n2_ref = bf16[2,48,1536]{2,1,0:T(8,128)(2,1)} collective-permute-done((bf16[2,48,1536]{2,1,0:T(8,128)(2,1)S(1)}, bf16[2,48,1536]{2,1,0:T(8,128)(2,1)}, u32[]{:S(2)}, u32[]{:S(2)}) %collective-permute-start.2) | collective-permute-done | bytes 294944 | tf_op jit(solution)/shard_map/ppermute | solution.py:348
  41.5 1.1 pad_maximum_fusion
  42.7 1.2 collective-permute-start.3
  43.9 2.1 %collective-permute-start.4 = (bf16[1,48,1536]{2,1,0:T(8,128)(2,1)S(1)}, bf16[1,48,1536]{2,1,0:T(8,128)(2,1)S(1)}, u32[]{:S(2)}, u32[]{:S(2)}) collective-permute-start(bf16[1,48,1536]{2,1,0:T(8,128)(2,1)S(1)} %copy-done.17), channel_id=1, source_target_pairs={{0,6},{2,0},{4,2},{6,4},{1,7},{3,1},{5,3},{7,5},{8,14},{10,8},{12,... | collective-permute-start | bytes 442376 | tf_op jit(solution)/shard_map/ppermute | solution.py:348
  47.0 2.1 %project.2.refs_2_ = bf16[2,256,384]{2,1,0:T(8,128)(2,1)S(1)} custom-call(s32[2]{0:T(128)S(1)} %pad_add_fusion.pos_ref, bf16[256,1536]{1,0:T(8,128)(2,1)S(1)} %bitcast.26, bf16[3,96,1536]{2,1,0:T(8,128)(2,1)S(1)} %bitcast.28, bf16[2,48,1536]{2,1,0:T(8,128)(2,1)S(1)} %collective-permute-done.n0_ref, bf16[2,48,1536]{2,1,0:T(8,128)(2,1)S(1)} %copy-done.3, ...), custom_call_target="tpu_custom_call" | custom-call | tf_op jit(solution)/shard_map/project/pallas_call | solution.py:86
  49.1 4.2 %collective-permute-done.3.n0_ref = bf16[1,48,1536]{2,1,0:T(8,128)(2,1)S(1)} collective-permute-done((bf16[1,48,1536]{2,1,0:T(8,128)(2,1)S(1)}, bf16[1,48,1536]{2,1,0:T(8,128)(2,1)S(1)}, u32[]{:S(2)}, u32[]{:S(2)}) %collective-permute-start.3) | collective-permute-done | bytes 147488 | tf_op jit(solution)/shard_map/ppermute | solution.py:348
  55.1 2.3 %collective-permute-start.10 = (bf16[2,256,384]{2,1,0:T(8,128)(2,1)S(1)}, bf16[2,256,384]{2,1,0:T(8,128)(2,1)}, u32[]{:S(2)}, u32[]{:S(2)}) collective-permute-start(bf16[2,256,384]{2,1,0:T(8,128)(2,1)S(1)} %project.2.refs_2_), channel_id=1, source_target_pairs={{0,6},{2,0},{4,2},{6,4},{1,7},{3,1},{5,3},{7,5},{8,14},{10,8},{12,... | collective-permute-start | bytes 1179656 | tf_op jit(solution)/shard_map/ppermute | solution.py:348
  57.5 1.5 collective-permute-start.8
  61.7 1.7 %project.3 = bf16[1,256,384]{2,1,0:T(8,128)(2,1)S(1)} custom-call(s32[2]{0:T(128)S(1)} %pad_add_fusion.pos_ref, bf16[256,1536]{1,0:T(8,128)(2,1)S(1)} %bitcast.27, bf16[3,96,1536]{2,1,0:T(8,128)(2,1)S(1)} %bitcast.29, bf16[1,48,1536]{2,1,0:T(8,128)(2,1)S(1)} %collective-permute-done.3.n0_ref, bf16[1,48,1536]{2,1,0:T(8,128)(2,1)S(1)} %copy-done.10, ...), custom_call_target="tpu_custom_call" | custom-call | tf_op jit(solution)/shard_map/project/pallas_call | solution.py:86
  63.4 2.1 %attention.3 = (f32[256,384]{1,0:T(8,128)S(1)}, f32[256,384]{1,0:T(8,128)S(1)}, f32[256,384]{1,0:T(8,128)S(1)}) custom-call(s32[1]{0:T(128)S(6)} %copy.17.refs_0_, bf16[256,384]{1,0:T(8,128)(2,1)S(1)} %bitcast.32, bf16[2,256,384]{2,1,0:T(8,128)(2,1)S(1)} %project.2.refs_2_, bf16[2,154,384]{2,1,0:T(8,128)(2,1)S(1)} %bitcast.37), custom_call_target="tpu_custom_call" | custom-call | tf_op jit(solution)/shard_map/attention/pallas_call | solution.py:169
  65.4 1.6 %collective-permute-done.9.refs_1_ = bf16[2,256,384]{2,1,0:T(8,128)(2,1)} collective-permute-done((bf16[2,256,384]{2,1,0:T(8,128)(2,1)S(1)}, bf16[2,256,384]{2,1,0:T(8,128)(2,1)}, u32[]{:S(2)}, u32[]{:S(2)}) %collective-permute-start.9) | collective-permute-done | bytes 393248 | tf_op jit(solution)/shard_map/ppermute | solution.py:348
  67.1 7.6 %collective-permute-done.10.refs_2_ = bf16[2,256,384]{2,1,0:T(8,128)(2,1)} collective-permute-done((bf16[2,256,384]{2,1,0:T(8,128)(2,1)S(1)}, bf16[2,256,384]{2,1,0:T(8,128)(2,1)}, u32[]{:S(2)}, u32[]{:S(2)}) %collective-permute-start.10) | collective-permute-done | bytes 393248 | tf_op jit(solution)/shard_map/ppermute | solution.py:348
  74.7 3.9 %attention.4 = (f32[256,384]{1,0:T(8,128)S(1)}, f32[256,384]{1,0:T(8,128)S(1)}, f32[256,384]{1,0:T(8,128)S(1)}) custom-call(bf16[256,384]{1,0:T(8,128)(2,1)S(1)} %bitcast.33, bf16[2,256,384]{2,1,0:T(8,128)(2,1)} %collective-permute-done.9.refs_1_, bf16[2,256,384]{2,1,0:T(8,128)(2,1)} %collective-permute-done.10.refs_2_, ...), custom_call_target="tpu_custom_call" | custom-call | tf_op jit(solution)/shard_map/attention/pallas_call | solution.py:169
  78.6 3.8 %attention.5.a_ref = bf16[256,384]{1,0:T(8,128)(2,1)S(1)} custom-call(bf16[256,384]{1,0:T(8,128)(2,1)S(1)} %bitcast.34, bf16[2,256,384]{2,1,0:T(8,128)(2,1)} %collective-permute-done.8.refs_1_, f32[256,384]{1,0:T(8,128)S(1)} %get-tuple-element.39.refs_2_, f32[256,384]{1,0:T(8,128)S(1)} %get-tuple-element.40.refs_3_, f32[256,384]{1,0:T(8,128)S(1)} %get-tuple-element.41.refs_4_), custom_call_target="tpu_custom_call" | custom-call | tf_op jit(solution)/shard_map/attention/pallas_call | solution.py:169
  82.5 1.3 copy-done.4
  84.4 25.3 %all_to_all.20.part_ref = bf16[4,64,1536]{2,1,0:T(8,128)(2,1)S(1)} all-to-all(bf16[4,64,1536]{2,1,0:T(8,128)(2,1)S(1)} %bitcast.31), channel_id=1, replica_groups=mesh['zl'=4,'core'=2,'tx'=4,'ty'=4,'blk'=2] {'tx'}, dimensions={0} | all-to-all | bytes 1572864 | tf_op jit(solution)/shard_map/all_to_all | solution.py:381
  110.0 15.7 %all_to_all.21 = bf16[4,64,1536]{2,1,0:T(8,128)(2,1)S(1)} all-to-all(bf16[4,64,1536]{2,1,0:T(8,128)(2,1)S(1)} %get-tuple-element.43), channel_id=1, replica_groups=mesh['zl'=4,'core'=2,'tx'=4,'ty'=4,'blk'=2] {'ty'}, dimensions={0} | all-to-all | bytes 1572864 | tf_op jit(solution)/shard_map/all_to_all | solution.py:383
  125.7 7.5 %feed_forward.1 = bf16[256,1536]{1,0:T(8,128)(2,1)} custom-call(bf16[256,1536]{1,0:T(8,128)(2,1)S(1)} %bitcast.30, bf16[2,4,1536,384]{3,2,1,0:T(8,128)(2,1)} %bitcast.46, bf16[2,4,1536,384]{3,2,1,0:T(8,128)(2,1)} %bitcast.47), custom_call_target="tpu_custom_call" | custom-call | tf_op jit(solution)/shard_map/feed_forward/pallas_call | solution.py:289
  133.2 3.6 %all-to-all-start.3 = ((bf16[4,64,1536]{2,1,0:T(8,128)(2,1)}), bf16[4,64,1536]{2,1,0:T(8,128)(2,1)S(1)}, u32[]{:S(2)}, u32[]{:S(2)}) async-start(bf16[4,64,1536]{2,1,0:T(8,128)(2,1)} %bitcast.19), calls=%async_computation.3 | async-start | bytes 1572864 | tf_op jit(solution)/shard_map/all_to_all | solution.py:385
  137.9 9.6 %all-to-all-done.3.part_ref = bf16[4,64,1536]{2,1,0:T(8,128)(2,1)S(1)} async-done(((bf16[4,64,1536]{2,1,0:T(8,128)(2,1)}), bf16[4,64,1536]{2,1,0:T(8,128)(2,1)S(1)}, u32[]{:S(2)}, u32[]{:S(2)}) %all-to-all-start.3) | async-done | bytes 786464 | tf_op jit(solution)/shard_map/all_to_all | solution.py:385
  147.5 1.1 last_stage.1
  (64 shorter events, 8.8 us)
Async XLA Ops:
  7.2 52.4 %copy-start = (bf16[1,154,2,1536]{3,2,1,0:T(2,128)(2,1)S(1)}, bf16[1,154,2,1536]{3,2,1,0:T(2,128)(2,1)}, u32[]{:S(2)}) copy-start(bf16[1,154,2,1536]{3,2,1,0:T(2,128)(2,1)} %param.14) | copy-start | bytes 2838532
  7.2 4.9 %copy-start.1 = (bf16[1536,3,96]{0,2,1:T(8,128)(2,1)S(1)}, bf16[1536,3,96]{0,2,1:T(8,128)(2,1)}, u32[]{:S(2)}) copy-start(bf16[1536,3,96]{0,2,1:T(8,128)(2,1)} %param.17) | copy-start | bytes 2654212
  7.2 75.3 %all-gather.4.cloned.1.call-start = ((), (), s32[]{:S(2)}) async-start(), calls=%async_computation.4 | async-start | bytes 1327104 | tf_op jit(solution)/shard_map/all_gather | solution.py:351
  7.2 4.8 %copy-start.5 = (bf16[1536,384]{1,0:T(8,128)(2,1)S(1)}, bf16[1536,384]{1,0:T(8,128)(2,1)}, u32[]{:S(2)}) copy-start(bf16[1536,384]{1,0:T(8,128)(2,1)} %up_ref.1) | copy-start | bytes 3538948
  9.0 116.7 %all-gather.6.cloned.1.call-start = ((), (), s32[]{:S(2)}) async-start(), calls=%async_computation.5 | async-start | bytes 10616832 | tf_op jit(solution)/shard_map/all_gather | solution.py:359
  9.1 0.9 copy-start.7
  12.1 1.3 copy-start.6
  13.4 5.9 %copy-start.15 = (bf16[3,48,1536]{2,1,0:T(8,128)(2,1)}, bf16[3,48,1536]{2,1,0:T(8,128)(2,1)S(1)}, u32[]{:S(2)}) copy-start(bf16[3,48,1536]{2,1,0:T(8,128)(2,1)S(1)} %dynamic-slice_bitcast_fusion) | copy-start | bytes 1327108
  15.0 26.5 %all-to-all-start = ((bf16[4,64,1536]{2,1,0:T(8,128)(2,1)}), bf16[4,64,1536]{2,1,0:T(8,128)(2,1)S(1)}, u32[]{:S(2)}, u32[]{:S(2)}) async-start(bf16[4,64,1536]{2,1,0:T(8,128)(2,1)} %first_norm.1), calls=%async_computation | async-start | bytes 1572864 | tf_op jit(solution)/shard_map/all_to_all | solution.py:361
  19.3 11.8 %collective-permute-start = (bf16[2,48,1536]{2,1,0:T(8,128)(2,1)S(1)}, bf16[2,48,1536]{2,1,0:T(8,128)(2,1)S(1)}, u32[]{:S(2)}, u32[]{:S(2)}) collective-permute-start(bf16[2,48,1536]{2,1,0:T(8,128)(2,1)S(1)} %slice.8), channel_id=1, source_target_pairs={{0,2},{2,4},{4,6},{6,0},{1,3},{3,5},{5,7},{7,1},{8,10},{10,12},{12... | collective-permute-start | bytes 884744 | tf_op jit(solution)/shard_map/ppermute | solution.py:348
  21.0 13.4 %collective-permute-start.1 = (bf16[2,48,1536]{2,1,0:T(8,128)(2,1)S(1)}, bf16[2,48,1536]{2,1,0:T(8,128)(2,1)S(1)}, u32[]{:S(2)}, u32[]{:S(2)}) collective-permute-start(bf16[2,48,1536]{2,1,0:T(8,128)(2,1)S(1)} %slice.8), channel_id=1, source_target_pairs={{0,6},{2,0},{4,2},{6,4},{1,7},{3,1},{5,3},{7,5},{8,14},{10,8},{12,... | collective-permute-start | bytes 884744 | tf_op jit(solution)/shard_map/ppermute | solution.py:348
  22.6 18.9 %collective-permute-start.2 = (bf16[2,48,1536]{2,1,0:T(8,128)(2,1)S(1)}, bf16[2,48,1536]{2,1,0:T(8,128)(2,1)}, u32[]{:S(2)}, u32[]{:S(2)}) collective-permute-start(bf16[2,48,1536]{2,1,0:T(8,128)(2,1)S(1)} %slice.8), channel_id=1, source_target_pairs={{0,4},{2,6},{4,0},{6,2},{1,5},{3,7},{5,1},{7,3},{8,12},{10,14},{12... | collective-permute-start | bytes 884744 | tf_op jit(solution)/shard_map/ppermute | solution.py:348
  34.3 11.8 %copy-start.2 = (bf16[2,48,1536]{2,1,0:T(8,128)(2,1)}, bf16[2,48,1536]{2,1,0:T(8,128)(2,1)S(1)}, u32[]{:S(2)}) copy-start(bf16[2,48,1536]{2,1,0:T(8,128)(2,1)S(1)} %collective-permute-done.1.n1_ref) | copy-start | bytes 884740
  41.5 1.2 copy-start.17
  42.6 3.5 %collective-permute-start.6 = (bf16[3,2,48,1536]{3,2,1,0:T(8,128)(2,1)S(1)}, bf16[3,2,48,1536]{3,2,1,0:T(8,128)(2,1)S(1)}, u32[]{:S(2)}, u32[]{:S(2)}) collective-permute-start(bf16[3,2,48,1536]{3,2,1,0:T(8,128)(2,1)S(1)} %pad_maximum_fusion), channel_id=1, source_target_pairs={{0,32},{32,0},{1,33},{33,1},{2,34},{34,2},{3,35},{35,3},{4,36},{36... | collective-permute-start | bytes 2654216 | tf_op jit(solution)/shard_map/ppermute | solution.py:364
  42.7 10.6 %collective-permute-start.3 = (bf16[1,48,1536]{2,1,0:T(8,128)(2,1)S(1)}, bf16[1,48,1536]{2,1,0:T(8,128)(2,1)S(1)}, u32[]{:S(2)}, u32[]{:S(2)}) collective-permute-start(bf16[1,48,1536]{2,1,0:T(8,128)(2,1)S(1)} %copy-done.17), channel_id=1, source_target_pairs={{0,2},{2,4},{4,6},{6,0},{1,3},{3,5},{5,7},{7,1},{8,10},{10,12},{12... | collective-permute-start | bytes 442376 | tf_op jit(solution)/shard_map/ppermute | solution.py:348
  43.9 9.4 %collective-permute-start.4 = (bf16[1,48,1536]{2,1,0:T(8,128)(2,1)S(1)}, bf16[1,48,1536]{2,1,0:T(8,128)(2,1)S(1)}, u32[]{:S(2)}, u32[]{:S(2)}) collective-permute-start(bf16[1,48,1536]{2,1,0:T(8,128)(2,1)S(1)} %copy-done.17), channel_id=1, source_target_pairs={{0,6},{2,0},{4,2},{6,4},{1,7},{3,1},{5,3},{7,5},{8,14},{10,8},{12,... | collective-permute-start | bytes 442376 | tf_op jit(solution)/shard_map/ppermute | solution.py:348
  46.0 7.3 %collective-permute-start.5 = (bf16[1,48,1536]{2,1,0:T(8,128)(2,1)S(1)}, bf16[1,48,1536]{2,1,0:T(8,128)(2,1)S(1)}, u32[]{:S(2)}, u32[]{:S(2)}) collective-permute-start(bf16[1,48,1536]{2,1,0:T(8,128)(2,1)S(1)} %copy-done.17), channel_id=1, source_target_pairs={{0,4},{2,6},{4,0},{6,2},{1,5},{3,7},{5,1},{7,3},{8,12},{10,14},{12... | collective-permute-start | bytes 442376 | tf_op jit(solution)/shard_map/ppermute | solution.py:348
  46.1 1.0 copy-start.3
  53.3 1.8 %copy-start.9 = (bf16[1,48,1536]{2,1,0:T(8,128)(2,1)}, bf16[1,48,1536]{2,1,0:T(8,128)(2,1)S(1)}, u32[]{:S(2)}) copy-start(bf16[1,48,1536]{2,1,0:T(8,128)(2,1)S(1)} %collective-permute-done.4.n1_ref) | copy-start | bytes 442372
  53.3 4.1 %copy-start.11 = (bf16[1,48,1536]{2,1,0:T(8,128)(2,1)}, bf16[1,48,1536]{2,1,0:T(8,128)(2,1)S(1)}, u32[]{:S(2)}) copy-start(bf16[1,48,1536]{2,1,0:T(8,128)(2,1)S(1)} %collective-permute-done.5.n2_ref) | copy-start | bytes 442372
  54.2 5.6 %collective-permute-start.7 = (bf16[3,1,48,1536]{3,2,1,0:T(8,128)(2,1)}, bf16[3,1,48,1536]{3,2,1,0:T(8,128)(2,1)}, u32[]{:S(2)}, u32[]{:S(2)}) collective-permute-start(bf16[3,1,48,1536]{3,2,1,0:T(8,128)(2,1)} %pad_maximum_fusion.1), channel_id=1, source_target_pairs={{0,32},{32,0},{1,33},{33,1},{2,34},{34,2},{3,35},{35,3},{4,36},{36... | collective-permute-start | bytes 1327112 | tf_op jit(solution)/shard_map/ppermute | solution.py:370
  54.2 12.8 %collective-permute-start.9 = (bf16[2,256,384]{2,1,0:T(8,128)(2,1)S(1)}, bf16[2,256,384]{2,1,0:T(8,128)(2,1)}, u32[]{:S(2)}, u32[]{:S(2)}) collective-permute-start(bf16[2,256,384]{2,1,0:T(8,128)(2,1)S(1)} %project.2.refs_2_), channel_id=1, source_target_pairs={{0,2},{2,4},{4,6},{6,0},{1,3},{3,5},{5,7},{7,1},{8,10},{10,12},{12... | collective-permute-start | bytes 1179656 | tf_op jit(solution)/shard_map/ppermute | solution.py:348
  55.1 19.6 %collective-permute-start.10 = (bf16[2,256,384]{2,1,0:T(8,128)(2,1)S(1)}, bf16[2,256,384]{2,1,0:T(8,128)(2,1)}, u32[]{:S(2)}, u32[]{:S(2)}) collective-permute-start(bf16[2,256,384]{2,1,0:T(8,128)(2,1)S(1)} %project.2.refs_2_), channel_id=1, source_target_pairs={{0,6},{2,0},{4,2},{6,4},{1,7},{3,1},{5,3},{7,5},{8,14},{10,8},{12,... | collective-permute-start | bytes 1179656 | tf_op jit(solution)/shard_map/ppermute | solution.py:348
  57.5 21.1 %collective-permute-start.8 = (bf16[2,256,384]{2,1,0:T(8,128)(2,1)S(1)}, bf16[2,256,384]{2,1,0:T(8,128)(2,1)}, u32[]{:S(2)}, u32[]{:S(2)}) collective-permute-start(bf16[2,256,384]{2,1,0:T(8,128)(2,1)S(1)} %project.2.refs_2_), channel_id=1, source_target_pairs={{0,4},{2,6},{4,0},{6,2},{1,5},{3,7},{5,1},{7,3},{8,12},{10,14},{12... | collective-permute-start | bytes 1179656 | tf_op jit(solution)/shard_map/ppermute | solution.py:348
  60.7 0.9 copy-start.12
  82.5 1.3 copy-start.4
  84.4 25.3 %copy-start.8 = (bf16[1,64,1536]{2,1,0:T(8,128)(2,1)S(1)}, bf16[1,64,1536]{2,1,0:T(8,128)(2,1)}, u32[]{:S(2)}) copy-start(bf16[1,64,1536]{2,1,0:T(8,128)(2,1)} %param.11) | copy-start | bytes 589828
  84.4 25.3 %copy-start.14 = (f32[1,8,1536]{2,1,0:T(8,128)S(1)}, f32[1,8,1536]{2,1,0:T(8,128)}, u32[]{:S(2)}) copy-start(f32[1,8,1536]{2,1,0:T(8,128)} %param.13) | copy-start | bytes 147460
  133.2 4.3 %copy-start.16 = (bf16[1536,64]{0,1:T(8,128)(2,1)S(1)}, bf16[1536,64]{0,1:T(8,128)(2,1)}, u32[]{:S(2)}) copy-start(bf16[1536,64]{0,1:T(8,128)(2,1)} %param.21) | copy-start | bytes 589828
  133.2 14.2 %all-to-all-start.3 = ((bf16[4,64,1536]{2,1,0:T(8,128)(2,1)}), bf16[4,64,1536]{2,1,0:T(8,128)(2,1)S(1)}, u32[]{:S(2)}, u32[]{:S(2)}) async-start(bf16[4,64,1536]{2,1,0:T(8,128)(2,1)} %bitcast.19), calls=%async_computation.3 | async-start | bytes 1572864 | tf_op jit(solution)/shard_map/all_to_all | solution.py:385
  136.8 11.8 %copy-start.18 = (f32[1,32,128]{2,1,0:T(8,128)S(1)}, f32[1,32,128]{2,1,0:T(8,128)}, u32[]{:S(2)}) copy-start(f32[1,32,128]{2,1,0:T(8,128)} %param.12) | copy-start | bytes 49156
  (2 other events, 1.7 us)
Sparse Core Ops, SparseCore 0:
  9.9 31.0 all-gather.3
  42.9 68.3 all-gather.5

commit v4 on v3

--- a/solution.py
+++ b/solution.py
@@ -61,7 +61,7 @@
 
 
 def project_kernel(first, pos_ref, h_ref, own_ref, n0_ref, n1_ref, n2_ref, far_ref, out_ref, w_ref):
-    count = out_ref.shape[0]
+    count = out_ref.shape[1]
 
     def store(source, half, ref, index):
         for k in range(count):
@@ -77,15 +77,16 @@
     h = h_ref[...]
     for k in range(count):
         w = w_ref[k].reshape(384, h.shape[1])
-        out_ref[k] = lax.dot_general(h, w, NT, preferred_element_type=F32).astype(BF)
-
-
-def project(pos, h, own, first, near, far):
+        value = lax.dot_general(h, w, NT, preferred_element_type=F32).astype(BF)
+        for i in range(out_ref.shape[0]):
+            out_ref[i, k] = value
+
+
+def project(pos, h, own, first, count, copies, near, far):
     rows, width = h.shape
-    count = near[0].shape[0]
     return pl.pallas_call(
         functools.partial(project_kernel, first),
-        out_shape=jax.ShapeDtypeStruct((count, rows, 384), BF),
+        out_shape=jax.ShapeDtypeStruct((copies, count, rows, 384), BF),
         in_specs=[pl.BlockSpec(memory_space=pltpu.SMEM)]
         + [pl.BlockSpec(memory_space=pltpu.VMEM)] * 6,
         scratch_shapes=[pltpu.VMEM((count, 4, 2, 48, width), BF)],
@@ -94,17 +95,21 @@
     )(pos, h, own, *near, far)
 
 
-def attention_kernel(chunks, has_text, has_state, last, *refs):
+def attention_kernel(own, *refs):
     refs = list(refs)
-    len_ref = refs.pop(0) if has_text else None
-    q_ref = refs.pop(0)
-    kv_refs = [refs.pop(0) for _ in range(chunks)]
-    text_ref = refs.pop(0) if has_text else None
-    state_refs = [refs.pop(0) for _ in range(3)] if has_state else None
+    pos_ref, q_ref, kv_ref = refs[:3]
+    if own:
+        text_ref = refs[3]
+        state_refs = None
+        outs = refs[4:]
+    else:
+        state_refs = refs[3:6]
+        outs = refs[6:]
     rows = q_ref.shape[0]
-    if has_text:
-        live = lax.broadcasted_iota(jnp.int32, (rows, TXT), 1) < len_ref[0]
+    if own:
+        live = lax.broadcasted_iota(jnp.int32, (rows, TXT), 1) < pos_ref[2]
     first = lax.broadcasted_iota(jnp.int32, (rows, 128), 1) < HEAD_DIM
+    where = [0] if own else [lax.rem(pos_ref[1] + i, 4) for i in (1, 2, 3)]
     for g in range(q_ref.shape[1] // 128):
         cols = slice(g * 128, g * 128 + 128)
         q = q_ref[:, cols]
@@ -113,10 +118,13 @@
             here = first if side == 0 else jnp.logical_not(first)
             qh = jnp.where(here, q, jnp.zeros_like(q))
             parts = []
-            for ref in kv_refs:
-                s = lax.dot_general(qh, ref[0, :, cols], NT, preferred_element_type=F32) * 0.125
-                parts.append((s, ref[1, :, cols]))
-            if has_text:
+            for i in where:
+                s = (
+                    lax.dot_general(qh, kv_ref[i, 0, :, cols], NT, preferred_element_type=F32)
+                    * 0.125
+                )
+                parts.append((s, kv_ref[i, 1, :, cols]))
+            if own:
                 s = (
                     lax.dot_general(qh, text_ref[0, :, cols], NT, preferred_element_type=F32)
                     * 0.125
@@ -126,7 +134,7 @@
             for s, _ in parts:
                 peak = jnp.max(s, axis=1, keepdims=True)
                 top = peak if top is None else jnp.maximum(top, peak)
-            if has_state:
+            if not own:
                 lane = g * 128 + side * HEAD_DIM
                 top = jnp.maximum(top, state_refs[1][:, lane : lane + 1])
             total = None
@@ -141,55 +149,62 @@
         acc = jnp.where(first, sides[0][0], sides[1][0])
         top = jnp.where(first, sides[0][1], sides[1][1])
         total = jnp.where(first, sides[0][2], sides[1][2])
-        if has_state:
+        if own:
+            outs[0][:, cols] = acc
+            outs[1][:, cols] = top
+            outs[2][:, cols] = total
+        else:
             factor = jnp.exp(state_refs[1][:, cols] - top)
             acc = acc + state_refs[0][:, cols] * factor
             total = total + state_refs[2][:, cols] * factor
-        if last:
-            refs[0][:, cols] = (acc / total).astype(BF)
+            outs[0][:, cols] = (acc / total).astype(BF)
+
+
+def attention(pos, q, kv, text=None, state=None):
+    own = text is not None
+    args = [q, kv] + ([text] if own else list(state))
+    if own:
+        out = [jax.ShapeDtypeStruct(q.shape, F32)] * 3
+    else:
+        out = jax.ShapeDtypeStruct(q.shape, BF)
+    return pl.pallas_call(
+        functools.partial(attention_kernel, own),
+        out_shape=out,
+        in_specs=[pl.BlockSpec(memory_space=pltpu.SMEM)]
+        + [pl.BlockSpec(memory_space=pltpu.VMEM)] * len(args),
+        compiler_params=params(),
+        name="attention",
+    )(pos, *args)
+
+
+def out_kernel(pos_ref, a_ref, own_ref, n0_ref, n1_ref, n2_ref, far_ref, out_ref, w_ref):
+    def store(source, half, ref, index):
+        if ref is own_ref:
+            value = ref[index * 48 : index * 48 + 48, :]
+        elif index is None:
+            value = ref[1]
         else:
-            refs[0][:, cols] = acc
-            refs[1][:, cols] = top
-            refs[2][:, cols] = total
-
-
-def attention(q, kvs, text=None, length=None, state=None, last=False):
-    args = []
-    specs = []
-    if text is not None:
-        args.append(length)
-        specs.append(pl.BlockSpec(memory_space=pltpu.SMEM))
-    rest = [q, *kvs] + ([text] if text is not None else []) + list(state or [])
-    args += rest
-    specs += [pl.BlockSpec(memory_space=pltpu.VMEM)] * len(rest)
-    if last:
-        out = jax.ShapeDtypeStruct(q.shape, BF)
-    else:
-        out = [jax.ShapeDtypeStruct(q.shape, F32)] * 3
-    return pl.pallas_call(
-        functools.partial(
-            attention_kernel, len(kvs), text is not None, state is not None, last
-        ),
-        out_shape=out,
-        in_specs=specs,
-        compiler_params=params(),
-        name="attention",
-    )(*args)
-
-
-def out_kernel(a_ref, w_ref, out_ref):
+            value = ref[index, 1]
+        w_ref[source, half] = value
+
+    assemble(pos_ref, own_ref, (n0_ref, n1_ref, n2_ref), far_ref, store)
+    w = w_ref[...].reshape(384, out_ref.shape[1])
     out_ref[...] = lax.dot_general(
-        a_ref[...], w_ref[...], NN, preferred_element_type=F32
+        a_ref[...], w, NN, preferred_element_type=F32
     ).astype(BF)
 
 
-def out_projection(a, w):
+def out_projection(pos, a, own, near, far):
+    width = own.shape[1]
     return pl.pallas_call(
         out_kernel,
-        out_shape=jax.ShapeDtypeStruct((a.shape[0], w.shape[1]), BF),
+        out_shape=jax.ShapeDtypeStruct((a.shape[0], width), BF),
+        in_specs=[pl.BlockSpec(memory_space=pltpu.SMEM)]
+        + [pl.BlockSpec(memory_space=pltpu.VMEM)] * 6,
+        scratch_shapes=[pltpu.VMEM((4, 2, 48, width), BF)],
         compiler_params=params(),
         name="out_projection",
-    )(a, w)
+    )(pos, a, own, *near, far)
 
 
 def pack_kernel(pos_ref, up_ref, down_ref, out_ref, sem):
@@ -341,42 +356,42 @@
     mods = modulation[0]
     rows, width = tokens.shape
     core = lax.axis_index("core")
-    pos = jnp.stack([core, lax.axis_index("ty")]).astype(jnp.int32)
+    pos = jnp.concatenate([jnp.stack([core, lax.axis_index("ty")]).astype(jnp.int32), text_len])
     swap2 = [(0, 1), (1, 0)]
 
     def to_lines(value, step):
         return lax.ppermute(value, "ty", [(i, (i + step) % 4) for i in range(4)])
 
-    half_out = lax.dynamic_slice_in_dim(w_out, core * 48, 48, 0)
-    out_full = lax.all_gather(half_out, ("ty", "core"), axis=0, tiled=True)
-
     own_qkv = jnp.transpose(w_qkv, (1, 2, 0))
-    half_qkv = lax.dynamic_slice_in_dim(own_qkv, core * 48, 48, 1)
+    half_kv = lax.dynamic_slice(own_qkv, (1, core * 48, 0), (2, 48, width))
+    near_kv = [to_lines(half_kv, step) for step in STRIDES]
+
     h1 = first_norm(tokens, mods, 4)
-    h1, half_qkv, pos = lax.optimization_barrier((h1, half_qkv, pos))
-    near_kv = [to_lines(half_qkv[1:], step) for step in STRIDES]
-    half_ffn = pack_ffn(pos, w_up, w_down)
+    h1 = lax.all_to_all(h1, "tx", split_axis=0, concat_axis=0, tiled=True)
+
+    half_q = lax.dynamic_slice(own_qkv, (0, core * 48, 0), (1, 48, width))
+    half_out = lax.dynamic_slice(w_out, (core * 48, 0), (48, width))
+    half_qo = jnp.concatenate([half_q, half_out[None]])
+    text = lax.dynamic_slice_in_dim(text_kv[0], lax.axis_index("tx") * 384, 384, 2)
+    text = jnp.transpose(text, (1, 0, 2))
+    half_ffn = pack_ffn(core[None].astype(jnp.int32), w_up, w_down)
     ffn_full = lax.all_gather(half_ffn, ("core", "tx"), axis=0, tiled=False)
     ffn_full = ffn_full.reshape(2, 4, width, w_up.shape[1])
-    h1 = lax.all_to_all(h1, "tx", split_axis=0, concat_axis=0, tiled=True)
-
-    *near_kv, h1, half_q = lax.optimization_barrier((*near_kv, h1, half_qkv[:1]))
+
+    *near_kv, h1, half_qo, text = lax.optimization_barrier((*near_kv, h1, half_qo, text))
     far_kv = lax.ppermute(jnp.stack(near_kv), "core", swap2)
-    near_q = [to_lines(half_q, step) for step in STRIDES]
+    near_qo = [to_lines(half_qo, step) for step in STRIDES]
     h1 = h1.reshape(4 * rows, width)
-    keyval = project(pos, h1, own_qkv, 1, near_kv, far_kv)
-    chunks = [to_lines(keyval, step) for step in STRIDES]
-    *near_q, keyval = lax.optimization_barrier((*near_q, keyval))
-    far_q = lax.ppermute(jnp.stack(near_q), "core", swap2)
-    query = project(pos, h1, own_qkv, 0, near_q, far_q)[0]
-
-    text = lax.dynamic_slice_in_dim(text_kv[0], lax.axis_index("tx") * 384, 384, 2)
-    text = jnp.transpose(text, (1, 0, 2))
-    state = attention(query, [keyval], text=text, length=text_len)
-    state = attention(query, chunks[:2], state=state)
-    attended = attention(query, chunks[2:], state=state, last=True)
-
-    partial = out_projection(attended, out_full)
+    own_kv = project(pos, h1, own_qkv, 1, 2, 4, near_kv, far_kv)
+    all_kv = lax.all_to_all(own_kv, "ty", split_axis=0, concat_axis=0, tiled=True)
+    *near_qo, own_kv = lax.optimization_barrier((*near_qo, own_kv))
+    far_qo = lax.ppermute(jnp.stack(near_qo), "core", swap2)
+    query = project(pos, h1, own_qkv, 0, 1, 1, near_qo, far_qo)[0, 0]
+
+    state = attention(pos, query, own_kv, text=text)
+    attended = attention(pos, query, all_kv, state=state)
+
+    partial = out_projection(pos, attended, w_out, near_qo, far_qo)
     partial = partial.reshape(4, rows, width)
     partial = lax.all_to_all(partial, "tx", split_axis=0, concat_axis=0, tiled=True)
     second, h2 = second_norm(tokens, partial, mods)

time: 157 us -> 144 us (0.917)
  the two profiles are of different devices: /device:TPU:32 before, /device:TPU:128 now
where the time goes in v4:
time: 144 us; the launch traced here: 142 us
  waiting for transfers between devices  37.3 us (26%)
  blocking collectives  26 us (18%)
  Pallas kernels  24.6 us (17%)
  starting transfers between devices  21.6 us (15%)
  between operations  15.7 us (11%)
  local copies, waits for them, and re-layouts  13.1 us (9%)
  other arithmetic  3.48 us (2%)
    all_to_all x1, blocking collectives, on_device(): lax.all_to_all(partial, 'tx', split_axis=0, concat_axis=0, tiled=True)  13.6 us
    all_to_all x1, blocking collectives, on_device(): h2 = lax.all_to_all(h2, 'ty', split_axis=0, concat_axis=0, tiled=True)  12.4 us
    all_to_all x1, waiting for transfers between devices, on_device(): h1 = lax.all_to_all(h1, 'tx', split_axis=0, concat_axis=0, tiled=True)  11.1 us
    all_to_all x1, waiting for transfers between devices, on_device(): lax.all_to_all(own_kv, 'ty', split_axis=0, concat_axis=0, tiled=True)  10.4 us
    unnamed x51, local copies, waits for them, and re-layouts  9.77 us
    ppermute x6, starting transfers between devices, to_lines(): return lax.ppermute(value, 'ty', [(i, (i + step) % 4) for i in range(4)])  8.52 us
    all_to_all x1, waiting for transfers between devices, on_device(): lax.all_to_all(partial, 'ty', split_axis=0, concat_axis=0, tiled=True)  8.46 us
    pallas_call x2, Pallas kernels, attention(): pl.pallas_call(functools.partial(attention_kernel, own), out_shape=out, i...  7.57 us
  transfers between devices with their start and end apart: 12, of which 7 were waited for; matrix products, arithmetic and copies ran while one was open for 4% of the time, Pallas kernels for 11%

profile of v4, /device:TPU:128, one launch (start us, length us, event | category | flops | bytes accessed | tf_op | source)
XLA Modules:
  0.0 141.9 jit_solution(12257443278573023508)
XLA Ops:
  7.2 1.3 copy-done.6
  8.6 1.3 copy-done.7
  9.8 1.0 pack_ffn.1
  12.2 1.6 %collective-permute-start = (bf16[2,48,1536]{2,1,0:T(8,128)(2,1)}, bf16[2,48,1536]{2,1,0:T(8,128)(2,1)S(1)}, u32[]{:S(2)}, u32[]{:S(2)}) collective-permute-start(bf16[2,48,1536]{2,1,0:T(8,128)(2,1)} %dynamic-slice_bitcast_fusion), channel_id=1, source_target_pairs={{0,2},{2,4},{4,6},{6,0},{1,3},{3,5},{5,7},{7,1},{8,10},{10,12},{12... | collective-permute-start | bytes 884744 | tf_op jit(solution)/shard_map/ppermute | solution.py:363
  13.8 1.7 %collective-permute-start.1 = (bf16[2,48,1536]{2,1,0:T(8,128)(2,1)}, bf16[2,48,1536]{2,1,0:T(8,128)(2,1)S(1)}, u32[]{:S(2)}, u32[]{:S(2)}) collective-permute-start(bf16[2,48,1536]{2,1,0:T(8,128)(2,1)} %dynamic-slice_bitcast_fusion), channel_id=1, source_target_pairs={{0,6},{2,0},{4,2},{6,4},{1,7},{3,1},{5,3},{7,5},{8,14},{10,8},{12,... | collective-permute-start | bytes 884744 | tf_op jit(solution)/shard_map/ppermute | solution.py:363
  15.4 2.0 %collective-permute-start.2 = (bf16[2,48,1536]{2,1,0:T(8,128)(2,1)}, bf16[2,48,1536]{2,1,0:T(8,128)(2,1)S(1)}, u32[]{:S(2)}, u32[]{:S(2)}) collective-permute-start(bf16[2,48,1536]{2,1,0:T(8,128)(2,1)} %dynamic-slice_bitcast_fusion), channel_id=1, source_target_pairs={{0,4},{2,6},{4,0},{6,2},{1,5},{3,7},{5,1},{7,3},{8,12},{10,14},{12... | collective-permute-start | bytes 884744 | tf_op jit(solution)/shard_map/ppermute | solution.py:363
  17.4 1.2 first_norm.1
  18.6 4.3 %all-to-all-start = ((bf16[4,64,1536]{2,1,0:T(8,128)(2,1)}), bf16[4,64,1536]{2,1,0:T(8,128)(2,1)S(1)}, u32[]{:S(2)}, u32[]{:S(2)}) async-start(bf16[4,64,1536]{2,1,0:T(8,128)(2,1)} %first_norm.1), calls=%async_computation | async-start | bytes 1572864 | tf_op jit(solution)/shard_map/all_to_all | solution.py:370
  25.4 1.7 %pad_maximum_fusion.2 = bf16[2,48,1536]{2,1,0:T(8,128)(2,1)} fusion(bf16[1,48,1536]{2,1,0:T(8,128)(2,1)S(1)} %dynamic-slice_bitcast_fusion.1, bf16[1,48,1536]{2,1,0:T(8,128)(2,1)} %dynamic-slice_bitcast_fusion.2), kind=kLoop, calls=%fused_computation.2 | loop fusion | flops 147456 | bytes 589824 | tf_op jit(solution)/shard_map/concatenate | solution.py:374
  27.1 2.8 %collective-permute-done.2.n2_ref = bf16[2,48,1536]{2,1,0:T(8,128)(2,1)S(1)} collective-permute-done((bf16[2,48,1536]{2,1,0:T(8,128)(2,1)}, bf16[2,48,1536]{2,1,0:T(8,128)(2,1)S(1)}, u32[]{:S(2)}, u32[]{:S(2)}) %collective-permute-start.2) | collective-permute-done | bytes 294944 | tf_op jit(solution)/shard_map/ppermute | solution.py:363
  29.9 11.1 %all-to-all-done = bf16[4,64,1536]{2,1,0:T(8,128)(2,1)S(1)} async-done(((bf16[4,64,1536]{2,1,0:T(8,128)(2,1)}), bf16[4,64,1536]{2,1,0:T(8,128)(2,1)S(1)}, u32[]{:S(2)}, u32[]{:S(2)}) %all-to-all-start) | async-done | bytes 786464 | tf_op jit(solution)/shard_map/all_to_all | solution.py:370
  41.0 1.0 pad_maximum_fusion
  42.2 3.2 %collective-permute-start.4 = (bf16[2,48,1536]{2,1,0:T(8,128)(2,1)}, bf16[2,48,1536]{2,1,0:T(8,128)(2,1)S(1)}, u32[]{:S(2)}, u32[]{:S(2)}) collective-permute-start(bf16[2,48,1536]{2,1,0:T(8,128)(2,1)} %pad_maximum_fusion.2), channel_id=1, source_target_pairs={{0,6},{2,0},{4,2},{6,4},{1,7},{3,1},{5,3},{7,5},{8,14},{10,8},{12,... | collective-permute-start | bytes 884744 | tf_op jit(solution)/shard_map/ppermute | solution.py:363
  46.1 1.0 copy-done.9
  48.1 1.0 copy-done.13
  49.0 3.5 %project.2.refs_2_ = bf16[4,2,256,384]{3,2,1,0:T(8,128)(2,1)} custom-call(s32[3]{0:T(128)S(1)} %pad_add_fusion.pos_ref.refs_0_, bf16[256,1536]{1,0:T(8,128)(2,1)S(1)} %bitcast.30, bf16[3,96,1536]{2,1,0:T(8,128)(2,1)S(1)} %bitcast.32, bf16[2,48,1536]{2,1,0:T(8,128)(2,1)S(1)} %copy-done.9, bf16[2,48,1536]{2,1,0:T(8,128)(2,1)S(1)} %copy-done.11, ...), custom_call_target="tpu_custom_call" | custom-call | tf_op jit(solution)/shard_map/project/pallas_call | solution.py:87
  52.6 4.8 %all-to-all-start.1 = ((bf16[4,2,256,384]{3,2,1,0:T(8,128)(2,1)}), bf16[4,2,256,384]{3,2,1,0:T(8,128)(2,1)}, u32[]{:S(2)}, u32[]{:S(2)}) async-start(bf16[4,2,256,384]{3,2,1,0:T(8,128)(2,1)} %project.2.refs_2_), calls=%async_computation.1 | async-start | bytes 3145728 | tf_op jit(solution)/shard_map/all_to_all | solution.py:386
  57.4 1.9 %collective-permute-done.3.n0_ref = bf16[2,48,1536]{2,1,0:T(8,128)(2,1)S(1)} collective-permute-done((bf16[2,48,1536]{2,1,0:T(8,128)(2,1)}, bf16[2,48,1536]{2,1,0:T(8,128)(2,1)S(1)}, u32[]{:S(2)}, u32[]{:S(2)}) %collective-permute-start.3) | collective-permute-done | bytes 294944 | tf_op jit(solution)/shard_map/ppermute | solution.py:363
  59.8 2.5 %collective-permute-done.7.far_ref = bf16[3,2,48,1536]{3,2,1,0:T(8,128)(2,1)S(1)} collective-permute-done((bf16[3,2,48,1536]{3,2,1,0:T(8,128)(2,1)S(1)}, bf16[3,2,48,1536]{3,2,1,0:T(8,128)(2,1)S(1)}, u32[]{:S(2)}, u32[]{:S(2)}) %collective-permute-start.7) | collective-permute-done | bytes 884768 | tf_op jit(solution)/shard_map/ppermute | solution.py:388
  62.3 1.2 project.3
  63.5 2.6 %attention.2 = (f32[256,384]{1,0:T(8,128)S(1)}, f32[256,384]{1,0:T(8,128)S(1)}, f32[256,384]{1,0:T(8,128)S(1)}) custom-call(s32[3]{0:T(128)S(1)} %pad_add_fusion.pos_ref.refs_0_, bf16[256,384]{1,0:T(8,128)(2,1)S(1)} %bitcast.39, bf16[4,2,256,384]{3,2,1,0:T(8,128)(2,1)S(1)} %copy-done.1, bf16[2,154,384]{2,1,0:T(8,128)(2,1)S(1)} %bitcast.44), custom_call_target="tpu_custom_call" | custom-call | tf_op jit(solution)/shard_map/attention/pallas_call | solution.py:170
  67.7 10.4 %all-to-all-done.1.refs_2_ = bf16[4,2,256,384]{3,2,1,0:T(8,128)(2,1)} async-done(((bf16[4,2,256,384]{3,2,1,0:T(8,128)(2,1)}), bf16[4,2,256,384]{3,2,1,0:T(8,128)(2,1)}, u32[]{:S(2)}, u32[]{:S(2)}) %all-to-all-start.1) | async-done | bytes 1572896 | tf_op jit(solution)/shard_map/all_to_all | solution.py:386
  78.0 1.0 copy-done.20
  79.0 1.0 copy-done.22
  80.0 5.0 %attention.3.a_ref = bf16[256,384]{1,0:T(8,128)(2,1)S(1)} custom-call(s32[3]{0:T(128)S(1)} %pad_add_fusion.pos_ref.refs_0_, bf16[256,384]{1,0:T(8,128)(2,1)S(1)} %bitcast.40, bf16[4,2,256,384]{3,2,1,0:T(8,128)(2,1)} %all-to-all-done.1.refs_2_, f32[256,384]{1,0:T(8,128)S(1)} %get-tuple-element.29.refs_3_, f32[256,384]{1,0:T(8,128)S(1)} %copy-done.20, ...), custom_call_target="tpu_custom_call" | custom-call | tf_op jit(solution)/shard_map/attention/pallas_call | solution.py:170
  85.0 1.2 out_projection.1
  86.2 13.6 %all_to_all.25.part_ref = bf16[4,64,1536]{2,1,0:T(8,128)(2,1)S(1)} all-to-all(bf16[4,64,1536]{2,1,0:T(8,128)(2,1)S(1)} %bitcast.35), channel_id=1, replica_groups=mesh['zl'=4,'core'=2,'tx'=4,'ty'=4,'blk'=2] {'tx'}, dimensions={0} | all-to-all | bytes 1572864 | tf_op jit(solution)/shard_map/all_to_all | solution.py:396
  100.3 12.4 %all_to_all.26 = bf16[4,64,1536]{2,1,0:T(8,128)(2,1)S(1)} all-to-all(bf16[4,64,1536]{2,1,0:T(8,128)(2,1)S(1)} %get-tuple-element.33), channel_id=1, replica_groups=mesh['zl'=4,'core'=2,'tx'=4,'ty'=4,'blk'=2] {'ty'}, dimensions={0} | all-to-all | bytes 1572864 | tf_op jit(solution)/shard_map/all_to_all | solution.py:398
  112.7 7.5 %feed_forward.1 = bf16[256,1536]{1,0:T(8,128)(2,1)} custom-call(bf16[256,1536]{1,0:T(8,128)(2,1)S(1)} %bitcast.34, bf16[2,4,1536,384]{3,2,1,0:T(8,128)(2,1)} %bitcast.50, bf16[2,4,1536,384]{3,2,1,0:T(8,128)(2,1)} %bitcast.51), custom_call_target="tpu_custom_call" | custom-call | tf_op jit(solution)/shard_map/feed_forward/pallas_call | solution.py:304
  120.2 3.6 %all-to-all-start.4 = ((bf16[4,64,1536]{2,1,0:T(8,128)(2,1)}), bf16[4,64,1536]{2,1,0:T(8,128)(2,1)S(1)}, u32[]{:S(2)}, u32[]{:S(2)}) async-start(bf16[4,64,1536]{2,1,0:T(8,128)(2,1)} %bitcast.21), calls=%async_computation.4 | async-start | bytes 1572864 | tf_op jit(solution)/shard_map/all_to_all | solution.py:400
  124.8 8.5 %all-to-all-done.4.part_ref = bf16[4,64,1536]{2,1,0:T(8,128)(2,1)S(1)} async-done(((bf16[4,64,1536]{2,1,0:T(8,128)(2,1)}), bf16[4,64,1536]{2,1,0:T(8,128)(2,1)S(1)}, u32[]{:S(2)}, u32[]{:S(2)}) %all-to-all-start.4) | async-done | bytes 786464 | tf_op jit(solution)/shard_map/all_to_all | solution.py:400
  133.3 1.1 last_stage.1
  (68 shorter events, 8.3 us)
Async XLA Ops:
  7.2 17.3 %copy-start = (bf16[1,154,2,1536]{3,2,1,0:T(2,128)(2,1)S(1)}, bf16[1,154,2,1536]{3,2,1,0:T(2,128)(2,1)}, u32[]{:S(2)}) copy-start(bf16[1,154,2,1536]{3,2,1,0:T(2,128)(2,1)} %param.14) | copy-start | bytes 2838532
  7.2 105.5 %all-gather.3.cloned.1.call-start = ((), (), s32[]{:S(2)}) async-start(), calls=%async_computation.5 | async-start | bytes 10616832 | tf_op jit(solution)/shard_map/all_gather | solution.py:378
  7.2 1.3 copy-start.6
  8.6 1.3 copy-start.7
  9.8 1.6 %copy-start.2 = (bf16[1536,3,96]{0,2,1:T(8,128)(2,1)S(1)}, bf16[1536,3,96]{0,2,1:T(8,128)(2,1)}, u32[]{:S(2)}) copy-start(bf16[1536,3,96]{0,2,1:T(8,128)(2,1)} %param.17) | copy-start | bytes 2654212
  10.9 6.5 %copy-start.15 = (bf16[1,64,1536]{2,1,0:T(8,128)(2,1)S(1)}, bf16[1,64,1536]{2,1,0:T(8,128)(2,1)}, u32[]{:S(2)}) copy-start(bf16[1,64,1536]{2,1,0:T(8,128)(2,1)} %param.11) | copy-start | bytes 589828
  10.9 6.5 %copy-start.18 = (f32[1,8,1536]{2,1,0:T(8,128)S(1)}, f32[1,8,1536]{2,1,0:T(8,128)}, u32[]{:S(2)}) copy-start(f32[1,8,1536]{2,1,0:T(8,128)} %param.13) | copy-start | bytes 147460
  12.2 14.9 %collective-permute-start = (bf16[2,48,1536]{2,1,0:T(8,128)(2,1)}, bf16[2,48,1536]{2,1,0:T(8,128)(2,1)S(1)}, u32[]{:S(2)}, u32[]{:S(2)}) collective-permute-start(bf16[2,48,1536]{2,1,0:T(8,128)(2,1)} %dynamic-slice_bitcast_fusion), channel_id=1, source_target_pairs={{0,2},{2,4},{4,6},{6,0},{1,3},{3,5},{5,7},{7,1},{8,10},{10,12},{12... | collective-permute-start | bytes 884744 | tf_op jit(solution)/shard_map/ppermute | solution.py:363
  13.8 13.3 %collective-permute-start.1 = (bf16[2,48,1536]{2,1,0:T(8,128)(2,1)}, bf16[2,48,1536]{2,1,0:T(8,128)(2,1)S(1)}, u32[]{:S(2)}, u32[]{:S(2)}) collective-permute-start(bf16[2,48,1536]{2,1,0:T(8,128)(2,1)} %dynamic-slice_bitcast_fusion), channel_id=1, source_target_pairs={{0,6},{2,0},{4,2},{6,4},{1,7},{3,1},{5,3},{7,5},{8,14},{10,8},{12,... | collective-permute-start | bytes 884744 | tf_op jit(solution)/shard_map/ppermute | solution.py:363
  15.4 14.5 %collective-permute-start.2 = (bf16[2,48,1536]{2,1,0:T(8,128)(2,1)}, bf16[2,48,1536]{2,1,0:T(8,128)(2,1)S(1)}, u32[]{:S(2)}, u32[]{:S(2)}) collective-permute-start(bf16[2,48,1536]{2,1,0:T(8,128)(2,1)} %dynamic-slice_bitcast_fusion), channel_id=1, source_target_pairs={{0,4},{2,6},{4,0},{6,2},{1,5},{3,7},{5,1},{7,3},{8,12},{10,14},{12... | collective-permute-start | bytes 884744 | tf_op jit(solution)/shard_map/ppermute | solution.py:363
  18.6 22.5 %all-to-all-start = ((bf16[4,64,1536]{2,1,0:T(8,128)(2,1)}), bf16[4,64,1536]{2,1,0:T(8,128)(2,1)S(1)}, u32[]{:S(2)}, u32[]{:S(2)}) async-start(bf16[4,64,1536]{2,1,0:T(8,128)(2,1)} %first_norm.1), calls=%async_computation | async-start | bytes 1572864 | tf_op jit(solution)/shard_map/all_to_all | solution.py:370
  27.1 15.0 %copy-start.8 = (bf16[2,48,1536]{2,1,0:T(8,128)(2,1)}, bf16[2,48,1536]{2,1,0:T(8,128)(2,1)S(1)}, u32[]{:S(2)}) copy-start(bf16[2,48,1536]{2,1,0:T(8,128)(2,1)S(1)} %collective-permute-done.n0_ref) | copy-start | bytes 884740
  27.1 15.0 %copy-start.10 = (bf16[2,48,1536]{2,1,0:T(8,128)(2,1)}, bf16[2,48,1536]{2,1,0:T(8,128)(2,1)S(1)}, u32[]{:S(2)}) copy-start(bf16[2,48,1536]{2,1,0:T(8,128)(2,1)S(1)} %collective-permute-done.1.n1_ref) | copy-start | bytes 884740
  29.9 12.3 %copy-start.12 = (bf16[2,48,1536]{2,1,0:T(8,128)(2,1)}, bf16[2,48,1536]{2,1,0:T(8,128)(2,1)S(1)}, u32[]{:S(2)}) copy-start(bf16[2,48,1536]{2,1,0:T(8,128)(2,1)S(1)} %collective-permute-done.2.n2_ref) | copy-start | bytes 884740
  42.1 4.1 %collective-permute-start.6 = (bf16[3,2,48,1536]{3,2,1,0:T(8,128)(2,1)}, bf16[3,2,48,1536]{3,2,1,0:T(8,128)(2,1)}, u32[]{:S(2)}, u32[]{:S(2)}) collective-permute-start(bf16[3,2,48,1536]{3,2,1,0:T(8,128)(2,1)} %pad_maximum_fusion), channel_id=1, source_target_pairs={{0,32},{32,0},{1,33},{33,1},{2,34},{34,2},{3,35},{35,3},{4,36},{36... | collective-permute-start | bytes 2654216 | tf_op jit(solution)/shard_map/ppermute | solution.py:382
  42.1 17.2 %collective-permute-start.3 = (bf16[2,48,1536]{2,1,0:T(8,128)(2,1)}, bf16[2,48,1536]{2,1,0:T(8,128)(2,1)S(1)}, u32[]{:S(2)}, u32[]{:S(2)}) collective-permute-start(bf16[2,48,1536]{2,1,0:T(8,128)(2,1)} %pad_maximum_fusion.2), channel_id=1, source_target_pairs={{0,2},{2,4},{4,6},{6,0},{1,3},{3,5},{5,7},{7,1},{8,10},{10,12},{12... | collective-permute-start | bytes 884744 | tf_op jit(solution)/shard_map/ppermute | solution.py:363
  42.2 17.2 %collective-permute-start.4 = (bf16[2,48,1536]{2,1,0:T(8,128)(2,1)}, bf16[2,48,1536]{2,1,0:T(8,128)(2,1)S(1)}, u32[]{:S(2)}, u32[]{:S(2)}) collective-permute-start(bf16[2,48,1536]{2,1,0:T(8,128)(2,1)} %pad_maximum_fusion.2), channel_id=1, source_target_pairs={{0,6},{2,0},{4,2},{6,4},{1,7},{3,1},{5,3},{7,5},{8,14},{10,8},{12,... | collective-permute-start | bytes 884744 | tf_op jit(solution)/shard_map/ppermute | solution.py:363
  45.4 14.0 %collective-permute-start.5 = (bf16[2,48,1536]{2,1,0:T(8,128)(2,1)}, bf16[2,48,1536]{2,1,0:T(8,128)(2,1)S(1)}, u32[]{:S(2)}, u32[]{:S(2)}) collective-permute-start(bf16[2,48,1536]{2,1,0:T(8,128)(2,1)} %pad_maximum_fusion.2), channel_id=1, source_target_pairs={{0,4},{2,6},{4,0},{6,2},{1,5},{3,7},{5,1},{7,3},{8,12},{10,14},{12... | collective-permute-start | bytes 884744 | tf_op jit(solution)/shard_map/ppermute | solution.py:363
  52.6 25.5 %all-to-all-start.1 = ((bf16[4,2,256,384]{3,2,1,0:T(8,128)(2,1)}), bf16[4,2,256,384]{3,2,1,0:T(8,128)(2,1)}, u32[]{:S(2)}, u32[]{:S(2)}) async-start(bf16[4,2,256,384]{3,2,1,0:T(8,128)(2,1)} %project.2.refs_2_), calls=%async_computation.1 | async-start | bytes 3145728 | tf_op jit(solution)/shard_map/all_to_all | solution.py:386
  57.4 4.9 %copy-start.3 = (bf16[1536,3,96]{0,2,1:T(8,128)(2,1)S(1)}, bf16[1536,3,96]{0,2,1:T(8,128)(2,1)}, u32[]{:S(2)}) copy-start(bf16[1536,3,96]{0,2,1:T(8,128)(2,1)} %param.17) | copy-start | bytes 2654212
  59.5 4.0 %copy-start.1 = (bf16[4,2,256,384]{3,2,1,0:T(8,128)(2,1)S(1)}, bf16[4,2,256,384]{3,2,1,0:T(8,128)(2,1)}, u32[]{:S(2)}) copy-start(bf16[4,2,256,384]{3,2,1,0:T(8,128)(2,1)} %project.2.refs_2_) | copy-start | bytes 4718596
  59.5 4.0 %copy-start.14 = (bf16[1,154,2,384]{3,1,2,0:T(8,128)(2,1)S(1)}, bf16[1,154,2,384]{3,1,2,0:T(8,128)(2,1)}, u32[]{:S(2)}) copy-start(bf16[1,154,2,384]{3,1,2,0:T(8,128)(2,1)} %copy.16) | copy-start | bytes 709636
  59.5 2.7 %collective-permute-start.7 = (bf16[3,2,48,1536]{3,2,1,0:T(8,128)(2,1)S(1)}, bf16[3,2,48,1536]{3,2,1,0:T(8,128)(2,1)S(1)}, u32[]{:S(2)}, u32[]{:S(2)}) collective-permute-start(bf16[3,2,48,1536]{3,2,1,0:T(8,128)(2,1)S(1)} %pad_maximum_fusion.1), channel_id=1, source_target_pairs={{0,32},{32,0},{1,33},{33,1},{2,34},{34,2},{3,35},{35,3},{4,36},{36... | collective-permute-start | bytes 2654216 | tf_op jit(solution)/shard_map/ppermute | solution.py:388
  62.3 1.2 copy-start.4
  78.0 1.0 copy-start.20
  79.0 1.0 copy-start.22
  80.0 5.0 %copy-start.5 = (bf16[3,2,48,1536]{3,2,1,0:T(8,128)(2,1)S(1)}, bf16[3,2,48,1536]{3,2,1,0:T(8,128)(2,1)}, u32[]{:S(2)}) copy-start(bf16[3,2,48,1536]{3,2,1,0:T(8,128)(2,1)} %copy-done.4) | copy-start | bytes 2654212
  80.0 5.0 %copy-start.17 = (bf16[96,1536]{1,0:T(8,128)(2,1)S(1)}, bf16[96,1536]{1,0:T(8,128)(2,1)}, u32[]{:S(2)}) copy-start(bf16[96,1536]{1,0:T(8,128)(2,1)} %own_ref.1) | copy-start | bytes 884740
  85.0 14.8 %copy-start.16 = (bf16[1,64,1536]{2,1,0:T(8,128)(2,1)S(1)}, bf16[1,64,1536]{2,1,0:T(8,128)(2,1)}, u32[]{:S(2)}) copy-start(bf16[1,64,1536]{2,1,0:T(8,128)(2,1)} %param.11) | copy-start | bytes 589828
  120.2 4.3 %copy-start.23 = (bf16[1536,64]{0,1:T(8,128)(2,1)S(1)}, bf16[1536,64]{0,1:T(8,128)(2,1)}, u32[]{:S(2)}) copy-start(bf16[1536,64]{0,1:T(8,128)(2,1)} %param.21) | copy-start | bytes 589828
  120.2 14.2 %copy-start.24 = (f32[1,32,128]{2,1,0:T(8,128)S(1)}, f32[1,32,128]{2,1,0:T(8,128)}, u32[]{:S(2)}) copy-start(f32[1,32,128]{2,1,0:T(8,128)} %param.12) | copy-start | bytes 49156
  120.2 13.1 %all-to-all-start.4 = ((bf16[4,64,1536]{2,1,0:T(8,128)(2,1)}), bf16[4,64,1536]{2,1,0:T(8,128)(2,1)S(1)}, u32[]{:S(2)}, u32[]{:S(2)}) async-start(bf16[4,64,1536]{2,1,0:T(8,128)(2,1)} %bitcast.21), calls=%async_computation.4 | async-start | bytes 1572864 | tf_op jit(solution)/shard_map/all_to_all | solution.py:400
  (5 other events, 4.4 us)
Sparse Core Ops, SparseCore 0:
  11.1 62.8 all-gather.2

commit v5 on v4

--- a/solution.py
+++ b/solution.py
@@ -17,8 +17,8 @@
 STRIDES = (1, 3, 2)
 
 
-def params():
-    return pltpu.CompilerParams(vmem_limit_bytes=50 * 1024 * 1024)
+def params(mebibytes):
+    return pltpu.CompilerParams(vmem_limit_bytes=mebibytes * 1024 * 1024)
 
 
 def layer_norm(full, shift, scale):
@@ -44,7 +44,7 @@
     return pl.pallas_call(
         functools.partial(norm_kernel, copies),
         out_shape=jax.ShapeDtypeStruct((copies, rows, width), BF),
-        compiler_params=params(),
+        compiler_params=params(6),
         name="first_norm",
     )(tokens, mods)
 
@@ -90,7 +90,7 @@
         in_specs=[pl.BlockSpec(memory_space=pltpu.SMEM)]
         + [pl.BlockSpec(memory_space=pltpu.VMEM)] * 6,
         scratch_shapes=[pltpu.VMEM((count, 4, 2, 48, width), BF)],
-        compiler_params=params(),
+        compiler_params=params(14),
         name="project",
     )(pos, h, own, *near, far)
 
@@ -100,21 +100,25 @@
     pos_ref, q_ref, kv_ref = refs[:3]
     if own:
         text_ref = refs[3]
-        state_refs = None
         outs = refs[4:]
     else:
-        state_refs = refs[3:6]
-        outs = refs[6:]
+        acc_ref, stat_ref = refs[3:5]
+        outs = refs[5:]
     rows = q_ref.shape[0]
     if own:
         live = lax.broadcasted_iota(jnp.int32, (rows, TXT), 1) < pos_ref[2]
     first = lax.broadcasted_iota(jnp.int32, (rows, 128), 1) < HEAD_DIM
     where = [0] if own else [lax.rem(pos_ref[1] + i, 4) for i in (1, 2, 3)]
+    lane = lax.broadcasted_iota(jnp.int32, (rows, 128), 1)
+    tops = jnp.zeros((rows, 128), F32)
+    totals = jnp.zeros((rows, 128), F32)
     for g in range(q_ref.shape[1] // 128):
         cols = slice(g * 128, g * 128 + 128)
         q = q_ref[:, cols]
-        sides = []
+        accs = []
+        scales = []
         for side in range(2):
+            head = 2 * g + side
             here = first if side == 0 else jnp.logical_not(first)
             qh = jnp.where(here, q, jnp.zeros_like(q))
             parts = []
@@ -135,8 +139,8 @@
                 peak = jnp.max(s, axis=1, keepdims=True)
                 top = peak if top is None else jnp.maximum(top, peak)
             if not own:
-                lane = g * 128 + side * HEAD_DIM
-                top = jnp.maximum(top, state_refs[1][:, lane : lane + 1])
+                old = stat_ref[0, :, head : head + 1]
+                top = jnp.maximum(top, old)
             total = None
             acc = None
             for s, values in parts:
@@ -145,26 +149,34 @@
                 part = lax.dot_general(p.astype(BF), values, NN, preferred_element_type=F32)
                 total = amount if total is None else total + amount
                 acc = part if acc is None else acc + part
-            sides.append((acc, top, total))
-        acc = jnp.where(first, sides[0][0], sides[1][0])
-        top = jnp.where(first, sides[0][1], sides[1][1])
-        total = jnp.where(first, sides[0][2], sides[1][2])
+            if own:
+                tops = jnp.where(lane == head, top, tops)
+                totals = jnp.where(lane == head, total, totals)
+            else:
+                factor = jnp.exp(old - top)
+                total = total + stat_ref[1, :, head : head + 1] * factor
+                scales.append((factor, total))
+            accs.append(acc)
+        acc = jnp.where(first, accs[0], accs[1])
         if own:
             outs[0][:, cols] = acc
-            outs[1][:, cols] = top
-            outs[2][:, cols] = total
         else:
-            factor = jnp.exp(state_refs[1][:, cols] - top)
-            acc = acc + state_refs[0][:, cols] * factor
-            total = total + state_refs[2][:, cols] * factor
-            outs[0][:, cols] = (acc / total).astype(BF)
+            factor = jnp.where(first, scales[0][0], scales[1][0])
+            total = jnp.where(first, scales[0][1], scales[1][1])
+            outs[0][:, cols] = ((acc + acc_ref[:, cols] * factor) / total).astype(BF)
+    if own:
+        outs[1][0] = tops
+        outs[1][1] = totals
 
 
 def attention(pos, q, kv, text=None, state=None):
     own = text is not None
     args = [q, kv] + ([text] if own else list(state))
     if own:
-        out = [jax.ShapeDtypeStruct(q.shape, F32)] * 3
+        out = [
+            jax.ShapeDtypeStruct(q.shape, F32),
+            jax.ShapeDtypeStruct((2, q.shape[0], 128), F32),
+        ]
     else:
         out = jax.ShapeDtypeStruct(q.shape, BF)
     return pl.pallas_call(
@@ -172,7 +184,7 @@
         out_shape=out,
         in_specs=[pl.BlockSpec(memory_space=pltpu.SMEM)]
         + [pl.BlockSpec(memory_space=pltpu.VMEM)] * len(args),
-        compiler_params=params(),
+        compiler_params=params(16),
         name="attention",
     )(pos, *args)
 
@@ -202,7 +214,7 @@
         in_specs=[pl.BlockSpec(memory_space=pltpu.SMEM)]
         + [pl.BlockSpec(memory_space=pltpu.VMEM)] * 6,
         scratch_shapes=[pltpu.VMEM((4, 2, 48, width), BF)],
-        compiler_params=params(),
+        compiler_params=params(8),
         name="out_projection",
     )(pos, a, own, *near, far)
 
@@ -243,7 +255,7 @@
         ],
         out_specs=pl.BlockSpec(memory_space=pltpu.HBM),
         scratch_shapes=[pltpu.SemaphoreType.DMA((4,))],
-        compiler_params=params(),
+        compiler_params=params(60),
         name="pack_ffn",
     )(pos, w_up, w_down)
 
@@ -266,7 +278,7 @@
             jax.ShapeDtypeStruct(tokens.shape, BF),
             jax.ShapeDtypeStruct(parts.shape, BF),
         ],
-        compiler_params=params(),
+        compiler_params=params(6),
         name="second_norm",
     )(tokens, parts, mods)
 
@@ -312,7 +324,7 @@
         ],
         out_specs=pl.BlockSpec((rows, 2 * part), lambda i: (0, jnp.maximum(i - 2, 0))),
         scratch_shapes=[pltpu.VMEM((2, rows, 2 * part), BF)],
-        compiler_params=params(),
+        compiler_params=params(58),
         name="feed_forward",
     )(h, weights, weights)
 
@@ -334,7 +346,7 @@
             jax.ShapeDtypeStruct(second.shape, BF),
             jax.ShapeDtypeStruct((second.shape[0], w_final.shape[1]), F32),
         ],
-        compiler_params=params(),
+        compiler_params=params(6),
         name="last_stage",
     )(second, parts, mods, w_final)
 
@@ -364,10 +376,10 @@
 
     own_qkv = jnp.transpose(w_qkv, (1, 2, 0))
     half_kv = lax.dynamic_slice(own_qkv, (1, core * 48, 0), (2, 48, width))
+    h1 = first_norm(tokens, mods, 4)
+    h1, half_kv = lax.optimization_barrier((h1, half_kv))
+    h1 = lax.all_to_all(h1, "tx", split_axis=0, concat_axis=0, tiled=True)
     near_kv = [to_lines(half_kv, step) for step in STRIDES]
-
-    h1 = first_norm(tokens, mods, 4)
-    h1 = lax.all_to_all(h1, "tx", split_axis=0, concat_axis=0, tiled=True)
 
     half_q = lax.dynamic_slice(own_qkv, (0, core * 48, 0), (1, 48, width))
     half_out = lax.dynamic_slice(w_out, (core * 48, 0), (48, width))
@@ -378,8 +390,8 @@
     ffn_full = lax.all_gather(half_ffn, ("core", "tx"), axis=0, tiled=False)
     ffn_full = ffn_full.reshape(2, 4, width, w_up.shape[1])
 
-    *near_kv, h1, half_qo, text = lax.optimization_barrier((*near_kv, h1, half_qo, text))
     far_kv = lax.ppermute(jnp.stack(near_kv), "core", swap2)
+    h1, half_qo, text = lax.optimization_barrier((h1, half_qo, text))
     near_qo = [to_lines(half_qo, step) for step in STRIDES]
     h1 = h1.reshape(4 * rows, width)
     own_kv = project(pos, h1, own_qkv, 1, 2, 4, near_kv, far_kv)

time: 144 us -> 169 us (1.17)
  Pallas kernels: 24.6 us -> 62 us
  local copies, waits for them, and re-layouts: 13.1 us -> 3.74 us
  waiting for transfers between devices: 37.3 us -> 31.6 us
  blocking collectives: 26 us -> 28.9 us
    pallas_call x1, Pallas kernels: 1.05 us -> 36.9 us  [pack_ffn(): pl.pallas_call(pack_kernel, out_shape=jax.ShapeDtypeStruct(w_up.shape, BF...]
    all_to_all x1, waiting for transfers between devices: 10.4 us -> 2.13 us  [on_device(): lax.all_to_all(own_kv, 'ty', split_axis=0, concat_axis=0, tiled=True)]
    unnamed x51 -> x31, local copies, waits for them, and re-layouts: 9.77 us -> 1.99 us
    ppermute x6, waiting for transfers between devices: 4.85 us -> 10.9 us  [to_lines(): return lax.ppermute(value, 'ty', [(i, (i + step) % 4) for i in range(4)])]
    all_to_all x1, waiting for transfers between devices: 11.1 us -> 7.66 us  [on_device(): h1 = lax.all_to_all(h1, 'tx', split_axis=0, concat_axis=0, tiled=True)]
    all_to_all x1, blocking collectives: 12.4 us -> 15.7 us  [on_device(): h2 = lax.all_to_all(h2, 'ty', split_axis=0, concat_axis=0, tiled=True)]
  transfers between devices with their start and end apart: 12 -> 12, of which waited for: 7 -> 7; matrix products, arithmetic and copies ran while one was open for 4% -> 3% of each run, Pallas kernels for 11% -> 10%
where the time goes in v5:
time: 169 us; the launch traced here: 167 us
  Pallas kernels  62 us (37%)
  waiting for transfers between devices  31.6 us (19%)
  blocking collectives  28.9 us (17%)
  starting transfers between devices  21.5 us (13%)
  between operations  15.7 us (9%)
  local copies, waits for them, and re-layouts  3.74 us (2%)
  other arithmetic  3.7 us (2%)
    pallas_call x1, Pallas kernels, pack_ffn(): pl.pallas_call(pack_kernel, out_shape=jax.ShapeDtypeStruct(w_up.shape, BF...  36.9 us
    all_to_all x1, blocking collectives, on_device(): h2 = lax.all_to_all(h2, 'ty', split_axis=0, concat_axis=0, tiled=True)  15.7 us
    all_to_all x1, blocking collectives, on_device(): lax.all_to_all(partial, 'tx', split_axis=0, concat_axis=0, tiled=True)  13.2 us
    ppermute x6, waiting for transfers between devices, to_lines(): return lax.ppermute(value, 'ty', [(i, (i + step) % 4) for i in range(4)])  10.9 us
    all_to_all x1, waiting for transfers between devices, on_device(): lax.all_to_all(partial, 'ty', split_axis=0, concat_axis=0, tiled=True)  8.46 us
    ppermute x6, starting transfers between devices, to_lines(): return lax.ppermute(value, 'ty', [(i, (i + step) % 4) for i in range(4)])  8.46 us
    all_to_all x1, waiting for transfers between devices, on_device(): h1 = lax.all_to_all(h1, 'tx', split_axis=0, concat_axis=0, tiled=True)  7.66 us
    pallas_call x1, Pallas kernels, feed_forward(): pl.pallas_call(ffn_kernel, grid=(4,), out_shape=jax.ShapeDtypeStruct((row...  7.64 us
  transfers between devices with their start and end apart: 12, of which 7 were waited for; matrix products, arithmetic and copies ran while one was open for 3% of the time, Pallas kernels for 10%

profile of v5, /device:TPU:128, one launch (start us, length us, event | category | flops | bytes accessed | tf_op | source)
XLA Modules:
  0.0 167.1 jit_solution(13700504063160416162)
XLA Ops:
  7.3 36.9 %pack_ffn.1 = bf16[1536,384]{1,0:T(8,128)(2,1)} custom-call(s32[1]{0:T(128)} %bitcast.1.pos_ref, bf16[1536,384]{1,0:T(8,128)(2,1)} %up_ref.1, bf16[384,1536]{1,0:T(8,128)(2,1)} %down_ref.1), custom_call_target="tpu_custom_call" | custom-call | tf_op jit(solution)/shard_map/pack_ffn/pallas_call | solution.py:248
  44.2 1.1 first_norm.1
  45.3 0.7 dynamic-slice_bitcast_fusion
  46.1 1.6 collective-permute-start.3
  47.6 1.7 collective-permute-start.4
  49.3 2.0 %collective-permute-start.5 = (bf16[2,48,1536]{2,1,0:T(8,128)(2,1)}, bf16[2,48,1536]{2,1,0:T(8,128)(2,1)S(1)}, u32[]{:S(2)}, u32[]{:S(2)}) collective-permute-start(bf16[2,48,1536]{2,1,0:T(8,128)(2,1)} %dynamic-slice_bitcast_fusion), channel_id=1, source_target_pairs={{0,4},{2,6},{4,0},{6,2},{1,5},{3,7},{5,1},{7,3},{8,12},{10,14},{12... | collective-permute-start | bytes 884744 | tf_op jit(solution)/shard_map/ppermute | solution.py:375
  51.3 4.3 %all-to-all-start = ((bf16[4,64,1536]{2,1,0:T(8,128)(2,1)}), bf16[4,64,1536]{2,1,0:T(8,128)(2,1)S(1)}, u32[]{:S(2)}, u32[]{:S(2)}) async-start(bf16[4,64,1536]{2,1,0:T(8,128)(2,1)} %first_norm.1), calls=%async_computation | async-start | bytes 1572864 | tf_op jit(solution)/shard_map/all_to_all | solution.py:381
  55.8 0.7 copy.16
  56.5 1.3 collective-permute-done.4.n1_ref
  57.8 6.0 %collective-permute-done.5.n2_ref = bf16[2,48,1536]{2,1,0:T(8,128)(2,1)S(1)} collective-permute-done((bf16[2,48,1536]{2,1,0:T(8,128)(2,1)}, bf16[2,48,1536]{2,1,0:T(8,128)(2,1)S(1)}, u32[]{:S(2)}, u32[]{:S(2)}) %collective-permute-start.5) | collective-permute-done | bytes 294944 | tf_op jit(solution)/shard_map/ppermute | solution.py:375
  63.8 1.0 pad_maximum_fusion
  64.9 0.7 pad_maximum_fusion.2
  65.6 7.7 %all-to-all-done = bf16[4,64,1536]{2,1,0:T(8,128)(2,1)S(1)} async-done(((bf16[4,64,1536]{2,1,0:T(8,128)(2,1)}), bf16[4,64,1536]{2,1,0:T(8,128)(2,1)S(1)}, u32[]{:S(2)}, u32[]{:S(2)}) %all-to-all-start) | async-done | bytes 786464 | tf_op jit(solution)/shard_map/all_to_all | solution.py:381
  73.3 3.2 %collective-permute-start.1 = (bf16[2,48,1536]{2,1,0:T(8,128)(2,1)}, bf16[2,48,1536]{2,1,0:T(8,128)(2,1)}, u32[]{:S(2)}, u32[]{:S(2)}) collective-permute-start(bf16[2,48,1536]{2,1,0:T(8,128)(2,1)} %pad_maximum_fusion.2), channel_id=1, source_target_pairs={{0,6},{2,0},{4,2},{6,4},{1,7},{3,1},{5,3},{7,5},{8,14},{10,8},{12,... | collective-permute-start | bytes 884744 | tf_op jit(solution)/shard_map/ppermute | solution.py:375
  77.3 3.5 %project.2.refs_2_ = bf16[4,2,256,384]{3,2,1,0:T(8,128)(2,1)} custom-call(s32[3]{0:T(128)S(1)} %pad_add_fusion.pos_ref.refs_0_, bf16[256,1536]{1,0:T(8,128)(2,1)S(1)} %bitcast.30, bf16[3,96,1536]{2,1,0:T(8,128)(2,1)S(1)} %bitcast.32, bf16[2,48,1536]{2,1,0:T(8,128)(2,1)S(1)} %collective-permute-done.3.n0_ref, ...), custom_call_target="tpu_custom_call" | custom-call | tf_op jit(solution)/shard_map/project/pallas_call | solution.py:87
  80.8 4.8 %all-to-all-start.1 = ((bf16[4,2,256,384]{3,2,1,0:T(8,128)(2,1)}), bf16[4,2,256,384]{3,2,1,0:T(8,128)(2,1)S(1)}, u32[]{:S(2)}, u32[]{:S(2)}) async-start(bf16[4,2,256,384]{3,2,1,0:T(8,128)(2,1)} %project.2.refs_2_), calls=%async_computation.1 | async-start | bytes 3145728 | tf_op jit(solution)/shard_map/all_to_all | solution.py:398
  85.5 3.6 %collective-permute-done.1.n1_ref = bf16[2,48,1536]{2,1,0:T(8,128)(2,1)} collective-permute-done((bf16[2,48,1536]{2,1,0:T(8,128)(2,1)}, bf16[2,48,1536]{2,1,0:T(8,128)(2,1)}, u32[]{:S(2)}, u32[]{:S(2)}) %collective-permute-start.1) | collective-permute-done | bytes 294944 | tf_op jit(solution)/shard_map/ppermute | solution.py:375
  89.1 1.2 pad_maximum_fusion.1
  90.7 2.4 %collective-permute-done.7.far_ref = bf16[3,2,48,1536]{3,2,1,0:T(8,128)(2,1)S(1)} collective-permute-done((bf16[3,2,48,1536]{3,2,1,0:T(8,128)(2,1)S(1)}, bf16[3,2,48,1536]{3,2,1,0:T(8,128)(2,1)S(1)}, u32[]{:S(2)}, u32[]{:S(2)}) %collective-permute-start.7) | collective-permute-done | bytes 884768 | tf_op jit(solution)/shard_map/ppermute | solution.py:400
  93.1 2.1 %project.3 = bf16[1,1,256,384]{3,2,1,0:T(8,128)(2,1)S(1)} custom-call(s32[3]{0:T(128)S(1)} %pad_add_fusion.pos_ref.refs_0_, bf16[256,1536]{1,0:T(8,128)(2,1)S(1)} %bitcast.31, bf16[3,96,1536]{2,1,0:T(8,128)(2,1)S(1)} %bitcast.33, bf16[2,48,1536]{2,1,0:T(8,128)(2,1)} %collective-permute-done.n0_ref, bf16[2,48,1536]{2,1,0:T(8,128)(2,1)} %collective-permute-done.1.n1_ref, ...), custom_call_target="tpu_custom_call" | custom-call | tf_op jit(solution)/shard_map/project/pallas_call | solution.py:87
  95.3 3.5 %attention.2 = (f32[256,384]{1,0:T(8,128)S(1)}, f32[2,256,128]{2,1,0:T(8,128)S(1)}) custom-call(s32[3]{0:T(128)S(1)} %pad_add_fusion.pos_ref.refs_0_, bf16[256,384]{1,0:T(8,128)(2,1)S(1)} %bitcast.35, bf16[4,2,256,384]{3,2,1,0:T(8,128)(2,1)} %project.2.refs_2_, bf16[2,154,384]{2,1,0:T(8,128)(2,1)S(1)} %bitcast.40), custom_call_target="tpu_custom_call" | custom-call | tf_op jit(solution)/shard_map/attention/pallas_call | solution.py:182
  98.8 0.7 copy-done.11
  99.5 2.1 %all-to-all-done.1.refs_2_ = bf16[4,2,256,384]{3,2,1,0:T(8,128)(2,1)S(1)} async-done(((bf16[4,2,256,384]{3,2,1,0:T(8,128)(2,1)}), bf16[4,2,256,384]{3,2,1,0:T(8,128)(2,1)S(1)}, u32[]{:S(2)}, u32[]{:S(2)}) %all-to-all-start.1) | async-done | bytes 1572896 | tf_op jit(solution)/shard_map/all_to_all | solution.py:398
  101.6 1.0 copy-done.12
  102.6 3.9 %attention.3.a_ref = bf16[256,384]{1,0:T(8,128)(2,1)S(1)} custom-call(s32[3]{0:T(128)S(1)} %pad_add_fusion.pos_ref.refs_0_, bf16[256,384]{1,0:T(8,128)(2,1)S(1)} %bitcast.36, bf16[4,2,256,384]{3,2,1,0:T(8,128)(2,1)S(1)} %all-to-all-done.1.refs_2_, f32[256,384]{1,0:T(8,128)S(1)} %get-tuple-element.26.refs_3_, f32[2,256,128]{2,1,0:T(8,128)S(1)} %copy-done.12), custom_call_target="tpu_custom_call" | custom-call | tf_op jit(solution)/shard_map/attention/pallas_call | solution.py:182
  106.6 1.8 %out_projection.1 = bf16[256,1536]{1,0:T(8,128)(2,1)S(1)} custom-call(s32[3]{0:T(128)S(1)} %pad_add_fusion.pos_ref.refs_0_, bf16[256,384]{1,0:T(8,128)(2,1)S(1)} %attention.3.a_ref, bf16[96,1536]{1,0:T(8,128)(2,1)S(1)} %copy-done.9, bf16[2,48,1536]{2,1,0:T(8,128)(2,1)} %collective-permute-done.n0_ref, bf16[2,48,1536]{2,1,0:T(8,128)(2,1)} %collective-permute-done.1.n1_ref, ...), custom_call_target="tpu_custom_call" | custom-call | tf_op jit(solution)/shard_map/out_projection/pallas_call | solution.py:211
  108.4 13.2 %all_to_all.25.part_ref = bf16[4,64,1536]{2,1,0:T(8,128)(2,1)S(1)} all-to-all(bf16[4,64,1536]{2,1,0:T(8,128)(2,1)S(1)} %bitcast.34), channel_id=1, replica_groups=mesh['zl'=4,'core'=2,'tx'=4,'ty'=4,'blk'=2] {'tx'}, dimensions={0} | all-to-all | bytes 1572864 | tf_op jit(solution)/shard_map/all_to_all | solution.py:408
  122.0 15.7 %all_to_all.26 = bf16[4,64,1536]{2,1,0:T(8,128)(2,1)} all-to-all(bf16[4,64,1536]{2,1,0:T(8,128)(2,1)S(1)} %get-tuple-element.29), channel_id=1, replica_groups=mesh['zl'=4,'core'=2,'tx'=4,'ty'=4,'blk'=2] {'ty'}, dimensions={0} | all-to-all | bytes 1572864 | tf_op jit(solution)/shard_map/all_to_all | solution.py:410
  137.7 7.6 %feed_forward.1 = bf16[256,1536]{1,0:T(8,128)(2,1)} custom-call(bf16[256,1536]{1,0:T(8,128)(2,1)} %bitcast.49, bf16[2,4,1536,384]{3,2,1,0:T(8,128)(2,1)} %bitcast.46, bf16[2,4,1536,384]{3,2,1,0:T(8,128)(2,1)} %bitcast.47), custom_call_target="tpu_custom_call" | custom-call | tf_op jit(solution)/shard_map/feed_forward/pallas_call | solution.py:316
  145.4 3.6 %all-to-all-start.4 = ((bf16[4,64,1536]{2,1,0:T(8,128)(2,1)}), bf16[4,64,1536]{2,1,0:T(8,128)(2,1)S(1)}, u32[]{:S(2)}, u32[]{:S(2)}) async-start(bf16[4,64,1536]{2,1,0:T(8,128)(2,1)} %bitcast.48), calls=%async_computation.4 | async-start | bytes 1572864 | tf_op jit(solution)/shard_map/all_to_all | solution.py:412
  150.0 8.5 %all-to-all-done.4.part_ref = bf16[4,64,1536]{2,1,0:T(8,128)(2,1)S(1)} async-done(((bf16[4,64,1536]{2,1,0:T(8,128)(2,1)}), bf16[4,64,1536]{2,1,0:T(8,128)(2,1)S(1)}, u32[]{:S(2)}, u32[]{:S(2)}) %all-to-all-start.4) | async-done | bytes 786464 | tf_op jit(solution)/shard_map/all_to_all | solution.py:412
  158.4 1.1 last_stage.1
  (48 shorter events, 2.0 us)
Async XLA Ops:
  7.2 48.4 %copy-start = (bf16[1,154,2,1536]{3,2,1,0:T(2,128)(2,1)S(1)}, bf16[1,154,2,1536]{3,2,1,0:T(2,128)(2,1)}, u32[]{:S(2)}) copy-start(bf16[1,154,2,1536]{3,2,1,0:T(2,128)(2,1)} %param.14) | copy-start | bytes 2838532
  7.2 130.5 %all-gather.3.cloned.1.call-start = ((), (), s32[]{:S(2)}) async-start(), calls=%async_computation.5 | async-start | bytes 10616832 | tf_op jit(solution)/shard_map/all_gather | solution.py:390
  7.2 36.9 %copy-start.6 = (bf16[1,64,1536]{2,1,0:T(8,128)(2,1)S(1)}, bf16[1,64,1536]{2,1,0:T(8,128)(2,1)}, u32[]{:S(2)}) copy-start(bf16[1,64,1536]{2,1,0:T(8,128)(2,1)} %param.11) | copy-start | bytes 589828
  7.2 36.9 %copy-start.10 = (f32[1,8,1536]{2,1,0:T(8,128)S(1)}, f32[1,8,1536]{2,1,0:T(8,128)}, u32[]{:S(2)}) copy-start(f32[1,8,1536]{2,1,0:T(8,128)} %param.13) | copy-start | bytes 147460
  44.1 1.2 copy-start.1
  46.1 10.4 %collective-permute-start.3 = (bf16[2,48,1536]{2,1,0:T(8,128)(2,1)}, bf16[2,48,1536]{2,1,0:T(8,128)(2,1)S(1)}, u32[]{:S(2)}, u32[]{:S(2)}) collective-permute-start(bf16[2,48,1536]{2,1,0:T(8,128)(2,1)} %dynamic-slice_bitcast_fusion), channel_id=1, source_target_pairs={{0,2},{2,4},{4,6},{6,0},{1,3},{3,5},{5,7},{7,1},{8,10},{10,12},{12... | collective-permute-start | bytes 884744 | tf_op jit(solution)/shard_map/ppermute | solution.py:375
  47.6 10.1 %collective-permute-start.4 = (bf16[2,48,1536]{2,1,0:T(8,128)(2,1)}, bf16[2,48,1536]{2,1,0:T(8,128)(2,1)S(1)}, u32[]{:S(2)}, u32[]{:S(2)}) collective-permute-start(bf16[2,48,1536]{2,1,0:T(8,128)(2,1)} %dynamic-slice_bitcast_fusion), channel_id=1, source_target_pairs={{0,6},{2,0},{4,2},{6,4},{1,7},{3,1},{5,3},{7,5},{8,14},{10,8},{12,... | collective-permute-start | bytes 884744 | tf_op jit(solution)/shard_map/ppermute | solution.py:375
  49.3 14.5 %collective-permute-start.5 = (bf16[2,48,1536]{2,1,0:T(8,128)(2,1)}, bf16[2,48,1536]{2,1,0:T(8,128)(2,1)S(1)}, u32[]{:S(2)}, u32[]{:S(2)}) collective-permute-start(bf16[2,48,1536]{2,1,0:T(8,128)(2,1)} %dynamic-slice_bitcast_fusion), channel_id=1, source_target_pairs={{0,4},{2,6},{4,0},{6,2},{1,5},{3,7},{5,1},{7,3},{8,12},{10,14},{12... | collective-permute-start | bytes 884744 | tf_op jit(solution)/shard_map/ppermute | solution.py:375
  51.3 22.0 %all-to-all-start = ((bf16[4,64,1536]{2,1,0:T(8,128)(2,1)}), bf16[4,64,1536]{2,1,0:T(8,128)(2,1)S(1)}, u32[]{:S(2)}, u32[]{:S(2)}) async-start(bf16[4,64,1536]{2,1,0:T(8,128)(2,1)} %first_norm.1), calls=%async_computation | async-start | bytes 1572864 | tf_op jit(solution)/shard_map/all_to_all | solution.py:381
  55.6 9.3 %copy-start.8 = (bf16[96,1536]{1,0:T(8,128)(2,1)S(1)}, bf16[96,1536]{1,0:T(8,128)(2,1)}, u32[]{:S(2)}) copy-start(bf16[96,1536]{1,0:T(8,128)(2,1)} %own_ref.1) | copy-start | bytes 884740
  64.8 12.4 %collective-permute-start.6 = (bf16[3,2,48,1536]{3,2,1,0:T(8,128)(2,1)}, bf16[3,2,48,1536]{3,2,1,0:T(8,128)(2,1)}, u32[]{:S(2)}, u32[]{:S(2)}) collective-permute-start(bf16[3,2,48,1536]{3,2,1,0:T(8,128)(2,1)} %pad_maximum_fusion), channel_id=1, source_target_pairs={{0,32},{32,0},{1,33},{33,1},{2,34},{34,2},{3,35},{35,3},{4,36},{36... | collective-permute-start | bytes 2654216 | tf_op jit(solution)/shard_map/ppermute | solution.py:393
  73.3 12.2 %collective-permute-start = (bf16[2,48,1536]{2,1,0:T(8,128)(2,1)}, bf16[2,48,1536]{2,1,0:T(8,128)(2,1)}, u32[]{:S(2)}, u32[]{:S(2)}) collective-permute-start(bf16[2,48,1536]{2,1,0:T(8,128)(2,1)} %pad_maximum_fusion.2), channel_id=1, source_target_pairs={{0,2},{2,4},{4,6},{6,0},{1,3},{3,5},{5,7},{7,1},{8,10},{10,12},{12... | collective-permute-start | bytes 884744 | tf_op jit(solution)/shard_map/ppermute | solution.py:375
  73.3 15.8 %collective-permute-start.1 = (bf16[2,48,1536]{2,1,0:T(8,128)(2,1)}, bf16[2,48,1536]{2,1,0:T(8,128)(2,1)}, u32[]{:S(2)}, u32[]{:S(2)}) collective-permute-start(bf16[2,48,1536]{2,1,0:T(8,128)(2,1)} %pad_maximum_fusion.2), channel_id=1, source_target_pairs={{0,6},{2,0},{4,2},{6,4},{1,7},{3,1},{5,3},{7,5},{8,14},{10,8},{12,... | collective-permute-start | bytes 884744 | tf_op jit(solution)/shard_map/ppermute | solution.py:375
  76.5 12.6 %collective-permute-start.2 = (bf16[2,48,1536]{2,1,0:T(8,128)(2,1)}, bf16[2,48,1536]{2,1,0:T(8,128)(2,1)}, u32[]{:S(2)}, u32[]{:S(2)}) collective-permute-start(bf16[2,48,1536]{2,1,0:T(8,128)(2,1)} %pad_maximum_fusion.2), channel_id=1, source_target_pairs={{0,4},{2,6},{4,0},{6,2},{1,5},{3,7},{5,1},{7,3},{8,12},{10,14},{12... | collective-permute-start | bytes 884744 | tf_op jit(solution)/shard_map/ppermute | solution.py:375
  80.8 20.9 %all-to-all-start.1 = ((bf16[4,2,256,384]{3,2,1,0:T(8,128)(2,1)}), bf16[4,2,256,384]{3,2,1,0:T(8,128)(2,1)S(1)}, u32[]{:S(2)}, u32[]{:S(2)}) async-start(bf16[4,2,256,384]{3,2,1,0:T(8,128)(2,1)} %project.2.refs_2_), calls=%async_computation.1 | async-start | bytes 3145728 | tf_op jit(solution)/shard_map/all_to_all | solution.py:398
  85.5 7.6 %copy-start.2 = (bf16[1536,3,96]{0,2,1:T(8,128)(2,1)S(1)}, bf16[1536,3,96]{0,2,1:T(8,128)(2,1)}, u32[]{:S(2)}) copy-start(bf16[1536,3,96]{0,2,1:T(8,128)(2,1)} %param.17) | copy-start | bytes 2654212
  90.4 4.9 %copy-start.5 = (bf16[1,154,2,384]{3,1,2,0:T(8,128)(2,1)S(1)}, bf16[1,154,2,384]{3,1,2,0:T(8,128)(2,1)}, u32[]{:S(2)}) copy-start(bf16[1,154,2,384]{3,1,2,0:T(8,128)(2,1)} %copy.16) | copy-start | bytes 709636
  90.4 2.7 %collective-permute-start.7 = (bf16[3,2,48,1536]{3,2,1,0:T(8,128)(2,1)S(1)}, bf16[3,2,48,1536]{3,2,1,0:T(8,128)(2,1)S(1)}, u32[]{:S(2)}, u32[]{:S(2)}) collective-permute-start(bf16[3,2,48,1536]{3,2,1,0:T(8,128)(2,1)S(1)} %pad_maximum_fusion.1), channel_id=1, source_target_pairs={{0,32},{32,0},{1,33},{33,1},{2,34},{34,2},{3,35},{35,3},{4,36},{36... | collective-permute-start | bytes 2654216 | tf_op jit(solution)/shard_map/ppermute | solution.py:400
  93.1 2.2 %copy-start.3 = (bf16[3,2,48,1536]{3,2,1,0:T(8,128)(2,1)}, bf16[3,2,48,1536]{3,2,1,0:T(8,128)(2,1)S(1)}, u32[]{:S(2)}) copy-start(bf16[3,2,48,1536]{3,2,1,0:T(8,128)(2,1)S(1)} %collective-permute-done.7.far_ref) | copy-start | bytes 2654212
  98.8 0.7 copy-start.11
  99.5 7.0 %copy-start.9 = (bf16[96,1536]{1,0:T(8,128)(2,1)S(1)}, bf16[96,1536]{1,0:T(8,128)(2,1)}, u32[]{:S(2)}) copy-start(bf16[96,1536]{1,0:T(8,128)(2,1)} %own_ref.1) | copy-start | bytes 884740
  101.6 4.9 %copy-start.4 = (bf16[3,2,48,1536]{3,2,1,0:T(8,128)(2,1)S(1)}, bf16[3,2,48,1536]{3,2,1,0:T(8,128)(2,1)}, u32[]{:S(2)}) copy-start(bf16[3,2,48,1536]{3,2,1,0:T(8,128)(2,1)} %copy-done.3) | copy-start | bytes 2654212
  101.6 1.0 copy-start.12
  106.6 15.1 %copy-start.7 = (bf16[1,64,1536]{2,1,0:T(8,128)(2,1)S(1)}, bf16[1,64,1536]{2,1,0:T(8,128)(2,1)}, u32[]{:S(2)}) copy-start(bf16[1,64,1536]{2,1,0:T(8,128)(2,1)} %param.11) | copy-start | bytes 589828
  145.4 4.3 %copy-start.13 = (bf16[1536,64]{0,1:T(8,128)(2,1)S(1)}, bf16[1536,64]{0,1:T(8,128)(2,1)}, u32[]{:S(2)}) copy-start(bf16[1536,64]{0,1:T(8,128)(2,1)} %param.21) | copy-start | bytes 589828
  145.4 14.2 %copy-start.14 = (f32[1,32,128]{2,1,0:T(8,128)S(1)}, f32[1,32,128]{2,1,0:T(8,128)}, u32[]{:S(2)}) copy-start(f32[1,32,128]{2,1,0:T(8,128)} %param.12) | copy-start | bytes 49156
  145.4 13.1 %all-to-all-start.4 = ((bf16[4,64,1536]{2,1,0:T(8,128)(2,1)}), bf16[4,64,1536]{2,1,0:T(8,128)(2,1)S(1)}, u32[]{:S(2)}, u32[]{:S(2)}) async-start(bf16[4,64,1536]{2,1,0:T(8,128)(2,1)} %bitcast.48), calls=%async_computation.4 | async-start | bytes 1572864 | tf_op jit(solution)/shard_map/all_to_all | solution.py:412
Sparse Core Ops, SparseCore 0:
  44.3 62.3 all-gather.2

commit v6 on v5

--- a/solution.py
+++ b/solution.py
@@ -219,43 +219,56 @@
     )(pos, a, own, *near, far)
 
 
-def pack_kernel(pos_ref, up_ref, down_ref, out_ref, sem):
-    @pl.when(pos_ref[0] == 0)
-    def _():
-        copy = pltpu.make_async_copy(up_ref, out_ref, sem.at[0])
-        copy.start()
-        copy.wait()
-
-    @pl.when(pos_ref[0] == 1)
-    def _():
-        part = down_ref.shape[0]
-        copies = []
-        for s in range(4):
-            copies.append(
-                pltpu.make_async_copy(
-                    down_ref.at[:, pl.ds(s * part, part)],
-                    out_ref.at[pl.ds(s * part, part), :],
-                    sem.at[s],
-                )
+def pack_kernel(pos_ref, up_ref, down_ref, out_ref, held, load_sem, store_sem):
+    core = pos_ref[0]
+    zone = pos_ref[1]
+    part = down_ref.shape[0]
+
+    def move(sources):
+        loads = []
+        stores = []
+        for i, source in enumerate(sources):
+            rows = pl.ds(i * part, part)
+            loads.append(pltpu.make_async_copy(source, held.at[rows, :], load_sem.at[i]))
+            stores.append(
+                pltpu.make_async_copy(held.at[rows, :], out_ref.at[rows, :], store_sem.at[i])
             )
-        for copy in copies:
-            copy.start()
-        for copy in copies:
-            copy.wait()
+        for load in loads:
+            load.start()
+        for load, store in zip(loads, stores):
+            load.wait()
+            store.start()
+        for store in stores:
+            store.wait()
+
+    for half in range(2):
+
+        @pl.when(jnp.logical_and(core == 0, zone == half))
+        def _():
+            move([up_ref.at[pl.ds((2 * half + i) * part, part), :] for i in range(2)])
+
+        @pl.when(jnp.logical_and(core == 1, zone == half))
+        def _():
+            move([down_ref.at[:, pl.ds((2 * half + i) * part, part)] for i in range(2)])
 
 
 def pack_ffn(pos, w_up, w_down):
+    part = w_down.shape[0]
     return pl.pallas_call(
         pack_kernel,
-        out_shape=jax.ShapeDtypeStruct(w_up.shape, BF),
+        out_shape=jax.ShapeDtypeStruct((2 * part, part), BF),
         in_specs=[
             pl.BlockSpec(memory_space=pltpu.SMEM),
             pl.BlockSpec(memory_space=pltpu.HBM),
             pl.BlockSpec(memory_space=pltpu.HBM),
         ],
         out_specs=pl.BlockSpec(memory_space=pltpu.HBM),
-        scratch_shapes=[pltpu.SemaphoreType.DMA((4,))],
-        compiler_params=params(60),
+        scratch_shapes=[
+            pltpu.VMEM((2 * part, part), BF),
+            pltpu.SemaphoreType.DMA((2,)),
+            pltpu.SemaphoreType.DMA((2,)),
+        ],
+        compiler_params=params(58),
         name="pack_ffn",
     )(pos, w_up, w_down)
 
@@ -386,8 +399,9 @@
     half_qo = jnp.concatenate([half_q, half_out[None]])
     text = lax.dynamic_slice_in_dim(text_kv[0], lax.axis_index("tx") * 384, 384, 2)
     text = jnp.transpose(text, (1, 0, 2))
-    half_ffn = pack_ffn(core[None].astype(jnp.int32), w_up, w_down)
-    ffn_full = lax.all_gather(half_ffn, ("core", "tx"), axis=0, tiled=False)
+    place = jnp.stack([core, lax.axis_index("zp")]).astype(jnp.int32)
+    quarter = pack_ffn(place, w_up, w_down)
+    ffn_full = lax.all_gather(quarter, ("core", "tx", "zp"), axis=0, tiled=False)
     ffn_full = ffn_full.reshape(2, 4, width, w_up.shape[1])
 
     far_kv = lax.ppermute(jnp.stack(near_kv), "core", swap2)
@@ -420,10 +434,10 @@
 
 def solution(mesh):
     fine = Mesh(
-        mesh.devices.reshape(mesh.shape["req"] // 2, 2, 4, 4, mesh.shape["blk"]),
-        ("zl", "core", "tx", "ty", "blk"),
+        mesh.devices.reshape(mesh.shape["req"] // 4, 2, 2, 4, 4, mesh.shape["blk"]),
+        ("zl", "zp", "core", "tx", "ty", "blk"),
     )
-    group = ("zl", "core", "blk")
+    group = ("zl", "zp", "core", "blk")
     tile = ("tx", "ty")
     in_specs = (
         P(group, tile, None),

time: 169 us -> 137 us (0.81); the launches traced: 167 us -> 137 us
  Pallas kernels: 62 us -> 27.8 us
  waiting for transfers between devices: 31.6 us -> 34 us
    pallas_call x1, Pallas kernels: 36.9 us -> 2.6 us  [pack_ffn(): pl.pallas_call(pack_kernel, out_shape=jax.ShapeDtypeStruct((2 * part, par...]
    all_to_all x1, waiting for transfers between devices: 7.66 us -> 9.73 us  [on_device(): h1 = lax.all_to_all(h1, 'tx', split_axis=0, concat_axis=0, tiled=True)]
  transfers between devices with their start and end apart: 12 -> 12, of which waited for: 7 -> 7; matrix products, arithmetic and copies ran while one was open for 3% -> 4% of each run, Pallas kernels for 10% -> 12%
where the time goes in v6:
time: 137 us
  waiting for transfers between devices  34 us (25%)
  blocking collectives  29.6 us (22%)
  Pallas kernels  27.8 us (20%)
  starting transfers between devices  21.5 us (16%)
  between operations  15.7 us (11%)
  other arithmetic  4.46 us (3%)
  local copies, waits for them, and re-layouts  3.78 us (3%)
    all_to_all x1, blocking collectives, on_device(): h2 = lax.all_to_all(h2, 'ty', split_axis=0, concat_axis=0, tiled=True)  16.2 us
    all_to_all x1, blocking collectives, on_device(): lax.all_to_all(partial, 'tx', split_axis=0, concat_axis=0, tiled=True)  13.3 us
    ppermute x6, waiting for transfers between devices, to_lines(): return lax.ppermute(value, 'ty', [(i, (i + step) % 4) for i in range(4)])  10.8 us
    all_to_all x1, waiting for transfers between devices, on_device(): h1 = lax.all_to_all(h1, 'tx', split_axis=0, concat_axis=0, tiled=True)  9.73 us
    all_to_all x1, waiting for transfers between devices, on_device(): lax.all_to_all(partial, 'ty', split_axis=0, concat_axis=0, tiled=True)  8.96 us
    ppermute x6, starting transfers between devices, to_lines(): return lax.ppermute(value, 'ty', [(i, (i + step) % 4) for i in range(4)])  8.46 us
    pallas_call x1, Pallas kernels, feed_forward(): pl.pallas_call(ffn_kernel, grid=(4,), out_shape=jax.ShapeDtypeStruct((row...  7.66 us
    pallas_call x2, Pallas kernels, attention(): pl.pallas_call(functools.partial(attention_kernel, own), out_shape=out, i...  7.49 us
  transfers between devices with their start and end apart: 12, of which 7 were waited for; matrix products, arithmetic and copies ran while one was open for 4% of the time, Pallas kernels for 12%

profile of v6, /device:TPU:128, one launch (start us, length us, event | category | flops | bytes accessed | tf_op | source)
XLA Modules:
  0.0 136.8 jit_solution(11145619792629166349)
XLA Ops:
  7.9 2.6 %pack_ffn.1 = bf16[768,384]{1,0:T(8,128)(2,1)} custom-call(s32[2]{0:T(128)} %pad_add_fusion.1.pos_ref, bf16[1536,384]{1,0:T(8,128)(2,1)} %up_ref.1, bf16[384,1536]{1,0:T(8,128)(2,1)} %down_ref.1), custom_call_target="tpu_custom_call" | custom-call | tf_op jit(solution)/shard_map/pack_ffn/pallas_call | solution.py:257
  10.5 1.1 first_norm.1
  11.7 0.7 dynamic-slice_bitcast_fusion
  12.4 1.6 %collective-permute-start.3 = (bf16[2,48,1536]{2,1,0:T(8,128)(2,1)}, bf16[2,48,1536]{2,1,0:T(8,128)(2,1)S(1)}, u32[]{:S(2)}, u32[]{:S(2)}) collective-permute-start(bf16[2,48,1536]{2,1,0:T(8,128)(2,1)} %dynamic-slice_bitcast_fusion), channel_id=1, source_target_pairs={{0,2},{2,4},{4,6},{6,0},{1,3},{3,5},{5,7},{7,1},{8,10},{10,12},{12... | collective-permute-start | bytes 884744 | tf_op jit(solution)/shard_map/ppermute | solution.py:388
  14.0 1.7 %collective-permute-start.4 = (bf16[2,48,1536]{2,1,0:T(8,128)(2,1)}, bf16[2,48,1536]{2,1,0:T(8,128)(2,1)S(1)}, u32[]{:S(2)}, u32[]{:S(2)}) collective-permute-start(bf16[2,48,1536]{2,1,0:T(8,128)(2,1)} %dynamic-slice_bitcast_fusion), channel_id=1, source_target_pairs={{0,6},{2,0},{4,2},{6,4},{1,7},{3,1},{5,3},{7,5},{8,14},{10,8},{12,... | collective-permute-start | bytes 884744 | tf_op jit(solution)/shard_map/ppermute | solution.py:388
  15.6 2.0 %collective-permute-start.5 = (bf16[2,48,1536]{2,1,0:T(8,128)(2,1)}, bf16[2,48,1536]{2,1,0:T(8,128)(2,1)S(1)}, u32[]{:S(2)}, u32[]{:S(2)}) collective-permute-start(bf16[2,48,1536]{2,1,0:T(8,128)(2,1)} %dynamic-slice_bitcast_fusion), channel_id=1, source_target_pairs={{0,4},{2,6},{4,0},{6,2},{1,5},{3,7},{5,1},{7,3},{8,12},{10,14},{12... | collective-permute-start | bytes 884744 | tf_op jit(solution)/shard_map/ppermute | solution.py:388
  17.6 4.3 %all-to-all-start = ((bf16[4,64,1536]{2,1,0:T(8,128)(2,1)}), bf16[4,64,1536]{2,1,0:T(8,128)(2,1)S(1)}, u32[]{:S(2)}, u32[]{:S(2)}) async-start(bf16[4,64,1536]{2,1,0:T(8,128)(2,1)} %first_norm.1), calls=%async_computation | async-start | bytes 1572864 | tf_op jit(solution)/shard_map/all_to_all | solution.py:394
  22.1 0.7 copy.16
  22.8 1.3 collective-permute-done.4.n1_ref
  24.1 6.0 %collective-permute-done.5.n2_ref = bf16[2,48,1536]{2,1,0:T(8,128)(2,1)S(1)} collective-permute-done((bf16[2,48,1536]{2,1,0:T(8,128)(2,1)}, bf16[2,48,1536]{2,1,0:T(8,128)(2,1)S(1)}, u32[]{:S(2)}, u32[]{:S(2)}) %collective-permute-start.5) | collective-permute-done | bytes 294944 | tf_op jit(solution)/shard_map/ppermute | solution.py:388
  30.1 1.1 pad_maximum_fusion
  31.3 0.8 pad_maximum_fusion.2
  32.0 9.7 %all-to-all-done = bf16[4,64,1536]{2,1,0:T(8,128)(2,1)S(1)} async-done(((bf16[4,64,1536]{2,1,0:T(8,128)(2,1)}), bf16[4,64,1536]{2,1,0:T(8,128)(2,1)S(1)}, u32[]{:S(2)}, u32[]{:S(2)}) %all-to-all-start) | async-done | bytes 786464 | tf_op jit(solution)/shard_map/all_to_all | solution.py:394
  41.8 3.2 %collective-permute-start.1 = (bf16[2,48,1536]{2,1,0:T(8,128)(2,1)}, bf16[2,48,1536]{2,1,0:T(8,128)(2,1)}, u32[]{:S(2)}, u32[]{:S(2)}) collective-permute-start(bf16[2,48,1536]{2,1,0:T(8,128)(2,1)} %pad_maximum_fusion.2), channel_id=1, source_target_pairs={{0,6},{2,0},{4,2},{6,4},{1,7},{3,1},{5,3},{7,5},{8,14},{10,8},{12,... | collective-permute-start | bytes 884744 | tf_op jit(solution)/shard_map/ppermute | solution.py:388
  45.7 3.5 %project.2.refs_2_ = bf16[4,2,256,384]{3,2,1,0:T(8,128)(2,1)} custom-call(s32[3]{0:T(128)S(1)} %pad_add_fusion.pos_ref.refs_0_, bf16[256,1536]{1,0:T(8,128)(2,1)S(1)} %bitcast.31, bf16[3,96,1536]{2,1,0:T(8,128)(2,1)S(1)} %bitcast.33, bf16[2,48,1536]{2,1,0:T(8,128)(2,1)S(1)} %collective-permute-done.3.n0_ref, ...), custom_call_target="tpu_custom_call" | custom-call | tf_op jit(solution)/shard_map/project/pallas_call | solution.py:87
  49.3 4.8 %all-to-all-start.1 = ((bf16[4,2,256,384]{3,2,1,0:T(8,128)(2,1)}), bf16[4,2,256,384]{3,2,1,0:T(8,128)(2,1)S(1)}, u32[]{:S(2)}, u32[]{:S(2)}) async-start(bf16[4,2,256,384]{3,2,1,0:T(8,128)(2,1)} %project.2.refs_2_), calls=%async_computation.1 | async-start | bytes 3145728 | tf_op jit(solution)/shard_map/all_to_all | solution.py:412
  54.0 3.5 %collective-permute-done.1.n1_ref = bf16[2,48,1536]{2,1,0:T(8,128)(2,1)} collective-permute-done((bf16[2,48,1536]{2,1,0:T(8,128)(2,1)}, bf16[2,48,1536]{2,1,0:T(8,128)(2,1)}, u32[]{:S(2)}, u32[]{:S(2)}) %collective-permute-start.1) | collective-permute-done | bytes 294944 | tf_op jit(solution)/shard_map/ppermute | solution.py:388
  57.6 1.3 pad_maximum_fusion.1
  59.2 2.4 %collective-permute-done.7.far_ref = bf16[3,2,48,1536]{3,2,1,0:T(8,128)(2,1)S(1)} collective-permute-done((bf16[3,2,48,1536]{3,2,1,0:T(8,128)(2,1)S(1)}, bf16[3,2,48,1536]{3,2,1,0:T(8,128)(2,1)S(1)}, u32[]{:S(2)}, u32[]{:S(2)}) %collective-permute-start.7) | collective-permute-done | bytes 884768 | tf_op jit(solution)/shard_map/ppermute | solution.py:414
  61.6 2.1 %project.3 = bf16[1,1,256,384]{3,2,1,0:T(8,128)(2,1)S(1)} custom-call(s32[3]{0:T(128)S(1)} %pad_add_fusion.pos_ref.refs_0_, bf16[256,1536]{1,0:T(8,128)(2,1)S(1)} %bitcast.32, bf16[3,96,1536]{2,1,0:T(8,128)(2,1)S(1)} %bitcast.34, bf16[2,48,1536]{2,1,0:T(8,128)(2,1)} %collective-permute-done.n0_ref, bf16[2,48,1536]{2,1,0:T(8,128)(2,1)} %collective-permute-done.1.n1_ref, ...), custom_call_target="tpu_custom_call" | custom-call | tf_op jit(solution)/shard_map/project/pallas_call | solution.py:87
  63.8 3.6 %attention.2 = (f32[256,384]{1,0:T(8,128)S(1)}, f32[2,256,128]{2,1,0:T(8,128)S(1)}) custom-call(s32[3]{0:T(128)S(1)} %pad_add_fusion.pos_ref.refs_0_, bf16[256,384]{1,0:T(8,128)(2,1)S(1)} %bitcast.36, bf16[4,2,256,384]{3,2,1,0:T(8,128)(2,1)} %project.2.refs_2_, bf16[2,154,384]{2,1,0:T(8,128)(2,1)S(1)} %bitcast.41), custom_call_target="tpu_custom_call" | custom-call | tf_op jit(solution)/shard_map/attention/pallas_call | solution.py:182
  67.4 0.7 copy-done.11
  68.1 2.0 %all-to-all-done.1.refs_2_ = bf16[4,2,256,384]{3,2,1,0:T(8,128)(2,1)S(1)} async-done(((bf16[4,2,256,384]{3,2,1,0:T(8,128)(2,1)}), bf16[4,2,256,384]{3,2,1,0:T(8,128)(2,1)S(1)}, u32[]{:S(2)}, u32[]{:S(2)}) %all-to-all-start.1) | async-done | bytes 1572896 | tf_op jit(solution)/shard_map/all_to_all | solution.py:412
  70.1 1.1 copy-done.12
  71.2 3.9 %attention.3.a_ref = bf16[256,384]{1,0:T(8,128)(2,1)S(1)} custom-call(s32[3]{0:T(128)S(1)} %pad_add_fusion.pos_ref.refs_0_, bf16[256,384]{1,0:T(8,128)(2,1)S(1)} %bitcast.37, bf16[4,2,256,384]{3,2,1,0:T(8,128)(2,1)S(1)} %all-to-all-done.1.refs_2_, f32[256,384]{1,0:T(8,128)S(1)} %get-tuple-element.26.refs_3_, f32[2,256,128]{2,1,0:T(8,128)S(1)} %copy-done.12), custom_call_target="tpu_custom_call" | custom-call | tf_op jit(solution)/shard_map/attention/pallas_call | solution.py:182
  75.1 1.8 %out_projection.1 = bf16[256,1536]{1,0:T(8,128)(2,1)S(1)} custom-call(s32[3]{0:T(128)S(1)} %pad_add_fusion.pos_ref.refs_0_, bf16[256,384]{1,0:T(8,128)(2,1)S(1)} %attention.3.a_ref, bf16[96,1536]{1,0:T(8,128)(2,1)S(1)} %copy-done.9, bf16[2,48,1536]{2,1,0:T(8,128)(2,1)} %collective-permute-done.n0_ref, bf16[2,48,1536]{2,1,0:T(8,128)(2,1)} %collective-permute-done.1.n1_ref, ...), custom_call_target="tpu_custom_call" | custom-call | tf_op jit(solution)/shard_map/out_projection/pallas_call | solution.py:211
  77.0 13.3 %all_to_all.25.part_ref = bf16[4,64,1536]{2,1,0:T(8,128)(2,1)S(1)} all-to-all(bf16[4,64,1536]{2,1,0:T(8,128)(2,1)S(1)} %bitcast.35), channel_id=1, replica_groups=mesh['zl'=2,'zp'=2,'core'=2,'tx'=4,'ty'=4,'blk'=2] {'tx'}, dimensions={0} | all-to-all | bytes 1572864 | tf_op jit(solution)/shard_map/all_to_all | solution.py:422
  90.7 16.2 %all_to_all.26 = bf16[4,64,1536]{2,1,0:T(8,128)(2,1)} all-to-all(bf16[4,64,1536]{2,1,0:T(8,128)(2,1)S(1)} %get-tuple-element.29), channel_id=1, replica_groups=mesh['zl'=2,'zp'=2,'core'=2,'tx'=4,'ty'=4,'blk'=2] {'ty'}, dimensions={0} | all-to-all | bytes 1572864 | tf_op jit(solution)/shard_map/all_to_all | solution.py:424
  106.9 7.7 %feed_forward.1 = bf16[256,1536]{1,0:T(8,128)(2,1)} custom-call(bf16[256,1536]{1,0:T(8,128)(2,1)} %bitcast.50, bf16[2,4,1536,384]{3,2,1,0:T(8,128)(2,1)} %bitcast.47, bf16[2,4,1536,384]{3,2,1,0:T(8,128)(2,1)} %bitcast.48), custom_call_target="tpu_custom_call" | custom-call | tf_op jit(solution)/shard_map/feed_forward/pallas_call | solution.py:329
  114.6 3.6 %all-to-all-start.4 = ((bf16[4,64,1536]{2,1,0:T(8,128)(2,1)}), bf16[4,64,1536]{2,1,0:T(8,128)(2,1)S(1)}, u32[]{:S(2)}, u32[]{:S(2)}) async-start(bf16[4,64,1536]{2,1,0:T(8,128)(2,1)} %bitcast.49), calls=%async_computation.4 | async-start | bytes 1572864 | tf_op jit(solution)/shard_map/all_to_all | solution.py:426
  119.2 9.0 %all-to-all-done.4.part_ref = bf16[4,64,1536]{2,1,0:T(8,128)(2,1)S(1)} async-done(((bf16[4,64,1536]{2,1,0:T(8,128)(2,1)}), bf16[4,64,1536]{2,1,0:T(8,128)(2,1)S(1)}, u32[]{:S(2)}, u32[]{:S(2)}) %all-to-all-start.4) | async-done | bytes 786464 | tf_op jit(solution)/shard_map/all_to_all | solution.py:426
  128.2 1.1 last_stage.1
  (49 shorter events, 2.6 us)
Async XLA Ops:
  7.2 14.7 %copy-start = (bf16[1,154,2,1536]{3,2,1,0:T(2,128)(2,1)S(1)}, bf16[1,154,2,1536]{3,2,1,0:T(2,128)(2,1)}, u32[]{:S(2)}) copy-start(bf16[1,154,2,1536]{3,2,1,0:T(2,128)(2,1)} %param.14) | copy-start | bytes 2838532
  7.2 99.7 %all-gather.3.cloned.1.call-start = ((), (), s32[]{:S(2)}) async-start(), calls=%async_computation.5 | async-start | bytes 10027008 | tf_op jit(solution)/shard_map/all_gather | solution.py:404
  7.8 2.6 %copy-start.6 = (bf16[1,64,1536]{2,1,0:T(8,128)(2,1)S(1)}, bf16[1,64,1536]{2,1,0:T(8,128)(2,1)}, u32[]{:S(2)}) copy-start(bf16[1,64,1536]{2,1,0:T(8,128)(2,1)} %param.11) | copy-start | bytes 589828
  7.8 2.7 %copy-start.10 = (f32[1,8,1536]{2,1,0:T(8,128)S(1)}, f32[1,8,1536]{2,1,0:T(8,128)}, u32[]{:S(2)}) copy-start(f32[1,8,1536]{2,1,0:T(8,128)} %param.13) | copy-start | bytes 147460
  7.9 3.8 %copy-start.1 = (bf16[1536,3,96]{0,2,1:T(8,128)(2,1)S(1)}, bf16[1536,3,96]{0,2,1:T(8,128)(2,1)}, u32[]{:S(2)}) copy-start(bf16[1536,3,96]{0,2,1:T(8,128)(2,1)} %param.17) | copy-start | bytes 2654212
  12.4 10.4 %collective-permute-start.3 = (bf16[2,48,1536]{2,1,0:T(8,128)(2,1)}, bf16[2,48,1536]{2,1,0:T(8,128)(2,1)S(1)}, u32[]{:S(2)}, u32[]{:S(2)}) collective-permute-start(bf16[2,48,1536]{2,1,0:T(8,128)(2,1)} %dynamic-slice_bitcast_fusion), channel_id=1, source_target_pairs={{0,2},{2,4},{4,6},{6,0},{1,3},{3,5},{5,7},{7,1},{8,10},{10,12},{12... | collective-permute-start | bytes 884744 | tf_op jit(solution)/shard_map/ppermute | solution.py:388
  14.0 10.1 %collective-permute-start.4 = (bf16[2,48,1536]{2,1,0:T(8,128)(2,1)}, bf16[2,48,1536]{2,1,0:T(8,128)(2,1)S(1)}, u32[]{:S(2)}, u32[]{:S(2)}) collective-permute-start(bf16[2,48,1536]{2,1,0:T(8,128)(2,1)} %dynamic-slice_bitcast_fusion), channel_id=1, source_target_pairs={{0,6},{2,0},{4,2},{6,4},{1,7},{3,1},{5,3},{7,5},{8,14},{10,8},{12,... | collective-permute-start | bytes 884744 | tf_op jit(solution)/shard_map/ppermute | solution.py:388
  15.6 14.5 %collective-permute-start.5 = (bf16[2,48,1536]{2,1,0:T(8,128)(2,1)}, bf16[2,48,1536]{2,1,0:T(8,128)(2,1)S(1)}, u32[]{:S(2)}, u32[]{:S(2)}) collective-permute-start(bf16[2,48,1536]{2,1,0:T(8,128)(2,1)} %dynamic-slice_bitcast_fusion), channel_id=1, source_target_pairs={{0,4},{2,6},{4,0},{6,2},{1,5},{3,7},{5,1},{7,3},{8,12},{10,14},{12... | collective-permute-start | bytes 884744 | tf_op jit(solution)/shard_map/ppermute | solution.py:388
  17.6 24.1 %all-to-all-start = ((bf16[4,64,1536]{2,1,0:T(8,128)(2,1)}), bf16[4,64,1536]{2,1,0:T(8,128)(2,1)S(1)}, u32[]{:S(2)}, u32[]{:S(2)}) async-start(bf16[4,64,1536]{2,1,0:T(8,128)(2,1)} %first_norm.1), calls=%async_computation | async-start | bytes 1572864 | tf_op jit(solution)/shard_map/all_to_all | solution.py:394
  21.9 9.3 %copy-start.8 = (bf16[96,1536]{1,0:T(8,128)(2,1)S(1)}, bf16[96,1536]{1,0:T(8,128)(2,1)}, u32[]{:S(2)}) copy-start(bf16[96,1536]{1,0:T(8,128)(2,1)} %own_ref.1) | copy-start | bytes 884740
  31.2 14.5 %collective-permute-start.6 = (bf16[3,2,48,1536]{3,2,1,0:T(8,128)(2,1)}, bf16[3,2,48,1536]{3,2,1,0:T(8,128)(2,1)}, u32[]{:S(2)}, u32[]{:S(2)}) collective-permute-start(bf16[3,2,48,1536]{3,2,1,0:T(8,128)(2,1)} %pad_maximum_fusion), channel_id=1, source_target_pairs={{0,32},{32,0},{1,33},{33,1},{2,34},{34,2},{3,35},{35,3},{4,36},{36... | collective-permute-start | bytes 2654216 | tf_op jit(solution)/shard_map/ppermute | solution.py:407
  41.8 12.3 %collective-permute-start = (bf16[2,48,1536]{2,1,0:T(8,128)(2,1)}, bf16[2,48,1536]{2,1,0:T(8,128)(2,1)}, u32[]{:S(2)}, u32[]{:S(2)}) collective-permute-start(bf16[2,48,1536]{2,1,0:T(8,128)(2,1)} %pad_maximum_fusion.2), channel_id=1, source_target_pairs={{0,2},{2,4},{4,6},{6,0},{1,3},{3,5},{5,7},{7,1},{8,10},{10,12},{12... | collective-permute-start | bytes 884744 | tf_op jit(solution)/shard_map/ppermute | solution.py:388
  41.8 15.8 %collective-permute-start.1 = (bf16[2,48,1536]{2,1,0:T(8,128)(2,1)}, bf16[2,48,1536]{2,1,0:T(8,128)(2,1)}, u32[]{:S(2)}, u32[]{:S(2)}) collective-permute-start(bf16[2,48,1536]{2,1,0:T(8,128)(2,1)} %pad_maximum_fusion.2), channel_id=1, source_target_pairs={{0,6},{2,0},{4,2},{6,4},{1,7},{3,1},{5,3},{7,5},{8,14},{10,8},{12,... | collective-permute-start | bytes 884744 | tf_op jit(solution)/shard_map/ppermute | solution.py:388
  45.0 12.6 %collective-permute-start.2 = (bf16[2,48,1536]{2,1,0:T(8,128)(2,1)}, bf16[2,48,1536]{2,1,0:T(8,128)(2,1)}, u32[]{:S(2)}, u32[]{:S(2)}) collective-permute-start(bf16[2,48,1536]{2,1,0:T(8,128)(2,1)} %pad_maximum_fusion.2), channel_id=1, source_target_pairs={{0,4},{2,6},{4,0},{6,2},{1,5},{3,7},{5,1},{7,3},{8,12},{10,14},{12... | collective-permute-start | bytes 884744 | tf_op jit(solution)/shard_map/ppermute | solution.py:388
  49.3 20.9 %all-to-all-start.1 = ((bf16[4,2,256,384]{3,2,1,0:T(8,128)(2,1)}), bf16[4,2,256,384]{3,2,1,0:T(8,128)(2,1)S(1)}, u32[]{:S(2)}, u32[]{:S(2)}) async-start(bf16[4,2,256,384]{3,2,1,0:T(8,128)(2,1)} %project.2.refs_2_), calls=%async_computation.1 | async-start | bytes 3145728 | tf_op jit(solution)/shard_map/all_to_all | solution.py:412
  54.0 7.5 %copy-start.2 = (bf16[1536,3,96]{0,2,1:T(8,128)(2,1)S(1)}, bf16[1536,3,96]{0,2,1:T(8,128)(2,1)}, u32[]{:S(2)}) copy-start(bf16[1536,3,96]{0,2,1:T(8,128)(2,1)} %param.17) | copy-start | bytes 2654212
  58.9 4.9 %copy-start.5 = (bf16[1,154,2,384]{3,1,2,0:T(8,128)(2,1)S(1)}, bf16[1,154,2,384]{3,1,2,0:T(8,128)(2,1)}, u32[]{:S(2)}) copy-start(bf16[1,154,2,384]{3,1,2,0:T(8,128)(2,1)} %copy.16) | copy-start | bytes 709636
  58.9 2.7 %collective-permute-start.7 = (bf16[3,2,48,1536]{3,2,1,0:T(8,128)(2,1)S(1)}, bf16[3,2,48,1536]{3,2,1,0:T(8,128)(2,1)S(1)}, u32[]{:S(2)}, u32[]{:S(2)}) collective-permute-start(bf16[3,2,48,1536]{3,2,1,0:T(8,128)(2,1)S(1)} %pad_maximum_fusion.1), channel_id=1, source_target_pairs={{0,32},{32,0},{1,33},{33,1},{2,34},{34,2},{3,35},{35,3},{4,36},{36... | collective-permute-start | bytes 2654216 | tf_op jit(solution)/shard_map/ppermute | solution.py:414
  61.6 2.2 %copy-start.3 = (bf16[3,2,48,1536]{3,2,1,0:T(8,128)(2,1)}, bf16[3,2,48,1536]{3,2,1,0:T(8,128)(2,1)S(1)}, u32[]{:S(2)}) copy-start(bf16[3,2,48,1536]{3,2,1,0:T(8,128)(2,1)S(1)} %collective-permute-done.7.far_ref) | copy-start | bytes 2654212
  67.4 0.7 copy-start.11
  68.1 7.0 %copy-start.9 = (bf16[96,1536]{1,0:T(8,128)(2,1)S(1)}, bf16[96,1536]{1,0:T(8,128)(2,1)}, u32[]{:S(2)}) copy-start(bf16[96,1536]{1,0:T(8,128)(2,1)} %own_ref.1) | copy-start | bytes 884740
  70.1 5.0 %copy-start.4 = (bf16[3,2,48,1536]{3,2,1,0:T(8,128)(2,1)S(1)}, bf16[3,2,48,1536]{3,2,1,0:T(8,128)(2,1)}, u32[]{:S(2)}) copy-start(bf16[3,2,48,1536]{3,2,1,0:T(8,128)(2,1)} %copy-done.3) | copy-start | bytes 2654212
  70.1 1.1 copy-start.12
  75.1 15.2 %copy-start.7 = (bf16[1,64,1536]{2,1,0:T(8,128)(2,1)S(1)}, bf16[1,64,1536]{2,1,0:T(8,128)(2,1)}, u32[]{:S(2)}) copy-start(bf16[1,64,1536]{2,1,0:T(8,128)(2,1)} %param.11) | copy-start | bytes 589828
  114.6 4.3 %copy-start.13 = (bf16[1536,64]{0,1:T(8,128)(2,1)S(1)}, bf16[1536,64]{0,1:T(8,128)(2,1)}, u32[]{:S(2)}) copy-start(bf16[1536,64]{0,1:T(8,128)(2,1)} %param.21) | copy-start | bytes 589828
  114.6 14.7 %copy-start.14 = (f32[1,32,128]{2,1,0:T(8,128)S(1)}, f32[1,32,128]{2,1,0:T(8,128)}, u32[]{:S(2)}) copy-start(f32[1,32,128]{2,1,0:T(8,128)} %param.12) | copy-start | bytes 49156
  114.6 13.6 %all-to-all-start.4 = ((bf16[4,64,1536]{2,1,0:T(8,128)(2,1)}), bf16[4,64,1536]{2,1,0:T(8,128)(2,1)S(1)}, u32[]{:S(2)}, u32[]{:S(2)}) async-start(bf16[4,64,1536]{2,1,0:T(8,128)(2,1)} %bitcast.49), calls=%async_computation.4 | async-start | bytes 1572864 | tf_op jit(solution)/shard_map/all_to_all | solution.py:426
Sparse Core Ops, SparseCore 0:
  10.6 67.0 all-gather.2

commit v7 on v6

--- a/solution.py
+++ b/solution.py
@@ -102,16 +102,15 @@
         text_ref = refs[3]
         outs = refs[4:]
     else:
-        acc_ref, stat_ref = refs[3:5]
-        outs = refs[5:]
+        state_ref = refs[3]
+        outs = refs[4:]
     rows = q_ref.shape[0]
     if own:
         live = lax.broadcasted_iota(jnp.int32, (rows, TXT), 1) < pos_ref[2]
     first = lax.broadcasted_iota(jnp.int32, (rows, 128), 1) < HEAD_DIM
     where = [0] if own else [lax.rem(pos_ref[1] + i, 4) for i in (1, 2, 3)]
     lane = lax.broadcasted_iota(jnp.int32, (rows, 128), 1)
-    tops = jnp.zeros((rows, 128), F32)
-    totals = jnp.zeros((rows, 128), F32)
+    stats = jnp.zeros((rows, 128), F32)
     for g in range(q_ref.shape[1] // 128):
         cols = slice(g * 128, g * 128 + 128)
         q = q_ref[:, cols]
@@ -139,7 +138,7 @@
                 peak = jnp.max(s, axis=1, keepdims=True)
                 top = peak if top is None else jnp.maximum(top, peak)
             if not own:
-                old = stat_ref[0, :, head : head + 1]
+                old = state_ref[:, 384 + head : 385 + head]
                 top = jnp.maximum(top, old)
             total = None
             acc = None
@@ -150,11 +149,11 @@
                 total = amount if total is None else total + amount
                 acc = part if acc is None else acc + part
             if own:
-                tops = jnp.where(lane == head, top, tops)
-                totals = jnp.where(lane == head, total, totals)
+                stats = jnp.where(lane == head, top, stats)
+                stats = jnp.where(lane == HEAD_DIM + head, total, stats)
             else:
                 factor = jnp.exp(old - top)
-                total = total + stat_ref[1, :, head : head + 1] * factor
+                total = total + state_ref[:, 448 + head : 449 + head] * factor
                 scales.append((factor, total))
             accs.append(acc)
         acc = jnp.where(first, accs[0], accs[1])
@@ -163,20 +162,16 @@
         else:
             factor = jnp.where(first, scales[0][0], scales[1][0])
             total = jnp.where(first, scales[0][1], scales[1][1])
-            outs[0][:, cols] = ((acc + acc_ref[:, cols] * factor) / total).astype(BF)
+            outs[0][:, cols] = ((acc + state_ref[:, cols] * factor) / total).astype(BF)
     if own:
-        outs[1][0] = tops
-        outs[1][1] = totals
+        outs[0][:, 384:] = stats
 
 
 def attention(pos, q, kv, text=None, state=None):
     own = text is not None
-    args = [q, kv] + ([text] if own else list(state))
+    args = [q, kv, text if own else state]
     if own:
-        out = [
-            jax.ShapeDtypeStruct(q.shape, F32),
-            jax.ShapeDtypeStruct((2, q.shape[0], 128), F32),
-        ]
+        out = jax.ShapeDtypeStruct((q.shape[0], 512), F32)
     else:
         out = jax.ShapeDtypeStruct(q.shape, BF)
     return pl.pallas_call(
@@ -219,7 +214,9 @@
     )(pos, a, own, *near, far)
 
 
-def pack_kernel(pos_ref, up_ref, down_ref, out_ref, held, load_sem, store_sem):
+def pack_kernel(
+    pos_ref, n0_ref, n1_ref, n2_ref, up_ref, down_ref, stack_ref, out_ref, held, load_sem, store_sem
+):
     core = pos_ref[0]
     zone = pos_ref[1]
     part = down_ref.shape[0]
@@ -235,6 +232,8 @@
             )
         for load in loads:
             load.start()
+        for i, ref in enumerate((n0_ref, n1_ref, n2_ref)):
+            stack_ref[i] = ref[...]
         for load, store in zip(loads, stores):
             load.wait()
             store.start()
@@ -252,25 +251,29 @@
             move([down_ref.at[:, pl.ds((2 * half + i) * part, part)] for i in range(2)])
 
 
-def pack_ffn(pos, w_up, w_down):
+def stack_and_pack(pos, near, w_up, w_down):
     part = w_down.shape[0]
     return pl.pallas_call(
         pack_kernel,
-        out_shape=jax.ShapeDtypeStruct((2 * part, part), BF),
-        in_specs=[
-            pl.BlockSpec(memory_space=pltpu.SMEM),
+        out_shape=[
+            jax.ShapeDtypeStruct((3, *near[0].shape), BF),
+            jax.ShapeDtypeStruct((2 * part, part), BF),
+        ],
+        in_specs=[pl.BlockSpec(memory_space=pltpu.SMEM)]
+        + [pl.BlockSpec(memory_space=pltpu.VMEM)] * 3
+        + [pl.BlockSpec(memory_space=pltpu.HBM)] * 2,
+        out_specs=[
+            pl.BlockSpec(memory_space=pltpu.VMEM),
             pl.BlockSpec(memory_space=pltpu.HBM),
-            pl.BlockSpec(memory_space=pltpu.HBM),
-        ],
-        out_specs=pl.BlockSpec(memory_space=pltpu.HBM),
+        ],
         scratch_shapes=[
             pltpu.VMEM((2 * part, part), BF),
             pltpu.SemaphoreType.DMA((2,)),
             pltpu.SemaphoreType.DMA((2,)),
         ],
         compiler_params=params(58),
-        name="pack_ffn",
-    )(pos, w_up, w_down)
+        name="stack_and_pack",
+    )(pos, *near, w_up, w_down)
 
 
 def second_norm_kernel(x_ref, part_ref, mod_ref, second_ref, out_ref):
@@ -400,12 +403,13 @@
     text = lax.dynamic_slice_in_dim(text_kv[0], lax.axis_index("tx") * 384, 384, 2)
     text = jnp.transpose(text, (1, 0, 2))
     place = jnp.stack([core, lax.axis_index("zp")]).astype(jnp.int32)
-    quarter = pack_ffn(place, w_up, w_down)
+    *near_kv, h1, half_qo, text = lax.optimization_barrier((*near_kv, h1, half_qo, text))
+    stacked, quarter = stack_and_pack(place, near_kv, w_up, w_down)
     ffn_full = lax.all_gather(quarter, ("core", "tx", "zp"), axis=0, tiled=False)
     ffn_full = ffn_full.reshape(2, 4, width, w_up.shape[1])
 
-    far_kv = lax.ppermute(jnp.stack(near_kv), "core", swap2)
-    h1, half_qo, text = lax.optimization_barrier((h1, half_qo, text))
+    stacked, half_qo = lax.optimization_barrier((stacked, half_qo))
+    far_kv = lax.ppermute(stacked, "core", swap2)
     near_qo = [to_lines(half_qo, step) for step in STRIDES]
     h1 = h1.reshape(4 * rows, width)
     own_kv = project(pos, h1, own_qkv, 1, 2, 4, near_kv, far_kv)

time: 137 us -> 146 us (1.066)
  blocking collectives: 29.6 us -> 37 us
  waiting for transfers between devices: 34 us -> 28.4 us
  local copies, waits for them, and re-layouts: 3.78 us -> 9.22 us
    all_to_all x1, blocking collectives: 13.3 us -> 23.6 us  [on_device(): lax.all_to_all(partial, 'tx', split_axis=0, concat_axis=0, tiled=True)]
    all_to_all x1, waiting for transfers between devices: 9.73 us -> 3.23 us  [on_device(): h1 = lax.all_to_all(h1, 'tx', split_axis=0, concat_axis=0, tiled=True)]
    all_to_all x1, waiting for transfers between devices: 2.04 us -> 8.05 us  [on_device(): lax.all_to_all(own_kv, 'ty', split_axis=0, concat_axis=0, tiled=True)]
    ppermute x6, waiting for transfers between devices: 10.8 us -> 6.2 us  [to_lines(): return lax.ppermute(value, 'ty', [(i, (i + step) % 4) for i in range(4)])]
    unnamed x31 -> x39, local copies, waits for them, and re-layouts: 2.05 us -> 4.97 us
    all_to_all x1, blocking collectives: 16.2 us -> 13.4 us  [on_device(): h2 = lax.all_to_all(h2, 'ty', split_axis=0, concat_axis=0, tiled=True)]
  transfers between devices with their start and end apart: 12 -> 12, of which waited for: 7 -> 6; matrix products, arithmetic and copies ran while one was open for 4% -> 4% of each run, Pallas kernels for 12% -> 10%
where the time goes in v7:
time: 146 us; the launch traced here: 145 us
  blocking collectives  37 us (25%)
  Pallas kernels  28.7 us (20%)
  waiting for transfers between devices  28.4 us (19%)
  starting transfers between devices  21.6 us (15%)
  between operations  15.6 us (11%)
  local copies, waits for them, and re-layouts  9.22 us (6%)
  other arithmetic  4.2 us (3%)
    all_to_all x1, blocking collectives, on_device(): lax.all_to_all(partial, 'tx', split_axis=0, concat_axis=0, tiled=True)  23.6 us
    all_to_all x1, blocking collectives, on_device(): h2 = lax.all_to_all(h2, 'ty', split_axis=0, concat_axis=0, tiled=True)  13.4 us
    ppermute x6, starting transfers between devices, to_lines(): return lax.ppermute(value, 'ty', [(i, (i + step) % 4) for i in range(4)])  8.93 us
    all_to_all x1, waiting for transfers between devices, on_device(): lax.all_to_all(partial, 'ty', split_axis=0, concat_axis=0, tiled=True)  8.46 us
    all_to_all x1, waiting for transfers between devices, on_device(): lax.all_to_all(own_kv, 'ty', split_axis=0, concat_axis=0, tiled=True)  8.05 us
    pallas_call x2, Pallas kernels, attention(): pl.pallas_call(functools.partial(attention_kernel, own), out_shape=out, i...  7.71 us
    pallas_call x1, Pallas kernels, feed_forward(): pl.pallas_call(ffn_kernel, grid=(4,), out_shape=jax.ShapeDtypeStruct((row...  7.64 us
    ppermute x6, waiting for transfers between devices, to_lines(): return lax.ppermute(value, 'ty', [(i, (i + step) % 4) for i in range(4)])  6.2 us
  transfers between devices with their start and end apart: 12, of which 6 were waited for; matrix products, arithmetic and copies ran while one was open for 4% of the time, Pallas kernels for 10%

profile of v7, /device:TPU:128, one launch (start us, length us, event | category | flops | bytes accessed | tf_op | source)
XLA Modules:
  0.0 144.8 jit_solution(16591104340816958455)
XLA Ops:
  7.2 1.0 copy-done.12
  9.0 1.1 first_norm.1
  10.1 1.7 %dynamic-slice_bitcast_fusion = bf16[2,48,1536]{2,1,0:T(8,128)(2,1)} fusion(bf16[1536,3,96]{0,2,1:T(8,128)(2,1)} %param.17, s32[]{:T(128)S(6)} %select_n.8), kind=kLoop, calls=%fused_computation.2 | loop fusion | bytes 589828 | tf_op jit(solution)/shard_map/dynamic_slice | solution.py:394
  11.8 1.6 %collective-permute-start = (bf16[2,48,1536]{2,1,0:T(8,128)(2,1)}, bf16[2,48,1536]{2,1,0:T(8,128)(2,1)S(1)}, u32[]{:S(2)}, u32[]{:S(2)}) collective-permute-start(bf16[2,48,1536]{2,1,0:T(8,128)(2,1)} %dynamic-slice_bitcast_fusion), channel_id=1, source_target_pairs={{0,2},{2,4},{4,6},{6,0},{1,3},{3,5},{5,7},{7,1},{8,10},{10,12},{12... | collective-permute-start | bytes 884744 | tf_op jit(solution)/shard_map/ppermute | solution.py:391
  13.4 1.7 %collective-permute-start.1 = (bf16[2,48,1536]{2,1,0:T(8,128)(2,1)}, bf16[2,48,1536]{2,1,0:T(8,128)(2,1)S(1)}, u32[]{:S(2)}, u32[]{:S(2)}) collective-permute-start(bf16[2,48,1536]{2,1,0:T(8,128)(2,1)} %dynamic-slice_bitcast_fusion), channel_id=1, source_target_pairs={{0,6},{2,0},{4,2},{6,4},{1,7},{3,1},{5,3},{7,5},{8,14},{10,8},{12,... | collective-permute-start | bytes 884744 | tf_op jit(solution)/shard_map/ppermute | solution.py:391
  15.1 2.0 %collective-permute-start.2 = (bf16[2,48,1536]{2,1,0:T(8,128)(2,1)}, bf16[2,48,1536]{2,1,0:T(8,128)(2,1)S(1)}, u32[]{:S(2)}, u32[]{:S(2)}) collective-permute-start(bf16[2,48,1536]{2,1,0:T(8,128)(2,1)} %dynamic-slice_bitcast_fusion), channel_id=1, source_target_pairs={{0,4},{2,6},{4,0},{6,2},{1,5},{3,7},{5,1},{7,3},{8,12},{10,14},{12... | collective-permute-start | bytes 884744 | tf_op jit(solution)/shard_map/ppermute | solution.py:391
  17.1 4.3 %all-to-all-start = ((bf16[4,64,1536]{2,1,0:T(8,128)(2,1)}), bf16[4,64,1536]{2,1,0:T(8,128)(2,1)S(1)}, u32[]{:S(2)}, u32[]{:S(2)}) async-start(bf16[4,64,1536]{2,1,0:T(8,128)(2,1)} %first_norm.1), calls=%async_computation | async-start | bytes 1572864 | tf_op jit(solution)/shard_map/all_to_all | solution.py:397
  22.9 0.9 dynamic-slice_bitcast_fusion.1
  24.5 1.6 %pad_maximum_fusion.1 = bf16[2,48,1536]{2,1,0:T(8,128)(2,1)} fusion(bf16[1,48,1536]{2,1,0:T(8,128)(2,1)S(1)} %dynamic-slice_bitcast_fusion.1, bf16[1,48,1536]{2,1,0:T(8,128)(2,1)} %dynamic-slice_bitcast_fusion.2), kind=kLoop, calls=%fused_computation.1 | loop fusion | flops 147456 | bytes 589824 | tf_op jit(solution)/shard_map/concatenate | solution.py:402
  26.1 3.4 %collective-permute-done.2.n2_ref = bf16[2,48,1536]{2,1,0:T(8,128)(2,1)S(1)} collective-permute-done((bf16[2,48,1536]{2,1,0:T(8,128)(2,1)}, bf16[2,48,1536]{2,1,0:T(8,128)(2,1)S(1)}, u32[]{:S(2)}, u32[]{:S(2)}) %collective-permute-start.2) | collective-permute-done | bytes 294944 | tf_op jit(solution)/shard_map/ppermute | solution.py:391
  29.6 3.2 %all-to-all-done = bf16[4,64,1536]{2,1,0:T(8,128)(2,1)S(1)} async-done(((bf16[4,64,1536]{2,1,0:T(8,128)(2,1)}), bf16[4,64,1536]{2,1,0:T(8,128)(2,1)S(1)}, u32[]{:S(2)}, u32[]{:S(2)}) %all-to-all-start) | async-done | bytes 786464 | tf_op jit(solution)/shard_map/all_to_all | solution.py:397
  32.8 3.9 %stack_and_pack.1 = (bf16[3,2,48,1536]{3,2,1,0:T(8,128)(2,1)}, bf16[768,384]{1,0:T(8,128)(2,1)}) custom-call(s32[2]{0:T(128)} %pad_add_fusion.1.pos_ref, bf16[2,48,1536]{2,1,0:T(8,128)(2,1)} %copy-done.5, bf16[2,48,1536]{2,1,0:T(8,128)(2,1)} %copy-done.7, bf16[2,48,1536]{2,1,0:T(8,128)(2,1)} %copy-done.9, bf16[1536,384]{1,0:T(8,128)(2,1)} %up_ref.1, ...), custom_call_target="tpu_custom_call" | custom-call | tf_op jit(solution)/shard_map/stack_and_pack/pallas_call | solution.py:256
  37.6 2.6 %collective-permute-start.4 = (bf16[2,48,1536]{2,1,0:T(8,128)(2,1)}, bf16[2,48,1536]{2,1,0:T(8,128)(2,1)}, u32[]{:S(2)}, u32[]{:S(2)}) collective-permute-start(bf16[2,48,1536]{2,1,0:T(8,128)(2,1)} %pad_maximum_fusion.1), channel_id=1, source_target_pairs={{0,6},{2,0},{4,2},{6,4},{1,7},{3,1},{5,3},{7,5},{8,14},{10,8},{12,... | collective-permute-start | bytes 884744 | tf_op jit(solution)/shard_map/ppermute | solution.py:391
  41.3 1.0 copy-done.6
  42.3 1.0 copy-done.8
  43.3 1.0 copy-done.10
  44.2 2.8 %project.2.refs_2_ = bf16[4,2,256,384]{3,2,1,0:T(8,128)(2,1)} custom-call(s32[3]{0:T(128)S(1)} %pad_add_fusion.pos_ref.refs_0_, bf16[256,1536]{1,0:T(8,128)(2,1)S(1)} %bitcast.28, bf16[3,96,1536]{2,1,0:T(8,128)(2,1)S(1)} %bitcast.30, bf16[2,48,1536]{2,1,0:T(8,128)(2,1)S(1)} %copy-done.6, bf16[2,48,1536]{2,1,0:T(8,128)(2,1)S(1)} %copy-done.8, ...), custom_call_target="tpu_custom_call" | custom-call | tf_op jit(solution)/shard_map/project/pallas_call | solution.py:87
  47.0 4.4 %all-to-all-start.1 = ((bf16[4,2,256,384]{3,2,1,0:T(8,128)(2,1)}), bf16[4,2,256,384]{3,2,1,0:T(8,128)(2,1)S(1)}, u32[]{:S(2)}, u32[]{:S(2)}) async-start(bf16[4,2,256,384]{3,2,1,0:T(8,128)(2,1)} %project.2.refs_2_), calls=%async_computation.1 | async-start | bytes 3145728 | tf_op jit(solution)/shard_map/all_to_all | solution.py:416
  51.4 2.7 %collective-permute-done.3.n0_ref = bf16[2,48,1536]{2,1,0:T(8,128)(2,1)} collective-permute-done((bf16[2,48,1536]{2,1,0:T(8,128)(2,1)}, bf16[2,48,1536]{2,1,0:T(8,128)(2,1)}, u32[]{:S(2)}, u32[]{:S(2)}) %collective-permute-start.3) | collective-permute-done | bytes 294944 | tf_op jit(solution)/shard_map/ppermute | solution.py:391
  54.2 1.2 pad_maximum_fusion
  55.7 2.4 %collective-permute-done.7.far_ref = bf16[3,2,48,1536]{3,2,1,0:T(8,128)(2,1)S(1)} collective-permute-done((bf16[3,2,48,1536]{3,2,1,0:T(8,128)(2,1)S(1)}, bf16[3,2,48,1536]{3,2,1,0:T(8,128)(2,1)S(1)}, u32[]{:S(2)}, u32[]{:S(2)}) %collective-permute-start.7) | collective-permute-done | bytes 884768 | tf_op jit(solution)/shard_map/ppermute | solution.py:418
  58.2 2.1 %project.3 = bf16[1,1,256,384]{3,2,1,0:T(8,128)(2,1)S(1)} custom-call(s32[3]{0:T(128)S(1)} %pad_add_fusion.pos_ref.refs_0_, bf16[256,1536]{1,0:T(8,128)(2,1)S(1)} %bitcast.29, bf16[3,96,1536]{2,1,0:T(8,128)(2,1)S(1)} %bitcast.31, bf16[2,48,1536]{2,1,0:T(8,128)(2,1)} %collective-permute-done.3.n0_ref, bf16[2,48,1536]{2,1,0:T(8,128)(2,1)} %collective-permute-done.4.n1_ref, ...), custom_call_target="tpu_custom_call" | custom-call | tf_op jit(solution)/shard_map/project/pallas_call | solution.py:87
  60.3 3.5 %attention.2.refs_3_ = f32[256,512]{1,0:T(8,128)S(1)} custom-call(s32[3]{0:T(128)S(1)} %pad_add_fusion.pos_ref.refs_0_, bf16[256,384]{1,0:T(8,128)(2,1)S(1)} %bitcast.33, bf16[4,2,256,384]{3,2,1,0:T(8,128)(2,1)} %project.2.refs_2_, bf16[2,154,384]{2,1,0:T(8,128)(2,1)S(1)} %bitcast.35), custom_call_target="tpu_custom_call" | custom-call | tf_op jit(solution)/shard_map/attention/pallas_call | solution.py:177
  63.9 8.1 %all-to-all-done.1.refs_2_ = bf16[4,2,256,384]{3,2,1,0:T(8,128)(2,1)S(1)} async-done(((bf16[4,2,256,384]{3,2,1,0:T(8,128)(2,1)}), bf16[4,2,256,384]{3,2,1,0:T(8,128)(2,1)S(1)}, u32[]{:S(2)}, u32[]{:S(2)}) %all-to-all-start.1) | async-done | bytes 1572896 | tf_op jit(solution)/shard_map/all_to_all | solution.py:416
  71.9 4.2 %attention.3.a_ref = bf16[256,384]{1,0:T(8,128)(2,1)S(1)} custom-call(s32[3]{0:T(128)S(1)} %pad_add_fusion.pos_ref.refs_0_, bf16[256,384]{1,0:T(8,128)(2,1)S(1)} %bitcast.34, bf16[4,2,256,384]{3,2,1,0:T(8,128)(2,1)S(1)} %all-to-all-done.1.refs_2_, f32[256,512]{1,0:T(8,128)S(1)} %attention.2.refs_3_), custom_call_target="tpu_custom_call" | custom-call | tf_op jit(solution)/shard_map/attention/pallas_call | solution.py:177
  76.2 1.9 %out_projection.1 = bf16[256,1536]{1,0:T(8,128)(2,1)S(1)} custom-call(s32[3]{0:T(128)S(1)} %pad_add_fusion.pos_ref.refs_0_, bf16[256,384]{1,0:T(8,128)(2,1)S(1)} %attention.3.a_ref, bf16[96,1536]{1,0:T(8,128)(2,1)S(1)} %copy-done.14, bf16[2,48,1536]{2,1,0:T(8,128)(2,1)} %collective-permute-done.3.n0_ref, bf16[2,48,1536]{2,1,0:T(8,128)(2,1)} %collective-permute-done.4.n1_ref, ...), custom_call_target="tpu_custom_call" | custom-call | tf_op jit(solution)/shard_map/out_projection/pallas_call | solution.py:206
  78.0 23.6 %all_to_all.25.part_ref = bf16[4,64,1536]{2,1,0:T(8,128)(2,1)S(1)} all-to-all(bf16[4,64,1536]{2,1,0:T(8,128)(2,1)S(1)} %bitcast.32), channel_id=1, replica_groups=mesh['zl'=2,'zp'=2,'core'=2,'tx'=4,'ty'=4,'blk'=2] {'tx'}, dimensions={0} | all-to-all | bytes 1572864 | tf_op jit(solution)/shard_map/all_to_all | solution.py:426
  102.1 13.4 %all_to_all.26 = bf16[4,64,1536]{2,1,0:T(8,128)(2,1)} all-to-all(bf16[4,64,1536]{2,1,0:T(8,128)(2,1)S(1)} %get-tuple-element.38), channel_id=1, replica_groups=mesh['zl'=2,'zp'=2,'core'=2,'tx'=4,'ty'=4,'blk'=2] {'ty'}, dimensions={0} | all-to-all | bytes 1572864 | tf_op jit(solution)/shard_map/all_to_all | solution.py:428
  115.4 7.6 %feed_forward.1 = bf16[256,1536]{1,0:T(8,128)(2,1)} custom-call(bf16[256,1536]{1,0:T(8,128)(2,1)} %bitcast.44, bf16[2,4,1536,384]{3,2,1,0:T(8,128)(2,1)} %bitcast.41, bf16[2,4,1536,384]{3,2,1,0:T(8,128)(2,1)} %bitcast.42), custom_call_target="tpu_custom_call" | custom-call | tf_op jit(solution)/shard_map/feed_forward/pallas_call | solution.py:332
  123.1 3.6 %all-to-all-start.4 = ((bf16[4,64,1536]{2,1,0:T(8,128)(2,1)}), bf16[4,64,1536]{2,1,0:T(8,128)(2,1)S(1)}, u32[]{:S(2)}, u32[]{:S(2)}) async-start(bf16[4,64,1536]{2,1,0:T(8,128)(2,1)} %bitcast.43), calls=%async_computation.4 | async-start | bytes 1572864 | tf_op jit(solution)/shard_map/all_to_all | solution.py:430
  127.7 8.5 %all-to-all-done.4.part_ref = bf16[4,64,1536]{2,1,0:T(8,128)(2,1)S(1)} async-done(((bf16[4,64,1536]{2,1,0:T(8,128)(2,1)}), bf16[4,64,1536]{2,1,0:T(8,128)(2,1)S(1)}, u32[]{:S(2)}, u32[]{:S(2)}) %all-to-all-start.4) | async-done | bytes 786464 | tf_op jit(solution)/shard_map/all_to_all | solution.py:430
  136.2 1.1 last_stage.1
  (56 shorter events, 6.0 us)
Async XLA Ops:
  7.2 14.9 %copy-start = (bf16[1,154,2,1536]{3,2,1,0:T(2,128)(2,1)S(1)}, bf16[1,154,2,1536]{3,2,1,0:T(2,128)(2,1)}, u32[]{:S(2)}) copy-start(bf16[1,154,2,1536]{3,2,1,0:T(2,128)(2,1)} %param.14) | copy-start | bytes 2838532
  7.2 1.0 copy-start.12
  8.2 0.8 copy-start.15
  9.0 12.4 %copy-start.1 = (bf16[1536,3,96]{0,2,1:T(8,128)(2,1)S(1)}, bf16[1536,3,96]{0,2,1:T(8,128)(2,1)}, u32[]{:S(2)}) copy-start(bf16[1536,3,96]{0,2,1:T(8,128)(2,1)} %param.17) | copy-start | bytes 2654212
  11.8 14.3 %collective-permute-start = (bf16[2,48,1536]{2,1,0:T(8,128)(2,1)}, bf16[2,48,1536]{2,1,0:T(8,128)(2,1)S(1)}, u32[]{:S(2)}, u32[]{:S(2)}) collective-permute-start(bf16[2,48,1536]{2,1,0:T(8,128)(2,1)} %dynamic-slice_bitcast_fusion), channel_id=1, source_target_pairs={{0,2},{2,4},{4,6},{6,0},{1,3},{3,5},{5,7},{7,1},{8,10},{10,12},{12... | collective-permute-start | bytes 884744 | tf_op jit(solution)/shard_map/ppermute | solution.py:391
  13.4 12.7 %collective-permute-start.1 = (bf16[2,48,1536]{2,1,0:T(8,128)(2,1)}, bf16[2,48,1536]{2,1,0:T(8,128)(2,1)S(1)}, u32[]{:S(2)}, u32[]{:S(2)}) collective-permute-start(bf16[2,48,1536]{2,1,0:T(8,128)(2,1)} %dynamic-slice_bitcast_fusion), channel_id=1, source_target_pairs={{0,6},{2,0},{4,2},{6,4},{1,7},{3,1},{5,3},{7,5},{8,14},{10,8},{12,... | collective-permute-start | bytes 884744 | tf_op jit(solution)/shard_map/ppermute | solution.py:391
  15.1 14.5 %collective-permute-start.2 = (bf16[2,48,1536]{2,1,0:T(8,128)(2,1)}, bf16[2,48,1536]{2,1,0:T(8,128)(2,1)S(1)}, u32[]{:S(2)}, u32[]{:S(2)}) collective-permute-start(bf16[2,48,1536]{2,1,0:T(8,128)(2,1)} %dynamic-slice_bitcast_fusion), channel_id=1, source_target_pairs={{0,4},{2,6},{4,0},{6,2},{1,5},{3,7},{5,1},{7,3},{8,12},{10,14},{12... | collective-permute-start | bytes 884744 | tf_op jit(solution)/shard_map/ppermute | solution.py:391
  17.1 15.7 %all-to-all-start = ((bf16[4,64,1536]{2,1,0:T(8,128)(2,1)}), bf16[4,64,1536]{2,1,0:T(8,128)(2,1)S(1)}, u32[]{:S(2)}, u32[]{:S(2)}) async-start(bf16[4,64,1536]{2,1,0:T(8,128)(2,1)} %first_norm.1), calls=%async_computation | async-start | bytes 1572864 | tf_op jit(solution)/shard_map/all_to_all | solution.py:397
  21.4 94.1 %all-gather.3.cloned.1.call-start = ((), (), s32[]{:S(2)}) async-start(), calls=%async_computation.5 | async-start | bytes 10027008 | tf_op jit(solution)/shard_map/all_gather | solution.py:408
  26.1 6.7 %copy-start.5 = (bf16[2,48,1536]{2,1,0:T(8,128)(2,1)}, bf16[2,48,1536]{2,1,0:T(8,128)(2,1)S(1)}, u32[]{:S(2)}) copy-start(bf16[2,48,1536]{2,1,0:T(8,128)(2,1)S(1)} %collective-permute-done.n0_ref) | copy-start | bytes 884740
  26.1 6.7 %copy-start.7 = (bf16[2,48,1536]{2,1,0:T(8,128)(2,1)}, bf16[2,48,1536]{2,1,0:T(8,128)(2,1)S(1)}, u32[]{:S(2)}) copy-start(bf16[2,48,1536]{2,1,0:T(8,128)(2,1)S(1)} %collective-permute-done.1.n1_ref) | copy-start | bytes 884740
  29.6 3.2 %copy-start.9 = (bf16[2,48,1536]{2,1,0:T(8,128)(2,1)}, bf16[2,48,1536]{2,1,0:T(8,128)(2,1)S(1)}, u32[]{:S(2)}) copy-start(bf16[2,48,1536]{2,1,0:T(8,128)(2,1)S(1)} %collective-permute-done.2.n2_ref) | copy-start | bytes 884740
  36.8 4.5 %collective-permute-start.6 = (bf16[3,2,48,1536]{3,2,1,0:T(8,128)(2,1)}, bf16[3,2,48,1536]{3,2,1,0:T(8,128)(2,1)S(1)}, u32[]{:S(2)}, u32[]{:S(2)}) collective-permute-start(bf16[3,2,48,1536]{3,2,1,0:T(8,128)(2,1)} %get-tuple-element.31), channel_id=1, source_target_pairs={{0,32},{32,0},{1,33},{33,1},{2,34},{34,2},{3,35},{35,3},{4,36},{36... | collective-permute-start | bytes 2654216 | tf_op jit(solution)/shard_map/ppermute | solution.py:412
  36.9 17.3 %collective-permute-start.3 = (bf16[2,48,1536]{2,1,0:T(8,128)(2,1)}, bf16[2,48,1536]{2,1,0:T(8,128)(2,1)}, u32[]{:S(2)}, u32[]{:S(2)}) collective-permute-start(bf16[2,48,1536]{2,1,0:T(8,128)(2,1)} %pad_maximum_fusion.1), channel_id=1, source_target_pairs={{0,2},{2,4},{4,6},{6,0},{1,3},{3,5},{5,7},{7,1},{8,10},{10,12},{12... | collective-permute-start | bytes 884744 | tf_op jit(solution)/shard_map/ppermute | solution.py:391
  37.6 16.6 %collective-permute-start.4 = (bf16[2,48,1536]{2,1,0:T(8,128)(2,1)}, bf16[2,48,1536]{2,1,0:T(8,128)(2,1)}, u32[]{:S(2)}, u32[]{:S(2)}) collective-permute-start(bf16[2,48,1536]{2,1,0:T(8,128)(2,1)} %pad_maximum_fusion.1), channel_id=1, source_target_pairs={{0,6},{2,0},{4,2},{6,4},{1,7},{3,1},{5,3},{7,5},{8,14},{10,8},{12,... | collective-permute-start | bytes 884744 | tf_op jit(solution)/shard_map/ppermute | solution.py:391
  40.2 14.0 %collective-permute-start.5 = (bf16[2,48,1536]{2,1,0:T(8,128)(2,1)}, bf16[2,48,1536]{2,1,0:T(8,128)(2,1)}, u32[]{:S(2)}, u32[]{:S(2)}) collective-permute-start(bf16[2,48,1536]{2,1,0:T(8,128)(2,1)} %pad_maximum_fusion.1), channel_id=1, source_target_pairs={{0,4},{2,6},{4,0},{6,2},{1,5},{3,7},{5,1},{7,3},{8,12},{10,14},{12... | collective-permute-start | bytes 884744 | tf_op jit(solution)/shard_map/ppermute | solution.py:391
  41.3 1.0 copy-start.6
  42.3 1.0 copy-start.8
  43.3 1.0 copy-start.10
  47.0 24.9 %all-to-all-start.1 = ((bf16[4,2,256,384]{3,2,1,0:T(8,128)(2,1)}), bf16[4,2,256,384]{3,2,1,0:T(8,128)(2,1)S(1)}, u32[]{:S(2)}, u32[]{:S(2)}) async-start(bf16[4,2,256,384]{3,2,1,0:T(8,128)(2,1)} %project.2.refs_2_), calls=%async_computation.1 | async-start | bytes 3145728 | tf_op jit(solution)/shard_map/all_to_all | solution.py:416
  51.4 6.7 %copy-start.2 = (bf16[1536,3,96]{0,2,1:T(8,128)(2,1)S(1)}, bf16[1536,3,96]{0,2,1:T(8,128)(2,1)}, u32[]{:S(2)}) copy-start(bf16[1536,3,96]{0,2,1:T(8,128)(2,1)} %param.17) | copy-start | bytes 2654212
  55.5 4.9 %copy-start.11 = (bf16[1,154,2,384]{3,1,2,0:T(8,128)(2,1)S(1)}, bf16[1,154,2,384]{3,1,2,0:T(8,128)(2,1)}, u32[]{:S(2)}) copy-start(bf16[1,154,2,384]{3,1,2,0:T(8,128)(2,1)} %copy.16) | copy-start | bytes 709636
  55.5 2.7 %collective-permute-start.7 = (bf16[3,2,48,1536]{3,2,1,0:T(8,128)(2,1)S(1)}, bf16[3,2,48,1536]{3,2,1,0:T(8,128)(2,1)S(1)}, u32[]{:S(2)}, u32[]{:S(2)}) collective-permute-start(bf16[3,2,48,1536]{3,2,1,0:T(8,128)(2,1)S(1)} %pad_maximum_fusion), channel_id=1, source_target_pairs={{0,32},{32,0},{1,33},{33,1},{2,34},{34,2},{3,35},{35,3},{4,36},{36... | collective-permute-start | bytes 2654216 | tf_op jit(solution)/shard_map/ppermute | solution.py:418
  58.2 2.2 %copy-start.3 = (bf16[3,2,48,1536]{3,2,1,0:T(8,128)(2,1)}, bf16[3,2,48,1536]{3,2,1,0:T(8,128)(2,1)S(1)}, u32[]{:S(2)}) copy-start(bf16[3,2,48,1536]{3,2,1,0:T(8,128)(2,1)S(1)} %collective-permute-done.7.far_ref) | copy-start | bytes 2654212
  71.9 4.2 %copy-start.4 = (bf16[3,2,48,1536]{3,2,1,0:T(8,128)(2,1)S(1)}, bf16[3,2,48,1536]{3,2,1,0:T(8,128)(2,1)}, u32[]{:S(2)}) copy-start(bf16[3,2,48,1536]{3,2,1,0:T(8,128)(2,1)} %copy-done.3) | copy-start | bytes 2654212
  71.9 4.2 %copy-start.14 = (bf16[96,1536]{1,0:T(8,128)(2,1)S(1)}, bf16[96,1536]{1,0:T(8,128)(2,1)}, u32[]{:S(2)}) copy-start(bf16[96,1536]{1,0:T(8,128)(2,1)} %own_ref.1) | copy-start | bytes 884740
  76.1 25.5 %copy-start.13 = (bf16[1,64,1536]{2,1,0:T(8,128)(2,1)S(1)}, bf16[1,64,1536]{2,1,0:T(8,128)(2,1)}, u32[]{:S(2)}) copy-start(bf16[1,64,1536]{2,1,0:T(8,128)(2,1)} %param.11) | copy-start | bytes 589828
  76.2 25.5 %copy-start.16 = (f32[1,8,1536]{2,1,0:T(8,128)S(1)}, f32[1,8,1536]{2,1,0:T(8,128)}, u32[]{:S(2)}) copy-start(f32[1,8,1536]{2,1,0:T(8,128)} %param.13) | copy-start | bytes 147460
  123.1 4.3 %copy-start.17 = (bf16[1536,64]{0,1:T(8,128)(2,1)S(1)}, bf16[1536,64]{0,1:T(8,128)(2,1)}, u32[]{:S(2)}) copy-start(bf16[1536,64]{0,1:T(8,128)(2,1)} %param.21) | copy-start | bytes 589828
  123.1 14.2 %copy-start.18 = (f32[1,32,128]{2,1,0:T(8,128)S(1)}, f32[1,32,128]{2,1,0:T(8,128)}, u32[]{:S(2)}) copy-start(f32[1,32,128]{2,1,0:T(8,128)} %param.12) | copy-start | bytes 49156
  123.1 13.1 %all-to-all-start.4 = ((bf16[4,64,1536]{2,1,0:T(8,128)(2,1)}), bf16[4,64,1536]{2,1,0:T(8,128)(2,1)S(1)}, u32[]{:S(2)}, u32[]{:S(2)}) async-start(bf16[4,64,1536]{2,1,0:T(8,128)(2,1)} %bitcast.43), calls=%async_computation.4 | async-start | bytes 1572864 | tf_op jit(solution)/shard_map/all_to_all | solution.py:430
Sparse Core Ops, SparseCore 0:
  36.9 65.9 all-gather.2

commit v8 on v7

--- a/solution.py
+++ b/solution.py
@@ -33,20 +33,89 @@
     return 3.0 * frac / (1.0 + 2.0 * frac)
 
 
-def norm_kernel(copies, x_ref, mod_ref, out_ref):
-    h = layer_norm(x_ref[...].astype(F32), mod_ref[0:1, :], mod_ref[1:2, :]).astype(BF)
-    for i in range(copies):
-        out_ref[i] = h
-
-
-def first_norm(tokens, mods, copies):
+def first_kernel(
+    pos_ref,
+    x_ref,
+    mod_ref,
+    up_ref,
+    down_ref,
+    qkv_ref,
+    wout_ref,
+    h_ref,
+    kv_ref,
+    qo_ref,
+    pack_ref,
+    held,
+    load_sem,
+    store_sem,
+    half_sem,
+):
+    core = pos_ref[0]
+    zone = pos_ref[1]
+    part = down_ref.shape[0]
+
+    def move(core_here, sources):
+        mine = pl.ds(core_here * 48, 48)
+        halves = [
+            pltpu.make_async_copy(qkv_ref.at[pl.ds(1, 2), mine, :], kv_ref, half_sem.at[0]),
+            pltpu.make_async_copy(qkv_ref.at[0, mine, :], qo_ref.at[0], half_sem.at[1]),
+            pltpu.make_async_copy(wout_ref.at[mine, :], qo_ref.at[1], half_sem.at[2]),
+        ]
+        loads = []
+        stores = []
+        for i, source in enumerate(sources):
+            rows = pl.ds(i * part, part)
+            loads.append(pltpu.make_async_copy(source, held.at[rows, :], load_sem.at[i]))
+            stores.append(
+                pltpu.make_async_copy(held.at[rows, :], pack_ref.at[rows, :], store_sem.at[i])
+            )
+        for copy in loads + halves:
+            copy.start()
+        h = layer_norm(x_ref[...].astype(F32), mod_ref[0:1, :], mod_ref[1:2, :]).astype(BF)
+        for i in range(h_ref.shape[0]):
+            h_ref[i] = h
+        for load, store in zip(loads, stores):
+            load.wait()
+            store.start()
+        for copy in halves + stores:
+            copy.wait()
+
+    for half in range(2):
+
+        @pl.when(jnp.logical_and(core == 0, zone == half))
+        def _():
+            move(0, [up_ref.at[pl.ds((2 * half + i) * part, part), :] for i in range(2)])
+
+        @pl.when(jnp.logical_and(core == 1, zone == half))
+        def _():
+            move(1, [down_ref.at[:, pl.ds((2 * half + i) * part, part)] for i in range(2)])
+
+
+def first_stage(pos, tokens, mods, w_up, w_down, own_qkv, w_out, copies):
     rows, width = tokens.shape
-    return pl.pallas_call(
-        functools.partial(norm_kernel, copies),
-        out_shape=jax.ShapeDtypeStruct((copies, rows, width), BF),
-        compiler_params=params(6),
-        name="first_norm",
-    )(tokens, mods)
+    part = w_down.shape[0]
+    return pl.pallas_call(
+        first_kernel,
+        out_shape=[
+            jax.ShapeDtypeStruct((copies, rows, width), BF),
+            jax.ShapeDtypeStruct((2, 48, width), BF),
+            jax.ShapeDtypeStruct((2, 48, width), BF),
+            jax.ShapeDtypeStruct((2 * part, part), BF),
+        ],
+        in_specs=[pl.BlockSpec(memory_space=pltpu.SMEM)]
+        + [pl.BlockSpec(memory_space=pltpu.VMEM)] * 2
+        + [pl.BlockSpec(memory_space=pltpu.HBM)] * 4,
+        out_specs=[pl.BlockSpec(memory_space=pltpu.VMEM)] * 3
+        + [pl.BlockSpec(memory_space=pltpu.HBM)],
+        scratch_shapes=[
+            pltpu.VMEM((2 * part, part), BF),
+            pltpu.SemaphoreType.DMA((2,)),
+            pltpu.SemaphoreType.DMA((2,)),
+            pltpu.SemaphoreType.DMA((3,)),
+        ],
+        compiler_params=params(58),
+        name="first_stage",
+    )(pos, tokens, mods, w_up, w_down, own_qkv, w_out)
 
 
 def assemble(pos_ref, own_ref, near_refs, far_ref, store):
@@ -214,68 +283,6 @@
     )(pos, a, own, *near, far)
 
 
-def pack_kernel(
-    pos_ref, n0_ref, n1_ref, n2_ref, up_ref, down_ref, stack_ref, out_ref, held, load_sem, store_sem
-):
-    core = pos_ref[0]
-    zone = pos_ref[1]
-    part = down_ref.shape[0]
-
-    def move(sources):
-        loads = []
-        stores = []
-        for i, source in enumerate(sources):
-            rows = pl.ds(i * part, part)
-            loads.append(pltpu.make_async_copy(source, held.at[rows, :], load_sem.at[i]))
-            stores.append(
-                pltpu.make_async_copy(held.at[rows, :], out_ref.at[rows, :], store_sem.at[i])
-            )
-        for load in loads:
-            load.start()
-        for i, ref in enumerate((n0_ref, n1_ref, n2_ref)):
-            stack_ref[i] = ref[...]
-        for load, store in zip(loads, stores):
-            load.wait()
-            store.start()
-        for store in stores:
-            store.wait()
-
-    for half in range(2):
-
-        @pl.when(jnp.logical_and(core == 0, zone == half))
-        def _():
-            move([up_ref.at[pl.ds((2 * half + i) * part, part), :] for i in range(2)])
-
-        @pl.when(jnp.logical_and(core == 1, zone == half))
-        def _():
-            move([down_ref.at[:, pl.ds((2 * half + i) * part, part)] for i in range(2)])
-
-
-def stack_and_pack(pos, near, w_up, w_down):
-    part = w_down.shape[0]
-    return pl.pallas_call(
-        pack_kernel,
-        out_shape=[
-            jax.ShapeDtypeStruct((3, *near[0].shape), BF),
-            jax.ShapeDtypeStruct((2 * part, part), BF),
-        ],
-        in_specs=[pl.BlockSpec(memory_space=pltpu.SMEM)]
-        + [pl.BlockSpec(memory_space=pltpu.VMEM)] * 3
-        + [pl.BlockSpec(memory_space=pltpu.HBM)] * 2,
-        out_specs=[
-            pl.BlockSpec(memory_space=pltpu.VMEM),
-            pl.BlockSpec(memory_space=pltpu.HBM),
-        ],
-        scratch_shapes=[
-            pltpu.VMEM((2 * part, part), BF),
-            pltpu.SemaphoreType.DMA((2,)),
-            pltpu.SemaphoreType.DMA((2,)),
-        ],
-        compiler_params=params(58),
-        name="stack_and_pack",
-    )(pos, *near, w_up, w_down)
-
-
 def second_norm_kernel(x_ref, part_ref, mod_ref, second_ref, out_ref):
     proj = part_ref[0].astype(F32)
     for i in range(1, part_ref.shape[0]):
@@ -391,30 +398,24 @@
         return lax.ppermute(value, "ty", [(i, (i + step) % 4) for i in range(4)])
 
     own_qkv = jnp.transpose(w_qkv, (1, 2, 0))
-    half_kv = lax.dynamic_slice(own_qkv, (1, core * 48, 0), (2, 48, width))
-    h1 = first_norm(tokens, mods, 4)
-    h1, half_kv = lax.optimization_barrier((h1, half_kv))
+    place = jnp.stack([core, lax.axis_index("zp")]).astype(jnp.int32)
+    h1, half_kv, half_qo, quarter = first_stage(
+        place, tokens, mods, w_up, w_down, own_qkv, w_out, 4
+    )
+    ffn_full = lax.all_gather(quarter, ("core", "tx", "zp"), axis=0, tiled=False)
+    ffn_full = ffn_full.reshape(2, 4, width, w_up.shape[1])
     h1 = lax.all_to_all(h1, "tx", split_axis=0, concat_axis=0, tiled=True)
     near_kv = [to_lines(half_kv, step) for step in STRIDES]
-
-    half_q = lax.dynamic_slice(own_qkv, (0, core * 48, 0), (1, 48, width))
-    half_out = lax.dynamic_slice(w_out, (core * 48, 0), (48, width))
-    half_qo = jnp.concatenate([half_q, half_out[None]])
-    text = lax.dynamic_slice_in_dim(text_kv[0], lax.axis_index("tx") * 384, 384, 2)
-    text = jnp.transpose(text, (1, 0, 2))
-    place = jnp.stack([core, lax.axis_index("zp")]).astype(jnp.int32)
-    *near_kv, h1, half_qo, text = lax.optimization_barrier((*near_kv, h1, half_qo, text))
-    stacked, quarter = stack_and_pack(place, near_kv, w_up, w_down)
-    ffn_full = lax.all_gather(quarter, ("core", "tx", "zp"), axis=0, tiled=False)
-    ffn_full = ffn_full.reshape(2, 4, width, w_up.shape[1])
-
-    stacked, half_qo = lax.optimization_barrier((stacked, half_qo))
+    *near_kv, h1 = lax.optimization_barrier((*near_kv, h1))
+    stacked, half_qo = lax.optimization_barrier((jnp.stack(near_kv), half_qo))
     far_kv = lax.ppermute(stacked, "core", swap2)
     near_qo = [to_lines(half_qo, step) for step in STRIDES]
     h1 = h1.reshape(4 * rows, width)
     own_kv = project(pos, h1, own_qkv, 1, 2, 4, near_kv, far_kv)
     all_kv = lax.all_to_all(own_kv, "ty", split_axis=0, concat_axis=0, tiled=True)
-    *near_qo, own_kv = lax.optimization_barrier((*near_qo, own_kv))
+    *near_qo, own_kv, text_kv = lax.optimization_barrier((*near_qo, own_kv, text_kv))
+    text = lax.dynamic_slice_in_dim(text_kv[0], lax.axis_index("tx") * 384, 384, 2)
+    text = jnp.transpose(text, (1, 0, 2))
     far_qo = lax.ppermute(jnp.stack(near_qo), "core", swap2)
     query = project(pos, h1, own_qkv, 0, 1, 1, near_qo, far_qo)[0, 0]
 

time: 146 us -> 137 us (0.938)
  blocking collectives: 37 us -> 28.4 us
    all_to_all x1, blocking collectives: 23.6 us -> 15.3 us  [on_device(): lax.all_to_all(partial, 'tx', split_axis=0, concat_axis=0, tiled=True)]
    ppermute x6, waiting for transfers between devices: 6.2 us -> 14.3 us  [to_lines(): return lax.ppermute(value, 'ty', [(i, (i + step) % 4) for i in range(4)])]
    unnamed x39 -> x49, local copies, waits for them, and re-layouts: 4.97 us -> 9.83 us
    all_to_all x1, waiting for transfers between devices: 8.05 us -> 4.51 us  [on_device(): lax.all_to_all(own_kv, 'ty', split_axis=0, concat_axis=0, tiled=True)]
    all_to_all x1, waiting for transfers between devices: 3.23 us -> 0.01 us  [on_device(): h1 = lax.all_to_all(h1, 'tx', split_axis=0, concat_axis=0, tiled=True)]
    dynamic_slice x2 -> x0, local copies, waits for them, and re-layouts: 2.37 us -> none  [the longest x1 1.7 us: on_device(): half_kv = lax.dynamic_slice(own_qkv, (1, core * 48, 0), (2, 48, width))]
    concatenate x1 -> x0, other arithmetic: 1.65 us -> none  [on_device(): half_qo = jnp.concatenate([half_q, half_out[None]])]
    pallas_call x2 -> x1, Pallas kernels: 5.08 us -> 3.99 us  [first_stage(): pl.pallas_call(first_kernel, out_shape=[jax.ShapeDtypeStruct((copies, row...]
  transfers between devices with their start and end apart: 12 -> 12, of which waited for: 6 -> 8; matrix products, arithmetic and copies ran while one was open for 4% -> 2% of each run, Pallas kernels for 10% -> 11%
where the time goes in v8:
time: 137 us; the launch traced here: 136 us
  waiting for transfers between devices  29.8 us (22%)
  blocking collectives  28.4 us (21%)
  Pallas kernels  27.6 us (20%)
  starting transfers between devices  21.4 us (16%)
  between operations  15.6 us (11%)
  local copies, waits for them, and re-layouts  10.1 us (7%)
  other arithmetic  3.36 us (2%)
    all_to_all x1, blocking collectives, on_device(): lax.all_to_all(partial, 'tx', split_axis=0, concat_axis=0, tiled=True)  15.3 us
    ppermute x6, waiting for transfers between devices, to_lines(): return lax.ppermute(value, 'ty', [(i, (i + step) % 4) for i in range(4)])  14.3 us
    all_to_all x1, blocking collectives, on_device(): h2 = lax.all_to_all(h2, 'ty', split_axis=0, concat_axis=0, tiled=True)  13.1 us
    unnamed x49, local copies, waits for them, and re-layouts  9.83 us
    ppermute x6, starting transfers between devices, to_lines(): return lax.ppermute(value, 'ty', [(i, (i + step) % 4) for i in range(4)])  8.63 us
    pallas_call x2, Pallas kernels, attention(): pl.pallas_call(functools.partial(attention_kernel, own), out_shape=out, i...  8.63 us
    all_to_all x1, waiting for transfers between devices, on_device(): lax.all_to_all(partial, 'ty', split_axis=0, concat_axis=0, tiled=True)  8.46 us
    pallas_call x1, Pallas kernels, feed_forward(): pl.pallas_call(ffn_kernel, grid=(4,), out_shape=jax.ShapeDtypeStruct((row...  7.63 us
  transfers between devices with their start and end apart: 12, of which 8 were waited for; matrix products, arithmetic and copies ran while one was open for 2% of the time, Pallas kernels for 11%

profile of v8, /device:TPU:128, one launch (start us, length us, event | category | flops | bytes accessed | tf_op | source)
XLA Modules:
  0.0 136.3 jit_solution(4800792894537509430)
XLA Ops:
  7.8 4.0 %first_stage.1 = (bf16[4,64,1536]{2,1,0:T(8,128)(2,1)}, bf16[2,48,1536]{2,1,0:T(8,128)(2,1)}, bf16[2,48,1536]{2,1,0:T(8,128)(2,1)}, bf16[768,384]{1,0:T(8,128)(2,1)}) custom-call(s32[2]{0:T(128)} %pad_add_fusion.1.pos_ref, bf16[64,1536]{1,0:T(8,128)(2,1)} %bitcast.40, f32[8,1536]{1,0:T(8,128)} %bitcast.42, bf16[1536,384]{1,0:T(8,128)(2,1)} %up_ref.1, ...), custom_call_target="tpu_custom_call" | custom-call | tf_op jit(solution)/shard_map/first_stage/pallas_call | solution.py:97
  11.9 4.4 %all-to-all-start = ((bf16[4,64,1536]{2,1,0:T(8,128)(2,1)}), bf16[4,64,1536]{2,1,0:T(8,128)(2,1)S(1)}, u32[]{:S(2)}, u32[]{:S(2)}) async-start(bf16[4,64,1536]{2,1,0:T(8,128)(2,1)} %get-tuple-element.22), calls=%async_computation | async-start | bytes 1572864 | tf_op jit(solution)/shard_map/all_to_all | solution.py:407
  16.3 1.6 %collective-permute-start = (bf16[2,48,1536]{2,1,0:T(8,128)(2,1)}, bf16[2,48,1536]{2,1,0:T(8,128)(2,1)S(1)}, u32[]{:S(2)}, u32[]{:S(2)}) collective-permute-start(bf16[2,48,1536]{2,1,0:T(8,128)(2,1)} %get-tuple-element.21), channel_id=1, source_target_pairs={{0,2},{2,4},{4,6},{6,0},{1,3},{3,5},{5,7},{7,1},{8,10},{10,12},{12... | collective-permute-start | bytes 884744 | tf_op jit(solution)/shard_map/ppermute | solution.py:398
  17.9 1.7 %collective-permute-start.1 = (bf16[2,48,1536]{2,1,0:T(8,128)(2,1)}, bf16[2,48,1536]{2,1,0:T(8,128)(2,1)S(1)}, u32[]{:S(2)}, u32[]{:S(2)}) collective-permute-start(bf16[2,48,1536]{2,1,0:T(8,128)(2,1)} %get-tuple-element.21), channel_id=1, source_target_pairs={{0,6},{2,0},{4,2},{6,4},{1,7},{3,1},{5,3},{7,5},{8,14},{10,8},{12,... | collective-permute-start | bytes 884744 | tf_op jit(solution)/shard_map/ppermute | solution.py:398
  19.5 2.0 %collective-permute-start.2 = (bf16[2,48,1536]{2,1,0:T(8,128)(2,1)}, bf16[2,48,1536]{2,1,0:T(8,128)(2,1)S(1)}, u32[]{:S(2)}, u32[]{:S(2)}) collective-permute-start(bf16[2,48,1536]{2,1,0:T(8,128)(2,1)} %get-tuple-element.21), channel_id=1, source_target_pairs={{0,4},{2,6},{4,0},{6,2},{1,5},{3,7},{5,1},{7,3},{8,12},{10,14},{12... | collective-permute-start | bytes 884744 | tf_op jit(solution)/shard_map/ppermute | solution.py:398
  21.5 5.0 %collective-permute-done.n0_ref = bf16[2,48,1536]{2,1,0:T(8,128)(2,1)S(1)} collective-permute-done((bf16[2,48,1536]{2,1,0:T(8,128)(2,1)}, bf16[2,48,1536]{2,1,0:T(8,128)(2,1)S(1)}, u32[]{:S(2)}, u32[]{:S(2)}) %collective-permute-start) | collective-permute-done | bytes 294944 | tf_op jit(solution)/shard_map/ppermute | solution.py:398
  26.5 1.5 %collective-permute-done.1.n1_ref = bf16[2,48,1536]{2,1,0:T(8,128)(2,1)S(1)} collective-permute-done((bf16[2,48,1536]{2,1,0:T(8,128)(2,1)}, bf16[2,48,1536]{2,1,0:T(8,128)(2,1)S(1)}, u32[]{:S(2)}, u32[]{:S(2)}) %collective-permute-start.1) | collective-permute-done | bytes 294944 | tf_op jit(solution)/shard_map/ppermute | solution.py:398
  28.0 5.7 %collective-permute-done.2.n2_ref = bf16[2,48,1536]{2,1,0:T(8,128)(2,1)S(1)} collective-permute-done((bf16[2,48,1536]{2,1,0:T(8,128)(2,1)}, bf16[2,48,1536]{2,1,0:T(8,128)(2,1)S(1)}, u32[]{:S(2)}, u32[]{:S(2)}) %collective-permute-start.2) | collective-permute-done | bytes 294944 | tf_op jit(solution)/shard_map/ppermute | solution.py:398
  33.8 1.1 pad_maximum_fusion
  34.8 1.2 collective-permute-start.3
  36.1 2.1 %collective-permute-start.4 = (bf16[2,48,1536]{2,1,0:T(8,128)(2,1)}, bf16[2,48,1536]{2,1,0:T(8,128)(2,1)S(1)}, u32[]{:S(2)}, u32[]{:S(2)}) collective-permute-start(bf16[2,48,1536]{2,1,0:T(8,128)(2,1)} %get-tuple-element.28), channel_id=1, source_target_pairs={{0,6},{2,0},{4,2},{6,4},{1,7},{3,1},{5,3},{7,5},{8,14},{10,8},{12,... | collective-permute-start | bytes 884744 | tf_op jit(solution)/shard_map/ppermute | solution.py:398
  39.0 1.0 copy-done.15
  40.0 1.0 copy-done.17
  40.9 1.0 copy-done.19
  41.9 3.5 %project.2.refs_2_ = bf16[4,2,256,384]{3,2,1,0:T(8,128)(2,1)} custom-call(s32[3]{0:T(128)S(1)} %pad_add_fusion.pos_ref.refs_0_, bf16[256,1536]{1,0:T(8,128)(2,1)S(1)} %bitcast.28, bf16[3,96,1536]{2,1,0:T(8,128)(2,1)S(1)} %bitcast.26, bf16[2,48,1536]{2,1,0:T(8,128)(2,1)S(1)} %copy-done.15, bf16[2,48,1536]{2,1,0:T(8,128)(2,1)S(1)} %copy-done.17, ...), custom_call_target="tpu_custom_call" | custom-call | tf_op jit(solution)/shard_map/project/pallas_call | solution.py:156
  45.4 4.7 %all-to-all-start.1 = ((bf16[4,2,256,384]{3,2,1,0:T(8,128)(2,1)}), bf16[4,2,256,384]{3,2,1,0:T(8,128)(2,1)}, u32[]{:S(2)}, u32[]{:S(2)}) async-start(bf16[4,2,256,384]{3,2,1,0:T(8,128)(2,1)} %project.2.refs_2_), calls=%async_computation.1 | async-start | bytes 3145728 | tf_op jit(solution)/shard_map/all_to_all | solution.py:415
  50.1 1.6 %collective-permute-done.4.n1_ref = bf16[2,48,1536]{2,1,0:T(8,128)(2,1)S(1)} collective-permute-done((bf16[2,48,1536]{2,1,0:T(8,128)(2,1)}, bf16[2,48,1536]{2,1,0:T(8,128)(2,1)S(1)}, u32[]{:S(2)}, u32[]{:S(2)}) %collective-permute-start.4) | collective-permute-done | bytes 294944 | tf_op jit(solution)/shard_map/ppermute | solution.py:398
  52.1 1.0 pad_maximum_fusion.1
  55.5 2.5 %collective-permute-done.7.far_ref = bf16[3,2,48,1536]{3,2,1,0:T(8,128)(2,1)S(1)} collective-permute-done((bf16[3,2,48,1536]{3,2,1,0:T(8,128)(2,1)}, bf16[3,2,48,1536]{3,2,1,0:T(8,128)(2,1)S(1)}, u32[]{:S(2)}, u32[]{:S(2)}) %collective-permute-start.7) | collective-permute-done | bytes 884768 | tf_op jit(solution)/shard_map/ppermute | solution.py:419
  58.0 1.0 copy-done.3
  60.0 1.0 copy-done.9
  60.9 1.2 project.3
  62.1 3.5 %attention.2.refs_3_ = f32[256,512]{1,0:T(8,128)S(1)} custom-call(s32[3]{0:T(128)S(1)} %pad_add_fusion.pos_ref.refs_0_, bf16[256,384]{1,0:T(8,128)(2,1)S(1)} %bitcast.34, bf16[4,2,256,384]{3,2,1,0:T(8,128)(2,1)} %project.2.refs_2_, bf16[2,154,384]{2,1,0:T(8,128)(2,1)S(1)} %bitcast.39), custom_call_target="tpu_custom_call" | custom-call | tf_op jit(solution)/shard_map/attention/pallas_call | solution.py:246
  66.3 4.5 %all-to-all-done.1.refs_2_ = bf16[4,2,256,384]{3,2,1,0:T(8,128)(2,1)} async-done(((bf16[4,2,256,384]{3,2,1,0:T(8,128)(2,1)}), bf16[4,2,256,384]{3,2,1,0:T(8,128)(2,1)}, u32[]{:S(2)}, u32[]{:S(2)}) %all-to-all-start.1) | async-done | bytes 1572896 | tf_op jit(solution)/shard_map/all_to_all | solution.py:415
  71.8 5.1 %attention.3.a_ref = bf16[256,384]{1,0:T(8,128)(2,1)S(1)} custom-call(s32[3]{0:T(128)S(1)} %pad_add_fusion.pos_ref.refs_0_, bf16[256,384]{1,0:T(8,128)(2,1)S(1)} %bitcast.35, bf16[4,2,256,384]{3,2,1,0:T(8,128)(2,1)} %all-to-all-done.1.refs_2_, f32[256,512]{1,0:T(8,128)S(1)} %attention.2.refs_3_), custom_call_target="tpu_custom_call" | custom-call | tf_op jit(solution)/shard_map/attention/pallas_call | solution.py:246
  77.0 1.2 out_projection.1
  78.2 15.3 %all_to_all.25.part_ref = bf16[4,64,1536]{2,1,0:T(8,128)(2,1)S(1)} all-to-all(bf16[4,64,1536]{2,1,0:T(8,128)(2,1)S(1)} %bitcast.30), channel_id=1, replica_groups=mesh['zl'=2,'zp'=2,'core'=2,'tx'=4,'ty'=4,'blk'=2] {'tx'}, dimensions={0} | all-to-all | bytes 1572864 | tf_op jit(solution)/shard_map/all_to_all | solution.py:427
  93.9 13.1 %all_to_all.26 = bf16[4,64,1536]{2,1,0:T(8,128)(2,1)} all-to-all(bf16[4,64,1536]{2,1,0:T(8,128)(2,1)S(1)} %get-tuple-element.36), channel_id=1, replica_groups=mesh['zl'=2,'zp'=2,'core'=2,'tx'=4,'ty'=4,'blk'=2] {'ty'}, dimensions={0} | all-to-all | bytes 1572864 | tf_op jit(solution)/shard_map/all_to_all | solution.py:429
  107.0 7.6 %feed_forward.1 = bf16[256,1536]{1,0:T(8,128)(2,1)} custom-call(bf16[256,1536]{1,0:T(8,128)(2,1)} %bitcast.48, bf16[2,4,1536,384]{3,2,1,0:T(8,128)(2,1)} %bitcast.45, bf16[2,4,1536,384]{3,2,1,0:T(8,128)(2,1)} %bitcast.46), custom_call_target="tpu_custom_call" | custom-call | tf_op jit(solution)/shard_map/feed_forward/pallas_call | solution.py:339
  114.6 3.6 %all-to-all-start.4 = ((bf16[4,64,1536]{2,1,0:T(8,128)(2,1)}), bf16[4,64,1536]{2,1,0:T(8,128)(2,1)S(1)}, u32[]{:S(2)}, u32[]{:S(2)}) async-start(bf16[4,64,1536]{2,1,0:T(8,128)(2,1)} %bitcast.47), calls=%async_computation.4 | async-start | bytes 1572864 | tf_op jit(solution)/shard_map/all_to_all | solution.py:431
  119.2 8.5 %all-to-all-done.4.part_ref = bf16[4,64,1536]{2,1,0:T(8,128)(2,1)S(1)} async-done(((bf16[4,64,1536]{2,1,0:T(8,128)(2,1)}), bf16[4,64,1536]{2,1,0:T(8,128)(2,1)S(1)}, u32[]{:S(2)}, u32[]{:S(2)}) %all-to-all-start.4) | async-done | bytes 786464 | tf_op jit(solution)/shard_map/all_to_all | solution.py:431
  127.7 1.1 last_stage.1
  (62 shorter events, 7.5 us)
Async XLA Ops:
  7.2 48.1 %copy-start = (bf16[1,154,2,1536]{3,2,1,0:T(2,128)(2,1)S(1)}, bf16[1,154,2,1536]{3,2,1,0:T(2,128)(2,1)}, u32[]{:S(2)}) copy-start(bf16[1,154,2,1536]{3,2,1,0:T(2,128)(2,1)} %param.14) | copy-start | bytes 2838532
  7.2 99.8 %all-gather.3.cloned.1.call-start = ((), (), s32[]{:S(2)}) async-start(), calls=%async_computation.5 | async-start | bytes 10027008 | tf_op jit(solution)/shard_map/all_gather | solution.py:405
  11.9 27.1 %copy-start.1 = (bf16[1536,3,96]{0,2,1:T(8,128)(2,1)S(1)}, bf16[1536,3,96]{0,2,1:T(8,128)(2,1)}, u32[]{:S(2)}) copy-start(bf16[1536,3,96]{0,2,1:T(8,128)(2,1)} %param.17) | copy-start | bytes 2654212
  11.9 21.9 %all-to-all-start = ((bf16[4,64,1536]{2,1,0:T(8,128)(2,1)}), bf16[4,64,1536]{2,1,0:T(8,128)(2,1)S(1)}, u32[]{:S(2)}, u32[]{:S(2)}) async-start(bf16[4,64,1536]{2,1,0:T(8,128)(2,1)} %get-tuple-element.22), calls=%async_computation | async-start | bytes 1572864 | tf_op jit(solution)/shard_map/all_to_all | solution.py:407
  16.3 10.2 %collective-permute-start = (bf16[2,48,1536]{2,1,0:T(8,128)(2,1)}, bf16[2,48,1536]{2,1,0:T(8,128)(2,1)S(1)}, u32[]{:S(2)}, u32[]{:S(2)}) collective-permute-start(bf16[2,48,1536]{2,1,0:T(8,128)(2,1)} %get-tuple-element.21), channel_id=1, source_target_pairs={{0,2},{2,4},{4,6},{6,0},{1,3},{3,5},{5,7},{7,1},{8,10},{10,12},{12... | collective-permute-start | bytes 884744 | tf_op jit(solution)/shard_map/ppermute | solution.py:398
  17.9 10.2 %collective-permute-start.1 = (bf16[2,48,1536]{2,1,0:T(8,128)(2,1)}, bf16[2,48,1536]{2,1,0:T(8,128)(2,1)S(1)}, u32[]{:S(2)}, u32[]{:S(2)}) collective-permute-start(bf16[2,48,1536]{2,1,0:T(8,128)(2,1)} %get-tuple-element.21), channel_id=1, source_target_pairs={{0,6},{2,0},{4,2},{6,4},{1,7},{3,1},{5,3},{7,5},{8,14},{10,8},{12,... | collective-permute-start | bytes 884744 | tf_op jit(solution)/shard_map/ppermute | solution.py:398
  19.5 14.2 %collective-permute-start.2 = (bf16[2,48,1536]{2,1,0:T(8,128)(2,1)}, bf16[2,48,1536]{2,1,0:T(8,128)(2,1)S(1)}, u32[]{:S(2)}, u32[]{:S(2)}) collective-permute-start(bf16[2,48,1536]{2,1,0:T(8,128)(2,1)} %get-tuple-element.21), channel_id=1, source_target_pairs={{0,4},{2,6},{4,0},{6,2},{1,5},{3,7},{5,1},{7,3},{8,12},{10,14},{12... | collective-permute-start | bytes 884744 | tf_op jit(solution)/shard_map/ppermute | solution.py:398
  26.5 8.3 %copy-start.14 = (bf16[2,48,1536]{2,1,0:T(8,128)(2,1)}, bf16[2,48,1536]{2,1,0:T(8,128)(2,1)S(1)}, u32[]{:S(2)}) copy-start(bf16[2,48,1536]{2,1,0:T(8,128)(2,1)S(1)} %collective-permute-done.n0_ref) | copy-start | bytes 884740
  28.0 6.8 %copy-start.16 = (bf16[2,48,1536]{2,1,0:T(8,128)(2,1)}, bf16[2,48,1536]{2,1,0:T(8,128)(2,1)S(1)}, u32[]{:S(2)}) copy-start(bf16[2,48,1536]{2,1,0:T(8,128)(2,1)S(1)} %collective-permute-done.1.n1_ref) | copy-start | bytes 884740
  33.8 2.3 %copy-start.18 = (bf16[2,48,1536]{2,1,0:T(8,128)(2,1)}, bf16[2,48,1536]{2,1,0:T(8,128)(2,1)S(1)}, u32[]{:S(2)}) copy-start(bf16[2,48,1536]{2,1,0:T(8,128)(2,1)S(1)} %collective-permute-done.2.n2_ref) | copy-start | bytes 884740
  34.8 4.2 %collective-permute-start.6 = (bf16[3,2,48,1536]{3,2,1,0:T(8,128)(2,1)}, bf16[3,2,48,1536]{3,2,1,0:T(8,128)(2,1)}, u32[]{:S(2)}, u32[]{:S(2)}) collective-permute-start(bf16[3,2,48,1536]{3,2,1,0:T(8,128)(2,1)} %pad_maximum_fusion), channel_id=1, source_target_pairs={{0,32},{32,0},{1,33},{33,1},{2,34},{34,2},{3,35},{35,3},{4,36},{36... | collective-permute-start | bytes 2654216 | tf_op jit(solution)/shard_map/ppermute | solution.py:411
  34.8 15.2 %collective-permute-start.3 = (bf16[2,48,1536]{2,1,0:T(8,128)(2,1)}, bf16[2,48,1536]{2,1,0:T(8,128)(2,1)S(1)}, u32[]{:S(2)}, u32[]{:S(2)}) collective-permute-start(bf16[2,48,1536]{2,1,0:T(8,128)(2,1)} %get-tuple-element.28), channel_id=1, source_target_pairs={{0,2},{2,4},{4,6},{6,0},{1,3},{3,5},{5,7},{7,1},{8,10},{10,12},{12... | collective-permute-start | bytes 884744 | tf_op jit(solution)/shard_map/ppermute | solution.py:398
  36.1 15.6 %collective-permute-start.4 = (bf16[2,48,1536]{2,1,0:T(8,128)(2,1)}, bf16[2,48,1536]{2,1,0:T(8,128)(2,1)S(1)}, u32[]{:S(2)}, u32[]{:S(2)}) collective-permute-start(bf16[2,48,1536]{2,1,0:T(8,128)(2,1)} %get-tuple-element.28), channel_id=1, source_target_pairs={{0,6},{2,0},{4,2},{6,4},{1,7},{3,1},{5,3},{7,5},{8,14},{10,8},{12,... | collective-permute-start | bytes 884744 | tf_op jit(solution)/shard_map/ppermute | solution.py:398
  38.2 14.0 %collective-permute-start.5 = (bf16[2,48,1536]{2,1,0:T(8,128)(2,1)}, bf16[2,48,1536]{2,1,0:T(8,128)(2,1)S(1)}, u32[]{:S(2)}, u32[]{:S(2)}) collective-permute-start(bf16[2,48,1536]{2,1,0:T(8,128)(2,1)} %get-tuple-element.28), channel_id=1, source_target_pairs={{0,4},{2,6},{4,0},{6,2},{1,5},{3,7},{5,1},{7,3},{8,12},{10,14},{12... | collective-permute-start | bytes 884744 | tf_op jit(solution)/shard_map/ppermute | solution.py:398
  39.0 1.0 copy-start.15
  40.0 1.0 copy-start.17
  40.9 1.0 copy-start.19
  45.4 25.5 %all-to-all-start.1 = ((bf16[4,2,256,384]{3,2,1,0:T(8,128)(2,1)}), bf16[4,2,256,384]{3,2,1,0:T(8,128)(2,1)}, u32[]{:S(2)}, u32[]{:S(2)}) async-start(bf16[4,2,256,384]{3,2,1,0:T(8,128)(2,1)} %project.2.refs_2_), calls=%async_computation.1 | async-start | bytes 3145728 | tf_op jit(solution)/shard_map/all_to_all | solution.py:415
  55.3 2.7 %collective-permute-start.7 = (bf16[3,2,48,1536]{3,2,1,0:T(8,128)(2,1)}, bf16[3,2,48,1536]{3,2,1,0:T(8,128)(2,1)S(1)}, u32[]{:S(2)}, u32[]{:S(2)}) collective-permute-start(bf16[3,2,48,1536]{3,2,1,0:T(8,128)(2,1)} %pad_maximum_fusion.1), channel_id=1, source_target_pairs={{0,32},{32,0},{1,33},{33,1},{2,34},{34,2},{3,35},{35,3},{4,36},{36... | collective-permute-start | bytes 2654216 | tf_op jit(solution)/shard_map/ppermute | solution.py:419
  58.0 1.0 copy-start.3
  59.0 1.0 copy-start.6
  60.0 1.0 copy-start.9
  66.3 10.6 %copy-start.4 = (bf16[2,48,1536]{2,1,0:T(8,128)(2,1)S(1)}, bf16[2,48,1536]{2,1,0:T(8,128)(2,1)}, u32[]{:S(2)}) copy-start(bf16[2,48,1536]{2,1,0:T(8,128)(2,1)} %copy-done.2) | copy-start | bytes 884740
  66.3 10.6 %copy-start.7 = (bf16[2,48,1536]{2,1,0:T(8,128)(2,1)S(1)}, bf16[2,48,1536]{2,1,0:T(8,128)(2,1)}, u32[]{:S(2)}) copy-start(bf16[2,48,1536]{2,1,0:T(8,128)(2,1)} %copy-done.5) | copy-start | bytes 884740
  66.3 10.6 %copy-start.10 = (bf16[2,48,1536]{2,1,0:T(8,128)(2,1)S(1)}, bf16[2,48,1536]{2,1,0:T(8,128)(2,1)}, u32[]{:S(2)}) copy-start(bf16[2,48,1536]{2,1,0:T(8,128)(2,1)} %copy-done.8) | copy-start | bytes 884740
  70.8 0.9 copy-start.12
  71.8 5.2 %copy-start.13 = (bf16[96,1536]{1,0:T(8,128)(2,1)S(1)}, bf16[96,1536]{1,0:T(8,128)(2,1)}, u32[]{:S(2)}) copy-start(bf16[96,1536]{1,0:T(8,128)(2,1)} %own_ref.1) | copy-start | bytes 884740
  76.9 16.6 %copy-start.20 = (bf16[1,64,1536]{2,1,0:T(8,128)(2,1)S(1)}, bf16[1,64,1536]{2,1,0:T(8,128)(2,1)}, u32[]{:S(2)}) copy-start(bf16[1,64,1536]{2,1,0:T(8,128)(2,1)} %param.11) | copy-start | bytes 589828
  77.0 16.6 %copy-start.21 = (f32[1,8,1536]{2,1,0:T(8,128)S(1)}, f32[1,8,1536]{2,1,0:T(8,128)}, u32[]{:S(2)}) copy-start(f32[1,8,1536]{2,1,0:T(8,128)} %param.13) | copy-start | bytes 147460
  114.6 4.3 %copy-start.22 = (bf16[1536,64]{0,1:T(8,128)(2,1)S(1)}, bf16[1536,64]{0,1:T(8,128)(2,1)}, u32[]{:S(2)}) copy-start(bf16[1536,64]{0,1:T(8,128)(2,1)} %param.21) | copy-start | bytes 589828
  114.6 14.2 %copy-start.23 = (f32[1,32,128]{2,1,0:T(8,128)S(1)}, f32[1,32,128]{2,1,0:T(8,128)}, u32[]{:S(2)}) copy-start(f32[1,32,128]{2,1,0:T(8,128)} %param.12) | copy-start | bytes 49156
  114.6 13.1 %all-to-all-start.4 = ((bf16[4,64,1536]{2,1,0:T(8,128)(2,1)}), bf16[4,64,1536]{2,1,0:T(8,128)(2,1)S(1)}, u32[]{:S(2)}, u32[]{:S(2)}) async-start(bf16[4,64,1536]{2,1,0:T(8,128)(2,1)} %bitcast.47), calls=%async_computation.4 | async-start | bytes 1572864 | tf_op jit(solution)/shard_map/all_to_all | solution.py:431
  (4 other events, 2.8 us)
Sparse Core Ops, SparseCore 0:
  12.0 60.9 all-gather.2

commit v9 on v8

--- a/solution.py
+++ b/solution.py
@@ -118,31 +118,29 @@
     )(pos, tokens, mods, w_up, w_down, own_qkv, w_out)
 
 
-def assemble(pos_ref, own_ref, near_refs, far_ref, store):
+def assemble(pos_ref, own_ref, near_ref, far_ref, store):
     core = pos_ref[0]
     row = pos_ref[1]
     store(row, 0, own_ref, 0)
     store(row, 1, own_ref, 1)
-    for i, (near_ref, step) in enumerate(zip(near_refs, STRIDES)):
+    for i, step in enumerate(STRIDES):
         source = lax.rem(row + 4 - step, 4)
-        store(source, core, near_ref, None)
+        store(source, core, near_ref, i)
         store(source, 1 - core, far_ref, i)
 
 
-def project_kernel(first, pos_ref, h_ref, own_ref, n0_ref, n1_ref, n2_ref, far_ref, out_ref, w_ref):
+def project_kernel(first, pos_ref, h_ref, own_ref, near_ref, far_ref, out_ref, w_ref):
     count = out_ref.shape[1]
 
     def store(source, half, ref, index):
         for k in range(count):
             if ref is own_ref:
                 value = ref[first + k, index * 48 : index * 48 + 48, :]
-            elif index is None:
-                value = ref[k]
             else:
                 value = ref[index, k]
             w_ref[k, source, half] = value
 
-    assemble(pos_ref, own_ref, (n0_ref, n1_ref, n2_ref), far_ref, store)
+    assemble(pos_ref, own_ref, near_ref, far_ref, store)
     h = h_ref[...]
     for k in range(count):
         w = w_ref[k].reshape(384, h.shape[1])
@@ -157,32 +155,36 @@
         functools.partial(project_kernel, first),
         out_shape=jax.ShapeDtypeStruct((copies, count, rows, 384), BF),
         in_specs=[pl.BlockSpec(memory_space=pltpu.SMEM)]
-        + [pl.BlockSpec(memory_space=pltpu.VMEM)] * 6,
+        + [pl.BlockSpec(memory_space=pltpu.VMEM)] * 4,
         scratch_shapes=[pltpu.VMEM((count, 4, 2, 48, width), BF)],
         compiler_params=params(14),
         name="project",
-    )(pos, h, own, *near, far)
+    )(pos, h, own, near, far)
 
 
 def attention_kernel(own, *refs):
     refs = list(refs)
-    pos_ref, q_ref, kv_ref = refs[:3]
+    pos_ref, kv_ref = refs[:2]
     if own:
-        text_ref = refs[3]
+        q_ref, text_ref = refs[2:4]
         outs = refs[4:]
+        outs[0][:, 512:] = q_ref[...].astype(F32)
     else:
-        state_ref = refs[3]
-        outs = refs[4:]
-    rows = q_ref.shape[0]
+        state_ref = refs[2]
+        outs = refs[3:]
+    rows = outs[0].shape[0]
     if own:
         live = lax.broadcasted_iota(jnp.int32, (rows, TXT), 1) < pos_ref[2]
     first = lax.broadcasted_iota(jnp.int32, (rows, 128), 1) < HEAD_DIM
     where = [0] if own else [lax.rem(pos_ref[1] + i, 4) for i in (1, 2, 3)]
     lane = lax.broadcasted_iota(jnp.int32, (rows, 128), 1)
     stats = jnp.zeros((rows, 128), F32)
-    for g in range(q_ref.shape[1] // 128):
+    for g in range(3):
         cols = slice(g * 128, g * 128 + 128)
-        q = q_ref[:, cols]
+        if own:
+            q = q_ref[:, cols]
+        else:
+            q = state_ref[:, 512 + g * 128 : 640 + g * 128].astype(BF)
         accs = []
         scales = []
         for side in range(2):
@@ -233,16 +235,17 @@
             total = jnp.where(first, scales[0][1], scales[1][1])
             outs[0][:, cols] = ((acc + state_ref[:, cols] * factor) / total).astype(BF)
     if own:
-        outs[0][:, 384:] = stats
-
-
-def attention(pos, q, kv, text=None, state=None):
-    own = text is not None
-    args = [q, kv, text if own else state]
+        outs[0][:, 384:512] = stats
+
+
+def attention(pos, kv, query=None, text=None, state=None):
+    own = state is None
+    args = [kv, query, text] if own else [kv, state]
+    rows = kv.shape[2]
     if own:
-        out = jax.ShapeDtypeStruct((q.shape[0], 512), F32)
+        out = jax.ShapeDtypeStruct((rows, 896), F32)
     else:
-        out = jax.ShapeDtypeStruct(q.shape, BF)
+        out = jax.ShapeDtypeStruct((rows, 384), BF)
     return pl.pallas_call(
         functools.partial(attention_kernel, own),
         out_shape=out,
@@ -253,17 +256,15 @@
     )(pos, *args)
 
 
-def out_kernel(pos_ref, a_ref, own_ref, n0_ref, n1_ref, n2_ref, far_ref, out_ref, w_ref):
+def out_kernel(pos_ref, a_ref, own_ref, near_ref, far_ref, out_ref, w_ref):
     def store(source, half, ref, index):
         if ref is own_ref:
             value = ref[index * 48 : index * 48 + 48, :]
-        elif index is None:
-            value = ref[1]
         else:
             value = ref[index, 1]
         w_ref[source, half] = value
 
-    assemble(pos_ref, own_ref, (n0_ref, n1_ref, n2_ref), far_ref, store)
+    assemble(pos_ref, own_ref, near_ref, far_ref, store)
     w = w_ref[...].reshape(384, out_ref.shape[1])
     out_ref[...] = lax.dot_general(
         a_ref[...], w, NN, preferred_element_type=F32
@@ -276,11 +277,11 @@
         out_kernel,
         out_shape=jax.ShapeDtypeStruct((a.shape[0], width), BF),
         in_specs=[pl.BlockSpec(memory_space=pltpu.SMEM)]
-        + [pl.BlockSpec(memory_space=pltpu.VMEM)] * 6,
+        + [pl.BlockSpec(memory_space=pltpu.VMEM)] * 4,
         scratch_shapes=[pltpu.VMEM((4, 2, 48, width), BF)],
         compiler_params=params(8),
         name="out_projection",
-    )(pos, a, own, *near, far)
+    )(pos, a, own, near, far)
 
 
 def second_norm_kernel(x_ref, part_ref, mod_ref, second_ref, out_ref):
@@ -411,16 +412,17 @@
     far_kv = lax.ppermute(stacked, "core", swap2)
     near_qo = [to_lines(half_qo, step) for step in STRIDES]
     h1 = h1.reshape(4 * rows, width)
-    own_kv = project(pos, h1, own_qkv, 1, 2, 4, near_kv, far_kv)
+    own_kv = project(pos, h1, own_qkv, 1, 2, 4, stacked, far_kv)
     all_kv = lax.all_to_all(own_kv, "ty", split_axis=0, concat_axis=0, tiled=True)
     *near_qo, own_kv, text_kv = lax.optimization_barrier((*near_qo, own_kv, text_kv))
     text = lax.dynamic_slice_in_dim(text_kv[0], lax.axis_index("tx") * 384, 384, 2)
     text = jnp.transpose(text, (1, 0, 2))
-    far_qo = lax.ppermute(jnp.stack(near_qo), "core", swap2)
+    near_qo = jnp.stack(near_qo)
+    far_qo = lax.ppermute(near_qo, "core", swap2)
     query = project(pos, h1, own_qkv, 0, 1, 1, near_qo, far_qo)[0, 0]
 
-    state = attention(pos, query, own_kv, text=text)
-    attended = attention(pos, query, all_kv, state=state)
+    state = attention(pos, own_kv, query=query, text=text)
+    attended = attention(pos, all_kv, state=state)
 
     partial = out_projection(pos, attended, w_out, near_qo, far_qo)
     partial = partial.reshape(4, rows, width)

time: 137 us -> 139 us (1.015)
  local copies, waits for them, and re-layouts: 10.1 us -> 1.24 us
  waiting for transfers between devices: 29.8 us -> 35.9 us
  blocking collectives: 28.4 us -> 31.3 us
    unnamed x49 -> x21, local copies, waits for them, and re-layouts: 9.83 us -> 0.97 us
    ppermute x6, waiting for transfers between devices: 14.3 us -> 17.7 us  [to_lines(): return lax.ppermute(value, 'ty', [(i, (i + step) % 4) for i in range(4)])]
    all_to_all x1, waiting for transfers between devices: 4.51 us -> 6.86 us  [on_device(): lax.all_to_all(own_kv, 'ty', split_axis=0, concat_axis=0, tiled=True)]
    all_to_all x1, blocking collectives: 13.1 us -> 14.9 us  [on_device(): h2 = lax.all_to_all(h2, 'ty', split_axis=0, concat_axis=0, tiled=True)]
  transfers between devices with their start and end apart: 12 -> 12, of which waited for: 8 -> 8; matrix products, arithmetic and copies ran while one was open for 2% -> 2% of each run, Pallas kernels for 11% -> 12%
where the time goes in v9:
time: 139 us
  waiting for transfers between devices  35.9 us (26%)
  blocking collectives  31.3 us (23%)
  Pallas kernels  28.8 us (21%)
  starting transfers between devices  21.8 us (16%)
  between operations  15.6 us (11%)
  other arithmetic  3.8 us (3%)
    ppermute x6, waiting for transfers between devices, to_lines(): return lax.ppermute(value, 'ty', [(i, (i + step) % 4) for i in range(4)])  17.7 us
    all_to_all x1, blocking collectives, on_device(): lax.all_to_all(partial, 'tx', split_axis=0, concat_axis=0, tiled=True)  16.4 us
    all_to_all x1, blocking collectives, on_device(): h2 = lax.all_to_all(h2, 'ty', split_axis=0, concat_axis=0, tiled=True)  14.9 us
    all_to_all x1, waiting for transfers between devices, on_device(): lax.all_to_all(partial, 'ty', split_axis=0, concat_axis=0, tiled=True)  8.94 us
    ppermute x6, starting transfers between devices, to_lines(): return lax.ppermute(value, 'ty', [(i, (i + step) % 4) for i in range(4)])  8.65 us
    pallas_call x2, Pallas kernels, attention(): pl.pallas_call(functools.partial(attention_kernel, own), out_shape=out, i...  8.55 us
    pallas_call x1, Pallas kernels, feed_forward(): pl.pallas_call(ffn_kernel, grid=(4,), out_shape=jax.ShapeDtypeStruct((row...  7.66 us
    all_to_all x1, waiting for transfers between devices, on_device(): lax.all_to_all(own_kv, 'ty', split_axis=0, concat_axis=0, tiled=True)  6.86 us
  transfers between devices with their start and end apart: 12, of which 8 were waited for; matrix products, arithmetic and copies ran while one was open for 2% of the time, Pallas kernels for 12%

profile of v9, /device:TPU:128, one launch (start us, length us, event | category | flops | bytes accessed | tf_op | source)
XLA Modules:
  0.0 138.5 jit_solution(6227610015878044356)
XLA Ops:
  7.2 0.6 pad_add_fusion.1.pos_ref
  7.8 4.0 %first_stage.1 = (bf16[4,64,1536]{2,1,0:T(8,128)(2,1)}, bf16[2,48,1536]{2,1,0:T(8,128)(2,1)}, bf16[2,48,1536]{2,1,0:T(8,128)(2,1)}, bf16[768,384]{1,0:T(8,128)(2,1)}) custom-call(s32[2]{0:T(128)} %pad_add_fusion.1.pos_ref, bf16[64,1536]{1,0:T(8,128)(2,1)} %bitcast.32, f32[8,1536]{1,0:T(8,128)} %bitcast.35, bf16[1536,384]{1,0:T(8,128)(2,1)} %up_ref.1, ...), custom_call_target="tpu_custom_call" | custom-call | tf_op jit(solution)/shard_map/first_stage/pallas_call | solution.py:97
  11.8 4.4 %all-to-all-start = ((bf16[4,64,1536]{2,1,0:T(8,128)(2,1)}), bf16[4,64,1536]{2,1,0:T(8,128)(2,1)S(1)}, u32[]{:S(2)}, u32[]{:S(2)}) async-start(bf16[4,64,1536]{2,1,0:T(8,128)(2,1)} %get-tuple-element.22), calls=%async_computation | async-start | bytes 1572864 | tf_op jit(solution)/shard_map/all_to_all | solution.py:408
  16.3 1.6 %collective-permute-start = (bf16[2,48,1536]{2,1,0:T(8,128)(2,1)}, bf16[2,48,1536]{2,1,0:T(8,128)(2,1)S(1)}, u32[]{:S(2)}, u32[]{:S(2)}) collective-permute-start(bf16[2,48,1536]{2,1,0:T(8,128)(2,1)} %get-tuple-element.21), channel_id=1, source_target_pairs={{0,2},{2,4},{4,6},{6,0},{1,3},{3,5},{5,7},{7,1},{8,10},{10,12},{12... | collective-permute-start | bytes 884744 | tf_op jit(solution)/shard_map/ppermute | solution.py:399
  17.8 1.7 %collective-permute-start.1 = (bf16[2,48,1536]{2,1,0:T(8,128)(2,1)}, bf16[2,48,1536]{2,1,0:T(8,128)(2,1)S(1)}, u32[]{:S(2)}, u32[]{:S(2)}) collective-permute-start(bf16[2,48,1536]{2,1,0:T(8,128)(2,1)} %get-tuple-element.21), channel_id=1, source_target_pairs={{0,6},{2,0},{4,2},{6,4},{1,7},{3,1},{5,3},{7,5},{8,14},{10,8},{12,... | collective-permute-start | bytes 884744 | tf_op jit(solution)/shard_map/ppermute | solution.py:399
  19.5 2.0 %collective-permute-start.2 = (bf16[2,48,1536]{2,1,0:T(8,128)(2,1)}, bf16[2,48,1536]{2,1,0:T(8,128)(2,1)S(1)}, u32[]{:S(2)}, u32[]{:S(2)}) collective-permute-start(bf16[2,48,1536]{2,1,0:T(8,128)(2,1)} %get-tuple-element.21), channel_id=1, source_target_pairs={{0,4},{2,6},{4,0},{6,2},{1,5},{3,7},{5,1},{7,3},{8,12},{10,14},{12... | collective-permute-start | bytes 884744 | tf_op jit(solution)/shard_map/ppermute | solution.py:399
  21.5 5.0 %collective-permute-done = bf16[2,48,1536]{2,1,0:T(8,128)(2,1)S(1)} collective-permute-done((bf16[2,48,1536]{2,1,0:T(8,128)(2,1)}, bf16[2,48,1536]{2,1,0:T(8,128)(2,1)S(1)}, u32[]{:S(2)}, u32[]{:S(2)}) %collective-permute-start) | collective-permute-done | bytes 294944 | tf_op jit(solution)/shard_map/ppermute | solution.py:399
  26.5 1.5 %collective-permute-done.1 = bf16[2,48,1536]{2,1,0:T(8,128)(2,1)S(1)} collective-permute-done((bf16[2,48,1536]{2,1,0:T(8,128)(2,1)}, bf16[2,48,1536]{2,1,0:T(8,128)(2,1)S(1)}, u32[]{:S(2)}, u32[]{:S(2)}) %collective-permute-start.1) | collective-permute-done | bytes 294944 | tf_op jit(solution)/shard_map/ppermute | solution.py:399
  28.0 5.7 %collective-permute-done.2 = bf16[2,48,1536]{2,1,0:T(8,128)(2,1)S(1)} collective-permute-done((bf16[2,48,1536]{2,1,0:T(8,128)(2,1)}, bf16[2,48,1536]{2,1,0:T(8,128)(2,1)S(1)}, u32[]{:S(2)}, u32[]{:S(2)}) %collective-permute-start.2) | collective-permute-done | bytes 294944 | tf_op jit(solution)/shard_map/ppermute | solution.py:399
  33.7 0.7 copy-done.7
  34.4 1.2 pad_maximum_fusion.near_ref
  35.8 1.2 collective-permute-start.4
  37.0 2.1 %collective-permute-start.5 = (bf16[2,48,1536]{2,1,0:T(8,128)(2,1)}, bf16[2,48,1536]{2,1,0:T(8,128)(2,1)}, u32[]{:S(2)}, u32[]{:S(2)}) collective-permute-start(bf16[2,48,1536]{2,1,0:T(8,128)(2,1)} %get-tuple-element.29), channel_id=1, source_target_pairs={{0,6},{2,0},{4,2},{6,4},{1,7},{3,1},{5,3},{7,5},{8,14},{10,8},{12,... | collective-permute-start | bytes 884744 | tf_op jit(solution)/shard_map/ppermute | solution.py:399
  40.0 3.5 %project.2.refs_1_ = bf16[4,2,256,384]{3,2,1,0:T(8,128)(2,1)} custom-call(s32[3]{0:T(128)S(1)} %pad_add_fusion.pos_ref.refs_0_, bf16[256,1536]{1,0:T(8,128)(2,1)S(1)} %bitcast.28, bf16[3,96,1536]{2,1,0:T(8,128)(2,1)S(1)} %bitcast.26, bf16[3,2,48,1536]{3,2,1,0:T(8,128)(2,1)S(1)} %pad_maximum_fusion.near_ref, ...), custom_call_target="tpu_custom_call" | custom-call | tf_op jit(solution)/shard_map/project/pallas_call | solution.py:154
  43.4 4.7 %all-to-all-start.1 = ((bf16[4,2,256,384]{3,2,1,0:T(8,128)(2,1)}), bf16[4,2,256,384]{3,2,1,0:T(8,128)(2,1)}, u32[]{:S(2)}, u32[]{:S(2)}) async-start(bf16[4,2,256,384]{3,2,1,0:T(8,128)(2,1)} %project.2.refs_1_), calls=%async_computation.1 | async-start | bytes 3145728 | tf_op jit(solution)/shard_map/all_to_all | solution.py:416
  48.1 4.3 %collective-permute-done.5 = bf16[2,48,1536]{2,1,0:T(8,128)(2,1)} collective-permute-done((bf16[2,48,1536]{2,1,0:T(8,128)(2,1)}, bf16[2,48,1536]{2,1,0:T(8,128)(2,1)}, u32[]{:S(2)}, u32[]{:S(2)}) %collective-permute-start.5) | collective-permute-done | bytes 294944 | tf_op jit(solution)/shard_map/ppermute | solution.py:399
  52.5 1.1 collective-permute-done.6
  53.6 1.3 pad_maximum_fusion.1.near_ref
  55.4 2.4 %collective-permute-done.7.far_ref = bf16[3,2,48,1536]{3,2,1,0:T(8,128)(2,1)} collective-permute-done((bf16[3,2,48,1536]{3,2,1,0:T(8,128)(2,1)S(1)}, bf16[3,2,48,1536]{3,2,1,0:T(8,128)(2,1)}, u32[]{:S(2)}, u32[]{:S(2)}) %collective-permute-start.7) | collective-permute-done | bytes 884768 | tf_op jit(solution)/shard_map/ppermute | solution.py:421
  57.8 1.9 %project.3 = bf16[1,1,256,384]{3,2,1,0:T(8,128)(2,1)S(1)} custom-call(s32[3]{0:T(128)S(1)} %pad_add_fusion.pos_ref.refs_0_, bf16[256,1536]{1,0:T(8,128)(2,1)S(1)} %bitcast.29, bf16[3,96,1536]{2,1,0:T(8,128)(2,1)S(1)} %bitcast.27, bf16[3,2,48,1536]{3,2,1,0:T(8,128)(2,1)S(1)} %pad_maximum_fusion.1.near_ref, bf16[3,2,48,1536]{3,2,1,0:T(8,128)(2,1)} %collective-permute-done.7.far_ref), custom_call_target="tpu_custom_call" | custom-call | tf_op jit(solution)/shard_map/project/pallas_call | solution.py:154
  59.7 3.5 %attention.2.refs_2_ = f32[256,896]{1,0:T(8,128)S(1)} custom-call(s32[3]{0:T(128)S(1)} %pad_add_fusion.pos_ref.refs_0_, bf16[4,2,256,384]{3,2,1,0:T(8,128)(2,1)} %project.2.refs_1_, bf16[256,384]{1,0:T(8,128)(2,1)S(1)} %bitcast.34, bf16[2,154,384]{2,1,0:T(8,128)(2,1)S(1)} %bitcast.31), custom_call_target="tpu_custom_call" | custom-call | tf_op jit(solution)/shard_map/attention/pallas_call | solution.py:249
  63.2 6.9 %all-to-all-done.1.refs_1_ = bf16[4,2,256,384]{3,2,1,0:T(8,128)(2,1)} async-done(((bf16[4,2,256,384]{3,2,1,0:T(8,128)(2,1)}), bf16[4,2,256,384]{3,2,1,0:T(8,128)(2,1)}, u32[]{:S(2)}, u32[]{:S(2)}) %all-to-all-start.1) | async-done | bytes 1572896 | tf_op jit(solution)/shard_map/all_to_all | solution.py:416
  70.0 5.1 %attention.3.a_ref = bf16[256,384]{1,0:T(8,128)(2,1)S(1)} custom-call(s32[3]{0:T(128)S(1)} %pad_add_fusion.pos_ref.refs_0_, bf16[4,2,256,384]{3,2,1,0:T(8,128)(2,1)} %all-to-all-done.1.refs_1_, f32[256,896]{1,0:T(8,128)S(1)} %attention.2.refs_2_), custom_call_target="tpu_custom_call" | custom-call | tf_op jit(solution)/shard_map/attention/pallas_call | solution.py:249
  75.1 1.9 %out_projection.1 = bf16[256,1536]{1,0:T(8,128)(2,1)S(1)} custom-call(s32[3]{0:T(128)S(1)} %pad_add_fusion.pos_ref.refs_0_, bf16[256,384]{1,0:T(8,128)(2,1)S(1)} %attention.3.a_ref, bf16[96,1536]{1,0:T(8,128)(2,1)S(1)} %copy-done.2, bf16[3,2,48,1536]{3,2,1,0:T(8,128)(2,1)S(1)} %pad_maximum_fusion.1.near_ref, ...), custom_call_target="tpu_custom_call" | custom-call | tf_op jit(solution)/shard_map/out_projection/pallas_call | solution.py:276
  77.0 16.4 %all_to_all.25.part_ref = bf16[4,64,1536]{2,1,0:T(8,128)(2,1)S(1)} all-to-all(bf16[4,64,1536]{2,1,0:T(8,128)(2,1)S(1)} %bitcast.30), channel_id=1, replica_groups=mesh['zl'=2,'zp'=2,'core'=2,'tx'=4,'ty'=4,'blk'=2] {'tx'}, dimensions={0} | all-to-all | bytes 1572864 | tf_op jit(solution)/shard_map/all_to_all | solution.py:429
  93.4 0.4 second_norm.1
  93.8 14.9 %all_to_all.26 = bf16[4,64,1536]{2,1,0:T(8,128)(2,1)} all-to-all(bf16[4,64,1536]{2,1,0:T(8,128)(2,1)S(1)} %get-tuple-element.36), channel_id=1, replica_groups=mesh['zl'=2,'zp'=2,'core'=2,'tx'=4,'ty'=4,'blk'=2] {'ty'}, dimensions={0} | all-to-all | bytes 1572864 | tf_op jit(solution)/shard_map/all_to_all | solution.py:431
  108.7 7.7 %feed_forward.1 = bf16[256,1536]{1,0:T(8,128)(2,1)} custom-call(bf16[256,1536]{1,0:T(8,128)(2,1)} %bitcast.41, bf16[2,4,1536,384]{3,2,1,0:T(8,128)(2,1)} %bitcast.38, bf16[2,4,1536,384]{3,2,1,0:T(8,128)(2,1)} %bitcast.39), custom_call_target="tpu_custom_call" | custom-call | tf_op jit(solution)/shard_map/feed_forward/pallas_call | solution.py:340
  116.4 3.6 %all-to-all-start.4 = ((bf16[4,64,1536]{2,1,0:T(8,128)(2,1)}), bf16[4,64,1536]{2,1,0:T(8,128)(2,1)S(1)}, u32[]{:S(2)}, u32[]{:S(2)}) async-start(bf16[4,64,1536]{2,1,0:T(8,128)(2,1)} %bitcast.40), calls=%async_computation.4 | async-start | bytes 1572864 | tf_op jit(solution)/shard_map/all_to_all | solution.py:433
  121.0 8.9 %all-to-all-done.4.part_ref = bf16[4,64,1536]{2,1,0:T(8,128)(2,1)S(1)} async-done(((bf16[4,64,1536]{2,1,0:T(8,128)(2,1)}), bf16[4,64,1536]{2,1,0:T(8,128)(2,1)S(1)}, u32[]{:S(2)}, u32[]{:S(2)}) %all-to-all-start.4) | async-done | bytes 786464 | tf_op jit(solution)/shard_map/all_to_all | solution.py:433
  129.9 1.1 last_stage.1
  131.1 0.6 add.21
  (34 shorter events, 1.2 us)
Async XLA Ops:
  7.2 48.0 %copy-start = (bf16[1,154,2,1536]{3,2,1,0:T(2,128)(2,1)S(1)}, bf16[1,154,2,1536]{3,2,1,0:T(2,128)(2,1)}, u32[]{:S(2)}) copy-start(bf16[1,154,2,1536]{3,2,1,0:T(2,128)(2,1)} %param.14) | copy-start | bytes 2838532
  7.2 101.5 %all-gather.3.cloned.1.call-start = ((), (), s32[]{:S(2)}) async-start(), calls=%async_computation.5 | async-start | bytes 10027008 | tf_op jit(solution)/shard_map/all_gather | solution.py:406
  11.8 28.1 %copy-start.1 = (bf16[1536,3,96]{0,2,1:T(8,128)(2,1)S(1)}, bf16[1536,3,96]{0,2,1:T(8,128)(2,1)}, u32[]{:S(2)}) copy-start(bf16[1536,3,96]{0,2,1:T(8,128)(2,1)} %param.17) | copy-start | bytes 2654212
  11.8 21.9 %all-to-all-start = ((bf16[4,64,1536]{2,1,0:T(8,128)(2,1)}), bf16[4,64,1536]{2,1,0:T(8,128)(2,1)S(1)}, u32[]{:S(2)}, u32[]{:S(2)}) async-start(bf16[4,64,1536]{2,1,0:T(8,128)(2,1)} %get-tuple-element.22), calls=%async_computation | async-start | bytes 1572864 | tf_op jit(solution)/shard_map/all_to_all | solution.py:408
  16.3 10.2 %collective-permute-start = (bf16[2,48,1536]{2,1,0:T(8,128)(2,1)}, bf16[2,48,1536]{2,1,0:T(8,128)(2,1)S(1)}, u32[]{:S(2)}, u32[]{:S(2)}) collective-permute-start(bf16[2,48,1536]{2,1,0:T(8,128)(2,1)} %get-tuple-element.21), channel_id=1, source_target_pairs={{0,2},{2,4},{4,6},{6,0},{1,3},{3,5},{5,7},{7,1},{8,10},{10,12},{12... | collective-permute-start | bytes 884744 | tf_op jit(solution)/shard_map/ppermute | solution.py:399
  17.8 10.2 %collective-permute-start.1 = (bf16[2,48,1536]{2,1,0:T(8,128)(2,1)}, bf16[2,48,1536]{2,1,0:T(8,128)(2,1)S(1)}, u32[]{:S(2)}, u32[]{:S(2)}) collective-permute-start(bf16[2,48,1536]{2,1,0:T(8,128)(2,1)} %get-tuple-element.21), channel_id=1, source_target_pairs={{0,6},{2,0},{4,2},{6,4},{1,7},{3,1},{5,3},{7,5},{8,14},{10,8},{12,... | collective-permute-start | bytes 884744 | tf_op jit(solution)/shard_map/ppermute | solution.py:399
  19.5 14.2 %collective-permute-start.2 = (bf16[2,48,1536]{2,1,0:T(8,128)(2,1)}, bf16[2,48,1536]{2,1,0:T(8,128)(2,1)S(1)}, u32[]{:S(2)}, u32[]{:S(2)}) collective-permute-start(bf16[2,48,1536]{2,1,0:T(8,128)(2,1)} %get-tuple-element.21), channel_id=1, source_target_pairs={{0,4},{2,6},{4,0},{6,2},{1,5},{3,7},{5,1},{7,3},{8,12},{10,14},{12... | collective-permute-start | bytes 884744 | tf_op jit(solution)/shard_map/ppermute | solution.py:399
  26.5 7.2 %copy-start.5 = (bf16[2,48,1536]{2,1,0:T(8,128)(2,1)}, bf16[2,48,1536]{2,1,0:T(8,128)(2,1)S(1)}, u32[]{:S(2)}) copy-start(bf16[2,48,1536]{2,1,0:T(8,128)(2,1)S(1)} %collective-permute-done) | copy-start | bytes 884740
  28.0 5.7 %copy-start.6 = (bf16[2,48,1536]{2,1,0:T(8,128)(2,1)}, bf16[2,48,1536]{2,1,0:T(8,128)(2,1)S(1)}, u32[]{:S(2)}) copy-start(bf16[2,48,1536]{2,1,0:T(8,128)(2,1)S(1)} %collective-permute-done.1) | copy-start | bytes 884740
  33.7 0.7 copy-start.7
  35.7 4.3 %collective-permute-start.3 = (bf16[3,2,48,1536]{3,2,1,0:T(8,128)(2,1)S(1)}, bf16[3,2,48,1536]{3,2,1,0:T(8,128)(2,1)}, u32[]{:S(2)}, u32[]{:S(2)}) collective-permute-start(bf16[3,2,48,1536]{3,2,1,0:T(8,128)(2,1)S(1)} %pad_maximum_fusion.near_ref), channel_id=1, source_target_pairs={{0,32},{32,0},{1,33},{33,1},{2,34},{34,2},{3,35},{35,3},{4,36},{36... | collective-permute-start | bytes 2654216 | tf_op jit(solution)/shard_map/ppermute | solution.py:412
  35.8 12.4 %collective-permute-start.4 = (bf16[2,48,1536]{2,1,0:T(8,128)(2,1)}, bf16[2,48,1536]{2,1,0:T(8,128)(2,1)}, u32[]{:S(2)}, u32[]{:S(2)}) collective-permute-start(bf16[2,48,1536]{2,1,0:T(8,128)(2,1)} %get-tuple-element.29), channel_id=1, source_target_pairs={{0,2},{2,4},{4,6},{6,0},{1,3},{3,5},{5,7},{7,1},{8,10},{10,12},{12... | collective-permute-start | bytes 884744 | tf_op jit(solution)/shard_map/ppermute | solution.py:399
  37.0 15.5 %collective-permute-start.5 = (bf16[2,48,1536]{2,1,0:T(8,128)(2,1)}, bf16[2,48,1536]{2,1,0:T(8,128)(2,1)}, u32[]{:S(2)}, u32[]{:S(2)}) collective-permute-start(bf16[2,48,1536]{2,1,0:T(8,128)(2,1)} %get-tuple-element.29), channel_id=1, source_target_pairs={{0,6},{2,0},{4,2},{6,4},{1,7},{3,1},{5,3},{7,5},{8,14},{10,8},{12,... | collective-permute-start | bytes 884744 | tf_op jit(solution)/shard_map/ppermute | solution.py:399
  39.1 14.5 %collective-permute-start.6 = (bf16[2,48,1536]{2,1,0:T(8,128)(2,1)}, bf16[2,48,1536]{2,1,0:T(8,128)(2,1)}, u32[]{:S(2)}, u32[]{:S(2)}) collective-permute-start(bf16[2,48,1536]{2,1,0:T(8,128)(2,1)} %get-tuple-element.29), channel_id=1, source_target_pairs={{0,4},{2,6},{4,0},{6,2},{1,5},{3,7},{5,1},{7,3},{8,12},{10,14},{12... | collective-permute-start | bytes 884744 | tf_op jit(solution)/shard_map/ppermute | solution.py:399
  43.4 26.6 %all-to-all-start.1 = ((bf16[4,2,256,384]{3,2,1,0:T(8,128)(2,1)}), bf16[4,2,256,384]{3,2,1,0:T(8,128)(2,1)}, u32[]{:S(2)}, u32[]{:S(2)}) async-start(bf16[4,2,256,384]{3,2,1,0:T(8,128)(2,1)} %project.2.refs_1_), calls=%async_computation.1 | async-start | bytes 3145728 | tf_op jit(solution)/shard_map/all_to_all | solution.py:416
  54.9 2.9 %collective-permute-start.7 = (bf16[3,2,48,1536]{3,2,1,0:T(8,128)(2,1)S(1)}, bf16[3,2,48,1536]{3,2,1,0:T(8,128)(2,1)}, u32[]{:S(2)}, u32[]{:S(2)}) collective-permute-start(bf16[3,2,48,1536]{3,2,1,0:T(8,128)(2,1)S(1)} %pad_maximum_fusion.1.near_ref), channel_id=1, source_target_pairs={{0,32},{32,0},{1,33},{33,1},{2,34},{34,2},{3,35},{35,3},{4,36},{36... | collective-permute-start | bytes 2654216 | tf_op jit(solution)/shard_map/ppermute | solution.py:421
  63.2 12.0 %copy-start.2 = (bf16[96,1536]{1,0:T(8,128)(2,1)S(1)}, bf16[96,1536]{1,0:T(8,128)(2,1)}, u32[]{:S(2)}) copy-start(bf16[96,1536]{1,0:T(8,128)(2,1)} %own_ref.1) | copy-start | bytes 884740
  75.1 18.3 %copy-start.3 = (bf16[1,64,1536]{2,1,0:T(8,128)(2,1)S(1)}, bf16[1,64,1536]{2,1,0:T(8,128)(2,1)}, u32[]{:S(2)}) copy-start(bf16[1,64,1536]{2,1,0:T(8,128)(2,1)} %param.11) | copy-start | bytes 589828
  75.1 18.3 %copy-start.4 = (f32[1,8,1536]{2,1,0:T(8,128)S(1)}, f32[1,8,1536]{2,1,0:T(8,128)}, u32[]{:S(2)}) copy-start(f32[1,8,1536]{2,1,0:T(8,128)} %param.13) | copy-start | bytes 147460
  116.4 4.3 %copy-start.8 = (bf16[1536,64]{0,1:T(8,128)(2,1)S(1)}, bf16[1536,64]{0,1:T(8,128)(2,1)}, u32[]{:S(2)}) copy-start(bf16[1536,64]{0,1:T(8,128)(2,1)} %param.21) | copy-start | bytes 589828
  116.4 14.7 %copy-start.9 = (f32[1,32,128]{2,1,0:T(8,128)S(1)}, f32[1,32,128]{2,1,0:T(8,128)}, u32[]{:S(2)}) copy-start(f32[1,32,128]{2,1,0:T(8,128)} %param.12) | copy-start | bytes 49156
  116.4 13.6 %all-to-all-start.4 = ((bf16[4,64,1536]{2,1,0:T(8,128)(2,1)}), bf16[4,64,1536]{2,1,0:T(8,128)(2,1)S(1)}, u32[]{:S(2)}, u32[]{:S(2)}) async-start(bf16[4,64,1536]{2,1,0:T(8,128)(2,1)} %bitcast.40), calls=%async_computation.4 | async-start | bytes 1572864 | tf_op jit(solution)/shard_map/all_to_all | solution.py:433
Sparse Core Ops, SparseCore 0:
  11.9 60.9 all-gather.2

commit v10 on v9

--- a/solution.py
+++ b/solution.py
@@ -34,33 +34,13 @@
 
 
 def first_kernel(
-    pos_ref,
-    x_ref,
-    mod_ref,
-    up_ref,
-    down_ref,
-    qkv_ref,
-    wout_ref,
-    h_ref,
-    kv_ref,
-    qo_ref,
-    pack_ref,
-    held,
-    load_sem,
-    store_sem,
-    half_sem,
+    copies, pos_ref, x_ref, mod_ref, up_ref, down_ref, out_ref, pack_ref, held, load_sem, store_sem
 ):
     core = pos_ref[0]
     zone = pos_ref[1]
     part = down_ref.shape[0]
 
-    def move(core_here, sources):
-        mine = pl.ds(core_here * 48, 48)
-        halves = [
-            pltpu.make_async_copy(qkv_ref.at[pl.ds(1, 2), mine, :], kv_ref, half_sem.at[0]),
-            pltpu.make_async_copy(qkv_ref.at[0, mine, :], qo_ref.at[0], half_sem.at[1]),
-            pltpu.make_async_copy(wout_ref.at[mine, :], qo_ref.at[1], half_sem.at[2]),
-        ]
+    def move(sources):
         loads = []
         stores = []
         for i, source in enumerate(sources):
@@ -69,53 +49,52 @@
             stores.append(
                 pltpu.make_async_copy(held.at[rows, :], pack_ref.at[rows, :], store_sem.at[i])
             )
-        for copy in loads + halves:
-            copy.start()
+        for load in loads:
+            load.start()
         h = layer_norm(x_ref[...].astype(F32), mod_ref[0:1, :], mod_ref[1:2, :]).astype(BF)
-        for i in range(h_ref.shape[0]):
-            h_ref[i] = h
+        for i in range(copies):
+            out_ref[i] = h
         for load, store in zip(loads, stores):
             load.wait()
             store.start()
-        for copy in halves + stores:
-            copy.wait()
+        for store in stores:
+            store.wait()
 
     for half in range(2):
 
         @pl.when(jnp.logical_and(core == 0, zone == half))
         def _():
-            move(0, [up_ref.at[pl.ds((2 * half + i) * part, part), :] for i in range(2)])
+            move([up_ref.at[pl.ds((2 * half + i) * part, part), :] for i in range(2)])
 
         @pl.when(jnp.logical_and(core == 1, zone == half))
         def _():
-            move(1, [down_ref.at[:, pl.ds((2 * half + i) * part, part)] for i in range(2)])
-
-
-def first_stage(pos, tokens, mods, w_up, w_down, own_qkv, w_out, copies):
+            move([down_ref.at[:, pl.ds((2 * half + i) * part, part)] for i in range(2)])
+
+
+def first_norm_and_pack(pos, tokens, mods, w_up, w_down, copies):
     rows, width = tokens.shape
     part = w_down.shape[0]
     return pl.pallas_call(
-        first_kernel,
+        functools.partial(first_kernel, copies),
         out_shape=[
             jax.ShapeDtypeStruct((copies, rows, width), BF),
-            jax.ShapeDtypeStruct((2, 48, width), BF),
-            jax.ShapeDtypeStruct((2, 48, width), BF),
             jax.ShapeDtypeStruct((2 * part, part), BF),
         ],
         in_specs=[pl.BlockSpec(memory_space=pltpu.SMEM)]
         + [pl.BlockSpec(memory_space=pltpu.VMEM)] * 2
-        + [pl.BlockSpec(memory_space=pltpu.HBM)] * 4,
-        out_specs=[pl.BlockSpec(memory_space=pltpu.VMEM)] * 3
-        + [pl.BlockSpec(memory_space=pltpu.HBM)],
+        + [pl.BlockSpec(memory_space=pltpu.HBM)] * 2,
+        out_specs=[
+            pl.BlockSpec(memory_space=pltpu.VMEM),
+            pl.BlockSpec(memory_space=pltpu.HBM),
+        ],
         scratch_shapes=[
             pltpu.VMEM((2 * part, part), BF),
             pltpu.SemaphoreType.DMA((2,)),
             pltpu.SemaphoreType.DMA((2,)),
-            pltpu.SemaphoreType.DMA((3,)),
         ],
         compiler_params=params(58),
-        name="first_stage",
-    )(pos, tokens, mods, w_up, w_down, own_qkv, w_out)
+        name="first_norm_and_pack",
+    )(pos, tokens, mods, w_up, w_down)
 
 
 def assemble(pos_ref, own_ref, near_ref, far_ref, store):
@@ -399,18 +378,22 @@
         return lax.ppermute(value, "ty", [(i, (i + step) % 4) for i in range(4)])
 
     own_qkv = jnp.transpose(w_qkv, (1, 2, 0))
+    half_kv = lax.dynamic_slice(own_qkv, (1, core * 48, 0), (2, 48, width))
+    near_kv = [to_lines(half_kv, step) for step in STRIDES]
     place = jnp.stack([core, lax.axis_index("zp")]).astype(jnp.int32)
-    h1, half_kv, half_qo, quarter = first_stage(
-        place, tokens, mods, w_up, w_down, own_qkv, w_out, 4
-    )
+    h1, quarter = first_norm_and_pack(place, tokens, mods, w_up, w_down, 4)
     ffn_full = lax.all_gather(quarter, ("core", "tx", "zp"), axis=0, tiled=False)
     ffn_full = ffn_full.reshape(2, 4, width, w_up.shape[1])
     h1 = lax.all_to_all(h1, "tx", split_axis=0, concat_axis=0, tiled=True)
-    near_kv = [to_lines(half_kv, step) for step in STRIDES]
-    *near_kv, h1 = lax.optimization_barrier((*near_kv, h1))
-    stacked, half_qo = lax.optimization_barrier((jnp.stack(near_kv), half_qo))
+
+    half_q = lax.dynamic_slice(own_qkv, (0, core * 48, 0), (1, 48, width))
+    half_out = lax.dynamic_slice(w_out, (core * 48, 0), (48, width))
+    half_qo = jnp.concatenate([half_q, half_out[None]])
+    near_qo = [to_lines(half_qo, step) for step in STRIDES[:2]]
+    *near, h1, half_qo = lax.optimization_barrier((*near_kv, *near_qo, h1, half_qo))
+    stacked, half_qo = lax.optimization_barrier((jnp.stack(near[:3]), half_qo))
     far_kv = lax.ppermute(stacked, "core", swap2)
-    near_qo = [to_lines(half_qo, step) for step in STRIDES]
+    near_qo = [*near[3:], to_lines(half_qo, STRIDES[2])]
     h1 = h1.reshape(4 * rows, width)
     own_kv = project(pos, h1, own_qkv, 1, 2, 4, stacked, far_kv)
     all_kv = lax.all_to_all(own_kv, "ty", split_axis=0, concat_axis=0, tiled=True)

time: 139 us -> 141 us (1.014)
  waiting for transfers between devices: 35.9 us -> 38.6 us
  blocking collectives: 31.3 us -> 28.7 us
    ppermute x6, waiting for transfers between devices: 17.7 us -> 11.3 us  [to_lines(): return lax.ppermute(value, 'ty', [(i, (i + step) % 4) for i in range(4)])]
    all_to_all x1, waiting for transfers between devices: 6.86 us -> 11 us  [on_device(): lax.all_to_all(own_kv, 'ty', split_axis=0, concat_axis=0, tiled=True)]
    all_to_all x1, waiting for transfers between devices: 0.01 us -> 3.39 us  [on_device(): h1 = lax.all_to_all(h1, 'tx', split_axis=0, concat_axis=0, tiled=True)]
    all_to_all x1, blocking collectives: 16.4 us -> 14.5 us  [on_device(): lax.all_to_all(partial, 'tx', split_axis=0, concat_axis=0, tiled=True)]
    ppermute x1, waiting for transfers between devices: 0.01 us -> 1.66 us  [on_device(): far_kv = lax.ppermute(stacked, 'core', swap2)]
  transfers between devices with their start and end apart: 12 -> 12, of which waited for: 8 -> 8; matrix products, arithmetic and copies ran while one was open for 2% -> 3% of each run, Pallas kernels for 12% -> 12%
where the time goes in v10:
time: 141 us; the launch traced here: 139 us
  waiting for transfers between devices  38.6 us (27%)
  blocking collectives  28.7 us (20%)
  Pallas kernels  28.6 us (20%)
  starting transfers between devices  21.3 us (15%)
  between operations  15.7 us (11%)
  other arithmetic  4.58 us (3%)
  local copies, waits for them, and re-layouts  2.02 us (1%)
    all_to_all x1, blocking collectives, on_device(): lax.all_to_all(partial, 'tx', split_axis=0, concat_axis=0, tiled=True)  14.5 us
    all_to_all x1, blocking collectives, on_device(): h2 = lax.all_to_all(h2, 'ty', split_axis=0, concat_axis=0, tiled=True)  14.2 us
    ppermute x6, waiting for transfers between devices, to_lines(): return lax.ppermute(value, 'ty', [(i, (i + step) % 4) for i in range(4)])  11.3 us
    all_to_all x1, waiting for transfers between devices, on_device(): lax.all_to_all(own_kv, 'ty', split_axis=0, concat_axis=0, tiled=True)  11 us
    all_to_all x1, waiting for transfers between devices, on_device(): lax.all_to_all(partial, 'ty', split_axis=0, concat_axis=0, tiled=True)  8.89 us
    ppermute x6, starting transfers between devices, to_lines(): return lax.ppermute(value, 'ty', [(i, (i + step) % 4) for i in range(4)])  8.61 us
    pallas_call x2, Pallas kernels, attention(): pl.pallas_call(functools.partial(attention_kernel, own), out_shape=out, i...  8.59 us
    pallas_call x1, Pallas kernels, feed_forward(): pl.pallas_call(ffn_kernel, grid=(4,), out_shape=jax.ShapeDtypeStruct((row...  7.65 us
  transfers between devices with their start and end apart: 12, of which 8 were waited for; matrix products, arithmetic and copies ran while one was open for 3% of the time, Pallas kernels for 12%

profile of v10, /device:TPU:128, one launch (start us, length us, event | category | flops | bytes accessed | tf_op | source)
XLA Modules:
  0.0 139.4 jit_solution(315828956762279197)
XLA Ops:
  7.8 3.7 %first_norm_and_pack.1 = (bf16[4,64,1536]{2,1,0:T(8,128)(2,1)}, bf16[768,384]{1,0:T(8,128)(2,1)}) custom-call(s32[2]{0:T(128)} %pad_add_fusion.1.pos_ref, bf16[64,1536]{1,0:T(8,128)(2,1)} %bitcast.37, f32[8,1536]{1,0:T(8,128)} %bitcast.40, bf16[1536,384]{1,0:T(8,128)(2,1)} %up_ref.1, bf16[384,1536]{1,0:T(8,128)(2,1)} %down_ref.1), custom_call_target="tpu_custom_call" | custom-call | tf_op jit(solution)/shard_map/first_norm_and_pack/pallas_call | solution.py:77
  11.6 0.7 dynamic-slice_bitcast_fusion
  12.3 1.6 %collective-permute-start = (bf16[2,48,1536]{2,1,0:T(8,128)(2,1)}, bf16[2,48,1536]{2,1,0:T(8,128)(2,1)S(1)}, u32[]{:S(2)}, u32[]{:S(2)}) collective-permute-start(bf16[2,48,1536]{2,1,0:T(8,128)(2,1)} %dynamic-slice_bitcast_fusion), channel_id=1, source_target_pairs={{0,2},{2,4},{4,6},{6,0},{1,3},{3,5},{5,7},{7,1},{8,10},{10,12},{12... | collective-permute-start | bytes 884744 | tf_op jit(solution)/shard_map/ppermute | solution.py:378
  13.9 1.7 %collective-permute-start.1 = (bf16[2,48,1536]{2,1,0:T(8,128)(2,1)}, bf16[2,48,1536]{2,1,0:T(8,128)(2,1)S(1)}, u32[]{:S(2)}, u32[]{:S(2)}) collective-permute-start(bf16[2,48,1536]{2,1,0:T(8,128)(2,1)} %dynamic-slice_bitcast_fusion), channel_id=1, source_target_pairs={{0,6},{2,0},{4,2},{6,4},{1,7},{3,1},{5,3},{7,5},{8,14},{10,8},{12,... | collective-permute-start | bytes 884744 | tf_op jit(solution)/shard_map/ppermute | solution.py:378
  15.6 2.0 %collective-permute-start.2 = (bf16[2,48,1536]{2,1,0:T(8,128)(2,1)}, bf16[2,48,1536]{2,1,0:T(8,128)(2,1)}, u32[]{:S(2)}, u32[]{:S(2)}) collective-permute-start(bf16[2,48,1536]{2,1,0:T(8,128)(2,1)} %dynamic-slice_bitcast_fusion), channel_id=1, source_target_pairs={{0,4},{2,6},{4,0},{6,2},{1,5},{3,7},{5,1},{7,3},{8,12},{10,14},{12... | collective-permute-start | bytes 884744 | tf_op jit(solution)/shard_map/ppermute | solution.py:378
  17.6 4.3 %all-to-all-start = ((bf16[4,64,1536]{2,1,0:T(8,128)(2,1)}), bf16[4,64,1536]{2,1,0:T(8,128)(2,1)S(1)}, u32[]{:S(2)}, u32[]{:S(2)}) async-start(bf16[4,64,1536]{2,1,0:T(8,128)(2,1)} %get-tuple-element.22), calls=%async_computation | async-start | bytes 1572864 | tf_op jit(solution)/shard_map/all_to_all | solution.py:387
  21.9 0.8 pad_maximum_fusion.2
  22.7 0.7 collective-permute-start.3
  23.4 2.6 %collective-permute-start.4 = (bf16[2,48,1536]{2,1,0:T(8,128)(2,1)}, bf16[2,48,1536]{2,1,0:T(8,128)(2,1)}, u32[]{:S(2)}, u32[]{:S(2)}) collective-permute-start(bf16[2,48,1536]{2,1,0:T(8,128)(2,1)} %pad_maximum_fusion.2), channel_id=1, source_target_pairs={{0,6},{2,0},{4,2},{6,4},{1,7},{3,1},{5,3},{7,5},{8,14},{10,8},{12,... | collective-permute-start | bytes 884744 | tf_op jit(solution)/shard_map/ppermute | solution.py:378
  25.9 5.4 %collective-permute-done.2 = bf16[2,48,1536]{2,1,0:T(8,128)(2,1)} collective-permute-done((bf16[2,48,1536]{2,1,0:T(8,128)(2,1)}, bf16[2,48,1536]{2,1,0:T(8,128)(2,1)}, u32[]{:S(2)}, u32[]{:S(2)}) %collective-permute-start.2) | collective-permute-done | bytes 294944 | tf_op jit(solution)/shard_map/ppermute | solution.py:378
  31.4 5.0 %collective-permute-done.3 = bf16[2,48,1536]{2,1,0:T(8,128)(2,1)S(1)} collective-permute-done((bf16[2,48,1536]{2,1,0:T(8,128)(2,1)}, bf16[2,48,1536]{2,1,0:T(8,128)(2,1)S(1)}, u32[]{:S(2)}, u32[]{:S(2)}) %collective-permute-start.3) | collective-permute-done | bytes 294944 | tf_op jit(solution)/shard_map/ppermute | solution.py:378
  36.4 0.7 copy-done.6
  37.1 3.4 %all-to-all-done = bf16[4,64,1536]{2,1,0:T(8,128)(2,1)S(1)} async-done(((bf16[4,64,1536]{2,1,0:T(8,128)(2,1)}), bf16[4,64,1536]{2,1,0:T(8,128)(2,1)S(1)}, u32[]{:S(2)}, u32[]{:S(2)}) %all-to-all-start) | async-done | bytes 786464 | tf_op jit(solution)/shard_map/all_to_all | solution.py:387
  40.5 1.3 pad_maximum_fusion.near_ref
  42.7 1.7 %collective-permute-done.5.far_ref = bf16[3,2,48,1536]{3,2,1,0:T(8,128)(2,1)} collective-permute-done((bf16[3,2,48,1536]{3,2,1,0:T(8,128)(2,1)S(1)}, bf16[3,2,48,1536]{3,2,1,0:T(8,128)(2,1)}, u32[]{:S(2)}, u32[]{:S(2)}) %collective-permute-start.5) | collective-permute-done | bytes 884768 | tf_op jit(solution)/shard_map/ppermute | solution.py:395
  44.4 3.5 %project.2.refs_1_ = bf16[4,2,256,384]{3,2,1,0:T(8,128)(2,1)} custom-call(s32[3]{0:T(128)S(1)} %pad_add_fusion.pos_ref.refs_0_, bf16[256,1536]{1,0:T(8,128)(2,1)S(1)} %bitcast.31, bf16[3,96,1536]{2,1,0:T(8,128)(2,1)S(1)} %bitcast.33, bf16[3,2,48,1536]{3,2,1,0:T(8,128)(2,1)S(1)} %pad_maximum_fusion.near_ref, ...), custom_call_target="tpu_custom_call" | custom-call | tf_op jit(solution)/shard_map/project/pallas_call | solution.py:133
  47.9 4.4 %all-to-all-start.1 = ((bf16[4,2,256,384]{3,2,1,0:T(8,128)(2,1)}), bf16[4,2,256,384]{3,2,1,0:T(8,128)(2,1)}, u32[]{:S(2)}, u32[]{:S(2)}) async-start(bf16[4,2,256,384]{3,2,1,0:T(8,128)(2,1)} %project.2.refs_1_), calls=%async_computation.1 | async-start | bytes 3145728 | tf_op jit(solution)/shard_map/all_to_all | solution.py:399
  52.2 0.9 collective-permute-done.6
  53.1 1.3 pad_maximum_fusion.1.near_ref
  54.9 2.3 %collective-permute-done.7.far_ref = bf16[3,2,48,1536]{3,2,1,0:T(8,128)(2,1)} collective-permute-done((bf16[3,2,48,1536]{3,2,1,0:T(8,128)(2,1)S(1)}, bf16[3,2,48,1536]{3,2,1,0:T(8,128)(2,1)}, u32[]{:S(2)}, u32[]{:S(2)}) %collective-permute-start.7) | collective-permute-done | bytes 884768 | tf_op jit(solution)/shard_map/ppermute | solution.py:404
  57.2 1.8 %project.3 = bf16[1,1,256,384]{3,2,1,0:T(8,128)(2,1)S(1)} custom-call(s32[3]{0:T(128)S(1)} %pad_add_fusion.pos_ref.refs_0_, bf16[256,1536]{1,0:T(8,128)(2,1)S(1)} %bitcast.32, bf16[3,96,1536]{2,1,0:T(8,128)(2,1)S(1)} %bitcast.34, bf16[3,2,48,1536]{3,2,1,0:T(8,128)(2,1)S(1)} %pad_maximum_fusion.1.near_ref, bf16[3,2,48,1536]{3,2,1,0:T(8,128)(2,1)} %collective-permute-done.7.far_ref), custom_call_target="tpu_custom_call" | custom-call | tf_op jit(solution)/shard_map/project/pallas_call | solution.py:133
  59.0 3.5 %attention.2.refs_2_ = f32[256,896]{1,0:T(8,128)S(1)} custom-call(s32[3]{0:T(128)S(1)} %pad_add_fusion.pos_ref.refs_0_, bf16[4,2,256,384]{3,2,1,0:T(8,128)(2,1)} %project.2.refs_1_, bf16[256,384]{1,0:T(8,128)(2,1)S(1)} %bitcast.39, bf16[2,154,384]{2,1,0:T(8,128)(2,1)S(1)} %bitcast.36), custom_call_target="tpu_custom_call" | custom-call | tf_op jit(solution)/shard_map/attention/pallas_call | solution.py:228
  62.6 11.0 %all-to-all-done.1.refs_1_ = bf16[4,2,256,384]{3,2,1,0:T(8,128)(2,1)} async-done(((bf16[4,2,256,384]{3,2,1,0:T(8,128)(2,1)}), bf16[4,2,256,384]{3,2,1,0:T(8,128)(2,1)}, u32[]{:S(2)}, u32[]{:S(2)}) %all-to-all-start.1) | async-done | bytes 1572896 | tf_op jit(solution)/shard_map/all_to_all | solution.py:399
  73.6 5.0 %attention.3.a_ref = bf16[256,384]{1,0:T(8,128)(2,1)S(1)} custom-call(s32[3]{0:T(128)S(1)} %pad_add_fusion.pos_ref.refs_0_, bf16[4,2,256,384]{3,2,1,0:T(8,128)(2,1)} %all-to-all-done.1.refs_1_, f32[256,896]{1,0:T(8,128)S(1)} %attention.2.refs_2_), custom_call_target="tpu_custom_call" | custom-call | tf_op jit(solution)/shard_map/attention/pallas_call | solution.py:228
  78.7 1.9 %out_projection.1 = bf16[256,1536]{1,0:T(8,128)(2,1)S(1)} custom-call(s32[3]{0:T(128)S(1)} %pad_add_fusion.pos_ref.refs_0_, bf16[256,384]{1,0:T(8,128)(2,1)S(1)} %attention.3.a_ref, bf16[96,1536]{1,0:T(8,128)(2,1)S(1)} %copy-done.4, bf16[3,2,48,1536]{3,2,1,0:T(8,128)(2,1)S(1)} %pad_maximum_fusion.1.near_ref, ...), custom_call_target="tpu_custom_call" | custom-call | tf_op jit(solution)/shard_map/out_projection/pallas_call | solution.py:255
  80.6 14.5 %all_to_all.25.part_ref = bf16[4,64,1536]{2,1,0:T(8,128)(2,1)S(1)} all-to-all(bf16[4,64,1536]{2,1,0:T(8,128)(2,1)S(1)} %bitcast.35), channel_id=1, replica_groups=mesh['zl'=2,'zp'=2,'core'=2,'tx'=4,'ty'=4,'blk'=2] {'tx'}, dimensions={0} | all-to-all | bytes 1572864 | tf_op jit(solution)/shard_map/all_to_all | solution.py:412
  95.4 14.2 %all_to_all.26 = bf16[4,64,1536]{2,1,0:T(8,128)(2,1)} all-to-all(bf16[4,64,1536]{2,1,0:T(8,128)(2,1)S(1)} %get-tuple-element.38), channel_id=1, replica_groups=mesh['zl'=2,'zp'=2,'core'=2,'tx'=4,'ty'=4,'blk'=2] {'ty'}, dimensions={0} | all-to-all | bytes 1572864 | tf_op jit(solution)/shard_map/all_to_all | solution.py:414
  109.6 7.6 %feed_forward.1 = bf16[256,1536]{1,0:T(8,128)(2,1)} custom-call(bf16[256,1536]{1,0:T(8,128)(2,1)} %bitcast.46, bf16[2,4,1536,384]{3,2,1,0:T(8,128)(2,1)} %bitcast.43, bf16[2,4,1536,384]{3,2,1,0:T(8,128)(2,1)} %bitcast.44), custom_call_target="tpu_custom_call" | custom-call | tf_op jit(solution)/shard_map/feed_forward/pallas_call | solution.py:319
  117.3 3.6 %all-to-all-start.4 = ((bf16[4,64,1536]{2,1,0:T(8,128)(2,1)}), bf16[4,64,1536]{2,1,0:T(8,128)(2,1)S(1)}, u32[]{:S(2)}, u32[]{:S(2)}) async-start(bf16[4,64,1536]{2,1,0:T(8,128)(2,1)} %bitcast.45), calls=%async_computation.4 | async-start | bytes 1572864 | tf_op jit(solution)/shard_map/all_to_all | solution.py:416
  121.9 8.9 %all-to-all-done.4.part_ref = bf16[4,64,1536]{2,1,0:T(8,128)(2,1)S(1)} async-done(((bf16[4,64,1536]{2,1,0:T(8,128)(2,1)}), bf16[4,64,1536]{2,1,0:T(8,128)(2,1)S(1)}, u32[]{:S(2)}, u32[]{:S(2)}) %all-to-all-start.4) | async-done | bytes 786464 | tf_op jit(solution)/shard_map/all_to_all | solution.py:416
  130.8 1.1 last_stage.1
  132.0 0.6 add.27
  (40 shorter events, 2.2 us)
Async XLA Ops:
  7.2 47.5 %copy-start = (bf16[1,154,2,1536]{3,2,1,0:T(2,128)(2,1)S(1)}, bf16[1,154,2,1536]{3,2,1,0:T(2,128)(2,1)}, u32[]{:S(2)}) copy-start(bf16[1,154,2,1536]{3,2,1,0:T(2,128)(2,1)} %param.14) | copy-start | bytes 2838532
  7.2 102.5 %all-gather.3.cloned.1.call-start = ((), (), s32[]{:S(2)}) async-start(), calls=%async_computation.5 | async-start | bytes 10027008 | tf_op jit(solution)/shard_map/all_gather | solution.py:385
  7.8 3.8 %copy-start.1 = (bf16[1536,3,96]{0,2,1:T(8,128)(2,1)S(1)}, bf16[1536,3,96]{0,2,1:T(8,128)(2,1)}, u32[]{:S(2)}) copy-start(bf16[1536,3,96]{0,2,1:T(8,128)(2,1)} %param.17) | copy-start | bytes 2654212
  11.6 10.3 %copy-start.3 = (bf16[96,1536]{1,0:T(8,128)(2,1)S(1)}, bf16[96,1536]{1,0:T(8,128)(2,1)}, u32[]{:S(2)}) copy-start(bf16[96,1536]{1,0:T(8,128)(2,1)} %own_ref.1) | copy-start | bytes 884740
  12.3 13.6 %collective-permute-start = (bf16[2,48,1536]{2,1,0:T(8,128)(2,1)}, bf16[2,48,1536]{2,1,0:T(8,128)(2,1)S(1)}, u32[]{:S(2)}, u32[]{:S(2)}) collective-permute-start(bf16[2,48,1536]{2,1,0:T(8,128)(2,1)} %dynamic-slice_bitcast_fusion), channel_id=1, source_target_pairs={{0,2},{2,4},{4,6},{6,0},{1,3},{3,5},{5,7},{7,1},{8,10},{10,12},{12... | collective-permute-start | bytes 884744 | tf_op jit(solution)/shard_map/ppermute | solution.py:378
  13.9 12.0 %collective-permute-start.1 = (bf16[2,48,1536]{2,1,0:T(8,128)(2,1)}, bf16[2,48,1536]{2,1,0:T(8,128)(2,1)S(1)}, u32[]{:S(2)}, u32[]{:S(2)}) collective-permute-start(bf16[2,48,1536]{2,1,0:T(8,128)(2,1)} %dynamic-slice_bitcast_fusion), channel_id=1, source_target_pairs={{0,6},{2,0},{4,2},{6,4},{1,7},{3,1},{5,3},{7,5},{8,14},{10,8},{12,... | collective-permute-start | bytes 884744 | tf_op jit(solution)/shard_map/ppermute | solution.py:378
  15.6 15.8 %collective-permute-start.2 = (bf16[2,48,1536]{2,1,0:T(8,128)(2,1)}, bf16[2,48,1536]{2,1,0:T(8,128)(2,1)}, u32[]{:S(2)}, u32[]{:S(2)}) collective-permute-start(bf16[2,48,1536]{2,1,0:T(8,128)(2,1)} %dynamic-slice_bitcast_fusion), channel_id=1, source_target_pairs={{0,4},{2,6},{4,0},{6,2},{1,5},{3,7},{5,1},{7,3},{8,12},{10,14},{12... | collective-permute-start | bytes 884744 | tf_op jit(solution)/shard_map/ppermute | solution.py:378
  17.6 22.9 %all-to-all-start = ((bf16[4,64,1536]{2,1,0:T(8,128)(2,1)}), bf16[4,64,1536]{2,1,0:T(8,128)(2,1)S(1)}, u32[]{:S(2)}, u32[]{:S(2)}) async-start(bf16[4,64,1536]{2,1,0:T(8,128)(2,1)} %get-tuple-element.22), calls=%async_computation | async-start | bytes 1572864 | tf_op jit(solution)/shard_map/all_to_all | solution.py:387
  22.7 13.7 %collective-permute-start.3 = (bf16[2,48,1536]{2,1,0:T(8,128)(2,1)}, bf16[2,48,1536]{2,1,0:T(8,128)(2,1)S(1)}, u32[]{:S(2)}, u32[]{:S(2)}) collective-permute-start(bf16[2,48,1536]{2,1,0:T(8,128)(2,1)} %pad_maximum_fusion.2), channel_id=1, source_target_pairs={{0,2},{2,4},{4,6},{6,0},{1,3},{3,5},{5,7},{7,1},{8,10},{10,12},{12... | collective-permute-start | bytes 884744 | tf_op jit(solution)/shard_map/ppermute | solution.py:378
  23.4 13.7 %collective-permute-start.4 = (bf16[2,48,1536]{2,1,0:T(8,128)(2,1)}, bf16[2,48,1536]{2,1,0:T(8,128)(2,1)}, u32[]{:S(2)}, u32[]{:S(2)}) collective-permute-start(bf16[2,48,1536]{2,1,0:T(8,128)(2,1)} %pad_maximum_fusion.2), channel_id=1, source_target_pairs={{0,6},{2,0},{4,2},{6,4},{1,7},{3,1},{5,3},{7,5},{8,14},{10,8},{12,... | collective-permute-start | bytes 884744 | tf_op jit(solution)/shard_map/ppermute | solution.py:378
  25.9 14.6 %copy-start.7 = (bf16[2,48,1536]{2,1,0:T(8,128)(2,1)}, bf16[2,48,1536]{2,1,0:T(8,128)(2,1)S(1)}, u32[]{:S(2)}) copy-start(bf16[2,48,1536]{2,1,0:T(8,128)(2,1)S(1)} %collective-permute-done) | copy-start | bytes 884740
  25.9 14.6 %copy-start.8 = (bf16[2,48,1536]{2,1,0:T(8,128)(2,1)}, bf16[2,48,1536]{2,1,0:T(8,128)(2,1)S(1)}, u32[]{:S(2)}) copy-start(bf16[2,48,1536]{2,1,0:T(8,128)(2,1)S(1)} %collective-permute-done.1) | copy-start | bytes 884740
  36.4 0.7 copy-start.6
  41.8 2.6 %collective-permute-start.5 = (bf16[3,2,48,1536]{3,2,1,0:T(8,128)(2,1)S(1)}, bf16[3,2,48,1536]{3,2,1,0:T(8,128)(2,1)}, u32[]{:S(2)}, u32[]{:S(2)}) collective-permute-start(bf16[3,2,48,1536]{3,2,1,0:T(8,128)(2,1)S(1)} %pad_maximum_fusion.near_ref), channel_id=1, source_target_pairs={{0,32},{32,0},{1,33},{33,1},{2,34},{34,2},{3,35},{35,3},{4,36},{36... | collective-permute-start | bytes 2654216 | tf_op jit(solution)/shard_map/ppermute | solution.py:395
  41.9 11.2 %collective-permute-start.6 = (bf16[2,48,1536]{2,1,0:T(8,128)(2,1)}, bf16[2,48,1536]{2,1,0:T(8,128)(2,1)}, u32[]{:S(2)}, u32[]{:S(2)}) collective-permute-start(bf16[2,48,1536]{2,1,0:T(8,128)(2,1)} %pad_maximum_fusion.2), channel_id=1, source_target_pairs={{0,4},{2,6},{4,0},{6,2},{1,5},{3,7},{5,1},{7,3},{8,12},{10,14},{12... | collective-permute-start | bytes 884744 | tf_op jit(solution)/shard_map/ppermute | solution.py:378
  47.9 25.7 %all-to-all-start.1 = ((bf16[4,2,256,384]{3,2,1,0:T(8,128)(2,1)}), bf16[4,2,256,384]{3,2,1,0:T(8,128)(2,1)}, u32[]{:S(2)}, u32[]{:S(2)}) async-start(bf16[4,2,256,384]{3,2,1,0:T(8,128)(2,1)} %project.2.refs_1_), calls=%async_computation.1 | async-start | bytes 3145728 | tf_op jit(solution)/shard_map/all_to_all | solution.py:399
  54.4 2.8 %collective-permute-start.7 = (bf16[3,2,48,1536]{3,2,1,0:T(8,128)(2,1)S(1)}, bf16[3,2,48,1536]{3,2,1,0:T(8,128)(2,1)}, u32[]{:S(2)}, u32[]{:S(2)}) collective-permute-start(bf16[3,2,48,1536]{3,2,1,0:T(8,128)(2,1)S(1)} %pad_maximum_fusion.1.near_ref), channel_id=1, source_target_pairs={{0,32},{32,0},{1,33},{33,1},{2,34},{34,2},{3,35},{35,3},{4,36},{36... | collective-permute-start | bytes 2654216 | tf_op jit(solution)/shard_map/ppermute | solution.py:404
  62.6 16.1 %copy-start.4 = (bf16[96,1536]{1,0:T(8,128)(2,1)S(1)}, bf16[96,1536]{1,0:T(8,128)(2,1)}, u32[]{:S(2)}) copy-start(bf16[96,1536]{1,0:T(8,128)(2,1)} %own_ref.1) | copy-start | bytes 884740
  78.7 16.4 %copy-start.2 = (bf16[1,64,1536]{2,1,0:T(8,128)(2,1)S(1)}, bf16[1,64,1536]{2,1,0:T(8,128)(2,1)}, u32[]{:S(2)}) copy-start(bf16[1,64,1536]{2,1,0:T(8,128)(2,1)} %param.11) | copy-start | bytes 589828
  78.7 16.3 %copy-start.5 = (f32[1,8,1536]{2,1,0:T(8,128)S(1)}, f32[1,8,1536]{2,1,0:T(8,128)}, u32[]{:S(2)}) copy-start(f32[1,8,1536]{2,1,0:T(8,128)} %param.13) | copy-start | bytes 147460
  117.3 4.3 %copy-start.9 = (bf16[1536,64]{0,1:T(8,128)(2,1)S(1)}, bf16[1536,64]{0,1:T(8,128)(2,1)}, u32[]{:S(2)}) copy-start(bf16[1536,64]{0,1:T(8,128)(2,1)} %param.21) | copy-start | bytes 589828
  117.3 14.7 %copy-start.10 = (f32[1,32,128]{2,1,0:T(8,128)S(1)}, f32[1,32,128]{2,1,0:T(8,128)}, u32[]{:S(2)}) copy-start(f32[1,32,128]{2,1,0:T(8,128)} %param.12) | copy-start | bytes 49156
  117.3 13.5 %all-to-all-start.4 = ((bf16[4,64,1536]{2,1,0:T(8,128)(2,1)}), bf16[4,64,1536]{2,1,0:T(8,128)(2,1)S(1)}, u32[]{:S(2)}, u32[]{:S(2)}) async-start(bf16[4,64,1536]{2,1,0:T(8,128)(2,1)} %bitcast.45), calls=%async_computation.4 | async-start | bytes 1572864 | tf_op jit(solution)/shard_map/all_to_all | solution.py:416
Sparse Core Ops, SparseCore 0:
  11.7 65.9 all-gather.2

commit v11 on v8

--- a/solution.py
+++ b/solution.py
@@ -34,33 +34,13 @@
 
 
 def first_kernel(
-    pos_ref,
-    x_ref,
-    mod_ref,
-    up_ref,
-    down_ref,
-    qkv_ref,
-    wout_ref,
-    h_ref,
-    kv_ref,
-    qo_ref,
-    pack_ref,
-    held,
-    load_sem,
-    store_sem,
-    half_sem,
+    copies, pos_ref, x_ref, mod_ref, up_ref, down_ref, out_ref, pack_ref, held, load_sem, store_sem
 ):
     core = pos_ref[0]
     zone = pos_ref[1]
     part = down_ref.shape[0]
 
-    def move(core_here, sources):
-        mine = pl.ds(core_here * 48, 48)
-        halves = [
-            pltpu.make_async_copy(qkv_ref.at[pl.ds(1, 2), mine, :], kv_ref, half_sem.at[0]),
-            pltpu.make_async_copy(qkv_ref.at[0, mine, :], qo_ref.at[0], half_sem.at[1]),
-            pltpu.make_async_copy(wout_ref.at[mine, :], qo_ref.at[1], half_sem.at[2]),
-        ]
+    def move(sources):
         loads = []
         stores = []
         for i, source in enumerate(sources):
@@ -69,53 +49,52 @@
             stores.append(
                 pltpu.make_async_copy(held.at[rows, :], pack_ref.at[rows, :], store_sem.at[i])
             )
-        for copy in loads + halves:
-            copy.start()
+        for load in loads:
+            load.start()
         h = layer_norm(x_ref[...].astype(F32), mod_ref[0:1, :], mod_ref[1:2, :]).astype(BF)
-        for i in range(h_ref.shape[0]):
-            h_ref[i] = h
+        for i in range(copies):
+            out_ref[i] = h
         for load, store in zip(loads, stores):
             load.wait()
             store.start()
-        for copy in halves + stores:
-            copy.wait()
+        for store in stores:
+            store.wait()
 
     for half in range(2):
 
         @pl.when(jnp.logical_and(core == 0, zone == half))
         def _():
-            move(0, [up_ref.at[pl.ds((2 * half + i) * part, part), :] for i in range(2)])
+            move([up_ref.at[pl.ds((2 * half + i) * part, part), :] for i in range(2)])
 
         @pl.when(jnp.logical_and(core == 1, zone == half))
         def _():
-            move(1, [down_ref.at[:, pl.ds((2 * half + i) * part, part)] for i in range(2)])
-
-
-def first_stage(pos, tokens, mods, w_up, w_down, own_qkv, w_out, copies):
+            move([down_ref.at[:, pl.ds((2 * half + i) * part, part)] for i in range(2)])
+
+
+def first_norm_and_pack(pos, tokens, mods, w_up, w_down, copies):
     rows, width = tokens.shape
     part = w_down.shape[0]
     return pl.pallas_call(
-        first_kernel,
+        functools.partial(first_kernel, copies),
         out_shape=[
             jax.ShapeDtypeStruct((copies, rows, width), BF),
-            jax.ShapeDtypeStruct((2, 48, width), BF),
-            jax.ShapeDtypeStruct((2, 48, width), BF),
             jax.ShapeDtypeStruct((2 * part, part), BF),
         ],
         in_specs=[pl.BlockSpec(memory_space=pltpu.SMEM)]
         + [pl.BlockSpec(memory_space=pltpu.VMEM)] * 2
-        + [pl.BlockSpec(memory_space=pltpu.HBM)] * 4,
-        out_specs=[pl.BlockSpec(memory_space=pltpu.VMEM)] * 3
-        + [pl.BlockSpec(memory_space=pltpu.HBM)],
+        + [pl.BlockSpec(memory_space=pltpu.HBM)] * 2,
+        out_specs=[
+            pl.BlockSpec(memory_space=pltpu.VMEM),
+            pl.BlockSpec(memory_space=pltpu.HBM),
+        ],
         scratch_shapes=[
             pltpu.VMEM((2 * part, part), BF),
             pltpu.SemaphoreType.DMA((2,)),
             pltpu.SemaphoreType.DMA((2,)),
-            pltpu.SemaphoreType.DMA((3,)),
         ],
         compiler_params=params(58),
-        name="first_stage",
-    )(pos, tokens, mods, w_up, w_down, own_qkv, w_out)
+        name="first_norm_and_pack",
+    )(pos, tokens, mods, w_up, w_down)
 
 
 def assemble(pos_ref, own_ref, near_refs, far_ref, store):
@@ -398,24 +377,27 @@
         return lax.ppermute(value, "ty", [(i, (i + step) % 4) for i in range(4)])
 
     own_qkv = jnp.transpose(w_qkv, (1, 2, 0))
+    half_kv = lax.dynamic_slice(own_qkv, (1, core * 48, 0), (2, 48, width))
     place = jnp.stack([core, lax.axis_index("zp")]).astype(jnp.int32)
-    h1, half_kv, half_qo, quarter = first_stage(
-        place, tokens, mods, w_up, w_down, own_qkv, w_out, 4
-    )
+    h1, quarter = first_norm_and_pack(place, tokens, mods, w_up, w_down, 4)
     ffn_full = lax.all_gather(quarter, ("core", "tx", "zp"), axis=0, tiled=False)
     ffn_full = ffn_full.reshape(2, 4, width, w_up.shape[1])
+    h1, half_kv = lax.optimization_barrier((h1, half_kv))
     h1 = lax.all_to_all(h1, "tx", split_axis=0, concat_axis=0, tiled=True)
     near_kv = [to_lines(half_kv, step) for step in STRIDES]
-    *near_kv, h1 = lax.optimization_barrier((*near_kv, h1))
-    stacked, half_qo = lax.optimization_barrier((jnp.stack(near_kv), half_qo))
-    far_kv = lax.ppermute(stacked, "core", swap2)
+
+    half_q = lax.dynamic_slice(own_qkv, (0, core * 48, 0), (1, 48, width))
+    half_out = lax.dynamic_slice(w_out, (core * 48, 0), (48, width))
+    half_qo = jnp.concatenate([half_q, half_out[None]])
+    text = lax.dynamic_slice_in_dim(text_kv[0], lax.axis_index("tx") * 384, 384, 2)
+    text = jnp.transpose(text, (1, 0, 2))
+    far_kv = lax.ppermute(jnp.stack(near_kv), "core", swap2)
+    h1, half_qo, text = lax.optimization_barrier((h1, half_qo, text))
     near_qo = [to_lines(half_qo, step) for step in STRIDES]
     h1 = h1.reshape(4 * rows, width)
     own_kv = project(pos, h1, own_qkv, 1, 2, 4, near_kv, far_kv)
     all_kv = lax.all_to_all(own_kv, "ty", split_axis=0, concat_axis=0, tiled=True)
-    *near_qo, own_kv, text_kv = lax.optimization_barrier((*near_qo, own_kv, text_kv))
-    text = lax.dynamic_slice_in_dim(text_kv[0], lax.axis_index("tx") * 384, 384, 2)
-    text = jnp.transpose(text, (1, 0, 2))
+    *near_qo, own_kv = lax.optimization_barrier((*near_qo, own_kv))
     far_qo = lax.ppermute(jnp.stack(near_qo), "core", swap2)
     query = project(pos, h1, own_qkv, 0, 1, 1, near_qo, far_qo)[0, 0]
 

time: 137 us -> 135 us (0.985); the launches traced: 136 us -> 132 us
  local copies, waits for them, and re-layouts: 10.1 us -> 2.02 us
  waiting for transfers between devices: 29.8 us -> 33.1 us
    unnamed x49 -> x25, local copies, waits for them, and re-layouts: 9.83 us -> 0.28 us
    all_to_all x1, waiting for transfers between devices: 0.01 us -> 8.53 us  [on_device(): h1 = lax.all_to_all(h1, 'tx', split_axis=0, concat_axis=0, tiled=True)]
    ppermute x6, waiting for transfers between devices: 14.3 us -> 10.8 us  [to_lines(): return lax.ppermute(value, 'ty', [(i, (i + step) % 4) for i in range(4)])]
    all_to_all x1, blocking collectives: 15.3 us -> 12.4 us  [on_device(): lax.all_to_all(partial, 'tx', split_axis=0, concat_axis=0, tiled=True)]
    all_to_all x1, blocking collectives: 13.1 us -> 15 us  [on_device(): h2 = lax.all_to_all(h2, 'ty', split_axis=0, concat_axis=0, tiled=True)]
    all_to_all x1, waiting for transfers between devices: 4.51 us -> 2.87 us  [on_device(): lax.all_to_all(own_kv, 'ty', split_axis=0, concat_axis=0, tiled=True)]
  transfers between devices with their start and end apart: 12 -> 12, of which waited for: 8 -> 7; matrix products, arithmetic and copies ran while one was open for 2% -> 4% of each run, Pallas kernels for 11% -> 12%
where the time goes in v11:
time: 135 us; the launch traced here: 132 us
  waiting for transfers between devices  33.1 us (25%)
  Pallas kernels  28.1 us (21%)
  blocking collectives  27.4 us (20%)
  starting transfers between devices  21.6 us (16%)
  between operations  15.6 us (12%)
  other arithmetic  4.38 us (3%)
  local copies, waits for them, and re-layouts  2.02 us (1%)
    all_to_all x1, blocking collectives, on_device(): h2 = lax.all_to_all(h2, 'ty', split_axis=0, concat_axis=0, tiled=True)  15 us
    all_to_all x1, blocking collectives, on_device(): lax.all_to_all(partial, 'tx', split_axis=0, concat_axis=0, tiled=True)  12.4 us
    ppermute x6, waiting for transfers between devices, to_lines(): return lax.ppermute(value, 'ty', [(i, (i + step) % 4) for i in range(4)])  10.8 us
    all_to_all x1, waiting for transfers between devices, on_device(): h1 = lax.all_to_all(h1, 'tx', split_axis=0, concat_axis=0, tiled=True)  8.53 us
    all_to_all x1, waiting for transfers between devices, on_device(): lax.all_to_all(partial, 'ty', split_axis=0, concat_axis=0, tiled=True)  8.46 us
    ppermute x6, starting transfers between devices, to_lines(): return lax.ppermute(value, 'ty', [(i, (i + step) % 4) for i in range(4)])  8.46 us
    pallas_call x2, Pallas kernels, attention(): pl.pallas_call(functools.partial(attention_kernel, own), out_shape=out, i...  7.72 us
    pallas_call x1, Pallas kernels, feed_forward(): pl.pallas_call(ffn_kernel, grid=(4,), out_shape=jax.ShapeDtypeStruct((row...  7.66 us
  transfers between devices with their start and end apart: 12, of which 7 were waited for; matrix products, arithmetic and copies ran while one was open for 4% of the time, Pallas kernels for 12%

profile of v11, /device:TPU:128, one launch (start us, length us, event | category | flops | bytes accessed | tf_op | source)
XLA Modules:
  0.0 132.2 jit_solution(7005585997510352807)
XLA Ops:
  7.2 0.6 pad_add_fusion.1.pos_ref
  7.8 3.7 %first_norm_and_pack.1 = (bf16[4,64,1536]{2,1,0:T(8,128)(2,1)}, bf16[768,384]{1,0:T(8,128)(2,1)}) custom-call(s32[2]{0:T(128)} %pad_add_fusion.1.pos_ref, bf16[64,1536]{1,0:T(8,128)(2,1)} %bitcast.42, f32[8,1536]{1,0:T(8,128)} %bitcast.44, bf16[1536,384]{1,0:T(8,128)(2,1)} %up_ref.1, bf16[384,1536]{1,0:T(8,128)(2,1)} %down_ref.1), custom_call_target="tpu_custom_call" | custom-call | tf_op jit(solution)/shard_map/first_norm_and_pack/pallas_call | solution.py:77
  11.6 0.7 dynamic-slice_bitcast_fusion
  12.3 1.6 %collective-permute-start.3 = (bf16[2,48,1536]{2,1,0:T(8,128)(2,1)}, bf16[2,48,1536]{2,1,0:T(8,128)(2,1)S(1)}, u32[]{:S(2)}, u32[]{:S(2)}) collective-permute-start(bf16[2,48,1536]{2,1,0:T(8,128)(2,1)} %dynamic-slice_bitcast_fusion), channel_id=1, source_target_pairs={{0,2},{2,4},{4,6},{6,0},{1,3},{3,5},{5,7},{7,1},{8,10},{10,12},{12... | collective-permute-start | bytes 884744 | tf_op jit(solution)/shard_map/ppermute | solution.py:377
  13.9 1.7 %collective-permute-start.4 = (bf16[2,48,1536]{2,1,0:T(8,128)(2,1)}, bf16[2,48,1536]{2,1,0:T(8,128)(2,1)S(1)}, u32[]{:S(2)}, u32[]{:S(2)}) collective-permute-start(bf16[2,48,1536]{2,1,0:T(8,128)(2,1)} %dynamic-slice_bitcast_fusion), channel_id=1, source_target_pairs={{0,6},{2,0},{4,2},{6,4},{1,7},{3,1},{5,3},{7,5},{8,14},{10,8},{12,... | collective-permute-start | bytes 884744 | tf_op jit(solution)/shard_map/ppermute | solution.py:377
  15.6 2.0 %collective-permute-start.5 = (bf16[2,48,1536]{2,1,0:T(8,128)(2,1)}, bf16[2,48,1536]{2,1,0:T(8,128)(2,1)S(1)}, u32[]{:S(2)}, u32[]{:S(2)}) collective-permute-start(bf16[2,48,1536]{2,1,0:T(8,128)(2,1)} %dynamic-slice_bitcast_fusion), channel_id=1, source_target_pairs={{0,4},{2,6},{4,0},{6,2},{1,5},{3,7},{5,1},{7,3},{8,12},{10,14},{12... | collective-permute-start | bytes 884744 | tf_op jit(solution)/shard_map/ppermute | solution.py:377
  17.6 4.3 %all-to-all-start = ((bf16[4,64,1536]{2,1,0:T(8,128)(2,1)}), bf16[4,64,1536]{2,1,0:T(8,128)(2,1)S(1)}, u32[]{:S(2)}, u32[]{:S(2)}) async-start(bf16[4,64,1536]{2,1,0:T(8,128)(2,1)} %get-tuple-element.18), calls=%async_computation | async-start | bytes 1572864 | tf_op jit(solution)/shard_map/all_to_all | solution.py:386
  22.0 0.7 copy.16
  22.8 1.3 collective-permute-done.4.n1_ref
  24.1 6.0 %collective-permute-done.5.n2_ref = bf16[2,48,1536]{2,1,0:T(8,128)(2,1)S(1)} collective-permute-done((bf16[2,48,1536]{2,1,0:T(8,128)(2,1)}, bf16[2,48,1536]{2,1,0:T(8,128)(2,1)S(1)}, u32[]{:S(2)}, u32[]{:S(2)}) %collective-permute-start.5) | collective-permute-done | bytes 294944 | tf_op jit(solution)/shard_map/ppermute | solution.py:377
  30.1 1.1 pad_maximum_fusion
  31.2 0.7 pad_maximum_fusion.2
  32.0 8.5 %all-to-all-done = bf16[4,64,1536]{2,1,0:T(8,128)(2,1)S(1)} async-done(((bf16[4,64,1536]{2,1,0:T(8,128)(2,1)}), bf16[4,64,1536]{2,1,0:T(8,128)(2,1)S(1)}, u32[]{:S(2)}, u32[]{:S(2)}) %all-to-all-start) | async-done | bytes 786464 | tf_op jit(solution)/shard_map/all_to_all | solution.py:386
  40.5 3.2 %collective-permute-start.1 = (bf16[2,48,1536]{2,1,0:T(8,128)(2,1)}, bf16[2,48,1536]{2,1,0:T(8,128)(2,1)}, u32[]{:S(2)}, u32[]{:S(2)}) collective-permute-start(bf16[2,48,1536]{2,1,0:T(8,128)(2,1)} %pad_maximum_fusion.2), channel_id=1, source_target_pairs={{0,6},{2,0},{4,2},{6,4},{1,7},{3,1},{5,3},{7,5},{8,14},{10,8},{12,... | collective-permute-start | bytes 884744 | tf_op jit(solution)/shard_map/ppermute | solution.py:377
  44.5 3.5 %project.2.refs_2_ = bf16[4,2,256,384]{3,2,1,0:T(8,128)(2,1)} custom-call(s32[3]{0:T(128)S(1)} %pad_add_fusion.pos_ref.refs_0_, bf16[256,1536]{1,0:T(8,128)(2,1)S(1)} %bitcast.31, bf16[3,96,1536]{2,1,0:T(8,128)(2,1)S(1)} %bitcast.33, bf16[2,48,1536]{2,1,0:T(8,128)(2,1)S(1)} %collective-permute-done.3.n0_ref, ...), custom_call_target="tpu_custom_call" | custom-call | tf_op jit(solution)/shard_map/project/pallas_call | solution.py:135
  48.0 4.9 %all-to-all-start.1 = ((bf16[4,2,256,384]{3,2,1,0:T(8,128)(2,1)}), bf16[4,2,256,384]{3,2,1,0:T(8,128)(2,1)S(1)}, u32[]{:S(2)}, u32[]{:S(2)}) async-start(bf16[4,2,256,384]{3,2,1,0:T(8,128)(2,1)} %project.2.refs_2_), calls=%async_computation.1 | async-start | bytes 3145728 | tf_op jit(solution)/shard_map/all_to_all | solution.py:399
  52.8 3.5 %collective-permute-done.1.n1_ref = bf16[2,48,1536]{2,1,0:T(8,128)(2,1)} collective-permute-done((bf16[2,48,1536]{2,1,0:T(8,128)(2,1)}, bf16[2,48,1536]{2,1,0:T(8,128)(2,1)}, u32[]{:S(2)}, u32[]{:S(2)}) %collective-permute-start.1) | collective-permute-done | bytes 294944 | tf_op jit(solution)/shard_map/ppermute | solution.py:377
  56.3 1.3 pad_maximum_fusion.1
  57.9 2.4 %collective-permute-done.7.far_ref = bf16[3,2,48,1536]{3,2,1,0:T(8,128)(2,1)S(1)} collective-permute-done((bf16[3,2,48,1536]{3,2,1,0:T(8,128)(2,1)S(1)}, bf16[3,2,48,1536]{3,2,1,0:T(8,128)(2,1)S(1)}, u32[]{:S(2)}, u32[]{:S(2)}) %collective-permute-start.7) | collective-permute-done | bytes 884768 | tf_op jit(solution)/shard_map/ppermute | solution.py:401
  60.3 2.2 %project.3 = bf16[1,1,256,384]{3,2,1,0:T(8,128)(2,1)S(1)} custom-call(s32[3]{0:T(128)S(1)} %pad_add_fusion.pos_ref.refs_0_, bf16[256,1536]{1,0:T(8,128)(2,1)S(1)} %bitcast.32, bf16[3,96,1536]{2,1,0:T(8,128)(2,1)S(1)} %bitcast.34, bf16[2,48,1536]{2,1,0:T(8,128)(2,1)} %collective-permute-done.n0_ref, bf16[2,48,1536]{2,1,0:T(8,128)(2,1)} %collective-permute-done.1.n1_ref, ...), custom_call_target="tpu_custom_call" | custom-call | tf_op jit(solution)/shard_map/project/pallas_call | solution.py:135
  62.5 3.5 %attention.2.refs_3_ = f32[256,512]{1,0:T(8,128)S(1)} custom-call(s32[3]{0:T(128)S(1)} %pad_add_fusion.pos_ref.refs_0_, bf16[256,384]{1,0:T(8,128)(2,1)S(1)} %bitcast.36, bf16[4,2,256,384]{3,2,1,0:T(8,128)(2,1)} %project.2.refs_2_, bf16[2,154,384]{2,1,0:T(8,128)(2,1)S(1)} %bitcast.41), custom_call_target="tpu_custom_call" | custom-call | tf_op jit(solution)/shard_map/attention/pallas_call | solution.py:225
  66.0 2.9 %all-to-all-done.1.refs_2_ = bf16[4,2,256,384]{3,2,1,0:T(8,128)(2,1)S(1)} async-done(((bf16[4,2,256,384]{3,2,1,0:T(8,128)(2,1)}), bf16[4,2,256,384]{3,2,1,0:T(8,128)(2,1)S(1)}, u32[]{:S(2)}, u32[]{:S(2)}) %all-to-all-start.1) | async-done | bytes 1572896 | tf_op jit(solution)/shard_map/all_to_all | solution.py:399
  68.9 4.2 %attention.3.a_ref = bf16[256,384]{1,0:T(8,128)(2,1)S(1)} custom-call(s32[3]{0:T(128)S(1)} %pad_add_fusion.pos_ref.refs_0_, bf16[256,384]{1,0:T(8,128)(2,1)S(1)} %bitcast.37, bf16[4,2,256,384]{3,2,1,0:T(8,128)(2,1)S(1)} %all-to-all-done.1.refs_2_, f32[256,512]{1,0:T(8,128)S(1)} %attention.2.refs_3_), custom_call_target="tpu_custom_call" | custom-call | tf_op jit(solution)/shard_map/attention/pallas_call | solution.py:225
  73.1 1.9 %out_projection.1 = bf16[256,1536]{1,0:T(8,128)(2,1)S(1)} custom-call(s32[3]{0:T(128)S(1)} %pad_add_fusion.pos_ref.refs_0_, bf16[256,384]{1,0:T(8,128)(2,1)S(1)} %attention.3.a_ref, bf16[96,1536]{1,0:T(8,128)(2,1)S(1)} %copy-done.8, bf16[2,48,1536]{2,1,0:T(8,128)(2,1)} %collective-permute-done.n0_ref, bf16[2,48,1536]{2,1,0:T(8,128)(2,1)} %collective-permute-done.1.n1_ref, ...), custom_call_target="tpu_custom_call" | custom-call | tf_op jit(solution)/shard_map/out_projection/pallas_call | solution.py:254
  75.0 12.4 %all_to_all.25.part_ref = bf16[4,64,1536]{2,1,0:T(8,128)(2,1)S(1)} all-to-all(bf16[4,64,1536]{2,1,0:T(8,128)(2,1)S(1)} %bitcast.35), channel_id=1, replica_groups=mesh['zl'=2,'zp'=2,'core'=2,'tx'=4,'ty'=4,'blk'=2] {'tx'}, dimensions={0} | all-to-all | bytes 1572864 | tf_op jit(solution)/shard_map/all_to_all | solution.py:409
  87.4 0.4 second_norm.1
  87.8 15.0 %all_to_all.26 = bf16[4,64,1536]{2,1,0:T(8,128)(2,1)} all-to-all(bf16[4,64,1536]{2,1,0:T(8,128)(2,1)S(1)} %get-tuple-element.28), channel_id=1, replica_groups=mesh['zl'=2,'zp'=2,'core'=2,'tx'=4,'ty'=4,'blk'=2] {'ty'}, dimensions={0} | all-to-all | bytes 1572864 | tf_op jit(solution)/shard_map/all_to_all | solution.py:411
  102.8 7.7 %feed_forward.1 = bf16[256,1536]{1,0:T(8,128)(2,1)} custom-call(bf16[256,1536]{1,0:T(8,128)(2,1)} %bitcast.50, bf16[2,4,1536,384]{3,2,1,0:T(8,128)(2,1)} %bitcast.47, bf16[2,4,1536,384]{3,2,1,0:T(8,128)(2,1)} %bitcast.48), custom_call_target="tpu_custom_call" | custom-call | tf_op jit(solution)/shard_map/feed_forward/pallas_call | solution.py:318
  110.5 3.6 %all-to-all-start.4 = ((bf16[4,64,1536]{2,1,0:T(8,128)(2,1)}), bf16[4,64,1536]{2,1,0:T(8,128)(2,1)S(1)}, u32[]{:S(2)}, u32[]{:S(2)}) async-start(bf16[4,64,1536]{2,1,0:T(8,128)(2,1)} %bitcast.49), calls=%async_computation.4 | async-start | bytes 1572864 | tf_op jit(solution)/shard_map/all_to_all | solution.py:413
  115.1 8.5 %all-to-all-done.4.part_ref = bf16[4,64,1536]{2,1,0:T(8,128)(2,1)S(1)} async-done(((bf16[4,64,1536]{2,1,0:T(8,128)(2,1)}), bf16[4,64,1536]{2,1,0:T(8,128)(2,1)S(1)}, u32[]{:S(2)}, u32[]{:S(2)}) %all-to-all-start.4) | async-done | bytes 786464 | tf_op jit(solution)/shard_map/all_to_all | solution.py:413
  123.6 1.1 last_stage.1
  124.7 0.6 add.27
  (42 shorter events, 1.0 us)
Async XLA Ops:
  7.2 14.7 %copy-start = (bf16[1,154,2,1536]{3,2,1,0:T(2,128)(2,1)S(1)}, bf16[1,154,2,1536]{3,2,1,0:T(2,128)(2,1)}, u32[]{:S(2)}) copy-start(bf16[1,154,2,1536]{3,2,1,0:T(2,128)(2,1)} %param.14) | copy-start | bytes 2838532
  7.2 95.7 %all-gather.3.cloned.1.call-start = ((), (), s32[]{:S(2)}) async-start(), calls=%async_computation.5 | async-start | bytes 10027008 | tf_op jit(solution)/shard_map/all_gather | solution.py:383
  7.8 3.8 %copy-start.1 = (bf16[1536,3,96]{0,2,1:T(8,128)(2,1)S(1)}, bf16[1536,3,96]{0,2,1:T(8,128)(2,1)}, u32[]{:S(2)}) copy-start(bf16[1536,3,96]{0,2,1:T(8,128)(2,1)} %param.17) | copy-start | bytes 2654212
  12.3 10.4 %collective-permute-start.3 = (bf16[2,48,1536]{2,1,0:T(8,128)(2,1)}, bf16[2,48,1536]{2,1,0:T(8,128)(2,1)S(1)}, u32[]{:S(2)}, u32[]{:S(2)}) collective-permute-start(bf16[2,48,1536]{2,1,0:T(8,128)(2,1)} %dynamic-slice_bitcast_fusion), channel_id=1, source_target_pairs={{0,2},{2,4},{4,6},{6,0},{1,3},{3,5},{5,7},{7,1},{8,10},{10,12},{12... | collective-permute-start | bytes 884744 | tf_op jit(solution)/shard_map/ppermute | solution.py:377
  13.9 10.1 %collective-permute-start.4 = (bf16[2,48,1536]{2,1,0:T(8,128)(2,1)}, bf16[2,48,1536]{2,1,0:T(8,128)(2,1)S(1)}, u32[]{:S(2)}, u32[]{:S(2)}) collective-permute-start(bf16[2,48,1536]{2,1,0:T(8,128)(2,1)} %dynamic-slice_bitcast_fusion), channel_id=1, source_target_pairs={{0,6},{2,0},{4,2},{6,4},{1,7},{3,1},{5,3},{7,5},{8,14},{10,8},{12,... | collective-permute-start | bytes 884744 | tf_op jit(solution)/shard_map/ppermute | solution.py:377
  15.6 14.5 %collective-permute-start.5 = (bf16[2,48,1536]{2,1,0:T(8,128)(2,1)}, bf16[2,48,1536]{2,1,0:T(8,128)(2,1)S(1)}, u32[]{:S(2)}, u32[]{:S(2)}) collective-permute-start(bf16[2,48,1536]{2,1,0:T(8,128)(2,1)} %dynamic-slice_bitcast_fusion), channel_id=1, source_target_pairs={{0,4},{2,6},{4,0},{6,2},{1,5},{3,7},{5,1},{7,3},{8,12},{10,14},{12... | collective-permute-start | bytes 884744 | tf_op jit(solution)/shard_map/ppermute | solution.py:377
  17.6 22.9 %all-to-all-start = ((bf16[4,64,1536]{2,1,0:T(8,128)(2,1)}), bf16[4,64,1536]{2,1,0:T(8,128)(2,1)S(1)}, u32[]{:S(2)}, u32[]{:S(2)}) async-start(bf16[4,64,1536]{2,1,0:T(8,128)(2,1)} %get-tuple-element.18), calls=%async_computation | async-start | bytes 1572864 | tf_op jit(solution)/shard_map/all_to_all | solution.py:386
  21.9 9.3 %copy-start.7 = (bf16[96,1536]{1,0:T(8,128)(2,1)S(1)}, bf16[96,1536]{1,0:T(8,128)(2,1)}, u32[]{:S(2)}) copy-start(bf16[96,1536]{1,0:T(8,128)(2,1)} %own_ref.1) | copy-start | bytes 884740
  31.2 13.3 %collective-permute-start.6 = (bf16[3,2,48,1536]{3,2,1,0:T(8,128)(2,1)}, bf16[3,2,48,1536]{3,2,1,0:T(8,128)(2,1)}, u32[]{:S(2)}, u32[]{:S(2)}) collective-permute-start(bf16[3,2,48,1536]{3,2,1,0:T(8,128)(2,1)} %pad_maximum_fusion), channel_id=1, source_target_pairs={{0,32},{32,0},{1,33},{33,1},{2,34},{34,2},{3,35},{35,3},{4,36},{36... | collective-permute-start | bytes 2654216 | tf_op jit(solution)/shard_map/ppermute | solution.py:394
  40.5 12.3 %collective-permute-start = (bf16[2,48,1536]{2,1,0:T(8,128)(2,1)}, bf16[2,48,1536]{2,1,0:T(8,128)(2,1)}, u32[]{:S(2)}, u32[]{:S(2)}) collective-permute-start(bf16[2,48,1536]{2,1,0:T(8,128)(2,1)} %pad_maximum_fusion.2), channel_id=1, source_target_pairs={{0,2},{2,4},{4,6},{6,0},{1,3},{3,5},{5,7},{7,1},{8,10},{10,12},{12... | collective-permute-start | bytes 884744 | tf_op jit(solution)/shard_map/ppermute | solution.py:377
  40.5 15.8 %collective-permute-start.1 = (bf16[2,48,1536]{2,1,0:T(8,128)(2,1)}, bf16[2,48,1536]{2,1,0:T(8,128)(2,1)}, u32[]{:S(2)}, u32[]{:S(2)}) collective-permute-start(bf16[2,48,1536]{2,1,0:T(8,128)(2,1)} %pad_maximum_fusion.2), channel_id=1, source_target_pairs={{0,6},{2,0},{4,2},{6,4},{1,7},{3,1},{5,3},{7,5},{8,14},{10,8},{12,... | collective-permute-start | bytes 884744 | tf_op jit(solution)/shard_map/ppermute | solution.py:377
  43.7 12.6 %collective-permute-start.2 = (bf16[2,48,1536]{2,1,0:T(8,128)(2,1)}, bf16[2,48,1536]{2,1,0:T(8,128)(2,1)}, u32[]{:S(2)}, u32[]{:S(2)}) collective-permute-start(bf16[2,48,1536]{2,1,0:T(8,128)(2,1)} %pad_maximum_fusion.2), channel_id=1, source_target_pairs={{0,4},{2,6},{4,0},{6,2},{1,5},{3,7},{5,1},{7,3},{8,12},{10,14},{12... | collective-permute-start | bytes 884744 | tf_op jit(solution)/shard_map/ppermute | solution.py:377
  48.0 20.9 %all-to-all-start.1 = ((bf16[4,2,256,384]{3,2,1,0:T(8,128)(2,1)}), bf16[4,2,256,384]{3,2,1,0:T(8,128)(2,1)S(1)}, u32[]{:S(2)}, u32[]{:S(2)}) async-start(bf16[4,2,256,384]{3,2,1,0:T(8,128)(2,1)} %project.2.refs_2_), calls=%async_computation.1 | async-start | bytes 3145728 | tf_op jit(solution)/shard_map/all_to_all | solution.py:399
  52.8 7.5 %copy-start.2 = (bf16[1536,3,96]{0,2,1:T(8,128)(2,1)S(1)}, bf16[1536,3,96]{0,2,1:T(8,128)(2,1)}, u32[]{:S(2)}) copy-start(bf16[1536,3,96]{0,2,1:T(8,128)(2,1)} %param.17) | copy-start | bytes 2654212
  57.6 4.9 %copy-start.5 = (bf16[1,154,2,384]{3,1,2,0:T(8,128)(2,1)S(1)}, bf16[1,154,2,384]{3,1,2,0:T(8,128)(2,1)}, u32[]{:S(2)}) copy-start(bf16[1,154,2,384]{3,1,2,0:T(8,128)(2,1)} %copy.16) | copy-start | bytes 709636
  57.6 2.7 %collective-permute-start.7 = (bf16[3,2,48,1536]{3,2,1,0:T(8,128)(2,1)S(1)}, bf16[3,2,48,1536]{3,2,1,0:T(8,128)(2,1)S(1)}, u32[]{:S(2)}, u32[]{:S(2)}) collective-permute-start(bf16[3,2,48,1536]{3,2,1,0:T(8,128)(2,1)S(1)} %pad_maximum_fusion.1), channel_id=1, source_target_pairs={{0,32},{32,0},{1,33},{33,1},{2,34},{34,2},{3,35},{35,3},{4,36},{36... | collective-permute-start | bytes 2654216 | tf_op jit(solution)/shard_map/ppermute | solution.py:401
  60.3 2.2 %copy-start.3 = (bf16[3,2,48,1536]{3,2,1,0:T(8,128)(2,1)}, bf16[3,2,48,1536]{3,2,1,0:T(8,128)(2,1)S(1)}, u32[]{:S(2)}) copy-start(bf16[3,2,48,1536]{3,2,1,0:T(8,128)(2,1)S(1)} %collective-permute-done.7.far_ref) | copy-start | bytes 2654212
  68.9 4.2 %copy-start.4 = (bf16[3,2,48,1536]{3,2,1,0:T(8,128)(2,1)S(1)}, bf16[3,2,48,1536]{3,2,1,0:T(8,128)(2,1)}, u32[]{:S(2)}) copy-start(bf16[3,2,48,1536]{3,2,1,0:T(8,128)(2,1)} %copy-done.3) | copy-start | bytes 2654212
  68.9 4.2 %copy-start.8 = (bf16[96,1536]{1,0:T(8,128)(2,1)S(1)}, bf16[96,1536]{1,0:T(8,128)(2,1)}, u32[]{:S(2)}) copy-start(bf16[96,1536]{1,0:T(8,128)(2,1)} %own_ref.1) | copy-start | bytes 884740
  73.1 14.3 %copy-start.6 = (bf16[1,64,1536]{2,1,0:T(8,128)(2,1)S(1)}, bf16[1,64,1536]{2,1,0:T(8,128)(2,1)}, u32[]{:S(2)}) copy-start(bf16[1,64,1536]{2,1,0:T(8,128)(2,1)} %param.11) | copy-start | bytes 589828
  73.1 14.3 %copy-start.9 = (f32[1,8,1536]{2,1,0:T(8,128)S(1)}, f32[1,8,1536]{2,1,0:T(8,128)}, u32[]{:S(2)}) copy-start(f32[1,8,1536]{2,1,0:T(8,128)} %param.13) | copy-start | bytes 147460
  110.5 4.3 %copy-start.10 = (bf16[1536,64]{0,1:T(8,128)(2,1)S(1)}, bf16[1536,64]{0,1:T(8,128)(2,1)}, u32[]{:S(2)}) copy-start(bf16[1536,64]{0,1:T(8,128)(2,1)} %param.21) | copy-start | bytes 589828
  110.5 14.2 %copy-start.11 = (f32[1,32,128]{2,1,0:T(8,128)S(1)}, f32[1,32,128]{2,1,0:T(8,128)}, u32[]{:S(2)}) copy-start(f32[1,32,128]{2,1,0:T(8,128)} %param.12) | copy-start | bytes 49156
  110.5 13.1 %all-to-all-start.4 = ((bf16[4,64,1536]{2,1,0:T(8,128)(2,1)}), bf16[4,64,1536]{2,1,0:T(8,128)(2,1)S(1)}, u32[]{:S(2)}, u32[]{:S(2)}) async-start(bf16[4,64,1536]{2,1,0:T(8,128)(2,1)} %bitcast.49), calls=%async_computation.4 | async-start | bytes 1572864 | tf_op jit(solution)/shard_map/all_to_all | solution.py:413
Sparse Core Ops, SparseCore 0:
  11.7 65.9 all-gather.2

commit v12 on v11

--- a/solution.py
+++ b/solution.py
@@ -391,6 +391,7 @@
     half_qo = jnp.concatenate([half_q, half_out[None]])
     text = lax.dynamic_slice_in_dim(text_kv[0], lax.axis_index("tx") * 384, 384, 2)
     text = jnp.transpose(text, (1, 0, 2))
+    *near_kv, h1 = lax.optimization_barrier((*near_kv, h1))
     far_kv = lax.ppermute(jnp.stack(near_kv), "core", swap2)
     h1, half_qo, text = lax.optimization_barrier((h1, half_qo, text))
     near_qo = [to_lines(half_qo, step) for step in STRIDES]

time: 135 us -> 138 us (1.022); the launches traced: 132 us -> 138 us
  blocking collectives: 27.4 us -> 31.4 us
  waiting for transfers between devices: 33.1 us -> 34.8 us
    all_to_all x1, waiting for transfers between devices: 8.53 us -> 0.01 us  [on_device(): h1 = lax.all_to_all(h1, 'tx', split_axis=0, concat_axis=0, tiled=True)]
    ppermute x6, waiting for transfers between devices: 10.8 us -> 16.8 us  [to_lines(): return lax.ppermute(value, 'ty', [(i, (i + step) % 4) for i in range(4)])]
    all_to_all x1, blocking collectives: 12.4 us -> 16.5 us  [on_device(): lax.all_to_all(partial, 'tx', split_axis=0, concat_axis=0, tiled=True)]
    all_to_all x1, waiting for transfers between devices: 2.87 us -> 6.67 us  [on_device(): lax.all_to_all(own_kv, 'ty', split_axis=0, concat_axis=0, tiled=True)]
  transfers between devices with their start and end apart: 12 -> 12, of which waited for: 7 -> 8; matrix products, arithmetic and copies ran while one was open for 4% -> 4% of each run, Pallas kernels for 12% -> 11%
where the time goes in v12:
time: 138 us
  waiting for transfers between devices  34.8 us (25%)
  blocking collectives  31.4 us (23%)
  Pallas kernels  28 us (20%)
  starting transfers between devices  21.5 us (16%)
  between operations  15.6 us (11%)
  other arithmetic  4.34 us (3%)
  local copies, waits for them, and re-layouts  2.03 us (1%)
    ppermute x6, waiting for transfers between devices, to_lines(): return lax.ppermute(value, 'ty', [(i, (i + step) % 4) for i in range(4)])  16.8 us
    all_to_all x1, blocking collectives, on_device(): lax.all_to_all(partial, 'tx', split_axis=0, concat_axis=0, tiled=True)  16.5 us
    all_to_all x1, blocking collectives, on_device(): h2 = lax.all_to_all(h2, 'ty', split_axis=0, concat_axis=0, tiled=True)  14.9 us
    all_to_all x1, waiting for transfers between devices, on_device(): lax.all_to_all(partial, 'ty', split_axis=0, concat_axis=0, tiled=True)  8.95 us
    ppermute x6, starting transfers between devices, to_lines(): return lax.ppermute(value, 'ty', [(i, (i + step) % 4) for i in range(4)])  8.47 us
    pallas_call x2, Pallas kernels, attention(): pl.pallas_call(functools.partial(attention_kernel, own), out_shape=out, i...  7.74 us
    pallas_call x1, Pallas kernels, feed_forward(): pl.pallas_call(ffn_kernel, grid=(4,), out_shape=jax.ShapeDtypeStruct((row...  7.62 us
    all_to_all x1, waiting for transfers between devices, on_device(): lax.all_to_all(own_kv, 'ty', split_axis=0, concat_axis=0, tiled=True)  6.67 us
  transfers between devices with their start and end apart: 12, of which 8 were waited for; matrix products, arithmetic and copies ran while one was open for 4% of the time, Pallas kernels for 11%

profile of v12, /device:TPU:128, one launch (start us, length us, event | category | flops | bytes accessed | tf_op | source)
XLA Modules:
  0.0 137.7 jit_solution(14671507920476761252)
XLA Ops:
  7.2 0.6 pad_add_fusion.1.pos_ref
  7.9 3.7 %first_norm_and_pack.1 = (bf16[4,64,1536]{2,1,0:T(8,128)(2,1)}, bf16[768,384]{1,0:T(8,128)(2,1)}) custom-call(s32[2]{0:T(128)} %pad_add_fusion.1.pos_ref, bf16[64,1536]{1,0:T(8,128)(2,1)} %bitcast.42, f32[8,1536]{1,0:T(8,128)} %bitcast.44, bf16[1536,384]{1,0:T(8,128)(2,1)} %up_ref.1, bf16[384,1536]{1,0:T(8,128)(2,1)} %down_ref.1), custom_call_target="tpu_custom_call" | custom-call | tf_op jit(solution)/shard_map/first_norm_and_pack/pallas_call | solution.py:77
  11.6 0.8 dynamic-slice_bitcast_fusion
  12.4 4.3 %all-to-all-start = ((bf16[4,64,1536]{2,1,0:T(8,128)(2,1)}), bf16[4,64,1536]{2,1,0:T(8,128)(2,1)S(1)}, u32[]{:S(2)}, u32[]{:S(2)}) async-start(bf16[4,64,1536]{2,1,0:T(8,128)(2,1)} %get-tuple-element.23), calls=%async_computation | async-start | bytes 1572864 | tf_op jit(solution)/shard_map/all_to_all | solution.py:386
  16.7 1.6 %collective-permute-start = (bf16[2,48,1536]{2,1,0:T(8,128)(2,1)}, bf16[2,48,1536]{2,1,0:T(8,128)(2,1)S(1)}, u32[]{:S(2)}, u32[]{:S(2)}) collective-permute-start(bf16[2,48,1536]{2,1,0:T(8,128)(2,1)} %dynamic-slice_bitcast_fusion), channel_id=1, source_target_pairs={{0,2},{2,4},{4,6},{6,0},{1,3},{3,5},{5,7},{7,1},{8,10},{10,12},{12... | collective-permute-start | bytes 884744 | tf_op jit(solution)/shard_map/ppermute | solution.py:377
  18.3 1.7 %collective-permute-start.1 = (bf16[2,48,1536]{2,1,0:T(8,128)(2,1)}, bf16[2,48,1536]{2,1,0:T(8,128)(2,1)S(1)}, u32[]{:S(2)}, u32[]{:S(2)}) collective-permute-start(bf16[2,48,1536]{2,1,0:T(8,128)(2,1)} %dynamic-slice_bitcast_fusion), channel_id=1, source_target_pairs={{0,6},{2,0},{4,2},{6,4},{1,7},{3,1},{5,3},{7,5},{8,14},{10,8},{12,... | collective-permute-start | bytes 884744 | tf_op jit(solution)/shard_map/ppermute | solution.py:377
  19.9 2.0 %collective-permute-start.2 = (bf16[2,48,1536]{2,1,0:T(8,128)(2,1)}, bf16[2,48,1536]{2,1,0:T(8,128)(2,1)S(1)}, u32[]{:S(2)}, u32[]{:S(2)}) collective-permute-start(bf16[2,48,1536]{2,1,0:T(8,128)(2,1)} %dynamic-slice_bitcast_fusion), channel_id=1, source_target_pairs={{0,4},{2,6},{4,0},{6,2},{1,5},{3,7},{5,1},{7,3},{8,12},{10,14},{12... | collective-permute-start | bytes 884744 | tf_op jit(solution)/shard_map/ppermute | solution.py:377
  22.1 0.7 copy.16
  22.8 4.1 %collective-permute-done.n0_ref = bf16[2,48,1536]{2,1,0:T(8,128)(2,1)S(1)} collective-permute-done((bf16[2,48,1536]{2,1,0:T(8,128)(2,1)}, bf16[2,48,1536]{2,1,0:T(8,128)(2,1)S(1)}, u32[]{:S(2)}, u32[]{:S(2)}) %collective-permute-start) | collective-permute-done | bytes 294944 | tf_op jit(solution)/shard_map/ppermute | solution.py:377
  26.9 1.5 %collective-permute-done.1.n1_ref = bf16[2,48,1536]{2,1,0:T(8,128)(2,1)S(1)} collective-permute-done((bf16[2,48,1536]{2,1,0:T(8,128)(2,1)}, bf16[2,48,1536]{2,1,0:T(8,128)(2,1)S(1)}, u32[]{:S(2)}, u32[]{:S(2)}) %collective-permute-start.1) | collective-permute-done | bytes 294944 | tf_op jit(solution)/shard_map/ppermute | solution.py:377
  28.4 5.7 %collective-permute-done.2.n2_ref = bf16[2,48,1536]{2,1,0:T(8,128)(2,1)S(1)} collective-permute-done((bf16[2,48,1536]{2,1,0:T(8,128)(2,1)}, bf16[2,48,1536]{2,1,0:T(8,128)(2,1)S(1)}, u32[]{:S(2)}, u32[]{:S(2)}) %collective-permute-start.2) | collective-permute-done | bytes 294944 | tf_op jit(solution)/shard_map/ppermute | solution.py:377
  34.2 1.0 pad_maximum_fusion
  35.2 0.7 pad_maximum_fusion.2
  36.0 1.1 collective-permute-start.3
  37.1 2.1 %collective-permute-start.4 = (bf16[2,48,1536]{2,1,0:T(8,128)(2,1)}, bf16[2,48,1536]{2,1,0:T(8,128)(2,1)}, u32[]{:S(2)}, u32[]{:S(2)}) collective-permute-start(bf16[2,48,1536]{2,1,0:T(8,128)(2,1)} %pad_maximum_fusion.2), channel_id=1, source_target_pairs={{0,6},{2,0},{4,2},{6,4},{1,7},{3,1},{5,3},{7,5},{8,14},{10,8},{12,... | collective-permute-start | bytes 884744 | tf_op jit(solution)/shard_map/ppermute | solution.py:377
  40.0 3.5 %project.2.refs_2_ = bf16[4,2,256,384]{3,2,1,0:T(8,128)(2,1)} custom-call(s32[3]{0:T(128)S(1)} %pad_add_fusion.pos_ref.refs_0_, bf16[256,1536]{1,0:T(8,128)(2,1)S(1)} %bitcast.31, bf16[3,96,1536]{2,1,0:T(8,128)(2,1)S(1)} %bitcast.33, bf16[2,48,1536]{2,1,0:T(8,128)(2,1)S(1)} %collective-permute-done.n0_ref, ...), custom_call_target="tpu_custom_call" | custom-call | tf_op jit(solution)/shard_map/project/pallas_call | solution.py:135
  43.4 4.8 %all-to-all-start.1 = ((bf16[4,2,256,384]{3,2,1,0:T(8,128)(2,1)}), bf16[4,2,256,384]{3,2,1,0:T(8,128)(2,1)S(1)}, u32[]{:S(2)}, u32[]{:S(2)}) async-start(bf16[4,2,256,384]{3,2,1,0:T(8,128)(2,1)} %project.2.refs_2_), calls=%async_computation.1 | async-start | bytes 3145728 | tf_op jit(solution)/shard_map/all_to_all | solution.py:400
  48.2 4.6 %collective-permute-done.4.n1_ref = bf16[2,48,1536]{2,1,0:T(8,128)(2,1)} collective-permute-done((bf16[2,48,1536]{2,1,0:T(8,128)(2,1)}, bf16[2,48,1536]{2,1,0:T(8,128)(2,1)}, u32[]{:S(2)}, u32[]{:S(2)}) %collective-permute-start.4) | collective-permute-done | bytes 294944 | tf_op jit(solution)/shard_map/ppermute | solution.py:377
  52.8 0.8 collective-permute-done.5.n2_ref
  53.6 1.3 pad_maximum_fusion.1
  55.2 2.4 %collective-permute-done.7.far_ref = bf16[3,2,48,1536]{3,2,1,0:T(8,128)(2,1)S(1)} collective-permute-done((bf16[3,2,48,1536]{3,2,1,0:T(8,128)(2,1)S(1)}, bf16[3,2,48,1536]{3,2,1,0:T(8,128)(2,1)S(1)}, u32[]{:S(2)}, u32[]{:S(2)}) %collective-permute-start.7) | collective-permute-done | bytes 884768 | tf_op jit(solution)/shard_map/ppermute | solution.py:402
  57.6 2.1 %project.3 = bf16[1,1,256,384]{3,2,1,0:T(8,128)(2,1)S(1)} custom-call(s32[3]{0:T(128)S(1)} %pad_add_fusion.pos_ref.refs_0_, bf16[256,1536]{1,0:T(8,128)(2,1)S(1)} %bitcast.32, bf16[3,96,1536]{2,1,0:T(8,128)(2,1)S(1)} %bitcast.34, bf16[2,48,1536]{2,1,0:T(8,128)(2,1)} %collective-permute-done.3.n0_ref, bf16[2,48,1536]{2,1,0:T(8,128)(2,1)} %collective-permute-done.4.n1_ref, ...), custom_call_target="tpu_custom_call" | custom-call | tf_op jit(solution)/shard_map/project/pallas_call | solution.py:135
  59.8 3.5 %attention.2.refs_3_ = f32[256,512]{1,0:T(8,128)S(1)} custom-call(s32[3]{0:T(128)S(1)} %pad_add_fusion.pos_ref.refs_0_, bf16[256,384]{1,0:T(8,128)(2,1)S(1)} %bitcast.36, bf16[4,2,256,384]{3,2,1,0:T(8,128)(2,1)} %project.2.refs_2_, bf16[2,154,384]{2,1,0:T(8,128)(2,1)S(1)} %bitcast.41), custom_call_target="tpu_custom_call" | custom-call | tf_op jit(solution)/shard_map/attention/pallas_call | solution.py:225
  63.3 6.7 %all-to-all-done.1.refs_2_ = bf16[4,2,256,384]{3,2,1,0:T(8,128)(2,1)S(1)} async-done(((bf16[4,2,256,384]{3,2,1,0:T(8,128)(2,1)}), bf16[4,2,256,384]{3,2,1,0:T(8,128)(2,1)S(1)}, u32[]{:S(2)}, u32[]{:S(2)}) %all-to-all-start.1) | async-done | bytes 1572896 | tf_op jit(solution)/shard_map/all_to_all | solution.py:400
  70.0 4.2 %attention.3.a_ref = bf16[256,384]{1,0:T(8,128)(2,1)S(1)} custom-call(s32[3]{0:T(128)S(1)} %pad_add_fusion.pos_ref.refs_0_, bf16[256,384]{1,0:T(8,128)(2,1)S(1)} %bitcast.37, bf16[4,2,256,384]{3,2,1,0:T(8,128)(2,1)S(1)} %all-to-all-done.1.refs_2_, f32[256,512]{1,0:T(8,128)S(1)} %attention.2.refs_3_), custom_call_target="tpu_custom_call" | custom-call | tf_op jit(solution)/shard_map/attention/pallas_call | solution.py:225
  74.3 1.8 %out_projection.1 = bf16[256,1536]{1,0:T(8,128)(2,1)S(1)} custom-call(s32[3]{0:T(128)S(1)} %pad_add_fusion.pos_ref.refs_0_, bf16[256,384]{1,0:T(8,128)(2,1)S(1)} %attention.3.a_ref, bf16[96,1536]{1,0:T(8,128)(2,1)S(1)} %copy-done.8, bf16[2,48,1536]{2,1,0:T(8,128)(2,1)} %collective-permute-done.3.n0_ref, bf16[2,48,1536]{2,1,0:T(8,128)(2,1)} %collective-permute-done.4.n1_ref, ...), custom_call_target="tpu_custom_call" | custom-call | tf_op jit(solution)/shard_map/out_projection/pallas_call | solution.py:254
  76.1 16.5 %all_to_all.25.part_ref = bf16[4,64,1536]{2,1,0:T(8,128)(2,1)S(1)} all-to-all(bf16[4,64,1536]{2,1,0:T(8,128)(2,1)S(1)} %bitcast.35), channel_id=1, replica_groups=mesh['zl'=2,'zp'=2,'core'=2,'tx'=4,'ty'=4,'blk'=2] {'tx'}, dimensions={0} | all-to-all | bytes 1572864 | tf_op jit(solution)/shard_map/all_to_all | solution.py:410
  93.0 14.9 %all_to_all.26 = bf16[4,64,1536]{2,1,0:T(8,128)(2,1)} all-to-all(bf16[4,64,1536]{2,1,0:T(8,128)(2,1)S(1)} %get-tuple-element.36), channel_id=1, replica_groups=mesh['zl'=2,'zp'=2,'core'=2,'tx'=4,'ty'=4,'blk'=2] {'ty'}, dimensions={0} | all-to-all | bytes 1572864 | tf_op jit(solution)/shard_map/all_to_all | solution.py:412
  107.9 7.6 %feed_forward.1 = bf16[256,1536]{1,0:T(8,128)(2,1)} custom-call(bf16[256,1536]{1,0:T(8,128)(2,1)} %bitcast.50, bf16[2,4,1536,384]{3,2,1,0:T(8,128)(2,1)} %bitcast.47, bf16[2,4,1536,384]{3,2,1,0:T(8,128)(2,1)} %bitcast.48), custom_call_target="tpu_custom_call" | custom-call | tf_op jit(solution)/shard_map/feed_forward/pallas_call | solution.py:318
  115.6 3.6 %all-to-all-start.4 = ((bf16[4,64,1536]{2,1,0:T(8,128)(2,1)}), bf16[4,64,1536]{2,1,0:T(8,128)(2,1)S(1)}, u32[]{:S(2)}, u32[]{:S(2)}) async-start(bf16[4,64,1536]{2,1,0:T(8,128)(2,1)} %bitcast.49), calls=%async_computation.4 | async-start | bytes 1572864 | tf_op jit(solution)/shard_map/all_to_all | solution.py:414
  120.2 8.9 %all-to-all-done.4.part_ref = bf16[4,64,1536]{2,1,0:T(8,128)(2,1)S(1)} async-done(((bf16[4,64,1536]{2,1,0:T(8,128)(2,1)}), bf16[4,64,1536]{2,1,0:T(8,128)(2,1)S(1)}, u32[]{:S(2)}, u32[]{:S(2)}) %all-to-all-start.4) | async-done | bytes 786464 | tf_op jit(solution)/shard_map/all_to_all | solution.py:414
  129.1 1.1 last_stage.1
  (42 shorter events, 2.0 us)
Async XLA Ops:
  7.2 14.8 %copy-start = (bf16[1,154,2,1536]{3,2,1,0:T(2,128)(2,1)S(1)}, bf16[1,154,2,1536]{3,2,1,0:T(2,128)(2,1)}, u32[]{:S(2)}) copy-start(bf16[1,154,2,1536]{3,2,1,0:T(2,128)(2,1)} %param.14) | copy-start | bytes 2838532
  7.2 100.7 %all-gather.3.cloned.1.call-start = ((), (), s32[]{:S(2)}) async-start(), calls=%async_computation.5 | async-start | bytes 10027008 | tf_op jit(solution)/shard_map/all_gather | solution.py:383
  7.9 3.8 %copy-start.1 = (bf16[1536,3,96]{0,2,1:T(8,128)(2,1)S(1)}, bf16[1536,3,96]{0,2,1:T(8,128)(2,1)}, u32[]{:S(2)}) copy-start(bf16[1536,3,96]{0,2,1:T(8,128)(2,1)} %param.17) | copy-start | bytes 2654212
  12.4 21.8 %all-to-all-start = ((bf16[4,64,1536]{2,1,0:T(8,128)(2,1)}), bf16[4,64,1536]{2,1,0:T(8,128)(2,1)S(1)}, u32[]{:S(2)}, u32[]{:S(2)}) async-start(bf16[4,64,1536]{2,1,0:T(8,128)(2,1)} %get-tuple-element.23), calls=%async_computation | async-start | bytes 1572864 | tf_op jit(solution)/shard_map/all_to_all | solution.py:386
  16.7 10.2 %collective-permute-start = (bf16[2,48,1536]{2,1,0:T(8,128)(2,1)}, bf16[2,48,1536]{2,1,0:T(8,128)(2,1)S(1)}, u32[]{:S(2)}, u32[]{:S(2)}) collective-permute-start(bf16[2,48,1536]{2,1,0:T(8,128)(2,1)} %dynamic-slice_bitcast_fusion), channel_id=1, source_target_pairs={{0,2},{2,4},{4,6},{6,0},{1,3},{3,5},{5,7},{7,1},{8,10},{10,12},{12... | collective-permute-start | bytes 884744 | tf_op jit(solution)/shard_map/ppermute | solution.py:377
  18.3 10.2 %collective-permute-start.1 = (bf16[2,48,1536]{2,1,0:T(8,128)(2,1)}, bf16[2,48,1536]{2,1,0:T(8,128)(2,1)S(1)}, u32[]{:S(2)}, u32[]{:S(2)}) collective-permute-start(bf16[2,48,1536]{2,1,0:T(8,128)(2,1)} %dynamic-slice_bitcast_fusion), channel_id=1, source_target_pairs={{0,6},{2,0},{4,2},{6,4},{1,7},{3,1},{5,3},{7,5},{8,14},{10,8},{12,... | collective-permute-start | bytes 884744 | tf_op jit(solution)/shard_map/ppermute | solution.py:377
  19.9 14.2 %collective-permute-start.2 = (bf16[2,48,1536]{2,1,0:T(8,128)(2,1)}, bf16[2,48,1536]{2,1,0:T(8,128)(2,1)S(1)}, u32[]{:S(2)}, u32[]{:S(2)}) collective-permute-start(bf16[2,48,1536]{2,1,0:T(8,128)(2,1)} %dynamic-slice_bitcast_fusion), channel_id=1, source_target_pairs={{0,4},{2,6},{4,0},{6,2},{1,5},{3,7},{5,1},{7,3},{8,12},{10,14},{12... | collective-permute-start | bytes 884744 | tf_op jit(solution)/shard_map/ppermute | solution.py:377
  34.1 1.1 copy-start.7
  35.2 4.8 %collective-permute-start.6 = (bf16[3,2,48,1536]{3,2,1,0:T(8,128)(2,1)}, bf16[3,2,48,1536]{3,2,1,0:T(8,128)(2,1)}, u32[]{:S(2)}, u32[]{:S(2)}) collective-permute-start(bf16[3,2,48,1536]{3,2,1,0:T(8,128)(2,1)} %pad_maximum_fusion), channel_id=1, source_target_pairs={{0,32},{32,0},{1,33},{33,1},{2,34},{34,2},{3,35},{35,3},{4,36},{36... | collective-permute-start | bytes 2654216 | tf_op jit(solution)/shard_map/ppermute | solution.py:395
  36.0 12.2 %collective-permute-start.3 = (bf16[2,48,1536]{2,1,0:T(8,128)(2,1)}, bf16[2,48,1536]{2,1,0:T(8,128)(2,1)}, u32[]{:S(2)}, u32[]{:S(2)}) collective-permute-start(bf16[2,48,1536]{2,1,0:T(8,128)(2,1)} %pad_maximum_fusion.2), channel_id=1, source_target_pairs={{0,2},{2,4},{4,6},{6,0},{1,3},{3,5},{5,7},{7,1},{8,10},{10,12},{12... | collective-permute-start | bytes 884744 | tf_op jit(solution)/shard_map/ppermute | solution.py:377
  37.1 15.7 %collective-permute-start.4 = (bf16[2,48,1536]{2,1,0:T(8,128)(2,1)}, bf16[2,48,1536]{2,1,0:T(8,128)(2,1)}, u32[]{:S(2)}, u32[]{:S(2)}) collective-permute-start(bf16[2,48,1536]{2,1,0:T(8,128)(2,1)} %pad_maximum_fusion.2), channel_id=1, source_target_pairs={{0,6},{2,0},{4,2},{6,4},{1,7},{3,1},{5,3},{7,5},{8,14},{10,8},{12,... | collective-permute-start | bytes 884744 | tf_op jit(solution)/shard_map/ppermute | solution.py:377
  39.2 14.4 %collective-permute-start.5 = (bf16[2,48,1536]{2,1,0:T(8,128)(2,1)}, bf16[2,48,1536]{2,1,0:T(8,128)(2,1)}, u32[]{:S(2)}, u32[]{:S(2)}) collective-permute-start(bf16[2,48,1536]{2,1,0:T(8,128)(2,1)} %pad_maximum_fusion.2), channel_id=1, source_target_pairs={{0,4},{2,6},{4,0},{6,2},{1,5},{3,7},{5,1},{7,3},{8,12},{10,14},{12... | collective-permute-start | bytes 884744 | tf_op jit(solution)/shard_map/ppermute | solution.py:377
  43.4 26.6 %all-to-all-start.1 = ((bf16[4,2,256,384]{3,2,1,0:T(8,128)(2,1)}), bf16[4,2,256,384]{3,2,1,0:T(8,128)(2,1)S(1)}, u32[]{:S(2)}, u32[]{:S(2)}) async-start(bf16[4,2,256,384]{3,2,1,0:T(8,128)(2,1)} %project.2.refs_2_), calls=%async_computation.1 | async-start | bytes 3145728 | tf_op jit(solution)/shard_map/all_to_all | solution.py:400
  48.2 9.4 %copy-start.2 = (bf16[1536,3,96]{0,2,1:T(8,128)(2,1)S(1)}, bf16[1536,3,96]{0,2,1:T(8,128)(2,1)}, u32[]{:S(2)}) copy-start(bf16[1536,3,96]{0,2,1:T(8,128)(2,1)} %param.17) | copy-start | bytes 2654212
  54.9 4.9 %copy-start.5 = (bf16[1,154,2,384]{3,1,2,0:T(8,128)(2,1)S(1)}, bf16[1,154,2,384]{3,1,2,0:T(8,128)(2,1)}, u32[]{:S(2)}) copy-start(bf16[1,154,2,384]{3,1,2,0:T(8,128)(2,1)} %copy.16) | copy-start | bytes 709636
  54.9 2.7 %collective-permute-start.7 = (bf16[3,2,48,1536]{3,2,1,0:T(8,128)(2,1)S(1)}, bf16[3,2,48,1536]{3,2,1,0:T(8,128)(2,1)S(1)}, u32[]{:S(2)}, u32[]{:S(2)}) collective-permute-start(bf16[3,2,48,1536]{3,2,1,0:T(8,128)(2,1)S(1)} %pad_maximum_fusion.1), channel_id=1, source_target_pairs={{0,32},{32,0},{1,33},{33,1},{2,34},{34,2},{3,35},{35,3},{4,36},{36... | collective-permute-start | bytes 2654216 | tf_op jit(solution)/shard_map/ppermute | solution.py:402
  57.6 2.2 %copy-start.3 = (bf16[3,2,48,1536]{3,2,1,0:T(8,128)(2,1)}, bf16[3,2,48,1536]{3,2,1,0:T(8,128)(2,1)S(1)}, u32[]{:S(2)}) copy-start(bf16[3,2,48,1536]{3,2,1,0:T(8,128)(2,1)S(1)} %collective-permute-done.7.far_ref) | copy-start | bytes 2654212
  70.0 4.2 %copy-start.4 = (bf16[3,2,48,1536]{3,2,1,0:T(8,128)(2,1)S(1)}, bf16[3,2,48,1536]{3,2,1,0:T(8,128)(2,1)}, u32[]{:S(2)}) copy-start(bf16[3,2,48,1536]{3,2,1,0:T(8,128)(2,1)} %copy-done.3) | copy-start | bytes 2654212
  70.0 4.2 %copy-start.8 = (bf16[96,1536]{1,0:T(8,128)(2,1)S(1)}, bf16[96,1536]{1,0:T(8,128)(2,1)}, u32[]{:S(2)}) copy-start(bf16[96,1536]{1,0:T(8,128)(2,1)} %own_ref.1) | copy-start | bytes 884740
  74.2 18.4 %copy-start.6 = (bf16[1,64,1536]{2,1,0:T(8,128)(2,1)S(1)}, bf16[1,64,1536]{2,1,0:T(8,128)(2,1)}, u32[]{:S(2)}) copy-start(bf16[1,64,1536]{2,1,0:T(8,128)(2,1)} %param.11) | copy-start | bytes 589828
  74.2 18.4 %copy-start.9 = (f32[1,8,1536]{2,1,0:T(8,128)S(1)}, f32[1,8,1536]{2,1,0:T(8,128)}, u32[]{:S(2)}) copy-start(f32[1,8,1536]{2,1,0:T(8,128)} %param.13) | copy-start | bytes 147460
  115.5 4.3 %copy-start.10 = (bf16[1536,64]{0,1:T(8,128)(2,1)S(1)}, bf16[1536,64]{0,1:T(8,128)(2,1)}, u32[]{:S(2)}) copy-start(bf16[1536,64]{0,1:T(8,128)(2,1)} %param.21) | copy-start | bytes 589828
  115.5 14.7 %copy-start.11 = (f32[1,32,128]{2,1,0:T(8,128)S(1)}, f32[1,32,128]{2,1,0:T(8,128)}, u32[]{:S(2)}) copy-start(f32[1,32,128]{2,1,0:T(8,128)} %param.12) | copy-start | bytes 49156
  115.6 13.6 %all-to-all-start.4 = ((bf16[4,64,1536]{2,1,0:T(8,128)(2,1)}), bf16[4,64,1536]{2,1,0:T(8,128)(2,1)S(1)}, u32[]{:S(2)}, u32[]{:S(2)}) async-start(bf16[4,64,1536]{2,1,0:T(8,128)(2,1)} %bitcast.49), calls=%async_computation.4 | async-start | bytes 1572864 | tf_op jit(solution)/shard_map/all_to_all | solution.py:414
Sparse Core Ops, SparseCore 0:
  11.7 61.5 all-gather.2

commit v13 on v11

--- a/solution.py
+++ b/solution.py
@@ -109,35 +109,34 @@
 
 
 def project_kernel(first, pos_ref, h_ref, own_ref, n0_ref, n1_ref, n2_ref, far_ref, out_ref, w_ref):
-    count = out_ref.shape[1]
+    k = pl.program_id(0)
 
     def store(source, half, ref, index):
-        for k in range(count):
-            if ref is own_ref:
-                value = ref[first + k, index * 48 : index * 48 + 48, :]
-            elif index is None:
-                value = ref[k]
-            else:
-                value = ref[index, k]
-            w_ref[k, source, half] = value
+        if ref is own_ref:
+            value = ref[first + k, index * 48 : index * 48 + 48, :]
+        elif index is None:
+            value = ref[k]
+        else:
+            value = ref[index, k]
+        w_ref[source, half] = value
 
     assemble(pos_ref, own_ref, (n0_ref, n1_ref, n2_ref), far_ref, store)
-    h = h_ref[...]
-    for k in range(count):
-        w = w_ref[k].reshape(384, h.shape[1])
-        value = lax.dot_general(h, w, NT, preferred_element_type=F32).astype(BF)
-        for i in range(out_ref.shape[0]):
-            out_ref[i, k] = value
+    w = w_ref[...].reshape(384, h_ref.shape[1])
+    value = lax.dot_general(h_ref[...], w, NT, preferred_element_type=F32).astype(BF)
+    for i in range(out_ref.shape[0]):
+        out_ref[i, 0] = value
 
 
 def project(pos, h, own, first, count, copies, near, far):
     rows, width = h.shape
     return pl.pallas_call(
         functools.partial(project_kernel, first),
+        grid=(count,),
         out_shape=jax.ShapeDtypeStruct((copies, count, rows, 384), BF),
         in_specs=[pl.BlockSpec(memory_space=pltpu.SMEM)]
         + [pl.BlockSpec(memory_space=pltpu.VMEM)] * 6,
-        scratch_shapes=[pltpu.VMEM((count, 4, 2, 48, width), BF)],
+        out_specs=pl.BlockSpec((copies, 1, rows, 384), lambda k: (0, k, 0, 0)),
+        scratch_shapes=[pltpu.VMEM((4, 2, 48, width), BF)],
         compiler_params=params(14),
         name="project",
     )(pos, h, own, *near, far)

time: 135 us -> 135 us (level)
  no operation moved by 1% of the time
where the time goes in v13:
time: 135 us; the launch traced here: 132 us
  waiting for transfers between devices  33.1 us (25%)
  Pallas kernels  28 us (21%)
  blocking collectives  27.6 us (20%)
  starting transfers between devices  21.6 us (16%)
  between operations  15.6 us (12%)
  other arithmetic  4.38 us (3%)
  local copies, waits for them, and re-layouts  2.02 us (1%)
    all_to_all x1, blocking collectives, on_device(): h2 = lax.all_to_all(h2, 'ty', split_axis=0, concat_axis=0, tiled=True)  15.1 us
    all_to_all x1, blocking collectives, on_device(): lax.all_to_all(partial, 'tx', split_axis=0, concat_axis=0, tiled=True)  12.5 us
    ppermute x6, waiting for transfers between devices, to_lines(): return lax.ppermute(value, 'ty', [(i, (i + step) % 4) for i in range(4)])  10.9 us
    all_to_all x1, waiting for transfers between devices, on_device(): h1 = lax.all_to_all(h1, 'tx', split_axis=0, concat_axis=0, tiled=True)  8.53 us
    all_to_all x1, waiting for transfers between devices, on_device(): lax.all_to_all(partial, 'ty', split_axis=0, concat_axis=0, tiled=True)  8.46 us
    ppermute x6, starting transfers between devices, to_lines(): return lax.ppermute(value, 'ty', [(i, (i + step) % 4) for i in range(4)])  8.46 us
    pallas_call x2, Pallas kernels, attention(): pl.pallas_call(functools.partial(attention_kernel, own), out_shape=out, i...  7.71 us
    pallas_call x1, Pallas kernels, feed_forward(): pl.pallas_call(ffn_kernel, grid=(4,), out_shape=jax.ShapeDtypeStruct((row...  7.66 us
  transfers between devices with their start and end apart: 12, of which 7 were waited for; matrix products, arithmetic and copies ran while one was open for 4% of the time, Pallas kernels for 12%

profile of v13, /device:TPU:128, one launch (start us, length us, event | category | flops | bytes accessed | tf_op | source)
XLA Modules:
  0.0 132.3 jit_solution(2346287098790769686)
XLA Ops:
  7.2 0.6 pad_add_fusion.1.pos_ref
  7.8 3.7 %first_norm_and_pack.1 = (bf16[4,64,1536]{2,1,0:T(8,128)(2,1)}, bf16[768,384]{1,0:T(8,128)(2,1)}) custom-call(s32[2]{0:T(128)} %pad_add_fusion.1.pos_ref, bf16[64,1536]{1,0:T(8,128)(2,1)} %bitcast.42, f32[8,1536]{1,0:T(8,128)} %bitcast.44, bf16[1536,384]{1,0:T(8,128)(2,1)} %up_ref.1, bf16[384,1536]{1,0:T(8,128)(2,1)} %down_ref.1), custom_call_target="tpu_custom_call" | custom-call | tf_op jit(solution)/shard_map/first_norm_and_pack/pallas_call | solution.py:77
  11.6 0.7 dynamic-slice_bitcast_fusion
  12.3 1.6 %collective-permute-start.3 = (bf16[2,48,1536]{2,1,0:T(8,128)(2,1)}, bf16[2,48,1536]{2,1,0:T(8,128)(2,1)S(1)}, u32[]{:S(2)}, u32[]{:S(2)}) collective-permute-start(bf16[2,48,1536]{2,1,0:T(8,128)(2,1)} %dynamic-slice_bitcast_fusion), channel_id=1, source_target_pairs={{0,2},{2,4},{4,6},{6,0},{1,3},{3,5},{5,7},{7,1},{8,10},{10,12},{12... | collective-permute-start | bytes 884744 | tf_op jit(solution)/shard_map/ppermute | solution.py:376
  13.9 1.7 %collective-permute-start.4 = (bf16[2,48,1536]{2,1,0:T(8,128)(2,1)}, bf16[2,48,1536]{2,1,0:T(8,128)(2,1)S(1)}, u32[]{:S(2)}, u32[]{:S(2)}) collective-permute-start(bf16[2,48,1536]{2,1,0:T(8,128)(2,1)} %dynamic-slice_bitcast_fusion), channel_id=1, source_target_pairs={{0,6},{2,0},{4,2},{6,4},{1,7},{3,1},{5,3},{7,5},{8,14},{10,8},{12,... | collective-permute-start | bytes 884744 | tf_op jit(solution)/shard_map/ppermute | solution.py:376
  15.6 2.0 %collective-permute-start.5 = (bf16[2,48,1536]{2,1,0:T(8,128)(2,1)}, bf16[2,48,1536]{2,1,0:T(8,128)(2,1)S(1)}, u32[]{:S(2)}, u32[]{:S(2)}) collective-permute-start(bf16[2,48,1536]{2,1,0:T(8,128)(2,1)} %dynamic-slice_bitcast_fusion), channel_id=1, source_target_pairs={{0,4},{2,6},{4,0},{6,2},{1,5},{3,7},{5,1},{7,3},{8,12},{10,14},{12... | collective-permute-start | bytes 884744 | tf_op jit(solution)/shard_map/ppermute | solution.py:376
  17.6 4.3 %all-to-all-start = ((bf16[4,64,1536]{2,1,0:T(8,128)(2,1)}), bf16[4,64,1536]{2,1,0:T(8,128)(2,1)S(1)}, u32[]{:S(2)}, u32[]{:S(2)}) async-start(bf16[4,64,1536]{2,1,0:T(8,128)(2,1)} %get-tuple-element.18), calls=%async_computation | async-start | bytes 1572864 | tf_op jit(solution)/shard_map/all_to_all | solution.py:385
  22.0 0.7 copy.16
  22.8 1.3 collective-permute-done.4.n1_ref
  24.1 6.0 %collective-permute-done.5.n2_ref = bf16[2,48,1536]{2,1,0:T(8,128)(2,1)S(1)} collective-permute-done((bf16[2,48,1536]{2,1,0:T(8,128)(2,1)}, bf16[2,48,1536]{2,1,0:T(8,128)(2,1)S(1)}, u32[]{:S(2)}, u32[]{:S(2)}) %collective-permute-start.5) | collective-permute-done | bytes 294944 | tf_op jit(solution)/shard_map/ppermute | solution.py:376
  30.1 1.1 pad_maximum_fusion
  31.2 0.7 pad_maximum_fusion.2
  32.0 8.5 %all-to-all-done = bf16[4,64,1536]{2,1,0:T(8,128)(2,1)S(1)} async-done(((bf16[4,64,1536]{2,1,0:T(8,128)(2,1)}), bf16[4,64,1536]{2,1,0:T(8,128)(2,1)S(1)}, u32[]{:S(2)}, u32[]{:S(2)}) %all-to-all-start) | async-done | bytes 786464 | tf_op jit(solution)/shard_map/all_to_all | solution.py:385
  40.5 3.2 %collective-permute-start.1 = (bf16[2,48,1536]{2,1,0:T(8,128)(2,1)}, bf16[2,48,1536]{2,1,0:T(8,128)(2,1)}, u32[]{:S(2)}, u32[]{:S(2)}) collective-permute-start(bf16[2,48,1536]{2,1,0:T(8,128)(2,1)} %pad_maximum_fusion.2), channel_id=1, source_target_pairs={{0,6},{2,0},{4,2},{6,4},{1,7},{3,1},{5,3},{7,5},{8,14},{10,8},{12,... | collective-permute-start | bytes 884744 | tf_op jit(solution)/shard_map/ppermute | solution.py:376
  44.5 3.4 %project.2.refs_2_ = bf16[4,2,256,384]{3,2,1,0:T(8,128)(2,1)} custom-call(s32[3]{0:T(128)S(1)} %pad_add_fusion.pos_ref.refs_0_, bf16[256,1536]{1,0:T(8,128)(2,1)S(1)} %bitcast.31, bf16[3,96,1536]{2,1,0:T(8,128)(2,1)S(1)} %bitcast.33, bf16[2,48,1536]{2,1,0:T(8,128)(2,1)S(1)} %collective-permute-done.3.n0_ref, ...), custom_call_target="tpu_custom_call" | custom-call | tf_op jit(solution)/shard_map/project/pallas_call | solution.py:132
  47.9 4.9 %all-to-all-start.1 = ((bf16[4,2,256,384]{3,2,1,0:T(8,128)(2,1)}), bf16[4,2,256,384]{3,2,1,0:T(8,128)(2,1)S(1)}, u32[]{:S(2)}, u32[]{:S(2)}) async-start(bf16[4,2,256,384]{3,2,1,0:T(8,128)(2,1)} %project.2.refs_2_), calls=%async_computation.1 | async-start | bytes 3145728 | tf_op jit(solution)/shard_map/all_to_all | solution.py:398
  52.8 3.6 %collective-permute-done.1.n1_ref = bf16[2,48,1536]{2,1,0:T(8,128)(2,1)} collective-permute-done((bf16[2,48,1536]{2,1,0:T(8,128)(2,1)}, bf16[2,48,1536]{2,1,0:T(8,128)(2,1)}, u32[]{:S(2)}, u32[]{:S(2)}) %collective-permute-start.1) | collective-permute-done | bytes 294944 | tf_op jit(solution)/shard_map/ppermute | solution.py:376
  56.4 1.3 pad_maximum_fusion.1
  57.9 2.4 %collective-permute-done.7.far_ref = bf16[3,2,48,1536]{3,2,1,0:T(8,128)(2,1)S(1)} collective-permute-done((bf16[3,2,48,1536]{3,2,1,0:T(8,128)(2,1)S(1)}, bf16[3,2,48,1536]{3,2,1,0:T(8,128)(2,1)S(1)}, u32[]{:S(2)}, u32[]{:S(2)}) %collective-permute-start.7) | collective-permute-done | bytes 884768 | tf_op jit(solution)/shard_map/ppermute | solution.py:400
  60.3 2.2 %project.3 = bf16[1,1,256,384]{3,2,1,0:T(8,128)(2,1)S(1)} custom-call(s32[3]{0:T(128)S(1)} %pad_add_fusion.pos_ref.refs_0_, bf16[256,1536]{1,0:T(8,128)(2,1)S(1)} %bitcast.32, bf16[3,96,1536]{2,1,0:T(8,128)(2,1)S(1)} %bitcast.34, bf16[2,48,1536]{2,1,0:T(8,128)(2,1)} %collective-permute-done.n0_ref, bf16[2,48,1536]{2,1,0:T(8,128)(2,1)} %collective-permute-done.1.n1_ref, ...), custom_call_target="tpu_custom_call" | custom-call | tf_op jit(solution)/shard_map/project/pallas_call | solution.py:132
  62.5 3.5 %attention.2.refs_3_ = f32[256,512]{1,0:T(8,128)S(1)} custom-call(s32[3]{0:T(128)S(1)} %pad_add_fusion.pos_ref.refs_0_, bf16[256,384]{1,0:T(8,128)(2,1)S(1)} %bitcast.36, bf16[4,2,256,384]{3,2,1,0:T(8,128)(2,1)} %project.2.refs_2_, bf16[2,154,384]{2,1,0:T(8,128)(2,1)S(1)} %bitcast.41), custom_call_target="tpu_custom_call" | custom-call | tf_op jit(solution)/shard_map/attention/pallas_call | solution.py:224
  66.0 2.8 %all-to-all-done.1.refs_2_ = bf16[4,2,256,384]{3,2,1,0:T(8,128)(2,1)S(1)} async-done(((bf16[4,2,256,384]{3,2,1,0:T(8,128)(2,1)}), bf16[4,2,256,384]{3,2,1,0:T(8,128)(2,1)S(1)}, u32[]{:S(2)}, u32[]{:S(2)}) %all-to-all-start.1) | async-done | bytes 1572896 | tf_op jit(solution)/shard_map/all_to_all | solution.py:398
  68.8 4.2 %attention.3.a_ref = bf16[256,384]{1,0:T(8,128)(2,1)S(1)} custom-call(s32[3]{0:T(128)S(1)} %pad_add_fusion.pos_ref.refs_0_, bf16[256,384]{1,0:T(8,128)(2,1)S(1)} %bitcast.37, bf16[4,2,256,384]{3,2,1,0:T(8,128)(2,1)S(1)} %all-to-all-done.1.refs_2_, f32[256,512]{1,0:T(8,128)S(1)} %attention.2.refs_3_), custom_call_target="tpu_custom_call" | custom-call | tf_op jit(solution)/shard_map/attention/pallas_call | solution.py:224
  73.1 1.9 %out_projection.1 = bf16[256,1536]{1,0:T(8,128)(2,1)S(1)} custom-call(s32[3]{0:T(128)S(1)} %pad_add_fusion.pos_ref.refs_0_, bf16[256,384]{1,0:T(8,128)(2,1)S(1)} %attention.3.a_ref, bf16[96,1536]{1,0:T(8,128)(2,1)S(1)} %copy-done.8, bf16[2,48,1536]{2,1,0:T(8,128)(2,1)} %collective-permute-done.n0_ref, bf16[2,48,1536]{2,1,0:T(8,128)(2,1)} %collective-permute-done.1.n1_ref, ...), custom_call_target="tpu_custom_call" | custom-call | tf_op jit(solution)/shard_map/out_projection/pallas_call | solution.py:253
  75.0 12.5 %all_to_all.25.part_ref = bf16[4,64,1536]{2,1,0:T(8,128)(2,1)S(1)} all-to-all(bf16[4,64,1536]{2,1,0:T(8,128)(2,1)S(1)} %bitcast.35), channel_id=1, replica_groups=mesh['zl'=2,'zp'=2,'core'=2,'tx'=4,'ty'=4,'blk'=2] {'tx'}, dimensions={0} | all-to-all | bytes 1572864 | tf_op jit(solution)/shard_map/all_to_all | solution.py:408
  87.5 0.4 second_norm.1
  87.8 15.1 %all_to_all.26 = bf16[4,64,1536]{2,1,0:T(8,128)(2,1)} all-to-all(bf16[4,64,1536]{2,1,0:T(8,128)(2,1)S(1)} %get-tuple-element.28), channel_id=1, replica_groups=mesh['zl'=2,'zp'=2,'core'=2,'tx'=4,'ty'=4,'blk'=2] {'ty'}, dimensions={0} | all-to-all | bytes 1572864 | tf_op jit(solution)/shard_map/all_to_all | solution.py:410
  102.9 7.7 %feed_forward.1 = bf16[256,1536]{1,0:T(8,128)(2,1)} custom-call(bf16[256,1536]{1,0:T(8,128)(2,1)} %bitcast.50, bf16[2,4,1536,384]{3,2,1,0:T(8,128)(2,1)} %bitcast.47, bf16[2,4,1536,384]{3,2,1,0:T(8,128)(2,1)} %bitcast.48), custom_call_target="tpu_custom_call" | custom-call | tf_op jit(solution)/shard_map/feed_forward/pallas_call | solution.py:317
  110.6 3.6 %all-to-all-start.4 = ((bf16[4,64,1536]{2,1,0:T(8,128)(2,1)}), bf16[4,64,1536]{2,1,0:T(8,128)(2,1)S(1)}, u32[]{:S(2)}, u32[]{:S(2)}) async-start(bf16[4,64,1536]{2,1,0:T(8,128)(2,1)} %bitcast.49), calls=%async_computation.4 | async-start | bytes 1572864 | tf_op jit(solution)/shard_map/all_to_all | solution.py:412
  115.2 8.5 %all-to-all-done.4.part_ref = bf16[4,64,1536]{2,1,0:T(8,128)(2,1)S(1)} async-done(((bf16[4,64,1536]{2,1,0:T(8,128)(2,1)}), bf16[4,64,1536]{2,1,0:T(8,128)(2,1)S(1)}, u32[]{:S(2)}, u32[]{:S(2)}) %all-to-all-start.4) | async-done | bytes 786464 | tf_op jit(solution)/shard_map/all_to_all | solution.py:412
  123.7 1.1 last_stage.1
  124.8 0.6 add.27
  (42 shorter events, 1.0 us)
Async XLA Ops:
  7.2 14.7 %copy-start = (bf16[1,154,2,1536]{3,2,1,0:T(2,128)(2,1)S(1)}, bf16[1,154,2,1536]{3,2,1,0:T(2,128)(2,1)}, u32[]{:S(2)}) copy-start(bf16[1,154,2,1536]{3,2,1,0:T(2,128)(2,1)} %param.14) | copy-start | bytes 2838532
  7.2 95.8 %all-gather.3.cloned.1.call-start = ((), (), s32[]{:S(2)}) async-start(), calls=%async_computation.5 | async-start | bytes 10027008 | tf_op jit(solution)/shard_map/all_gather | solution.py:382
  7.8 3.8 %copy-start.1 = (bf16[1536,3,96]{0,2,1:T(8,128)(2,1)S(1)}, bf16[1536,3,96]{0,2,1:T(8,128)(2,1)}, u32[]{:S(2)}) copy-start(bf16[1536,3,96]{0,2,1:T(8,128)(2,1)} %param.17) | copy-start | bytes 2654212
  12.3 10.4 %collective-permute-start.3 = (bf16[2,48,1536]{2,1,0:T(8,128)(2,1)}, bf16[2,48,1536]{2,1,0:T(8,128)(2,1)S(1)}, u32[]{:S(2)}, u32[]{:S(2)}) collective-permute-start(bf16[2,48,1536]{2,1,0:T(8,128)(2,1)} %dynamic-slice_bitcast_fusion), channel_id=1, source_target_pairs={{0,2},{2,4},{4,6},{6,0},{1,3},{3,5},{5,7},{7,1},{8,10},{10,12},{12... | collective-permute-start | bytes 884744 | tf_op jit(solution)/shard_map/ppermute | solution.py:376
  13.9 10.1 %collective-permute-start.4 = (bf16[2,48,1536]{2,1,0:T(8,128)(2,1)}, bf16[2,48,1536]{2,1,0:T(8,128)(2,1)S(1)}, u32[]{:S(2)}, u32[]{:S(2)}) collective-permute-start(bf16[2,48,1536]{2,1,0:T(8,128)(2,1)} %dynamic-slice_bitcast_fusion), channel_id=1, source_target_pairs={{0,6},{2,0},{4,2},{6,4},{1,7},{3,1},{5,3},{7,5},{8,14},{10,8},{12,... | collective-permute-start | bytes 884744 | tf_op jit(solution)/shard_map/ppermute | solution.py:376
  15.6 14.5 %collective-permute-start.5 = (bf16[2,48,1536]{2,1,0:T(8,128)(2,1)}, bf16[2,48,1536]{2,1,0:T(8,128)(2,1)S(1)}, u32[]{:S(2)}, u32[]{:S(2)}) collective-permute-start(bf16[2,48,1536]{2,1,0:T(8,128)(2,1)} %dynamic-slice_bitcast_fusion), channel_id=1, source_target_pairs={{0,4},{2,6},{4,0},{6,2},{1,5},{3,7},{5,1},{7,3},{8,12},{10,14},{12... | collective-permute-start | bytes 884744 | tf_op jit(solution)/shard_map/ppermute | solution.py:376
  17.6 22.9 %all-to-all-start = ((bf16[4,64,1536]{2,1,0:T(8,128)(2,1)}), bf16[4,64,1536]{2,1,0:T(8,128)(2,1)S(1)}, u32[]{:S(2)}, u32[]{:S(2)}) async-start(bf16[4,64,1536]{2,1,0:T(8,128)(2,1)} %get-tuple-element.18), calls=%async_computation | async-start | bytes 1572864 | tf_op jit(solution)/shard_map/all_to_all | solution.py:385
  21.9 9.3 %copy-start.7 = (bf16[96,1536]{1,0:T(8,128)(2,1)S(1)}, bf16[96,1536]{1,0:T(8,128)(2,1)}, u32[]{:S(2)}) copy-start(bf16[96,1536]{1,0:T(8,128)(2,1)} %own_ref.1) | copy-start | bytes 884740
  31.2 13.3 %collective-permute-start.6 = (bf16[3,2,48,1536]{3,2,1,0:T(8,128)(2,1)}, bf16[3,2,48,1536]{3,2,1,0:T(8,128)(2,1)}, u32[]{:S(2)}, u32[]{:S(2)}) collective-permute-start(bf16[3,2,48,1536]{3,2,1,0:T(8,128)(2,1)} %pad_maximum_fusion), channel_id=1, source_target_pairs={{0,32},{32,0},{1,33},{33,1},{2,34},{34,2},{3,35},{35,3},{4,36},{36... | collective-permute-start | bytes 2654216 | tf_op jit(solution)/shard_map/ppermute | solution.py:393
  40.5 12.3 %collective-permute-start = (bf16[2,48,1536]{2,1,0:T(8,128)(2,1)}, bf16[2,48,1536]{2,1,0:T(8,128)(2,1)}, u32[]{:S(2)}, u32[]{:S(2)}) collective-permute-start(bf16[2,48,1536]{2,1,0:T(8,128)(2,1)} %pad_maximum_fusion.2), channel_id=1, source_target_pairs={{0,2},{2,4},{4,6},{6,0},{1,3},{3,5},{5,7},{7,1},{8,10},{10,12},{12... | collective-permute-start | bytes 884744 | tf_op jit(solution)/shard_map/ppermute | solution.py:376
  40.5 15.9 %collective-permute-start.1 = (bf16[2,48,1536]{2,1,0:T(8,128)(2,1)}, bf16[2,48,1536]{2,1,0:T(8,128)(2,1)}, u32[]{:S(2)}, u32[]{:S(2)}) collective-permute-start(bf16[2,48,1536]{2,1,0:T(8,128)(2,1)} %pad_maximum_fusion.2), channel_id=1, source_target_pairs={{0,6},{2,0},{4,2},{6,4},{1,7},{3,1},{5,3},{7,5},{8,14},{10,8},{12,... | collective-permute-start | bytes 884744 | tf_op jit(solution)/shard_map/ppermute | solution.py:376
  43.7 12.6 %collective-permute-start.2 = (bf16[2,48,1536]{2,1,0:T(8,128)(2,1)}, bf16[2,48,1536]{2,1,0:T(8,128)(2,1)}, u32[]{:S(2)}, u32[]{:S(2)}) collective-permute-start(bf16[2,48,1536]{2,1,0:T(8,128)(2,1)} %pad_maximum_fusion.2), channel_id=1, source_target_pairs={{0,4},{2,6},{4,0},{6,2},{1,5},{3,7},{5,1},{7,3},{8,12},{10,14},{12... | collective-permute-start | bytes 884744 | tf_op jit(solution)/shard_map/ppermute | solution.py:376
  47.9 20.9 %all-to-all-start.1 = ((bf16[4,2,256,384]{3,2,1,0:T(8,128)(2,1)}), bf16[4,2,256,384]{3,2,1,0:T(8,128)(2,1)S(1)}, u32[]{:S(2)}, u32[]{:S(2)}) async-start(bf16[4,2,256,384]{3,2,1,0:T(8,128)(2,1)} %project.2.refs_2_), calls=%async_computation.1 | async-start | bytes 3145728 | tf_op jit(solution)/shard_map/all_to_all | solution.py:398
  52.8 7.6 %copy-start.2 = (bf16[1536,3,96]{0,2,1:T(8,128)(2,1)S(1)}, bf16[1536,3,96]{0,2,1:T(8,128)(2,1)}, u32[]{:S(2)}) copy-start(bf16[1536,3,96]{0,2,1:T(8,128)(2,1)} %param.17) | copy-start | bytes 2654212
  57.6 4.9 %copy-start.5 = (bf16[1,154,2,384]{3,1,2,0:T(8,128)(2,1)S(1)}, bf16[1,154,2,384]{3,1,2,0:T(8,128)(2,1)}, u32[]{:S(2)}) copy-start(bf16[1,154,2,384]{3,1,2,0:T(8,128)(2,1)} %copy.16) | copy-start | bytes 709636
  57.6 2.7 %collective-permute-start.7 = (bf16[3,2,48,1536]{3,2,1,0:T(8,128)(2,1)S(1)}, bf16[3,2,48,1536]{3,2,1,0:T(8,128)(2,1)S(1)}, u32[]{:S(2)}, u32[]{:S(2)}) collective-permute-start(bf16[3,2,48,1536]{3,2,1,0:T(8,128)(2,1)S(1)} %pad_maximum_fusion.1), channel_id=1, source_target_pairs={{0,32},{32,0},{1,33},{33,1},{2,34},{34,2},{3,35},{35,3},{4,36},{36... | collective-permute-start | bytes 2654216 | tf_op jit(solution)/shard_map/ppermute | solution.py:400
  60.3 2.2 %copy-start.3 = (bf16[3,2,48,1536]{3,2,1,0:T(8,128)(2,1)}, bf16[3,2,48,1536]{3,2,1,0:T(8,128)(2,1)S(1)}, u32[]{:S(2)}) copy-start(bf16[3,2,48,1536]{3,2,1,0:T(8,128)(2,1)S(1)} %collective-permute-done.7.far_ref) | copy-start | bytes 2654212
  68.8 4.2 %copy-start.4 = (bf16[3,2,48,1536]{3,2,1,0:T(8,128)(2,1)S(1)}, bf16[3,2,48,1536]{3,2,1,0:T(8,128)(2,1)}, u32[]{:S(2)}) copy-start(bf16[3,2,48,1536]{3,2,1,0:T(8,128)(2,1)} %copy-done.3) | copy-start | bytes 2654212
  68.8 4.2 %copy-start.8 = (bf16[96,1536]{1,0:T(8,128)(2,1)S(1)}, bf16[96,1536]{1,0:T(8,128)(2,1)}, u32[]{:S(2)}) copy-start(bf16[96,1536]{1,0:T(8,128)(2,1)} %own_ref.1) | copy-start | bytes 884740
  73.1 14.4 %copy-start.6 = (bf16[1,64,1536]{2,1,0:T(8,128)(2,1)S(1)}, bf16[1,64,1536]{2,1,0:T(8,128)(2,1)}, u32[]{:S(2)}) copy-start(bf16[1,64,1536]{2,1,0:T(8,128)(2,1)} %param.11) | copy-start | bytes 589828
  73.1 14.4 %copy-start.9 = (f32[1,8,1536]{2,1,0:T(8,128)S(1)}, f32[1,8,1536]{2,1,0:T(8,128)}, u32[]{:S(2)}) copy-start(f32[1,8,1536]{2,1,0:T(8,128)} %param.13) | copy-start | bytes 147460
  110.6 4.3 %copy-start.10 = (bf16[1536,64]{0,1:T(8,128)(2,1)S(1)}, bf16[1536,64]{0,1:T(8,128)(2,1)}, u32[]{:S(2)}) copy-start(bf16[1536,64]{0,1:T(8,128)(2,1)} %param.21) | copy-start | bytes 589828
  110.6 14.2 %copy-start.11 = (f32[1,32,128]{2,1,0:T(8,128)S(1)}, f32[1,32,128]{2,1,0:T(8,128)}, u32[]{:S(2)}) copy-start(f32[1,32,128]{2,1,0:T(8,128)} %param.12) | copy-start | bytes 49156
  110.6 13.1 %all-to-all-start.4 = ((bf16[4,64,1536]{2,1,0:T(8,128)(2,1)}), bf16[4,64,1536]{2,1,0:T(8,128)(2,1)S(1)}, u32[]{:S(2)}, u32[]{:S(2)}) async-start(bf16[4,64,1536]{2,1,0:T(8,128)(2,1)} %bitcast.49), calls=%async_computation.4 | async-start | bytes 1572864 | tf_op jit(solution)/shard_map/all_to_all | solution.py:412
Sparse Core Ops, SparseCore 0:
  11.7 65.9 all-gather.2

commit v14 on v11

--- a/solution.py
+++ b/solution.py
@@ -14,7 +14,7 @@
 F32 = jnp.float32
 NT = (((1,), (1,)), ((), ()))
 NN = (((1,), (0,)), ((), ()))
-STRIDES = (1, 3, 2)
+STRIDES = (2, 1, 3)
 
 
 def params(mebibytes):

time: 135 us -> 134 us (level)
  blocking collectives: 27.4 us -> 24.5 us
  waiting for transfers between devices: 33.1 us -> 35.6 us
    all_to_all x1, waiting for transfers between devices: 8.53 us -> 11.5 us  [on_device(): h1 = lax.all_to_all(h1, 'tx', split_axis=0, concat_axis=0, tiled=True)]
    all_to_all x1, blocking collectives: 15 us -> 12.6 us  [on_device(): h2 = lax.all_to_all(h2, 'ty', split_axis=0, concat_axis=0, tiled=True)]
    ppermute x6, waiting for transfers between devices: 10.8 us -> 8.56 us  [to_lines(): return lax.ppermute(value, 'ty', [(i, (i + step) % 4) for i in range(4)])]
    all_to_all x1, waiting for transfers between devices: 2.87 us -> 4.64 us  [on_device(): lax.all_to_all(own_kv, 'ty', split_axis=0, concat_axis=0, tiled=True)]
where the time goes in v14:
time: 134 us; the launch traced here: 132 us
  waiting for transfers between devices  35.6 us (27%)
  Pallas kernels  28 us (21%)
  blocking collectives  24.5 us (18%)
  starting transfers between devices  21.5 us (16%)
  between operations  15.7 us (12%)
  other arithmetic  4.43 us (3%)
  local copies, waits for them, and re-layouts  2.02 us (2%)
    all_to_all x1, blocking collectives, on_device(): h2 = lax.all_to_all(h2, 'ty', split_axis=0, concat_axis=0, tiled=True)  12.6 us
    all_to_all x1, blocking collectives, on_device(): lax.all_to_all(partial, 'tx', split_axis=0, concat_axis=0, tiled=True)  11.9 us
    all_to_all x1, waiting for transfers between devices, on_device(): h1 = lax.all_to_all(h1, 'tx', split_axis=0, concat_axis=0, tiled=True)  11.5 us
    ppermute x6, starting transfers between devices, to_lines(): return lax.ppermute(value, 'ty', [(i, (i + step) % 4) for i in range(4)])  9.67 us
    ppermute x6, waiting for transfers between devices, to_lines(): return lax.ppermute(value, 'ty', [(i, (i + step) % 4) for i in range(4)])  8.56 us
    all_to_all x1, waiting for transfers between devices, on_device(): lax.all_to_all(partial, 'ty', split_axis=0, concat_axis=0, tiled=True)  8.46 us
    pallas_call x2, Pallas kernels, attention(): pl.pallas_call(functools.partial(attention_kernel, own), out_shape=out, i...  7.75 us
    pallas_call x1, Pallas kernels, feed_forward(): pl.pallas_call(ffn_kernel, grid=(4,), out_shape=jax.ShapeDtypeStruct((row...  7.66 us
  transfers between devices with their start and end apart: 12, of which 7 were waited for; matrix products, arithmetic and copies ran while one was open for 4% of the time, Pallas kernels for 12%

profile of v14, /device:TPU:128, one launch (start us, length us, event | category | flops | bytes accessed | tf_op | source)
XLA Modules:
  0.0 131.8 jit_solution(3371342767493147339)
XLA Ops:
  7.2 0.6 pad_add_fusion.1.pos_ref
  7.8 3.7 %first_norm_and_pack.1 = (bf16[4,64,1536]{2,1,0:T(8,128)(2,1)}, bf16[768,384]{1,0:T(8,128)(2,1)}) custom-call(s32[2]{0:T(128)} %pad_add_fusion.1.pos_ref, bf16[64,1536]{1,0:T(8,128)(2,1)} %bitcast.42, f32[8,1536]{1,0:T(8,128)} %bitcast.44, bf16[1536,384]{1,0:T(8,128)(2,1)} %up_ref.1, bf16[384,1536]{1,0:T(8,128)(2,1)} %down_ref.1), custom_call_target="tpu_custom_call" | custom-call | tf_op jit(solution)/shard_map/first_norm_and_pack/pallas_call | solution.py:77
  11.6 0.7 dynamic-slice_bitcast_fusion
  12.3 3.2 %collective-permute-start.3 = (bf16[2,48,1536]{2,1,0:T(8,128)(2,1)}, bf16[2,48,1536]{2,1,0:T(8,128)(2,1)S(1)}, u32[]{:S(2)}, u32[]{:S(2)}) collective-permute-start(bf16[2,48,1536]{2,1,0:T(8,128)(2,1)} %dynamic-slice_bitcast_fusion), channel_id=1, source_target_pairs={{0,4},{2,6},{4,0},{6,2},{1,5},{3,7},{5,1},{7,3},{8,12},{10,14},{12... | collective-permute-start | bytes 884744 | tf_op jit(solution)/shard_map/ppermute | solution.py:377
  15.5 0.7 collective-permute-start.4
  16.2 2.6 %collective-permute-start.5 = (bf16[2,48,1536]{2,1,0:T(8,128)(2,1)}, bf16[2,48,1536]{2,1,0:T(8,128)(2,1)S(1)}, u32[]{:S(2)}, u32[]{:S(2)}) collective-permute-start(bf16[2,48,1536]{2,1,0:T(8,128)(2,1)} %dynamic-slice_bitcast_fusion), channel_id=1, source_target_pairs={{0,6},{2,0},{4,2},{6,4},{1,7},{3,1},{5,3},{7,5},{8,14},{10,8},{12,... | collective-permute-start | bytes 884744 | tf_op jit(solution)/shard_map/ppermute | solution.py:377
  18.8 4.3 %all-to-all-start = ((bf16[4,64,1536]{2,1,0:T(8,128)(2,1)}), bf16[4,64,1536]{2,1,0:T(8,128)(2,1)S(1)}, u32[]{:S(2)}, u32[]{:S(2)}) async-start(bf16[4,64,1536]{2,1,0:T(8,128)(2,1)} %get-tuple-element.18), calls=%async_computation | async-start | bytes 1572864 | tf_op jit(solution)/shard_map/all_to_all | solution.py:386
  23.2 0.7 copy.16
  24.0 5.1 %collective-permute-done.4.n1_ref = bf16[2,48,1536]{2,1,0:T(8,128)(2,1)S(1)} collective-permute-done((bf16[2,48,1536]{2,1,0:T(8,128)(2,1)}, bf16[2,48,1536]{2,1,0:T(8,128)(2,1)S(1)}, u32[]{:S(2)}, u32[]{:S(2)}) %collective-permute-start.4) | collective-permute-done | bytes 294944 | tf_op jit(solution)/shard_map/ppermute | solution.py:377
  29.1 0.4 collective-permute-done.5.n2_ref
  29.5 1.1 pad_maximum_fusion
  30.7 0.7 pad_maximum_fusion.2
  31.4 11.5 %all-to-all-done = bf16[4,64,1536]{2,1,0:T(8,128)(2,1)S(1)} async-done(((bf16[4,64,1536]{2,1,0:T(8,128)(2,1)}), bf16[4,64,1536]{2,1,0:T(8,128)(2,1)S(1)}, u32[]{:S(2)}, u32[]{:S(2)}) %all-to-all-start) | async-done | bytes 786464 | tf_op jit(solution)/shard_map/all_to_all | solution.py:386
  42.9 3.2 %collective-permute-start.2 = (bf16[2,48,1536]{2,1,0:T(8,128)(2,1)}, bf16[2,48,1536]{2,1,0:T(8,128)(2,1)}, u32[]{:S(2)}, u32[]{:S(2)}) collective-permute-start(bf16[2,48,1536]{2,1,0:T(8,128)(2,1)} %pad_maximum_fusion.2), channel_id=1, source_target_pairs={{0,6},{2,0},{4,2},{6,4},{1,7},{3,1},{5,3},{7,5},{8,14},{10,8},{12,... | collective-permute-start | bytes 884744 | tf_op jit(solution)/shard_map/ppermute | solution.py:377
  46.9 3.5 %project.2.refs_2_ = bf16[4,2,256,384]{3,2,1,0:T(8,128)(2,1)} custom-call(s32[3]{0:T(128)S(1)} %pad_add_fusion.pos_ref.refs_0_, bf16[256,1536]{1,0:T(8,128)(2,1)S(1)} %bitcast.31, bf16[3,96,1536]{2,1,0:T(8,128)(2,1)S(1)} %bitcast.33, bf16[2,48,1536]{2,1,0:T(8,128)(2,1)S(1)} %collective-permute-done.3.n0_ref, ...), custom_call_target="tpu_custom_call" | custom-call | tf_op jit(solution)/shard_map/project/pallas_call | solution.py:135
  50.4 3.6 %all-to-all-start.1 = ((bf16[4,2,256,384]{3,2,1,0:T(8,128)(2,1)}), bf16[4,2,256,384]{3,2,1,0:T(8,128)(2,1)S(1)}, u32[]{:S(2)}, u32[]{:S(2)}) async-start(bf16[4,2,256,384]{3,2,1,0:T(8,128)(2,1)} %project.2.refs_2_), calls=%async_computation.1 | async-start | bytes 3145728 | tf_op jit(solution)/shard_map/all_to_all | solution.py:399
  54.0 3.0 %collective-permute-done.1.n1_ref = bf16[2,48,1536]{2,1,0:T(8,128)(2,1)} collective-permute-done((bf16[2,48,1536]{2,1,0:T(8,128)(2,1)}, bf16[2,48,1536]{2,1,0:T(8,128)(2,1)}, u32[]{:S(2)}, u32[]{:S(2)}) %collective-permute-start.1) | collective-permute-done | bytes 294944 | tf_op jit(solution)/shard_map/ppermute | solution.py:377
  57.1 1.3 pad_maximum_fusion.1
  58.7 2.4 %collective-permute-done.7.far_ref = bf16[3,2,48,1536]{3,2,1,0:T(8,128)(2,1)S(1)} collective-permute-done((bf16[3,2,48,1536]{3,2,1,0:T(8,128)(2,1)S(1)}, bf16[3,2,48,1536]{3,2,1,0:T(8,128)(2,1)S(1)}, u32[]{:S(2)}, u32[]{:S(2)}) %collective-permute-start.7) | collective-permute-done | bytes 884768 | tf_op jit(solution)/shard_map/ppermute | solution.py:401
  61.1 2.1 %project.3 = bf16[1,1,256,384]{3,2,1,0:T(8,128)(2,1)S(1)} custom-call(s32[3]{0:T(128)S(1)} %pad_add_fusion.pos_ref.refs_0_, bf16[256,1536]{1,0:T(8,128)(2,1)S(1)} %bitcast.32, bf16[3,96,1536]{2,1,0:T(8,128)(2,1)S(1)} %bitcast.34, bf16[2,48,1536]{2,1,0:T(8,128)(2,1)} %collective-permute-done.n0_ref, bf16[2,48,1536]{2,1,0:T(8,128)(2,1)} %collective-permute-done.1.n1_ref, ...), custom_call_target="tpu_custom_call" | custom-call | tf_op jit(solution)/shard_map/project/pallas_call | solution.py:135
  63.2 3.5 %attention.2.refs_3_ = f32[256,512]{1,0:T(8,128)S(1)} custom-call(s32[3]{0:T(128)S(1)} %pad_add_fusion.pos_ref.refs_0_, bf16[256,384]{1,0:T(8,128)(2,1)S(1)} %bitcast.36, bf16[4,2,256,384]{3,2,1,0:T(8,128)(2,1)} %project.2.refs_2_, bf16[2,154,384]{2,1,0:T(8,128)(2,1)S(1)} %bitcast.41), custom_call_target="tpu_custom_call" | custom-call | tf_op jit(solution)/shard_map/attention/pallas_call | solution.py:225
  66.8 4.6 %all-to-all-done.1.refs_2_ = bf16[4,2,256,384]{3,2,1,0:T(8,128)(2,1)S(1)} async-done(((bf16[4,2,256,384]{3,2,1,0:T(8,128)(2,1)}), bf16[4,2,256,384]{3,2,1,0:T(8,128)(2,1)S(1)}, u32[]{:S(2)}, u32[]{:S(2)}) %all-to-all-start.1) | async-done | bytes 1572896 | tf_op jit(solution)/shard_map/all_to_all | solution.py:399
  71.4 4.2 %attention.3.a_ref = bf16[256,384]{1,0:T(8,128)(2,1)S(1)} custom-call(s32[3]{0:T(128)S(1)} %pad_add_fusion.pos_ref.refs_0_, bf16[256,384]{1,0:T(8,128)(2,1)S(1)} %bitcast.37, bf16[4,2,256,384]{3,2,1,0:T(8,128)(2,1)S(1)} %all-to-all-done.1.refs_2_, f32[256,512]{1,0:T(8,128)S(1)} %attention.2.refs_3_), custom_call_target="tpu_custom_call" | custom-call | tf_op jit(solution)/shard_map/attention/pallas_call | solution.py:225
  75.7 1.8 %out_projection.1 = bf16[256,1536]{1,0:T(8,128)(2,1)S(1)} custom-call(s32[3]{0:T(128)S(1)} %pad_add_fusion.pos_ref.refs_0_, bf16[256,384]{1,0:T(8,128)(2,1)S(1)} %attention.3.a_ref, bf16[96,1536]{1,0:T(8,128)(2,1)S(1)} %copy-done.8, bf16[2,48,1536]{2,1,0:T(8,128)(2,1)} %collective-permute-done.n0_ref, bf16[2,48,1536]{2,1,0:T(8,128)(2,1)} %collective-permute-done.1.n1_ref, ...), custom_call_target="tpu_custom_call" | custom-call | tf_op jit(solution)/shard_map/out_projection/pallas_call | solution.py:254
  77.5 11.9 %all_to_all.25.part_ref = bf16[4,64,1536]{2,1,0:T(8,128)(2,1)S(1)} all-to-all(bf16[4,64,1536]{2,1,0:T(8,128)(2,1)S(1)} %bitcast.35), channel_id=1, replica_groups=mesh['zl'=2,'zp'=2,'core'=2,'tx'=4,'ty'=4,'blk'=2] {'tx'}, dimensions={0} | all-to-all | bytes 1572864 | tf_op jit(solution)/shard_map/all_to_all | solution.py:409
  89.4 0.4 second_norm.1
  89.8 12.6 %all_to_all.26 = bf16[4,64,1536]{2,1,0:T(8,128)(2,1)} all-to-all(bf16[4,64,1536]{2,1,0:T(8,128)(2,1)S(1)} %get-tuple-element.28), channel_id=1, replica_groups=mesh['zl'=2,'zp'=2,'core'=2,'tx'=4,'ty'=4,'blk'=2] {'ty'}, dimensions={0} | all-to-all | bytes 1572864 | tf_op jit(solution)/shard_map/all_to_all | solution.py:411
  102.4 7.7 %feed_forward.1 = bf16[256,1536]{1,0:T(8,128)(2,1)} custom-call(bf16[256,1536]{1,0:T(8,128)(2,1)} %bitcast.50, bf16[2,4,1536,384]{3,2,1,0:T(8,128)(2,1)} %bitcast.47, bf16[2,4,1536,384]{3,2,1,0:T(8,128)(2,1)} %bitcast.48), custom_call_target="tpu_custom_call" | custom-call | tf_op jit(solution)/shard_map/feed_forward/pallas_call | solution.py:318
  110.1 3.6 %all-to-all-start.4 = ((bf16[4,64,1536]{2,1,0:T(8,128)(2,1)}), bf16[4,64,1536]{2,1,0:T(8,128)(2,1)S(1)}, u32[]{:S(2)}, u32[]{:S(2)}) async-start(bf16[4,64,1536]{2,1,0:T(8,128)(2,1)} %bitcast.49), calls=%async_computation.4 | async-start | bytes 1572864 | tf_op jit(solution)/shard_map/all_to_all | solution.py:413
  114.7 8.5 %all-to-all-done.4.part_ref = bf16[4,64,1536]{2,1,0:T(8,128)(2,1)S(1)} async-done(((bf16[4,64,1536]{2,1,0:T(8,128)(2,1)}), bf16[4,64,1536]{2,1,0:T(8,128)(2,1)S(1)}, u32[]{:S(2)}, u32[]{:S(2)}) %all-to-all-start.4) | async-done | bytes 786464 | tf_op jit(solution)/shard_map/all_to_all | solution.py:413
  123.2 1.1 last_stage.1
  124.3 0.6 add.27
  (42 shorter events, 1.0 us)
Async XLA Ops:
  7.2 15.9 %copy-start = (bf16[1,154,2,1536]{3,2,1,0:T(2,128)(2,1)S(1)}, bf16[1,154,2,1536]{3,2,1,0:T(2,128)(2,1)}, u32[]{:S(2)}) copy-start(bf16[1,154,2,1536]{3,2,1,0:T(2,128)(2,1)} %param.14) | copy-start | bytes 2838532
  7.2 95.3 %all-gather.3.cloned.1.call-start = ((), (), s32[]{:S(2)}) async-start(), calls=%async_computation.5 | async-start | bytes 10027008 | tf_op jit(solution)/shard_map/all_gather | solution.py:383
  7.8 3.8 %copy-start.1 = (bf16[1536,3,96]{0,2,1:T(8,128)(2,1)S(1)}, bf16[1536,3,96]{0,2,1:T(8,128)(2,1)}, u32[]{:S(2)}) copy-start(bf16[1536,3,96]{0,2,1:T(8,128)(2,1)} %param.17) | copy-start | bytes 2654212
  12.3 11.7 %collective-permute-start.3 = (bf16[2,48,1536]{2,1,0:T(8,128)(2,1)}, bf16[2,48,1536]{2,1,0:T(8,128)(2,1)S(1)}, u32[]{:S(2)}, u32[]{:S(2)}) collective-permute-start(bf16[2,48,1536]{2,1,0:T(8,128)(2,1)} %dynamic-slice_bitcast_fusion), channel_id=1, source_target_pairs={{0,4},{2,6},{4,0},{6,2},{1,5},{3,7},{5,1},{7,3},{8,12},{10,14},{12... | collective-permute-start | bytes 884744 | tf_op jit(solution)/shard_map/ppermute | solution.py:377
  15.5 13.6 %collective-permute-start.4 = (bf16[2,48,1536]{2,1,0:T(8,128)(2,1)}, bf16[2,48,1536]{2,1,0:T(8,128)(2,1)S(1)}, u32[]{:S(2)}, u32[]{:S(2)}) collective-permute-start(bf16[2,48,1536]{2,1,0:T(8,128)(2,1)} %dynamic-slice_bitcast_fusion), channel_id=1, source_target_pairs={{0,2},{2,4},{4,6},{6,0},{1,3},{3,5},{5,7},{7,1},{8,10},{10,12},{12... | collective-permute-start | bytes 884744 | tf_op jit(solution)/shard_map/ppermute | solution.py:377
  16.2 13.3 %collective-permute-start.5 = (bf16[2,48,1536]{2,1,0:T(8,128)(2,1)}, bf16[2,48,1536]{2,1,0:T(8,128)(2,1)S(1)}, u32[]{:S(2)}, u32[]{:S(2)}) collective-permute-start(bf16[2,48,1536]{2,1,0:T(8,128)(2,1)} %dynamic-slice_bitcast_fusion), channel_id=1, source_target_pairs={{0,6},{2,0},{4,2},{6,4},{1,7},{3,1},{5,3},{7,5},{8,14},{10,8},{12,... | collective-permute-start | bytes 884744 | tf_op jit(solution)/shard_map/ppermute | solution.py:377
  18.8 24.2 %all-to-all-start = ((bf16[4,64,1536]{2,1,0:T(8,128)(2,1)}), bf16[4,64,1536]{2,1,0:T(8,128)(2,1)S(1)}, u32[]{:S(2)}, u32[]{:S(2)}) async-start(bf16[4,64,1536]{2,1,0:T(8,128)(2,1)} %get-tuple-element.18), calls=%async_computation | async-start | bytes 1572864 | tf_op jit(solution)/shard_map/all_to_all | solution.py:386
  23.1 7.6 %copy-start.7 = (bf16[96,1536]{1,0:T(8,128)(2,1)S(1)}, bf16[96,1536]{1,0:T(8,128)(2,1)}, u32[]{:S(2)}) copy-start(bf16[96,1536]{1,0:T(8,128)(2,1)} %own_ref.1) | copy-start | bytes 884740
  30.6 16.3 %collective-permute-start.6 = (bf16[3,2,48,1536]{3,2,1,0:T(8,128)(2,1)}, bf16[3,2,48,1536]{3,2,1,0:T(8,128)(2,1)}, u32[]{:S(2)}, u32[]{:S(2)}) collective-permute-start(bf16[3,2,48,1536]{3,2,1,0:T(8,128)(2,1)} %pad_maximum_fusion), channel_id=1, source_target_pairs={{0,32},{32,0},{1,33},{33,1},{2,34},{34,2},{3,35},{35,3},{4,36},{36... | collective-permute-start | bytes 2654216 | tf_op jit(solution)/shard_map/ppermute | solution.py:394
  42.9 11.1 %collective-permute-start = (bf16[2,48,1536]{2,1,0:T(8,128)(2,1)}, bf16[2,48,1536]{2,1,0:T(8,128)(2,1)}, u32[]{:S(2)}, u32[]{:S(2)}) collective-permute-start(bf16[2,48,1536]{2,1,0:T(8,128)(2,1)} %pad_maximum_fusion.2), channel_id=1, source_target_pairs={{0,4},{2,6},{4,0},{6,2},{1,5},{3,7},{5,1},{7,3},{8,12},{10,14},{12... | collective-permute-start | bytes 884744 | tf_op jit(solution)/shard_map/ppermute | solution.py:377
  42.9 14.1 %collective-permute-start.1 = (bf16[2,48,1536]{2,1,0:T(8,128)(2,1)}, bf16[2,48,1536]{2,1,0:T(8,128)(2,1)}, u32[]{:S(2)}, u32[]{:S(2)}) collective-permute-start(bf16[2,48,1536]{2,1,0:T(8,128)(2,1)} %pad_maximum_fusion.2), channel_id=1, source_target_pairs={{0,2},{2,4},{4,6},{6,0},{1,3},{3,5},{5,7},{7,1},{8,10},{10,12},{12... | collective-permute-start | bytes 884744 | tf_op jit(solution)/shard_map/ppermute | solution.py:377
  42.9 14.1 %collective-permute-start.2 = (bf16[2,48,1536]{2,1,0:T(8,128)(2,1)}, bf16[2,48,1536]{2,1,0:T(8,128)(2,1)}, u32[]{:S(2)}, u32[]{:S(2)}) collective-permute-start(bf16[2,48,1536]{2,1,0:T(8,128)(2,1)} %pad_maximum_fusion.2), channel_id=1, source_target_pairs={{0,6},{2,0},{4,2},{6,4},{1,7},{3,1},{5,3},{7,5},{8,14},{10,8},{12,... | collective-permute-start | bytes 884744 | tf_op jit(solution)/shard_map/ppermute | solution.py:377
  50.4 21.0 %all-to-all-start.1 = ((bf16[4,2,256,384]{3,2,1,0:T(8,128)(2,1)}), bf16[4,2,256,384]{3,2,1,0:T(8,128)(2,1)S(1)}, u32[]{:S(2)}, u32[]{:S(2)}) async-start(bf16[4,2,256,384]{3,2,1,0:T(8,128)(2,1)} %project.2.refs_2_), calls=%async_computation.1 | async-start | bytes 3145728 | tf_op jit(solution)/shard_map/all_to_all | solution.py:399
  54.0 7.0 %copy-start.2 = (bf16[1536,3,96]{0,2,1:T(8,128)(2,1)S(1)}, bf16[1536,3,96]{0,2,1:T(8,128)(2,1)}, u32[]{:S(2)}) copy-start(bf16[1536,3,96]{0,2,1:T(8,128)(2,1)} %param.17) | copy-start | bytes 2654212
  58.4 4.9 %copy-start.5 = (bf16[1,154,2,384]{3,1,2,0:T(8,128)(2,1)S(1)}, bf16[1,154,2,384]{3,1,2,0:T(8,128)(2,1)}, u32[]{:S(2)}) copy-start(bf16[1,154,2,384]{3,1,2,0:T(8,128)(2,1)} %copy.16) | copy-start | bytes 709636
  58.4 2.7 %collective-permute-start.7 = (bf16[3,2,48,1536]{3,2,1,0:T(8,128)(2,1)S(1)}, bf16[3,2,48,1536]{3,2,1,0:T(8,128)(2,1)S(1)}, u32[]{:S(2)}, u32[]{:S(2)}) collective-permute-start(bf16[3,2,48,1536]{3,2,1,0:T(8,128)(2,1)S(1)} %pad_maximum_fusion.1), channel_id=1, source_target_pairs={{0,32},{32,0},{1,33},{33,1},{2,34},{34,2},{3,35},{35,3},{4,36},{36... | collective-permute-start | bytes 2654216 | tf_op jit(solution)/shard_map/ppermute | solution.py:401
  61.1 2.2 %copy-start.3 = (bf16[3,2,48,1536]{3,2,1,0:T(8,128)(2,1)}, bf16[3,2,48,1536]{3,2,1,0:T(8,128)(2,1)S(1)}, u32[]{:S(2)}) copy-start(bf16[3,2,48,1536]{3,2,1,0:T(8,128)(2,1)S(1)} %collective-permute-done.7.far_ref) | copy-start | bytes 2654212
  71.4 4.2 %copy-start.4 = (bf16[3,2,48,1536]{3,2,1,0:T(8,128)(2,1)S(1)}, bf16[3,2,48,1536]{3,2,1,0:T(8,128)(2,1)}, u32[]{:S(2)}) copy-start(bf16[3,2,48,1536]{3,2,1,0:T(8,128)(2,1)} %copy-done.3) | copy-start | bytes 2654212
  71.4 4.2 %copy-start.8 = (bf16[96,1536]{1,0:T(8,128)(2,1)S(1)}, bf16[96,1536]{1,0:T(8,128)(2,1)}, u32[]{:S(2)}) copy-start(bf16[96,1536]{1,0:T(8,128)(2,1)} %own_ref.1) | copy-start | bytes 884740
  75.7 13.8 %copy-start.6 = (bf16[1,64,1536]{2,1,0:T(8,128)(2,1)S(1)}, bf16[1,64,1536]{2,1,0:T(8,128)(2,1)}, u32[]{:S(2)}) copy-start(bf16[1,64,1536]{2,1,0:T(8,128)(2,1)} %param.11) | copy-start | bytes 589828
  75.7 13.8 %copy-start.9 = (f32[1,8,1536]{2,1,0:T(8,128)S(1)}, f32[1,8,1536]{2,1,0:T(8,128)}, u32[]{:S(2)}) copy-start(f32[1,8,1536]{2,1,0:T(8,128)} %param.13) | copy-start | bytes 147460
  110.1 4.3 %copy-start.10 = (bf16[1536,64]{0,1:T(8,128)(2,1)S(1)}, bf16[1536,64]{0,1:T(8,128)(2,1)}, u32[]{:S(2)}) copy-start(bf16[1536,64]{0,1:T(8,128)(2,1)} %param.21) | copy-start | bytes 589828
  110.1 14.2 %copy-start.11 = (f32[1,32,128]{2,1,0:T(8,128)S(1)}, f32[1,32,128]{2,1,0:T(8,128)}, u32[]{:S(2)}) copy-start(f32[1,32,128]{2,1,0:T(8,128)} %param.12) | copy-start | bytes 49156
  110.1 13.1 %all-to-all-start.4 = ((bf16[4,64,1536]{2,1,0:T(8,128)(2,1)}), bf16[4,64,1536]{2,1,0:T(8,128)(2,1)S(1)}, u32[]{:S(2)}, u32[]{:S(2)}) async-start(bf16[4,64,1536]{2,1,0:T(8,128)(2,1)} %bitcast.49), calls=%async_computation.4 | async-start | bytes 1572864 | tf_op jit(solution)/shard_map/all_to_all | solution.py:413
Sparse Core Ops, SparseCore 0:
  11.7 67.1 all-gather.2
